TPU v7x, 32 devices: a whole 2x2x4 slice. The times are simulated.
32 devices in a mesh: parts: 2 (over y), dp: 8 (over z, x), tensor: 2 (over core).
Axes of the slice: x: 2, y: 2, z: 4, core: 2. Of those that a mesh axis runs over, the one named last changes fastest.
Arguments:
- acoustic: bfloat16 [3072, 4096], P(('parts', 'dp'), 'tensor'), parts along dimension 0, may hold values from -6 to 6
- norm_gain: float32 [4096], replicated, may hold values from 0.1 to 1.9
- up_weight: bfloat16 [64, 32, 16384], P('tensor', None, 'dp'), may hold values from -0.25 to 0.25
- down_weight: bfloat16 [64, 32, 16384], P('tensor', None, 'dp'), may hold values from -0.1875 to 0.1875
- up_keep: int32 [64, 64, 32], P(None, 'tensor'), may hold values from 0 to 1, as said below
- down_keep: int32 [64, 64, 32], P(None, 'tensor'), may hold values from 0 to 1, as said below
- language: int32 [16], P(('parts', 'dp')), parts along dimension 0, may hold values from 0 to 63
- lengths: int32 [16], P(('parts', 'dp')), parts along dimension 0, may hold values from 48 to 192, as said below
Outputs:
- encoded: bfloat16 [3072, 4096], P(('parts', 'dp'), 'tensor'), parts along dimension 0
There are 2 independent parts, one for each index of `parts`. A program takes and returns all parts, laid end to end along the dimension named above; an argument that names none is the same for every part. Nothing has to cross between parts.
Inputs may be any that keep to these rules, and one draw needn't show every extreme that they name: `up_keep`: for every language and hidden block, exactly one feature block of each aligned run of 8 (blocks k * 8 to k * 8 + 7) is kept (1), the others are 0. `down_keep`: for every language and hidden block, exactly one feature block of each aligned run of 8 is kept (1), the others are 0. `lengths`: some utterance is full in every draw.
All inputs are finite; a program needn't handle non-finite values.
Results may differ from a plain program's by a relative error of at most 0.006.
Values may be sent and summed in bfloat16 or wider, within the bound.
No kernel may reach another device: no remote copies, remote signals or barrier semaphores. Data moves between devices by JAX's collectives and lax.ppermute only.
A program may use at most 128 MiB of HBM per device.

v0:
```python
import jax
import jax.numpy as jnp
from jax import lax
from jax.sharding import PartitionSpec as P

BLK = 128
GROUP = 8


def kept_index(keep_mask):
    nlangs, hidden_blocks, feat_blocks = keep_mask.shape
    runs = feat_blocks // GROUP
    picks = jnp.arange(GROUP, dtype=jnp.int32)
    within = jnp.sum(keep_mask.reshape(nlangs, hidden_blocks, runs, GROUP) * picks, axis=-1)
    return within + jnp.arange(runs, dtype=jnp.int32) * GROUP


def body(acoustic, norm_gain, up_weight, down_weight, up_keep, down_keep, language, lengths):
    frames = acoustic.shape[0]
    nlangs, hidden_blocks, feat_blocks = up_keep.shape
    block_side = BLK
    runs = feat_blocks // GROUP
    whole = lax.all_gather(acoustic, "tensor", axis=1, tiled=True)
    widened = whole.astype(jnp.float32)
    scale = lax.rsqrt(jnp.mean(widened * widened, axis=-1, keepdims=True) + 1e-06)
    normed = (widened * scale * norm_gain).astype(jnp.bfloat16)
    languages = lax.all_gather(language, "dp", axis=0, tiled=True)
    chooser = (languages[:, None] == jnp.arange(nlangs, dtype=jnp.int32)).astype(jnp.int32)
    own_pick = (language[0] == jnp.arange(nlangs, dtype=jnp.int32)).astype(jnp.int32)
    up_table = kept_index(up_keep)
    down_table = kept_index(down_keep)
    up_wanted = jnp.einsum("nl,lhg->nhg", chooser, up_table)
    down_wanted = jnp.einsum("nl,lhg->nhg", chooser, down_table)
    own_up = jnp.einsum("l,lhg->hg", own_pick, up_table)
    own_down = jnp.einsum("l,lhg->hg", own_pick, down_table)
    row_index = jnp.arange(hidden_blocks, dtype=jnp.int32)[None, :, None]
    send_up = up_weight[row_index, up_wanted]
    send_down = down_weight[row_index, down_wanted]
    got_up = lax.all_to_all(send_up, "dp", split_axis=0, concat_axis=3, tiled=True)
    got_down = None
    up_local = got_up[0].reshape(hidden_blocks, runs, block_side, block_side)
    chosen = normed.reshape(frames, feat_blocks, block_side)[:, own_up]
    before = jnp.einsum("thgi,hgij->thj", chosen, up_local, preferred_element_type=jnp.float32)
    active = jax.nn.silu(before).astype(jnp.bfloat16)
    got_down = lax.all_to_all(send_down, "dp", split_axis=0, concat_axis=3, tiled=True)
    down_local = got_down[0].reshape(hidden_blocks, runs, block_side, block_side)
    pieces = []
    for run_at in range(runs):
        contrib = jnp.einsum(
            "thi,hij->thj", active, down_local[:, run_at], preferred_element_type=jnp.float32
        )
        targets = run_at * GROUP + jnp.arange(GROUP, dtype=jnp.int32)
        onehot = (own_down[:, run_at, None] == targets).astype(jnp.float32)
        pieces.append(jnp.einsum("thj,hk->tkj", contrib, onehot, precision=lax.Precision.HIGHEST))
    partial_value = jnp.concatenate(pieces, axis=1).reshape(frames, feat_blocks * block_side)
    feedfwd = lax.psum_scatter(
        partial_value.astype(jnp.bfloat16), "tensor", scatter_dimension=1, tiled=True
    ).astype(jnp.float32)
    valid = (jnp.arange(frames, dtype=jnp.int32) < lengths[0]).astype(jnp.float32)
    return ((acoustic.astype(jnp.float32) + feedfwd) * valid[:, None]).astype(jnp.bfloat16)


def solution(mesh):
    in_specs = (
        P(("parts", "dp"), "tensor"),
        P(),
        P("tensor", None, "dp"),
        P("tensor", None, "dp"),
        P(None, "tensor", None),
        P(None, "tensor", None),
        P(("parts", "dp")),
        P(("parts", "dp")),
    )
    out_specs = P(("parts", "dp"), "tensor")
    return jax.shard_map(body, mesh=mesh, in_specs=in_specs, out_specs=out_specs, check_vma=False)
```

profile of v0, /device:TPU:0, one launch (start us, length us, event | category | flops | bytes accessed | tf_op | source)
XLA Modules:
  0.0 303.2 jit_solution(4104737795416634155)
XLA Ops:
  7.2 1.3 dynamic-slice
  8.5 0.7 dynamic-update-slice
  9.2 13.1 %all-reduce = s32[8]{0:T(128)S(1)} all-reduce(s32[8]{0:T(128)S(1)} %dynamic-update-slice), channel_id=1, replica_groups=mesh['parts'=2,'dp'=8,'tensor'=2] {'dp'}, use_global_device_ids=true, to_apply=%add | all-reduce | flops 8 | bytes 64
  22.3 1.6 fusion.40
  23.8 0.1 broadcast_add_fusion.1
  23.9 0.3 fusion.61
  24.2 0.1 copy.33
  24.4 0.1 reshape.56
  24.5 25.4 %gather_fusion.1 = bf16[1024,2048]{1,0:T(8,128)(2,1)} fusion(bf16[32,32,2048]{2,1,0:T(8,128)(2,1)} %param.10, s32[1024]{0:T(1024)S(1)} %reshape.56), kind=kCustom, calls=%fused_computation.1 | custom fusion | bytes 8396800 | tf_op jit(solution)/shard_map/gather | solution.py:37
  49.9 7.2 %reshape.59 = bf16[8,32,4,2048]{3,2,1,0:T(4,128)(2,1)} reshape(bf16[1024,2048]{1,0:T(8,128)(2,1)} %gather_fusion.1) | data formatting | bytes 8388608 | tf_op jit(solution)/shard_map/gather | solution.py:37
  57.1 4.6 %all-to-all-start.1 = ((bf16[8,32,4,2048]{3,2,1,0:T(4,128)(2,1)}), bf16[8,32,4,2048]{3,2,1,0:T(4,128)(2,1)}, u32[]{:S(2)}, u32[]{:S(2)}) async-start(bf16[8,32,4,2048]{3,2,1,0:T(4,128)(2,1)} %reshape.59), calls=%async_computation.1 | async-start | bytes 8388608 | tf_op jit(solution)/shard_map/all_to_all | solution.py:39
  61.7 0.3 fusion.75
  62.0 0.1 copy.29
  62.1 0.1 reshape.50
  62.2 25.4 %gather_fusion = bf16[1024,2048]{1,0:T(8,128)(2,1)} fusion(bf16[32,32,2048]{2,1,0:T(8,128)(2,1)} %param.11, s32[1024]{0:T(1024)S(1)} %reshape.50), kind=kCustom, calls=%fused_computation | custom fusion | bytes 8396800 | tf_op jit(solution)/shard_map/gather | solution.py:38
  87.6 7.2 %reshape.53 = bf16[8,32,4,2048]{3,2,1,0:T(4,128)(2,1)} reshape(bf16[1024,2048]{1,0:T(8,128)(2,1)} %gather_fusion) | data formatting | bytes 8388608 | tf_op jit(solution)/shard_map/gather | solution.py:38
  94.8 0.0 copy-start.2
  94.8 57.4 %all-to-all-done.1 = bf16[8,32,4,2048]{3,2,1,0:T(4,128)(2,1)} async-done(((bf16[8,32,4,2048]{3,2,1,0:T(4,128)(2,1)}), bf16[8,32,4,2048]{3,2,1,0:T(4,128)(2,1)}, u32[]{:S(2)}, u32[]{:S(2)}) %all-to-all-start.1) | async-done | bytes 4194336 | tf_op jit(solution)/shard_map/all_to_all | solution.py:39
  152.2 4.6 %all-to-all-start = ((bf16[8,32,4,2048]{3,2,1,0:T(4,128)(2,1)}), bf16[8,32,4,2048]{3,2,1,0:T(4,128)(2,1)}, u32[]{:S(2)}, u32[]{:S(2)}) async-start(bf16[8,32,4,2048]{3,2,1,0:T(4,128)(2,1)} %reshape.53), calls=%async_computation | async-start | bytes 8388608 | tf_op jit(solution)/shard_map/all_to_all | solution.py:45
  156.8 0.0 all-gather.2.cloned.1.call-start
  156.9 0.7 all-gather.2.cloned.1.call-update
  157.6 0.2 reduce-scatter.2.cloned.1.call-start
  157.8 0.3 fusion.42
  158.1 0.1 copy.44
  158.2 0.1 reshape.64
  158.3 0.3 fusion.46
  158.6 11.8 %all-gather.2.cloned.1.call-done = bf16[192,4096]{1,0:T(8,128)(2,1)} async-done(((bf16[192,2048]{1,0:T(8,128)(2,1)}), bf16[192,4096]{1,0:T(8,128)(2,1)}) %all-gather.2.cloned.1.call-update) | async-done | bytes 1572880 | tf_op jit(solution)/shard_map/all_gather | solution.py:23
  170.4 1.8 fusion
  172.2 0.0 copy-done.2
  172.2 2.0 copy_bitcast_fusion.1
  174.2 4.0 %gather_fusion.2 = bf16[128,192,128]{2,1,0:T(8,128)(2,1)} fusion(bf16[192,32,128]{2,0,1:T(8,128)(2,1)S(1)} %copy_bitcast_fusion.1, s32[1024]{0:T(1024)S(1)} %pad_clamp_fusion), kind=kCustom, calls=%fused_computation.2 | custom fusion | bytes 12583424 | tf_op jit(solution)/shard_map/gather | solution.py:42
  178.2 8.6 %copy.34 = bf16[1,32,4,8,2048]{4,3,2,1,0:T(8,128)(2,1)} copy(bf16[1,32,4,8,2048]{4,2,1,3,0:T(4,128)(2,1)} %bitcast.15) | data formatting | bytes 8388608 | tf_op jit(solution)/shard_map/all_to_all | solution.py:39
  186.8 7.4 %reshape_squeeze.7 = bf16[32,4,128,128]{3,2,1,0:T(8,128)(2,1)} reshape(bf16[1,32,4,8,2048]{4,3,2,1,0:T(8,128)(2,1)} %copy.34) | data formatting | bytes 8388608 | tf_op jit(solution)/shard_map/reshape;squeeze | solution.py:41
  194.2 55.2 %all-to-all-done = bf16[8,32,4,2048]{3,2,1,0:T(4,128)(2,1)} async-done(((bf16[8,32,4,2048]{3,2,1,0:T(4,128)(2,1)}), bf16[8,32,4,2048]{3,2,1,0:T(4,128)(2,1)}, u32[]{:S(2)}, u32[]{:S(2)}) %all-to-all-start) | async-done | bytes 4194336 | tf_op jit(solution)/shard_map/all_to_all | solution.py:45
  249.3 6.5 %copy.46 = bf16[1,32,4,8,2048]{4,3,1,2,0:T(8,128)(2,1)} copy(bf16[1,32,4,8,2048]{4,2,1,3,0:T(4,128)(2,1)} %bitcast.10) | data formatting | bytes 8388608 | tf_op jit(solution)/shard_map/reshape;squeeze | solution.py:46
  255.8 7.4 %reshape.97 = bf16[32,4,128,128]{3,2,0,1:T(8,128)(2,1)} reshape(bf16[1,32,4,8,2048]{4,3,1,2,0:T(8,128)(2,1)} %copy.46) | data formatting | bytes 8388608 | tf_op jit(solution)/shard_map/reshape;squeeze | solution.py:46
  263.3 0.0 copy-start
  263.3 6.0 %fusion.14 = bf16[192,32,128]{2,0,1:T(8,128)(2,1)S(1)} fusion(bf16[192,32,4,128]{3,0,2,1:T(8,128)(2,1)} %bitcast.139, bf16[32,4,128,128]{3,2,1,0:T(8,128)(2,1)} %reshape_squeeze.7), kind=kOutput, calls=%fused_computation.21 | convolution fusion | flops 809238528 | bytes 12058624 | tf_op jit(solution)/shard_map/thgi,hgij->thj/dot_general | solution.py:43
  269.2 0.0 copy-done
  269.2 0.6 convolution_bitcast_fusion.1
  269.8 0.6 convolution_bitcast_fusion.2
  270.4 0.6 convolution_bitcast_fusion.3
  270.9 0.6 convolution_bitcast_fusion
  271.5 2.9 fusion.37
  274.4 3.0 fusion.31
  277.4 3.2 %fusion.34 = bf16[192,8,128]{2,1,0:T(8,128)(2,1)S(1)} fusion(f32[192,32,128]{2,0,1:T(8,128)S(1)} %convolution_bitcast_fusion.2, s32[32]{0:T(128)S(1)} %get-tuple-element.8, s32[8]{0:T(128)S(1)} %iota_add_fusion.2), kind=kOutput, calls=%fused_computation.37 | convolution fusion | flops 75694336 | bytes 3539104 | tf_op jit(solution)/shard_map/thj,hk->tkj/dot_general | solution.py:54
  280.6 3.0 fusion.28
  283.6 0.3 pad_maximum_fusion
  283.9 0.0 copy-start.1
  283.9 1.9 copy.104
  285.8 0.0 reduce-scatter.2.cloned.1.call-update
  286.4 7.6 %reduce-scatter.2.cloned.1.call-done = bf16[192,2048]{1,0:T(8,128)(2,1)} async-done(((bf16[192,4096]{1,0:T(8,128)(2,1)}), bf16[192,2048]{1,0:T(8,128)(2,1)}) %reduce-scatter.2.cloned.1.call-update) | async-done | bytes 786448 | tf_op jit(solution)/shard_map/reduce_scatter | solution.py:56
  294.1 0.0 copy-done.1
  294.1 2.3 multiply_convert_fusion
  (10 shorter events, 0.0 us)
Async XLA Ops:
  57.1 95.2 %all-to-all-start.1 = ((bf16[8,32,4,2048]{3,2,1,0:T(4,128)(2,1)}), bf16[8,32,4,2048]{3,2,1,0:T(4,128)(2,1)}, u32[]{:S(2)}, u32[]{:S(2)}) async-start(bf16[8,32,4,2048]{3,2,1,0:T(4,128)(2,1)} %reshape.59), calls=%async_computation.1 | async-start | bytes 8388608 | tf_op jit(solution)/shard_map/all_to_all | solution.py:39
  94.8 77.3 %copy-start.2 = (f32[4096]{0:T(1024)S(1)}, f32[4096]{0:T(1024)}, u32[]{:S(2)}) copy-start(f32[4096]{0:T(1024)} %param.9) | copy-start | bytes 49156
  152.2 97.1 %all-to-all-start = ((bf16[8,32,4,2048]{3,2,1,0:T(4,128)(2,1)}), bf16[8,32,4,2048]{3,2,1,0:T(4,128)(2,1)}, u32[]{:S(2)}, u32[]{:S(2)}) async-start(bf16[8,32,4,2048]{3,2,1,0:T(4,128)(2,1)} %reshape.53), calls=%async_computation | async-start | bytes 8388608 | tf_op jit(solution)/shard_map/all_to_all | solution.py:45
  156.8 13.6 %all-gather.2.cloned.1.call-start = ((), (), s32[]{:S(2)}) async-start(), calls=%async_computation.3 | async-start | bytes 2359296 | tf_op jit(solution)/shard_map/all_gather | solution.py:23
  157.6 136.5 %reduce-scatter.2.cloned.1.call-start = ((), (), s32[]{:S(2)}) async-start(), calls=%async_computation.4 | async-start | bytes 2359296 | tf_op jit(solution)/shard_map/reduce_scatter | solution.py:56
  263.3 6.0 %copy-start = (bf16[32,4,128,128]{3,2,0,1:T(8,128)(2,1)S(1)}, bf16[32,4,128,128]{3,2,0,1:T(8,128)(2,1)}, u32[]{:S(2)}) copy-start(bf16[32,4,128,128]{3,2,0,1:T(8,128)(2,1)} %reshape.97) | copy-start | bytes 12582916
  283.9 10.2 %copy-start.1 = (bf16[192,2048]{1,0:T(8,128)(2,1)S(1)}, bf16[192,2048]{1,0:T(8,128)(2,1)}, u32[]{:S(2)}) copy-start(bf16[192,2048]{1,0:T(8,128)(2,1)} %param.8) | copy-start | bytes 2359300
Sparse Core Ops, SparseCore 0:
  159.2 11.1 all-gather.1
  285.9 8.1 reduce-scatter.1
where the time goes:
time: 305 us; the launch traced here: 303 us
  waiting for transfers between devices  133 us (44%)
  local copies, waits for them, and re-layouts  104 us (34%)
  matrix products  21.4 us (7%)
  between operations  14.9 us (5%)
  blocking collectives  13.1 us (4%)
  starting transfers between devices  9.41 us (3%)
  other arithmetic  8.02 us (3%)
    all_to_all x1, waiting for transfers between devices, body(): lax.all_to_all(send_up, 'dp', split_axis=0, concat_axis=3, tiled=True)  57.4 us
    all_to_all x1, waiting for transfers between devices, body(): lax.all_to_all(send_down, 'dp', split_axis=0, concat_axis=3, tiled=True)  55.2 us
    gather x2, local copies, waits for them, and re-layouts, body(): send_down = down_weight[row_index, down_wanted]  32.6 us
    gather x2, local copies, waits for them, and re-layouts, body(): send_up = up_weight[row_index, up_wanted]  32.6 us
    another operation x2, local copies, waits for them, and re-layouts, body(): got_down[0].reshape(hidden_blocks, runs, block_side, block_side)  13.9 us
    unnamed x1, blocking collectives  13.1 us
    dot_general x4, matrix products, body(): jnp.einsum('thj,hk->tkj', contrib, onehot, precision=lax.Precision.HIGHEST)  12.1 us
    all_gather x1, waiting for transfers between devices, body(): whole = lax.all_gather(acoustic, 'tensor', axis=1, tiled=True)  11.8 us
  transfers between devices with their start and end apart: 4, of which 4 were waited for; matrix products, arithmetic and copies ran while one was open for 19% of the time, Pallas kernels for 0%

commit v1 on v0

--- a/solution.py
+++ b/solution.py
@@ -1,21 +1,263 @@
+import functools
+
 import jax
 import jax.numpy as jnp
 from jax import lax
+from jax.experimental import pallas as pl
+from jax.experimental.pallas import tpu as pltpu
 from jax.sharding import PartitionSpec as P
 
 BLK = 128
 GROUP = 8
-
-
-def kept_index(keep_mask):
+HSTEP = 4
+
+
+def kept_within(keep_mask):
     nlangs, hidden_blocks, feat_blocks = keep_mask.shape
     runs = feat_blocks // GROUP
     picks = jnp.arange(GROUP, dtype=jnp.int32)
-    within = jnp.sum(keep_mask.reshape(nlangs, hidden_blocks, runs, GROUP) * picks, axis=-1)
-    return within + jnp.arange(runs, dtype=jnp.int32) * GROUP
-
-
-def body(acoustic, norm_gain, up_weight, down_weight, up_keep, down_keep, language, lengths):
+    return jnp.sum(keep_mask.reshape(nlangs, hidden_blocks, runs, GROUP) * picks, axis=-1)
+
+
+def kept_index(keep_mask):
+    within = kept_within(keep_mask)
+    return within + jnp.arange(within.shape[-1], dtype=jnp.int32) * GROUP
+
+
+def pick_kernel(which, wanted, weight_ref, *refs, rows, runs):
+    out_refs, spread = refs[:-1], refs[-1]
+    step = pl.program_id(0)
+    for h in range(HSTEP):
+        for row in range(rows):
+            tile = weight_ref[h, :, row * BLK:(row + 1) * BLK].astype(jnp.float32)
+            for g in range(runs):
+                spread[h * runs + g, row * GROUP:(row + 1) * GROUP, :] = tile[g * GROUP:(g + 1) * GROUP]
+    for u, out_ref in enumerate(out_refs):
+        for h in range(HSTEP):
+            for g in range(runs):
+                at = wanted[u, (step * HSTEP + h) * runs + g]
+                block = spread[h * runs + g, pl.ds(at, rows, stride=GROUP), :]
+                out_ref[h, g] = block.astype(jnp.bfloat16)
+
+
+def pick_blocks(weight, wanted, which, runs):
+    hidden_blocks, _, width = weight.shape
+    rows = width // BLK
+    utts = wanted.shape[0]
+    out_shape = jax.ShapeDtypeStruct((hidden_blocks, runs, rows, BLK), jnp.bfloat16)
+    out_spec = pl.BlockSpec((HSTEP, runs, rows, BLK), lambda i, *_: (i, 0, 0, 0))
+    return pl.pallas_call(
+        functools.partial(pick_kernel, rows=rows, runs=runs),
+        grid_spec=pltpu.PrefetchScalarGridSpec(
+            num_scalar_prefetch=2,
+            grid=(hidden_blocks // HSTEP,),
+            in_specs=[pl.BlockSpec((HSTEP, runs * GROUP, width), lambda i, which, wanted: (i, which[0], 0))],
+            out_specs=[out_spec] * utts,
+            scratch_shapes=[pltpu.VMEM((HSTEP * runs, rows * GROUP, BLK), jnp.float32)],
+        ),
+        out_shape=[out_shape] * utts,
+        name="pick_blocks",
+    )(which, wanted, weight)
+
+
+def fill_weights(held, weight_refs, owner, h, runs, rows):
+    for k, ref in enumerate(weight_refs):
+        start = pl.multiple_of(owner[k] * rows, rows)
+        for g in range(runs):
+            held[g, pl.ds(start, rows), :] = ref[h, g]
+
+
+def up_kernel(owner, slots, normed_ref, *refs, runs, rows):
+    weight_refs, active_ref, held = refs[:-2], refs[-2], refs[-1]
+    step = pl.program_id(0)
+    for h in range(HSTEP):
+        fill_weights(held.at[h], weight_refs, owner, h, runs, rows)
+    for h in range(HSTEP):
+        before = None
+        for g in range(runs):
+            slot = slots[(step * HSTEP + h) * runs + g]
+            term = jnp.dot(normed_ref[slot], held[h, g], preferred_element_type=jnp.float32)
+            before = term if before is None else before + term
+        active_ref[h] = (before / (1.0 + jnp.exp(-before))).astype(jnp.bfloat16)
+
+
+def up_project(owner, slots, normed, weights):
+    hidden_blocks, runs, rows, _ = weights[0].shape
+    slots_all, frames, _ = normed.shape
+    return pl.pallas_call(
+        functools.partial(up_kernel, runs=runs, rows=rows),
+        grid_spec=pltpu.PrefetchScalarGridSpec(
+            num_scalar_prefetch=2,
+            grid=(hidden_blocks // HSTEP,),
+            in_specs=[pl.BlockSpec((slots_all, frames, BLK), lambda i, *_: (0, 0, 0))]
+            + [pl.BlockSpec((HSTEP, runs, rows, BLK), lambda i, *_: (i, 0, 0, 0))] * len(weights),
+            out_specs=pl.BlockSpec((HSTEP, frames, BLK), lambda i, *_: (i, 0, 0)),
+            scratch_shapes=[pltpu.VMEM((HSTEP, runs, BLK, BLK), jnp.bfloat16)],
+        ),
+        out_shape=jax.ShapeDtypeStruct((hidden_blocks, frames, BLK), jnp.bfloat16),
+        name="up_project",
+    )(owner, slots, normed, *weights)
+
+
+def down_steps(owner, wanted, active_ref, weight_refs, held, total, runs, rows):
+    step = pl.program_id(0)
+
+    @pl.when(step == 0)
+    def _():
+        total[...] = jnp.zeros_like(total)
+
+    for h in range(HSTEP):
+        fill_weights(held.at[h], weight_refs, owner, h, runs, rows)
+    for h in range(HSTEP):
+        for g in range(runs):
+            at = g * GROUP + wanted[(step * HSTEP + h) * runs + g]
+            total[at] += jnp.dot(active_ref[h], held[h, g], preferred_element_type=jnp.float32)
+
+
+def down_other_kernel(owner, wanted, active_ref, *refs, runs, rows):
+    weight_refs, out_ref, held, total = refs[:-3], refs[-3], refs[-2], refs[-1]
+    down_steps(owner, wanted, active_ref, weight_refs, held, total, runs, rows)
+
+    @pl.when(pl.program_id(0) == pl.num_programs(0) - 1)
+    def _():
+        out_ref[...] = total[...].astype(jnp.bfloat16)
+
+
+def down_own_kernel(owner, wanted, length, active_ref, acoustic_ref, peer_ref, *refs, runs, rows):
+    weight_refs, out_ref, held, total = refs[:-3], refs[-3], refs[-2], refs[-1]
+    down_steps(owner, wanted, active_ref, weight_refs, held, total, runs, rows)
+
+    @pl.when(pl.program_id(0) == pl.num_programs(0) - 1)
+    def _():
+        frames = out_ref.shape[0]
+        valid = lax.broadcasted_iota(jnp.int32, (frames, BLK), 0) < length[0]
+        for d in range(runs * GROUP):
+            lanes = slice(d * BLK, (d + 1) * BLK)
+            feedfwd = total[d].astype(jnp.bfloat16).astype(jnp.float32) + peer_ref[d].astype(jnp.float32)
+            summed = acoustic_ref[:, lanes].astype(jnp.float32) + feedfwd
+            out_ref[:, lanes] = jnp.where(valid, summed, 0.0).astype(jnp.bfloat16)
+
+
+def down_project(owner, wanted, active, weights, final=None):
+    hidden_blocks, runs, rows, _ = weights[0].shape
+    frames = active.shape[1]
+    outs = runs * GROUP
+    in_specs = [pl.BlockSpec((HSTEP, frames, BLK), lambda i, *_: (i, 0, 0))]
+    weight_specs = [pl.BlockSpec((HSTEP, runs, rows, BLK), lambda i, *_: (i, 0, 0, 0))] * len(weights)
+    scratch = [pltpu.VMEM((HSTEP, runs, BLK, BLK), jnp.bfloat16), pltpu.VMEM((outs, frames, BLK), jnp.float32)]
+    if final is None:
+        return pl.pallas_call(
+            functools.partial(down_other_kernel, runs=runs, rows=rows),
+            grid_spec=pltpu.PrefetchScalarGridSpec(
+                num_scalar_prefetch=2,
+                grid=(hidden_blocks // HSTEP,),
+                in_specs=in_specs + weight_specs,
+                out_specs=pl.BlockSpec((outs, frames, BLK), lambda i, *_: (0, 0, 0)),
+                scratch_shapes=scratch,
+            ),
+            out_shape=jax.ShapeDtypeStruct((outs, frames, BLK), jnp.bfloat16),
+            name="down_other",
+        )(owner, wanted, active, *weights)
+    lengths, acoustic, peer = final
+    in_specs += [
+        pl.BlockSpec((frames, outs * BLK), lambda i, *_: (0, 0)),
+        pl.BlockSpec((outs, frames, BLK), lambda i, *_: (0, 0, 0)),
+    ]
+    return pl.pallas_call(
+        functools.partial(down_own_kernel, runs=runs, rows=rows),
+        grid_spec=pltpu.PrefetchScalarGridSpec(
+            num_scalar_prefetch=3,
+            grid=(hidden_blocks // HSTEP,),
+            in_specs=in_specs + weight_specs,
+            out_specs=pl.BlockSpec((frames, outs * BLK), lambda i, *_: (0, 0)),
+            scratch_shapes=scratch,
+        ),
+        out_shape=jax.ShapeDtypeStruct((frames, outs * BLK), jnp.bfloat16),
+        name="down_own",
+    )(owner, wanted, lengths, active, acoustic, peer, *weights)
+
+
+def swap(value, axis, size, step):
+    return lax.ppermute(value, axis, [(i, i ^ step) for i in range(size)])
+
+
+def split_body(acoustic, norm_gain, up_weight, down_weight, up_keep, down_keep, language, lengths, *, dp):
+    frames, features = acoustic.shape
+    nlangs, hidden_blocks, feat_blocks = up_keep.shape
+    runs = feat_blocks // GROUP
+    own_runs = runs // 2
+    here = lax.axis_index("dp").astype(jnp.int32)
+    core = lax.axis_index("tensor").astype(jnp.int32)
+    order = list(range(dp // 2, dp)) + list(range(1, dp // 2))
+    heard = {k: swap(language, "dp", dp, k) for k in order}
+    heard[0] = language
+    far = order[:dp // 2]
+    near = order[dp // 2:] + [0]
+    up_table = kept_within(up_keep)
+    down_table = kept_within(down_keep)
+    core_first = jnp.where(
+        core == 0, down_table, jnp.concatenate([down_table[..., own_runs:], down_table[..., :own_runs]], axis=-1)
+    )
+
+    def wanted_of(peers, table):
+        langs = jnp.concatenate([heard[k] for k in peers])
+        chooser = (langs[:, None] == jnp.arange(nlangs, dtype=jnp.int32)).astype(jnp.int32)
+        return jnp.einsum("nl,lhg->nhg", chooser, table)
+
+    def flat(table):
+        return table.reshape(table.shape[0], -1)
+
+    zero = jnp.zeros((1,), jnp.int32)
+    up_sent, other_sent, own_sent = {}, {}, {}
+    wanted_up = {}
+    wanted_down = {}
+    for name, peers in (("far", far), ("near", near)):
+        wanted_up[name] = wanted_of(peers, up_table)
+        blocks = pick_blocks(up_weight, flat(wanted_up[name]), zero, runs)
+        up_sent.update(zip(peers, blocks))
+    for name, peers in (("far", far), ("near", near)):
+        wanted_down[name] = wanted_of(peers, core_first)
+        other = pick_blocks(down_weight, flat(wanted_down[name][..., own_runs:]), 1 - core[None], own_runs)
+        other_sent.update(zip(peers, other))
+    for name, peers in (("far", far), ("near", near)):
+        own = pick_blocks(down_weight, flat(wanted_down[name][..., :own_runs]), core[None], own_runs)
+        own_sent.update(zip(peers, own))
+    ranks = [0] + order
+    owner = jnp.stack([here ^ k for k in ranks])
+
+    def exchange(sent):
+        return [sent[0]] + [swap(sent[k], "dp", dp, k) for k in order]
+
+    up_got = exchange(up_sent)
+    other_got = exchange(other_sent)
+    own_got = exchange(own_sent)
+
+    peer_acoustic = swap(acoustic, "tensor", 2, 1)
+    gains = norm_gain.reshape(2, features)
+    gain_own = jnp.where(core == 0, gains[0], gains[1])
+    gain_peer = jnp.where(core == 0, gains[1], gains[0])
+    wide_own = acoustic.astype(jnp.float32)
+    wide_peer = peer_acoustic.astype(jnp.float32)
+    square = jnp.sum(wide_own * wide_own, axis=-1, keepdims=True) + jnp.sum(wide_peer * wide_peer, axis=-1, keepdims=True)
+    scale = lax.rsqrt(square / (2 * features) + 1e-06)
+    normed = jnp.concatenate(
+        [
+            (wide * scale * gain).astype(jnp.bfloat16).reshape(frames, -1, BLK).transpose(1, 0, 2)
+            for wide, gain in ((wide_own, gain_own), (wide_peer, gain_peer))
+        ]
+    )
+    up_own = wanted_up["near"][-1] + jnp.arange(runs, dtype=jnp.int32) * GROUP
+    slots = (up_own ^ (core * (feat_blocks // 2))).reshape(-1)
+    active = up_project(owner, slots, normed, up_got)
+    down_own = wanted_down["near"][-1]
+    partial_other = down_project(owner, down_own[:, own_runs:].reshape(-1), active, other_got)
+    peer_partial = swap(partial_other, "tensor", 2, 1)
+    return down_project(
+        owner, down_own[:, :own_runs].reshape(-1), active, own_got, final=(lengths, acoustic, peer_partial)
+    )
+
+
+def exchange_body(acoustic, norm_gain, up_weight, down_weight, up_keep, down_keep, language, lengths):
     frames = acoustic.shape[0]
     nlangs, hidden_blocks, feat_blocks = up_keep.shape
     block_side = BLK
@@ -72,4 +314,8 @@
         P(("parts", "dp")),
     )
     out_specs = P(("parts", "dp"), "tensor")
+    dp = mesh.shape["dp"]
+    rows = BLK // dp
+    whole_tiles = mesh.shape["tensor"] == 2 and dp & (dp - 1) == 0 and rows % 16 == 0
+    body = functools.partial(split_body, dp=dp) if whole_tiles else exchange_body
     return jax.shard_map(body, mesh=mesh, in_specs=in_specs, out_specs=out_specs, check_vma=False)

time: 305 us -> 284 us (0.931)
  the two profiles are of different devices: /device:TPU:0 before, /device:TPU:8 now
where the time goes in v1:
time: 284 us; the launch traced here: 282 us
  waiting for transfers between devices  160 us (56%)
  Pallas kernels  65.2 us (23%)
  starting transfers between devices  34.7 us (12%)
  other arithmetic  10 us (4%)
  local copies, waits for them, and re-layouts  8.54 us (3%)
    ppermute x30, waiting for transfers between devices, swap(): return lax.ppermute(value, axis, [(i, i ^ step) for i in range(size)])  160 us
    pallas_call x6, Pallas kernels, pick_blocks(): pl.pallas_call(functools.partial(pick_kernel, rows=rows, runs=runs), grid...  40.3 us
    ppermute x30, starting transfers between devices, swap(): return lax.ppermute(value, axis, [(i, i ^ step) for i in range(size)])  34.7 us
    pallas_call x1, Pallas kernels, up_project(): pl.pallas_call(functools.partial(up_kernel, runs=runs, rows=rows), grid_s...  8.89 us
    pallas_call x1, Pallas kernels, down_project(): pl.pallas_call(functools.partial(down_own_kernel, runs=runs, rows=rows),...  8.5 us
    pallas_call x1, Pallas kernels, down_project(): pl.pallas_call(functools.partial(down_other_kernel, runs=runs, rows=rows)...  7.49 us
  transfers between devices with their start and end apart: 30, of which 13 were waited for; matrix products, arithmetic and copies ran while one was open for 7% of the time, Pallas kernels for 17%

profile of v1, /device:TPU:8, one launch (start us, length us, event | category | flops | bytes accessed | tf_op | source)
XLA Modules:
  0.0 281.8 jit_solution(12326525899718253817)
XLA Ops:
  0.0 1.5 collective-permute-start
  1.5 0.4 collective-permute-start.1
  1.9 1.5 collective-permute-start.2
  3.5 2.6 collective-permute-start.4
  6.1 1.4 fusion
  8.1 1.2 fusion.8
  9.8 0.6 stack.35.owner
  10.4 1.3 collective-permute-start.5
  11.7 1.6 collective-permute-start.6
  13.3 0.4 collective-permute-start.7
  13.7 2.0 pad_add_fusion
  15.6 0.3 fusion.10
  15.9 0.3 fusion.14
  16.4 0.7 copy.41.wanted
  17.1 6.4 %pick_blocks.8 = (bf16[32,2,16,128]{3,2,1,0:T(8,128)(2,1)}, bf16[32,2,16,128]{3,2,1,0:T(8,128)(2,1)}, bf16[32,2,16,128]{3,2,1,0:T(8,128)(2,1)}, bf16[32,2,16,128]{3,2,1,0:T(8,128)(2,1)}) custom-call(s32[1]{0:T(128)S(6)} %sub.4.which, s32[4,64]{1,0:T(4,128)} %copy.41.wanted, bf16[32,32,2048]{2,1,0:T(8,128)(2,1)} %weight_ref.11), custom_call_target="tpu_custom_call" | custom-call | tf_op jit(solution)/shard_map/pick_blocks/pallas_call | solution.py:49
  23.4 2.1 collective-permute-start.20
  25.6 2.7 pad_add_fusion.1
  28.3 0.3 fusion.12
  28.7 0.7 reshape.68.wanted
  29.4 7.3 %pick_blocks.6 = (bf16[32,4,16,128]{3,2,1,0:T(8,128)(2,1)}, bf16[32,4,16,128]{3,2,1,0:T(8,128)(2,1)}, bf16[32,4,16,128]{3,2,1,0:T(8,128)(2,1)}, bf16[32,4,16,128]{3,2,1,0:T(8,128)(2,1)}) custom-call(s32[1]{0:T(128)} %constant.37.clone.1.which, s32[4,128]{1,0:T(4,128)} %reshape.68.wanted, bf16[32,32,2048]{2,1,0:T(8,128)(2,1)} %weight_ref.7), custom_call_target="tpu_custom_call" | custom-call | tf_op jit(solution)/shard_map/pick_blocks/pallas_call | solution.py:49
  36.7 1.6 collective-permute-start.12
  38.6 0.4 collective-permute-start.19
  39.0 0.8 fusion.17.wanted
  39.8 0.5 add_xor_fusion.slots
  40.4 7.4 %pick_blocks.7 = (bf16[32,4,16,128]{3,2,1,0:T(8,128)(2,1)}, bf16[32,4,16,128]{3,2,1,0:T(8,128)(2,1)}, bf16[32,4,16,128]{3,2,1,0:T(8,128)(2,1)}, bf16[32,4,16,128]{3,2,1,0:T(8,128)(2,1)}) custom-call(s32[1]{0:T(128)} %constant.37.clone.1.which, s32[4,128]{1,0:T(4,128)} %fusion.17.wanted, bf16[32,32,2048]{2,1,0:T(8,128)(2,1)} %weight_ref.7), custom_call_target="tpu_custom_call" | custom-call | tf_op jit(solution)/shard_map/pick_blocks/pallas_call | solution.py:49
  47.8 0.7 copy.44.wanted
  48.5 6.5 %pick_blocks.9 = (bf16[32,2,16,128]{3,2,1,0:T(8,128)(2,1)}, bf16[32,2,16,128]{3,2,1,0:T(8,128)(2,1)}, bf16[32,2,16,128]{3,2,1,0:T(8,128)(2,1)}, bf16[32,2,16,128]{3,2,1,0:T(8,128)(2,1)}) custom-call(s32[1]{0:T(128)S(6)} %sub.4.which, s32[4,64]{1,0:T(4,128)} %copy.44.wanted, bf16[32,32,2048]{2,1,0:T(8,128)(2,1)} %weight_ref.11), custom_call_target="tpu_custom_call" | custom-call | tf_op jit(solution)/shard_map/pick_blocks/pallas_call | solution.py:49
  55.1 0.7 reshape.69.wanted
  55.8 3.1 %collective-permute-start.14 = (bf16[32,4,16,128]{3,2,1,0:T(8,128)(2,1)S(1)}, bf16[32,4,16,128]{3,2,1,0:T(8,128)(2,1)S(1)}, u32[]{:S(2)}, u32[]{:S(2)}) collective-permute-start(bf16[32,4,16,128]{3,2,1,0:T(8,128)(2,1)S(1)} %copy-done.24), channel_id=1, source_target_pairs={{0,6},{2,4},{4,2},{6,0},{8,14},{10,12},{12,10},{14,8},{1,7},{3,5},... | collective-permute-start | bytes 1572872 | tf_op jit(solution)/shard_map/ppermute | solution.py:181
  59.1 2.8 collective-permute-start.10
  61.9 3.2 %collective-permute-start.8 = (bf16[32,4,16,128]{3,2,1,0:T(8,128)(2,1)}, bf16[32,4,16,128]{3,2,1,0:T(8,128)(2,1)S(1)}, u32[]{:S(2)}, u32[]{:S(2)}) collective-permute-start(bf16[32,4,16,128]{3,2,1,0:T(8,128)(2,1)} %get-tuple-element.30), channel_id=1, source_target_pairs={{0,8},{2,10},{4,12},{6,14},{8,0},{10,2},{12,4},{14,6},{1,9},{3,11}... | collective-permute-start | bytes 1572872 | tf_op jit(solution)/shard_map/ppermute | solution.py:181
  65.1 1.0 collective-permute-start.9
  66.2 0.5 fusion.7
  66.7 5.0 %collective-permute-done.14.refs_7_ = bf16[32,4,16,128]{3,2,1,0:T(8,128)(2,1)S(1)} collective-permute-done((bf16[32,4,16,128]{3,2,1,0:T(8,128)(2,1)S(1)}, bf16[32,4,16,128]{3,2,1,0:T(8,128)(2,1)S(1)}, u32[]{:S(2)}, u32[]{:S(2)}) %collective-permute-start.14) | collective-permute-done | bytes 524320 | tf_op jit(solution)/shard_map/ppermute | solution.py:181
  71.7 1.0 collective-permute-start.21
  72.7 50.6 %collective-permute-done.10.refs_3_ = bf16[32,4,16,128]{3,2,1,0:T(8,128)(2,1)S(1)} collective-permute-done((bf16[32,4,16,128]{3,2,1,0:T(8,128)(2,1)}, bf16[32,4,16,128]{3,2,1,0:T(8,128)(2,1)S(1)}, u32[]{:S(2)}, u32[]{:S(2)}) %collective-permute-start.10) | collective-permute-done | bytes 524320 | tf_op jit(solution)/shard_map/ppermute | solution.py:181
  123.3 18.4 %collective-permute-done.11.refs_4_ = bf16[32,4,16,128]{3,2,1,0:T(8,128)(2,1)S(1)} collective-permute-done((bf16[32,4,16,128]{3,2,1,0:T(8,128)(2,1)}, bf16[32,4,16,128]{3,2,1,0:T(8,128)(2,1)S(1)}, u32[]{:S(2)}, u32[]{:S(2)}) %collective-permute-start.11) | collective-permute-done | bytes 524320 | tf_op jit(solution)/shard_map/ppermute | solution.py:181
  141.7 14.3 %collective-permute-done.8.refs_1_ = bf16[32,4,16,128]{3,2,1,0:T(8,128)(2,1)S(1)} collective-permute-done((bf16[32,4,16,128]{3,2,1,0:T(8,128)(2,1)}, bf16[32,4,16,128]{3,2,1,0:T(8,128)(2,1)S(1)}, u32[]{:S(2)}, u32[]{:S(2)}) %collective-permute-start.8) | collective-permute-done | bytes 524320 | tf_op jit(solution)/shard_map/ppermute | solution.py:181
  156.0 14.2 %collective-permute-done.9.refs_2_ = bf16[32,4,16,128]{3,2,1,0:T(8,128)(2,1)S(1)} collective-permute-done((bf16[32,4,16,128]{3,2,1,0:T(8,128)(2,1)}, bf16[32,4,16,128]{3,2,1,0:T(8,128)(2,1)S(1)}, u32[]{:S(2)}, u32[]{:S(2)}) %collective-permute-start.9) | collective-permute-done | bytes 524320 | tf_op jit(solution)/shard_map/ppermute | solution.py:181
  170.2 2.1 collective-permute-start.18
  172.3 0.4 bitcast_bitcast_fusion
  172.7 1.3 pad_maximum_fusion.normed_ref
  174.0 8.9 %up_project.1.active_ref = bf16[32,192,128]{2,1,0:T(8,128)(2,1)} custom-call(s32[8]{0:T(128)} %stack.35.owner, s32[128]{0:T(128)} %add_xor_fusion.slots, bf16[32,192,128]{2,1,0:T(8,128)(2,1)} %pad_maximum_fusion.normed_ref, bf16[32,4,16,128]{3,2,1,0:T(8,128)(2,1)} %get-tuple-element.29.refs_0_, bf16[32,4,16,128]{3,2,1,0:T(8,128)(2,1)} %copy-done.8, ...), custom_call_target="tpu_custom_call" | custom-call | tf_op jit(solution)/shard_map/up_project/pallas_call | solution.py:87
  182.9 4.1 %collective-permute-done.16.refs_2_ = bf16[32,2,16,128]{3,2,1,0:T(8,128)(2,1)S(1)} collective-permute-done((bf16[32,2,16,128]{3,2,1,0:T(8,128)(2,1)}, bf16[32,2,16,128]{3,2,1,0:T(8,128)(2,1)S(1)}, u32[]{:S(2)}, u32[]{:S(2)}) %collective-permute-start.16) | collective-permute-done | bytes 262176 | tf_op jit(solution)/shard_map/ppermute | solution.py:181
  187.0 8.1 %collective-permute-done.17.refs_3_ = bf16[32,2,16,128]{3,2,1,0:T(8,128)(2,1)S(1)} collective-permute-done((bf16[32,2,16,128]{3,2,1,0:T(8,128)(2,1)}, bf16[32,2,16,128]{3,2,1,0:T(8,128)(2,1)S(1)}, u32[]{:S(2)}, u32[]{:S(2)}) %collective-permute-start.17) | collective-permute-done | bytes 262176 | tf_op jit(solution)/shard_map/ppermute | solution.py:181
  195.1 3.1 %collective-permute-done.18.refs_4_ = bf16[32,2,16,128]{3,2,1,0:T(8,128)(2,1)S(1)} collective-permute-done((bf16[32,2,16,128]{3,2,1,0:T(8,128)(2,1)}, bf16[32,2,16,128]{3,2,1,0:T(8,128)(2,1)S(1)}, u32[]{:S(2)}, u32[]{:S(2)}) %collective-permute-start.18) | collective-permute-done | bytes 262176 | tf_op jit(solution)/shard_map/ppermute | solution.py:181
  198.2 0.7 copy-done.15
  198.9 7.5 %down_other.1 = bf16[16,192,128]{2,1,0:T(8,128)(2,1)} custom-call(s32[8]{0:T(128)} %stack.35.owner, s32[64]{0:T(128)} %reshape.69.wanted, bf16[32,192,128]{2,1,0:T(8,128)(2,1)} %up_project.1.active_ref, bf16[32,2,16,128]{3,2,1,0:T(8,128)(2,1)} %get-tuple-element.37.refs_0_, bf16[32,2,16,128]{3,2,1,0:T(8,128)(2,1)} %copy-done.12, ...), custom_call_target="tpu_custom_call" | custom-call | tf_op jit(solution)/shard_map/down_other/pallas_call | solution.py:149
  206.5 0.7 copy.46.wanted
  207.2 6.4 %pick_blocks.10 = (bf16[32,2,16,128]{3,2,1,0:T(8,128)(2,1)}, bf16[32,2,16,128]{3,2,1,0:T(8,128)(2,1)}, bf16[32,2,16,128]{3,2,1,0:T(8,128)(2,1)}, bf16[32,2,16,128]{3,2,1,0:T(8,128)(2,1)}) custom-call(s32[1]{0:T(128)} %bitcast.16.which, s32[4,64]{1,0:T(4,128)} %copy.46.wanted, bf16[32,32,2048]{2,1,0:T(8,128)(2,1)} %weight_ref.11), custom_call_target="tpu_custom_call" | custom-call | tf_op jit(solution)/shard_map/pick_blocks/pallas_call | solution.py:49
  213.6 1.5 collective-permute-start.27
  215.1 2.0 collective-permute-start.29
  217.2 0.7 copy.48.wanted
  217.8 6.4 %pick_blocks.11 = (bf16[32,2,16,128]{3,2,1,0:T(8,128)(2,1)}, bf16[32,2,16,128]{3,2,1,0:T(8,128)(2,1)}, bf16[32,2,16,128]{3,2,1,0:T(8,128)(2,1)}, bf16[32,2,16,128]{3,2,1,0:T(8,128)(2,1)}) custom-call(s32[1]{0:T(128)} %bitcast.16.which, s32[4,64]{1,0:T(4,128)} %copy.48.wanted, bf16[32,32,2048]{2,1,0:T(8,128)(2,1)} %weight_ref.11), custom_call_target="tpu_custom_call" | custom-call | tf_op jit(solution)/shard_map/pick_blocks/pallas_call | solution.py:49
  224.2 3.8 %collective-permute-start.24 = (bf16[32,2,16,128]{3,2,1,0:T(8,128)(2,1)}, bf16[32,2,16,128]{3,2,1,0:T(8,128)(2,1)S(1)}, u32[]{:S(2)}, u32[]{:S(2)}) collective-permute-start(bf16[32,2,16,128]{3,2,1,0:T(8,128)(2,1)} %get-tuple-element.47), channel_id=1, source_target_pairs={{0,10},{2,8},{4,14},{6,12},{8,2},{10,0},{12,6},{14,4},{1,11},{3,9}... | collective-permute-start | bytes 786440 | tf_op jit(solution)/shard_map/ppermute | solution.py:181
  228.1 1.9 collective-permute-done.29.refs_7_
  230.0 0.6 collective-permute-start.26
  231.3 0.7 reshape.64.wanted
  232.0 21.7 %collective-permute-done.23.refs_1_ = bf16[32,2,16,128]{3,2,1,0:T(8,128)(2,1)S(1)} collective-permute-done((bf16[32,2,16,128]{3,2,1,0:T(8,128)(2,1)}, bf16[32,2,16,128]{3,2,1,0:T(8,128)(2,1)S(1)}, u32[]{:S(2)}, u32[]{:S(2)}) %collective-permute-start.23) | collective-permute-done | bytes 262176 | tf_op jit(solution)/shard_map/ppermute | solution.py:181
  253.7 5.6 %collective-permute-done.24.refs_2_ = bf16[32,2,16,128]{3,2,1,0:T(8,128)(2,1)S(1)} collective-permute-done((bf16[32,2,16,128]{3,2,1,0:T(8,128)(2,1)}, bf16[32,2,16,128]{3,2,1,0:T(8,128)(2,1)S(1)}, u32[]{:S(2)}, u32[]{:S(2)}) %collective-permute-start.24) | collective-permute-done | bytes 262176 | tf_op jit(solution)/shard_map/ppermute | solution.py:181
  259.3 7.5 %collective-permute-done.25.refs_3_ = bf16[32,2,16,128]{3,2,1,0:T(8,128)(2,1)S(1)} collective-permute-done((bf16[32,2,16,128]{3,2,1,0:T(8,128)(2,1)}, bf16[32,2,16,128]{3,2,1,0:T(8,128)(2,1)S(1)}, u32[]{:S(2)}, u32[]{:S(2)}) %collective-permute-start.25) | collective-permute-done | bytes 262176 | tf_op jit(solution)/shard_map/ppermute | solution.py:181
  266.8 5.5 %collective-permute-done.26.refs_4_ = bf16[32,2,16,128]{3,2,1,0:T(8,128)(2,1)S(1)} collective-permute-done((bf16[32,2,16,128]{3,2,1,0:T(8,128)(2,1)}, bf16[32,2,16,128]{3,2,1,0:T(8,128)(2,1)S(1)}, u32[]{:S(2)}, u32[]{:S(2)}) %collective-permute-start.26) | collective-permute-done | bytes 262176 | tf_op jit(solution)/shard_map/ppermute | solution.py:181
  272.4 0.6 copy-done.22
  273.3 8.5 %down_own.1 = bf16[192,2048]{1,0:T(8,128)(2,1)} custom-call(s32[8]{0:T(128)} %stack.35.owner, s32[64]{0:T(128)} %reshape.64.wanted, s32[1]{0:T(128)S(6)} %copy.60.length, bf16[32,192,128]{2,1,0:T(8,128)(2,1)} %up_project.1.active_ref, bf16[192,2048]{1,0:T(8,128)(2,1)} %acoustic_ref.1, bf16[16,192,128]{2,1,0:T(8,128)(2,1)} %copy-done.1, ...), custom_call_target="tpu_custom_call" | custom-call | tf_op jit(solution)/shard_map/down_own/pallas_call | solution.py:166
  (98 shorter events, 2.1 us)
Async XLA Ops:
  0.0 9.5 %copy-start.2 = (s32[64,32,32]{0,2,1:T(8,128)S(1)}, s32[64,32,32]{0,2,1:T(8,128)}, u32[]{:S(2)}) copy-start(s32[64,32,32]{0,2,1:T(8,128)} %param.13) | copy-start | bytes 786436
  0.0 9.7 %copy-start.23 = (f32[4096]{0:T(1024)S(1)}, f32[4096]{0:T(1024)}, u32[]{:S(2)}) copy-start(f32[4096]{0:T(1024)} %param.9) | copy-start | bytes 49156
  0.0 10.4 %collective-permute-start = (s32[1]{0:T(128)}, s32[1]{0:T(128)}, u32[]{:S(2)}, u32[]{:S(2)}) collective-permute-start(s32[1]{0:T(128)} %param.14), channel_id=1, source_target_pairs={{0,2},{2,0},{4,6},{6,4},{8,10},{10,8},{12,14},{14,12},{1,3},{3,1},... | collective-permute-start | bytes 20 | tf_op jit(solution)/shard_map/ppermute | solution.py:181
  1.5 10.2 %collective-permute-start.1 = (s32[1]{0:T(128)}, s32[1]{0:T(128)}, u32[]{:S(2)}, u32[]{:S(2)}) collective-permute-start(s32[1]{0:T(128)} %param.14), channel_id=1, source_target_pairs={{0,4},{2,6},{4,0},{6,2},{8,12},{10,14},{12,8},{14,10},{1,5},{3,7},... | collective-permute-start | bytes 20 | tf_op jit(solution)/shard_map/ppermute | solution.py:181
  1.9 11.3 %collective-permute-start.2 = (s32[1]{0:T(128)}, s32[1]{0:T(128)}, u32[]{:S(2)}, u32[]{:S(2)}) collective-permute-start(s32[1]{0:T(128)} %param.14), channel_id=1, source_target_pairs={{0,6},{2,4},{4,2},{6,0},{8,14},{10,12},{12,10},{14,8},{1,7},{3,5},... | collective-permute-start | bytes 20 | tf_op jit(solution)/shard_map/ppermute | solution.py:181
  3.5 19.9 %collective-permute-start.4 = (s32[1]{0:T(128)}, s32[1]{0:T(128)}, u32[]{:S(2)}, u32[]{:S(2)}) collective-permute-start(s32[1]{0:T(128)} %param.14), channel_id=1, source_target_pairs={{0,8},{2,10},{4,12},{6,14},{8,0},{10,2},{12,4},{14,6},{1,9},{3,11}... | collective-permute-start | bytes 20 | tf_op jit(solution)/shard_map/ppermute | solution.py:181
  6.1 49.7 %collective-permute-start.3 = (bf16[192,2048]{1,0:T(8,128)(2,1)}, bf16[192,2048]{1,0:T(8,128)(2,1)S(1)}, u32[]{:S(2)}, u32[]{:S(2)}) collective-permute-start(bf16[192,2048]{1,0:T(8,128)(2,1)} %acoustic_ref.1), channel_id=1, source_target_pairs={{0,1},{1,0},{2,3},{3,2},{4,5},{5,4},{6,7},{7,6},{8,9},{9,8},{10,11... | collective-permute-start | bytes 2359304 | tf_op jit(solution)/shard_map/ppermute | solution.py:181
  10.4 15.2 %collective-permute-start.5 = (s32[1]{0:T(128)}, s32[1]{0:T(128)}, u32[]{:S(2)}, u32[]{:S(2)}) collective-permute-start(s32[1]{0:T(128)} %param.14), channel_id=1, source_target_pairs={{0,10},{2,8},{4,14},{6,12},{8,2},{10,0},{12,6},{14,4},{1,11},{3,9}... | collective-permute-start | bytes 20 | tf_op jit(solution)/shard_map/ppermute | solution.py:181
  11.7 13.9 %collective-permute-start.6 = (s32[1]{0:T(128)}, s32[1]{0:T(128)}, u32[]{:S(2)}, u32[]{:S(2)}) collective-permute-start(s32[1]{0:T(128)} %param.14), channel_id=1, source_target_pairs={{0,12},{2,14},{4,8},{6,10},{8,4},{10,6},{12,0},{14,2},{1,13},{3,15... | collective-permute-start | bytes 20 | tf_op jit(solution)/shard_map/ppermute | solution.py:181
  13.3 12.3 %collective-permute-start.7 = (s32[1]{0:T(128)}, s32[1]{0:T(128)}, u32[]{:S(2)}, u32[]{:S(2)}) collective-permute-start(s32[1]{0:T(128)} %param.14), channel_id=1, source_target_pairs={{0,14},{2,12},{4,10},{6,8},{8,6},{10,4},{12,2},{14,0},{1,15},{3,13... | collective-permute-start | bytes 20 | tf_op jit(solution)/shard_map/ppermute | solution.py:181
  23.4 38.4 %collective-permute-start.20 = (bf16[32,2,16,128]{3,2,1,0:T(8,128)(2,1)}, bf16[32,2,16,128]{3,2,1,0:T(8,128)(2,1)S(1)}, u32[]{:S(2)}, u32[]{:S(2)}) collective-permute-start(bf16[32,2,16,128]{3,2,1,0:T(8,128)(2,1)} %get-tuple-element.43), channel_id=1, source_target_pairs={{0,4},{2,6},{4,0},{6,2},{8,12},{10,14},{12,8},{14,10},{1,5},{3,7},... | collective-permute-start | bytes 786440 | tf_op jit(solution)/shard_map/ppermute | solution.py:181
  36.7 25.2 %collective-permute-start.12 = (bf16[32,4,16,128]{3,2,1,0:T(8,128)(2,1)}, bf16[32,4,16,128]{3,2,1,0:T(8,128)(2,1)S(1)}, u32[]{:S(2)}, u32[]{:S(2)}) collective-permute-start(bf16[32,4,16,128]{3,2,1,0:T(8,128)(2,1)} %get-tuple-element.34), channel_id=1, source_target_pairs={{0,2},{2,0},{4,6},{6,4},{8,10},{10,8},{12,14},{14,12},{1,3},{3,1},... | collective-permute-start | bytes 1572872 | tf_op jit(solution)/shard_map/ppermute | solution.py:181
  38.4 26.8 %collective-permute-start.13 = (bf16[32,4,16,128]{3,2,1,0:T(8,128)(2,1)}, bf16[32,4,16,128]{3,2,1,0:T(8,128)(2,1)S(1)}, u32[]{:S(2)}, u32[]{:S(2)}) collective-permute-start(bf16[32,4,16,128]{3,2,1,0:T(8,128)(2,1)} %get-tuple-element.35), channel_id=1, source_target_pairs={{0,4},{2,6},{4,0},{6,2},{8,12},{10,14},{12,8},{14,10},{1,5},{3,7},... | collective-permute-start | bytes 1572872 | tf_op jit(solution)/shard_map/ppermute | solution.py:181
  38.6 20.5 %collective-permute-start.19 = (bf16[32,2,16,128]{3,2,1,0:T(8,128)(2,1)}, bf16[32,2,16,128]{3,2,1,0:T(8,128)(2,1)}, u32[]{:S(2)}, u32[]{:S(2)}) collective-permute-start(bf16[32,2,16,128]{3,2,1,0:T(8,128)(2,1)} %get-tuple-element.42), channel_id=1, source_target_pairs={{0,2},{2,0},{4,6},{6,4},{8,10},{10,8},{12,14},{14,12},{1,3},{3,1},... | collective-permute-start | bytes 786440 | tf_op jit(solution)/shard_map/ppermute | solution.py:181
  48.5 7.3 %copy-start.24 = (bf16[32,4,16,128]{3,2,1,0:T(8,128)(2,1)S(1)}, bf16[32,4,16,128]{3,2,1,0:T(8,128)(2,1)}, u32[]{:S(2)}) copy-start(bf16[32,4,16,128]{3,2,1,0:T(8,128)(2,1)} %get-tuple-element.36) | copy-start | bytes 1572868
  48.5 17.7 %copy-start = (bf16[192,2048]{1,0:T(8,128)(2,1)S(1)}, bf16[192,2048]{1,0:T(8,128)(2,1)}, u32[]{:S(2)}) copy-start(bf16[192,2048]{1,0:T(8,128)(2,1)} %acoustic_ref.1) | copy-start | bytes 2359300
  55.8 15.9 %collective-permute-start.14 = (bf16[32,4,16,128]{3,2,1,0:T(8,128)(2,1)S(1)}, bf16[32,4,16,128]{3,2,1,0:T(8,128)(2,1)S(1)}, u32[]{:S(2)}, u32[]{:S(2)}) collective-permute-start(bf16[32,4,16,128]{3,2,1,0:T(8,128)(2,1)S(1)} %copy-done.24), channel_id=1, source_target_pairs={{0,6},{2,4},{4,2},{6,0},{8,14},{10,12},{12,10},{14,8},{1,7},{3,5},... | collective-permute-start | bytes 1572872 | tf_op jit(solution)/shard_map/ppermute | solution.py:181
  59.1 64.2 %collective-permute-start.10 = (bf16[32,4,16,128]{3,2,1,0:T(8,128)(2,1)}, bf16[32,4,16,128]{3,2,1,0:T(8,128)(2,1)S(1)}, u32[]{:S(2)}, u32[]{:S(2)}) collective-permute-start(bf16[32,4,16,128]{3,2,1,0:T(8,128)(2,1)} %get-tuple-element.32), channel_id=1, source_target_pairs={{0,12},{2,14},{4,8},{6,10},{8,4},{10,6},{12,0},{14,2},{1,13},{3,15... | collective-permute-start | bytes 1572872 | tf_op jit(solution)/shard_map/ppermute | solution.py:181
  61.9 4.8 %copy-start.10 = (bf16[32,2,16,128]{3,2,1,0:T(8,128)(2,1)}, bf16[32,2,16,128]{3,2,1,0:T(8,128)(2,1)S(1)}, u32[]{:S(2)}) copy-start(bf16[32,2,16,128]{3,2,1,0:T(8,128)(2,1)S(1)} %collective-permute-done.20.refs_6_) | copy-start | bytes 786436
  61.9 79.8 %collective-permute-start.11 = (bf16[32,4,16,128]{3,2,1,0:T(8,128)(2,1)}, bf16[32,4,16,128]{3,2,1,0:T(8,128)(2,1)S(1)}, u32[]{:S(2)}, u32[]{:S(2)}) collective-permute-start(bf16[32,4,16,128]{3,2,1,0:T(8,128)(2,1)} %get-tuple-element.33), channel_id=1, source_target_pairs={{0,14},{2,12},{4,10},{6,8},{8,6},{10,4},{12,2},{14,0},{1,15},{3,13... | collective-permute-start | bytes 1572872 | tf_op jit(solution)/shard_map/ppermute | solution.py:181
  61.9 4.8 %copy-start.3 = (bf16[32,4,16,128]{3,2,1,0:T(8,128)(2,1)}, bf16[32,4,16,128]{3,2,1,0:T(8,128)(2,1)S(1)}, u32[]{:S(2)}) copy-start(bf16[32,4,16,128]{3,2,1,0:T(8,128)(2,1)S(1)} %collective-permute-done.12.refs_5_) | copy-start | bytes 1572868
  61.9 94.1 %collective-permute-start.8 = (bf16[32,4,16,128]{3,2,1,0:T(8,128)(2,1)}, bf16[32,4,16,128]{3,2,1,0:T(8,128)(2,1)S(1)}, u32[]{:S(2)}, u32[]{:S(2)}) collective-permute-start(bf16[32,4,16,128]{3,2,1,0:T(8,128)(2,1)} %get-tuple-element.30), channel_id=1, source_target_pairs={{0,8},{2,10},{4,12},{6,14},{8,0},{10,2},{12,4},{14,6},{1,9},{3,11}... | collective-permute-start | bytes 1572872 | tf_op jit(solution)/shard_map/ppermute | solution.py:181
  65.1 1.6 copy-start.4
  65.1 105.0 %collective-permute-start.9 = (bf16[32,4,16,128]{3,2,1,0:T(8,128)(2,1)}, bf16[32,4,16,128]{3,2,1,0:T(8,128)(2,1)S(1)}, u32[]{:S(2)}, u32[]{:S(2)}) collective-permute-start(bf16[32,4,16,128]{3,2,1,0:T(8,128)(2,1)} %get-tuple-element.31), channel_id=1, source_target_pairs={{0,10},{2,8},{4,14},{6,12},{8,2},{10,0},{12,6},{14,4},{1,11},{3,9}... | collective-permute-start | bytes 1572872 | tf_op jit(solution)/shard_map/ppermute | solution.py:181
  71.7 101.0 %copy-start.5 = (bf16[32,4,16,128]{3,2,1,0:T(8,128)(2,1)}, bf16[32,4,16,128]{3,2,1,0:T(8,128)(2,1)S(1)}, u32[]{:S(2)}) copy-start(bf16[32,4,16,128]{3,2,1,0:T(8,128)(2,1)S(1)} %collective-permute-done.14.refs_7_) | copy-start | bytes 1572868
  71.7 111.2 %collective-permute-start.21 = (bf16[32,2,16,128]{3,2,1,0:T(8,128)(2,1)}, bf16[32,2,16,128]{3,2,1,0:T(8,128)(2,1)S(1)}, u32[]{:S(2)}, u32[]{:S(2)}) collective-permute-start(bf16[32,2,16,128]{3,2,1,0:T(8,128)(2,1)} %get-tuple-element.44), channel_id=1, source_target_pairs={{0,6},{2,4},{4,2},{6,0},{8,14},{10,12},{12,10},{14,8},{1,7},{3,5},... | collective-permute-start | bytes 786440 | tf_op jit(solution)/shard_map/ppermute | solution.py:181
  123.3 49.0 %copy-start.6 = (bf16[32,4,16,128]{3,2,1,0:T(8,128)(2,1)}, bf16[32,4,16,128]{3,2,1,0:T(8,128)(2,1)S(1)}, u32[]{:S(2)}) copy-start(bf16[32,4,16,128]{3,2,1,0:T(8,128)(2,1)S(1)} %collective-permute-done.10.refs_3_) | copy-start | bytes 1572868
  123.3 59.6 %collective-permute-start.15 = (bf16[32,2,16,128]{3,2,1,0:T(8,128)(2,1)}, bf16[32,2,16,128]{3,2,1,0:T(8,128)(2,1)S(1)}, u32[]{:S(2)}, u32[]{:S(2)}) collective-permute-start(bf16[32,2,16,128]{3,2,1,0:T(8,128)(2,1)} %get-tuple-element.38), channel_id=1, source_target_pairs={{0,8},{2,10},{4,12},{6,14},{8,0},{10,2},{12,4},{14,6},{1,9},{3,11}... | collective-permute-start | bytes 786440 | tf_op jit(solution)/shard_map/ppermute | solution.py:181
  141.7 30.6 %copy-start.7 = (bf16[32,4,16,128]{3,2,1,0:T(8,128)(2,1)}, bf16[32,4,16,128]{3,2,1,0:T(8,128)(2,1)S(1)}, u32[]{:S(2)}) copy-start(bf16[32,4,16,128]{3,2,1,0:T(8,128)(2,1)S(1)} %collective-permute-done.11.refs_4_) | copy-start | bytes 1572868
  141.7 45.3 %collective-permute-start.16 = (bf16[32,2,16,128]{3,2,1,0:T(8,128)(2,1)}, bf16[32,2,16,128]{3,2,1,0:T(8,128)(2,1)S(1)}, u32[]{:S(2)}, u32[]{:S(2)}) collective-permute-start(bf16[32,2,16,128]{3,2,1,0:T(8,128)(2,1)} %get-tuple-element.39), channel_id=1, source_target_pairs={{0,10},{2,8},{4,14},{6,12},{8,2},{10,0},{12,6},{14,4},{1,11},{3,9}... | collective-permute-start | bytes 786440 | tf_op jit(solution)/shard_map/ppermute | solution.py:181
  156.0 16.7 %copy-start.8 = (bf16[32,4,16,128]{3,2,1,0:T(8,128)(2,1)}, bf16[32,4,16,128]{3,2,1,0:T(8,128)(2,1)S(1)}, u32[]{:S(2)}) copy-start(bf16[32,4,16,128]{3,2,1,0:T(8,128)(2,1)S(1)} %collective-permute-done.8.refs_1_) | copy-start | bytes 1572868
  156.0 39.1 %collective-permute-start.17 = (bf16[32,2,16,128]{3,2,1,0:T(8,128)(2,1)}, bf16[32,2,16,128]{3,2,1,0:T(8,128)(2,1)S(1)}, u32[]{:S(2)}, u32[]{:S(2)}) collective-permute-start(bf16[32,2,16,128]{3,2,1,0:T(8,128)(2,1)} %get-tuple-element.40), channel_id=1, source_target_pairs={{0,12},{2,14},{4,8},{6,10},{8,4},{10,6},{12,0},{14,2},{1,13},{3,15... | collective-permute-start | bytes 786440 | tf_op jit(solution)/shard_map/ppermute | solution.py:181
  170.2 2.5 copy-start.9
  170.2 28.0 %collective-permute-start.18 = (bf16[32,2,16,128]{3,2,1,0:T(8,128)(2,1)}, bf16[32,2,16,128]{3,2,1,0:T(8,128)(2,1)S(1)}, u32[]{:S(2)}, u32[]{:S(2)}) collective-permute-start(bf16[32,2,16,128]{3,2,1,0:T(8,128)(2,1)} %get-tuple-element.41), channel_id=1, source_target_pairs={{0,14},{2,12},{4,10},{6,8},{8,6},{10,4},{12,2},{14,0},{1,15},{3,13... | collective-permute-start | bytes 786440 | tf_op jit(solution)/shard_map/ppermute | solution.py:181
  182.9 15.3 %copy-start.11 = (bf16[32,2,16,128]{3,2,1,0:T(8,128)(2,1)}, bf16[32,2,16,128]{3,2,1,0:T(8,128)(2,1)S(1)}, u32[]{:S(2)}) copy-start(bf16[32,2,16,128]{3,2,1,0:T(8,128)(2,1)S(1)} %collective-permute-done.21.refs_7_) | copy-start | bytes 786436
  182.9 15.3 %copy-start.12 = (bf16[32,2,16,128]{3,2,1,0:T(8,128)(2,1)}, bf16[32,2,16,128]{3,2,1,0:T(8,128)(2,1)S(1)}, u32[]{:S(2)}) copy-start(bf16[32,2,16,128]{3,2,1,0:T(8,128)(2,1)S(1)} %collective-permute-done.15.refs_1_) | copy-start | bytes 786436
  187.0 11.2 %copy-start.13 = (bf16[32,2,16,128]{3,2,1,0:T(8,128)(2,1)}, bf16[32,2,16,128]{3,2,1,0:T(8,128)(2,1)S(1)}, u32[]{:S(2)}) copy-start(bf16[32,2,16,128]{3,2,1,0:T(8,128)(2,1)S(1)} %collective-permute-done.16.refs_2_) | copy-start | bytes 786436
  195.1 3.1 %copy-start.14 = (bf16[32,2,16,128]{3,2,1,0:T(8,128)(2,1)}, bf16[32,2,16,128]{3,2,1,0:T(8,128)(2,1)S(1)}, u32[]{:S(2)}) copy-start(bf16[32,2,16,128]{3,2,1,0:T(8,128)(2,1)S(1)} %collective-permute-done.17.refs_3_) | copy-start | bytes 786436
  198.2 0.7 copy-start.15
  206.4 65.9 %collective-permute-start.22 = (bf16[16,192,128]{2,1,0:T(8,128)(2,1)}, bf16[16,192,128]{2,1,0:T(8,128)(2,1)S(1)}, u32[]{:S(2)}, u32[]{:S(2)}) collective-permute-start(bf16[16,192,128]{2,1,0:T(8,128)(2,1)} %down_other.1), channel_id=1, source_target_pairs={{0,1},{1,0},{2,3},{3,2},{4,5},{5,4},{6,7},{7,6},{8,9},{9,8},{10,11... | collective-permute-start | bytes 2359304 | tf_op jit(solution)/shard_map/ppermute | solution.py:181
  213.6 10.6 %collective-permute-start.27 = (bf16[32,2,16,128]{3,2,1,0:T(8,128)(2,1)}, bf16[32,2,16,128]{3,2,1,0:T(8,128)(2,1)S(1)}, u32[]{:S(2)}, u32[]{:S(2)}) collective-permute-start(bf16[32,2,16,128]{3,2,1,0:T(8,128)(2,1)} %get-tuple-element.50), channel_id=1, source_target_pairs={{0,2},{2,0},{4,6},{6,4},{8,10},{10,8},{12,14},{14,12},{1,3},{3,1},... | collective-permute-start | bytes 786440 | tf_op jit(solution)/shard_map/ppermute | solution.py:181
  215.1 13.0 %collective-permute-start.28 = (bf16[32,2,16,128]{3,2,1,0:T(8,128)(2,1)}, bf16[32,2,16,128]{3,2,1,0:T(8,128)(2,1)S(1)}, u32[]{:S(2)}, u32[]{:S(2)}) collective-permute-start(bf16[32,2,16,128]{3,2,1,0:T(8,128)(2,1)} %get-tuple-element.51), channel_id=1, source_target_pairs={{0,4},{2,6},{4,0},{6,2},{8,12},{10,14},{12,8},{14,10},{1,5},{3,7},... | collective-permute-start | bytes 786440 | tf_op jit(solution)/shard_map/ppermute | solution.py:181
  215.1 14.9 %collective-permute-start.29 = (bf16[32,2,16,128]{3,2,1,0:T(8,128)(2,1)}, bf16[32,2,16,128]{3,2,1,0:T(8,128)(2,1)S(1)}, u32[]{:S(2)}, u32[]{:S(2)}) collective-permute-start(bf16[32,2,16,128]{3,2,1,0:T(8,128)(2,1)} %get-tuple-element.52), channel_id=1, source_target_pairs={{0,6},{2,4},{4,2},{6,0},{8,14},{10,12},{12,10},{14,8},{1,7},{3,5},... | collective-permute-start | bytes 786440 | tf_op jit(solution)/shard_map/ppermute | solution.py:181
  224.2 29.5 %collective-permute-start.23 = (bf16[32,2,16,128]{3,2,1,0:T(8,128)(2,1)}, bf16[32,2,16,128]{3,2,1,0:T(8,128)(2,1)S(1)}, u32[]{:S(2)}, u32[]{:S(2)}) collective-permute-start(bf16[32,2,16,128]{3,2,1,0:T(8,128)(2,1)} %get-tuple-element.46), channel_id=1, source_target_pairs={{0,8},{2,10},{4,12},{6,14},{8,0},{10,2},{12,4},{14,6},{1,9},{3,11}... | collective-permute-start | bytes 786440 | tf_op jit(solution)/shard_map/ppermute | solution.py:181
  224.2 48.1 %copy-start.16 = (bf16[32,2,16,128]{3,2,1,0:T(8,128)(2,1)}, bf16[32,2,16,128]{3,2,1,0:T(8,128)(2,1)S(1)}, u32[]{:S(2)}) copy-start(bf16[32,2,16,128]{3,2,1,0:T(8,128)(2,1)S(1)} %collective-permute-done.27.refs_5_) | copy-start | bytes 786436
  224.2 35.1 %collective-permute-start.24 = (bf16[32,2,16,128]{3,2,1,0:T(8,128)(2,1)}, bf16[32,2,16,128]{3,2,1,0:T(8,128)(2,1)S(1)}, u32[]{:S(2)}, u32[]{:S(2)}) collective-permute-start(bf16[32,2,16,128]{3,2,1,0:T(8,128)(2,1)} %get-tuple-element.47), channel_id=1, source_target_pairs={{0,10},{2,8},{4,14},{6,12},{8,2},{10,0},{12,6},{14,4},{1,11},{3,9}... | collective-permute-start | bytes 786440 | tf_op jit(solution)/shard_map/ppermute | solution.py:181
  228.1 44.3 %copy-start.17 = (bf16[32,2,16,128]{3,2,1,0:T(8,128)(2,1)}, bf16[32,2,16,128]{3,2,1,0:T(8,128)(2,1)S(1)}, u32[]{:S(2)}) copy-start(bf16[32,2,16,128]{3,2,1,0:T(8,128)(2,1)S(1)} %collective-permute-done.28.refs_6_) | copy-start | bytes 786436
  228.1 38.7 %collective-permute-start.25 = (bf16[32,2,16,128]{3,2,1,0:T(8,128)(2,1)}, bf16[32,2,16,128]{3,2,1,0:T(8,128)(2,1)S(1)}, u32[]{:S(2)}, u32[]{:S(2)}) collective-permute-start(bf16[32,2,16,128]{3,2,1,0:T(8,128)(2,1)} %get-tuple-element.48), channel_id=1, source_target_pairs={{0,12},{2,14},{4,8},{6,10},{8,4},{10,6},{12,0},{14,2},{1,13},{3,15... | collective-permute-start | bytes 786440 | tf_op jit(solution)/shard_map/ppermute | solution.py:181
  230.0 42.3 %copy-start.18 = (bf16[32,2,16,128]{3,2,1,0:T(8,128)(2,1)}, bf16[32,2,16,128]{3,2,1,0:T(8,128)(2,1)S(1)}, u32[]{:S(2)}) copy-start(bf16[32,2,16,128]{3,2,1,0:T(8,128)(2,1)S(1)} %collective-permute-done.29.refs_7_) | copy-start | bytes 786436
  230.0 42.3 %collective-permute-start.26 = (bf16[32,2,16,128]{3,2,1,0:T(8,128)(2,1)}, bf16[32,2,16,128]{3,2,1,0:T(8,128)(2,1)S(1)}, u32[]{:S(2)}, u32[]{:S(2)}) collective-permute-start(bf16[32,2,16,128]{3,2,1,0:T(8,128)(2,1)} %get-tuple-element.49), channel_id=1, source_target_pairs={{0,14},{2,12},{4,10},{6,8},{8,6},{10,4},{12,2},{14,0},{1,15},{3,13... | collective-permute-start | bytes 786440 | tf_op jit(solution)/shard_map/ppermute | solution.py:181
  253.7 18.7 %copy-start.19 = (bf16[32,2,16,128]{3,2,1,0:T(8,128)(2,1)}, bf16[32,2,16,128]{3,2,1,0:T(8,128)(2,1)S(1)}, u32[]{:S(2)}) copy-start(bf16[32,2,16,128]{3,2,1,0:T(8,128)(2,1)S(1)} %collective-permute-done.23.refs_1_) | copy-start | bytes 786436
  259.3 13.0 %copy-start.20 = (bf16[32,2,16,128]{3,2,1,0:T(8,128)(2,1)}, bf16[32,2,16,128]{3,2,1,0:T(8,128)(2,1)S(1)}, u32[]{:S(2)}) copy-start(bf16[32,2,16,128]{3,2,1,0:T(8,128)(2,1)S(1)} %collective-permute-done.24.refs_2_) | copy-start | bytes 786436
  266.8 5.6 %copy-start.21 = (bf16[32,2,16,128]{3,2,1,0:T(8,128)(2,1)}, bf16[32,2,16,128]{3,2,1,0:T(8,128)(2,1)S(1)}, u32[]{:S(2)}) copy-start(bf16[32,2,16,128]{3,2,1,0:T(8,128)(2,1)S(1)} %collective-permute-done.25.refs_3_) | copy-start | bytes 786436
  272.3 0.7 copy-start.22
  272.3 1.0 copy-start.1

commit v2 on v0

--- a/solution.py
+++ b/solution.py
@@ -1,21 +1,368 @@
+import functools
+
 import jax
 import jax.numpy as jnp
 from jax import lax
+from jax.experimental import pallas as pl
+from jax.experimental.pallas import tpu as pltpu
 from jax.sharding import PartitionSpec as P
 
 BLK = 128
+HALF = BLK // 2
 GROUP = 8
-
-
-def kept_index(keep_mask):
+HSTEP = 4
+CHUNKS = 2
+
+
+def kept_within(keep_mask):
     nlangs, hidden_blocks, feat_blocks = keep_mask.shape
     runs = feat_blocks // GROUP
     picks = jnp.arange(GROUP, dtype=jnp.int32)
-    within = jnp.sum(keep_mask.reshape(nlangs, hidden_blocks, runs, GROUP) * picks, axis=-1)
-    return within + jnp.arange(runs, dtype=jnp.int32) * GROUP
-
-
-def body(acoustic, norm_gain, up_weight, down_weight, up_keep, down_keep, language, lengths):
+    return jnp.sum(keep_mask.reshape(nlangs, hidden_blocks, runs, GROUP) * picks, axis=-1)
+
+
+def kept_index(keep_mask):
+    within = kept_within(keep_mask)
+    return within + jnp.arange(within.shape[-1], dtype=jnp.int32) * GROUP
+
+
+def low_lanes(shape):
+    return lax.broadcasted_iota(jnp.int32, shape, len(shape) - 1) < HALF
+
+
+def half_turn(value):
+    return pltpu.roll(value, HALF, value.ndim - 1)
+
+
+def norm_kernel(side, own_ref, peer_ref, gain_ref, near_ref, far_ref):
+    frames, features = own_ref.shape
+    slots = features // BLK
+
+    def square(ref):
+        total = jnp.zeros((frames, BLK), jnp.float32)
+        for d in range(slots):
+            wide = ref[:, d * BLK:(d + 1) * BLK].astype(jnp.float32)
+            total = total + wide * wide
+        return total
+
+    mean = jnp.sum(square(own_ref) + square(peer_ref), axis=-1, keepdims=True) / (2 * features)
+    scale = lax.rsqrt(mean + 1e-06)
+    low = low_lanes((frames, BLK))
+    near_low = low == (side[0] == 0)
+    for at, ref in enumerate((own_ref, peer_ref)):
+        for d in range(0, slots, 2):
+            far = []
+            for e in (d, d + 1):
+                lanes = slice(e * BLK, (e + 1) * BLK)
+                gain = gain_ref[at, :, lanes]
+                rounded = (ref[:, lanes].astype(jnp.float32) * scale * gain).astype(jnp.bfloat16).astype(jnp.float32)
+                turned = half_turn(rounded)
+                near_ref[at * slots + e] = jnp.where(near_low, rounded, turned).astype(jnp.bfloat16)
+                far.append(jnp.where(near_low, turned, rounded))
+            far_ref[(at * slots + d) // 2] = jnp.where(low, far[0], far[1]).astype(jnp.bfloat16)
+
+
+def norm_parts(side, own, peer, gains):
+    frames, features = own.shape
+    slots = 2 * features // BLK
+    return pl.pallas_call(
+        norm_kernel,
+        grid_spec=pltpu.PrefetchScalarGridSpec(
+            num_scalar_prefetch=1,
+            grid=(1,),
+            in_specs=[
+                pl.BlockSpec((frames, features), lambda i, *_: (0, 0)),
+                pl.BlockSpec((frames, features), lambda i, *_: (0, 0)),
+                pl.BlockSpec((2, 1, features), lambda i, *_: (0, 0, 0)),
+            ],
+            out_specs=[
+                pl.BlockSpec((slots, frames, BLK), lambda i, *_: (0, 0, 0)),
+                pl.BlockSpec((slots // 2, frames, BLK), lambda i, *_: (0, 0, 0)),
+            ],
+        ),
+        out_shape=[
+            jax.ShapeDtypeStruct((slots, frames, BLK), jnp.bfloat16),
+            jax.ShapeDtypeStruct((slots // 2, frames, BLK), jnp.bfloat16),
+        ],
+        name="norm_parts",
+    )(side, own, peer, gains)
+
+
+def pick_kernel(turns, wanted, weight_ref, *refs, rows, runs, base, turning):
+    out_refs, spread = refs[:-1], refs[-1]
+    step = pl.program_id(0) + base
+    for h in range(HSTEP):
+        for row in range(rows):
+            tile = weight_ref[h, :, row * BLK:(row + 1) * BLK].astype(jnp.float32)
+            for g in range(runs):
+                spread[h * runs + g, row * GROUP:(row + 1) * GROUP, :] = tile[g * GROUP:(g + 1) * GROUP]
+    for k, out_ref in enumerate(out_refs):
+        for u in range(2):
+            for h in range(HSTEP):
+                for g in range(runs):
+                    at = wanted[2 * k + u, (step * HSTEP + h) * runs + g]
+                    block = spread[h * runs + g, pl.ds(at, rows, stride=GROUP), :]
+                    if turning:
+                        block = pltpu.roll(block, turns[u], 1)
+                    out_ref[u, h, g] = block.astype(jnp.bfloat16)
+
+
+def pick_blocks(weight, wanted, turns, first, count, turning):
+    _, feat_blocks, width = weight.shape
+    rows = width // BLK
+    runs = feat_blocks // GROUP
+    targets = wanted.shape[0] // 2
+    base = first // HSTEP
+    out_shape = jax.ShapeDtypeStruct((2, count, runs, rows, BLK), jnp.bfloat16)
+    out_spec = pl.BlockSpec((2, HSTEP, runs, rows, BLK), lambda i, *_: (0, i, 0, 0, 0))
+    return pl.pallas_call(
+        functools.partial(pick_kernel, rows=rows, runs=runs, base=base, turning=turning),
+        grid_spec=pltpu.PrefetchScalarGridSpec(
+            num_scalar_prefetch=2,
+            grid=(count // HSTEP,),
+            in_specs=[pl.BlockSpec((HSTEP, feat_blocks, width), lambda i, *_: (i + base, 0, 0))],
+            out_specs=[out_spec] * targets,
+            scratch_shapes=[pltpu.VMEM((HSTEP * runs, rows * GROUP, BLK), jnp.float32)],
+        ),
+        out_shape=[out_shape] * targets,
+        name="pick_up" if turning else "pick_down",
+    )(turns, wanted, weight)
+
+
+def up_kernel(place, slots, own_ref, far_ref, *refs, runs, rows):
+    weight_refs, kept_ref, sent_ref, partner, held = refs[:-4], refs[-4], refs[-3], refs[-2], refs[-1]
+    step = pl.program_id(0)
+    frames = own_ref.shape[1]
+    low = low_lanes((frames, BLK))
+    side_rows = rows * len(weight_refs)
+
+    @pl.when(step == 0)
+    def _():
+        for m in range(far_ref.shape[0]):
+            pair = far_ref[m].astype(jnp.float32)
+            turned = half_turn(pair)
+            partner[2 * m] = jnp.where(low, pair, turned).astype(jnp.bfloat16)
+            partner[2 * m + 1] = jnp.where(low, turned, pair).astype(jnp.bfloat16)
+
+    for k, ref in enumerate(weight_refs):
+        start = pl.multiple_of(place[k] * rows, rows)
+        for u in range(2):
+            for h in range(HSTEP):
+                for g in range(runs):
+                    held[u, h, pl.ds(start + g * side_rows, rows), :] = ref[u, h, g]
+    for h in range(HSTEP):
+        parts = []
+        for u, source in enumerate((own_ref, partner)):
+            at = [slots[u, (step * HSTEP + h) * runs + g] for g in range(runs)]
+            left = jnp.concatenate(
+                [jnp.where(low, source[at[g]], source[at[g + 1]]) for g in range(0, runs, 2)], axis=1
+            )
+            parts.append(jnp.dot(left, held[u, h], preferred_element_type=jnp.float32))
+        own, other = parts
+        kept_ref[h] = jnp.where(low, other, own)
+        sent_ref[h] = jnp.where(low, own, other).astype(jnp.bfloat16)
+
+
+def up_project(place, slots, own, far, weights):
+    _, hidden_blocks, runs, rows, _ = weights[0].shape
+    slots_all, frames, _ = own.shape
+    out_spec = pl.BlockSpec((HSTEP, frames, BLK), lambda i, *_: (i, 0, 0))
+    return pl.pallas_call(
+        functools.partial(up_kernel, runs=runs, rows=rows),
+        grid_spec=pltpu.PrefetchScalarGridSpec(
+            num_scalar_prefetch=2,
+            grid=(hidden_blocks // HSTEP,),
+            in_specs=[
+                pl.BlockSpec((slots_all, frames, BLK), lambda i, *_: (0, 0, 0)),
+                pl.BlockSpec((slots_all // 2, frames, BLK), lambda i, *_: (0, 0, 0)),
+            ]
+            + [pl.BlockSpec((2, HSTEP, runs, rows, BLK), lambda i, *_: (0, i, 0, 0, 0))] * len(weights),
+            out_specs=[out_spec, out_spec],
+            scratch_shapes=[
+                pltpu.VMEM((slots_all, frames, BLK), jnp.bfloat16),
+                pltpu.VMEM((2, HSTEP, runs * rows * len(weights), BLK), jnp.bfloat16),
+            ],
+        ),
+        out_shape=[
+            jax.ShapeDtypeStruct((hidden_blocks, frames, BLK), jnp.float32),
+            jax.ShapeDtypeStruct((hidden_blocks, frames, BLK), jnp.bfloat16),
+        ],
+        compiler_params=pltpu.CompilerParams(vmem_limit_bytes=48 << 20),
+        name="up_project",
+    )(place, slots, own, far, *weights)
+
+
+def down_kernel(which, place, wanted, *refs, utt, parts, runs, rows):
+    refs = list(refs)
+    step = pl.program_id(0)
+    per_part = pl.num_programs(0) // max(parts, 1)
+    if parts:
+        kept_refs, got_refs, refs = refs[:parts], refs[parts:2 * parts], refs[2 * parts:]
+        weight_refs, out_ref, active_ref, held, total = refs[:-4], refs[-4], refs[-3], refs[-2], refs[-1]
+        for p in range(parts):
+            @pl.when(step // per_part == p)
+            def _():
+                before = kept_refs[p][...] + got_refs[p][...].astype(jnp.float32)
+                active_ref[...] = (before / (1.0 + jnp.exp(-before))).astype(jnp.bfloat16)
+    else:
+        active_ref, weight_refs, out_ref, held, total = refs[0], refs[1:-3], refs[-3], refs[-2], refs[-1]
+
+    @pl.when(step == 0)
+    def _():
+        total[...] = jnp.zeros_like(total)
+        held[...] = jnp.zeros_like(held)
+
+    top = HALF if utt == 0 else 0
+    for k, ref in enumerate(weight_refs):
+        start = pl.multiple_of(place[k] * rows, rows)
+        for h in range(HSTEP):
+            for g in range(runs):
+                held[h, pl.ds(start + top, rows), g * BLK:(g + 1) * BLK] = ref[0, h, g]
+    all_runs = 2 * runs
+    for h in range(HSTEP):
+        product = jnp.dot(active_ref[h], held[h], preferred_element_type=jnp.float32)
+        for g in range(runs):
+            at = g * GROUP + wanted[utt, (step * HSTEP + h) * all_runs + which[0] * runs + g]
+            total[at] += product[:, g * BLK:(g + 1) * BLK]
+
+    @pl.when(step == pl.num_programs(0) - 1)
+    def _():
+        out_ref[...] = total[...].astype(out_ref.dtype)
+
+
+def down_project(which, place, wanted, sources, weights, utt, out_dtype):
+    _, hidden_blocks, all_runs, rows, _ = weights[0].shape
+    runs = all_runs // 2
+    outs = runs * GROUP
+    frames = sources[-1].shape[1]
+    parts = len(sources) // 2
+    steps = hidden_blocks // HSTEP
+    per_part = steps // max(parts, 1)
+    active_spec = pl.BlockSpec((HSTEP, frames, BLK), lambda i, *_: (i, 0, 0))
+    if parts:
+        source_specs = [
+            pl.BlockSpec(
+                (HSTEP, frames, BLK), lambda i, *_, p=p: (jnp.clip(i - p * per_part, 0, per_part - 1), 0, 0)
+            )
+            for p in range(parts)
+        ] * 2
+    else:
+        source_specs = [active_spec]
+    out_specs = [pl.BlockSpec((outs, frames, BLK), lambda i, *_: (0, 0, 0))]
+    out_shape = [jax.ShapeDtypeStruct((outs, frames, BLK), out_dtype)]
+    if parts:
+        out_specs.append(active_spec)
+        out_shape.append(jax.ShapeDtypeStruct((hidden_blocks, frames, BLK), jnp.bfloat16))
+    return pl.pallas_call(
+        functools.partial(down_kernel, utt=utt, parts=parts, runs=runs, rows=rows),
+        grid_spec=pltpu.PrefetchScalarGridSpec(
+            num_scalar_prefetch=3,
+            grid=(steps,),
+            in_specs=source_specs
+            + [
+                pl.BlockSpec((1, HSTEP, runs, rows, BLK), lambda i, which, *_: (utt, i, which[0], 0, 0))
+            ] * len(weights),
+            out_specs=out_specs,
+            scratch_shapes=[
+                pltpu.VMEM((HSTEP, BLK, runs * BLK), jnp.bfloat16),
+                pltpu.VMEM((outs, frames, BLK), jnp.float32),
+            ],
+        ),
+        out_shape=out_shape,
+        compiler_params=pltpu.CompilerParams(vmem_limit_bytes=48 << 20),
+        name=f"down_{utt}",
+    )(which, place, wanted, *sources, *weights)
+
+
+def join_kernel(length, acoustic_ref, mine_ref, core_ref, side_ref, out_ref):
+    frames = out_ref.shape[0]
+    valid = lax.broadcasted_iota(jnp.int32, (frames, BLK), 0) < length[0]
+    for d in range(mine_ref.shape[0]):
+        lanes = slice(d * BLK, (d + 1) * BLK)
+        feedfwd = mine_ref[d] + core_ref[d].astype(jnp.float32) + side_ref[d].astype(jnp.float32)
+        summed = acoustic_ref[:, lanes].astype(jnp.float32) + feedfwd
+        out_ref[:, lanes] = jnp.where(valid, summed, 0.0).astype(jnp.bfloat16)
+
+
+def join(lengths, acoustic, mine, from_core, from_side):
+    outs, frames, _ = mine.shape
+    per = outs // 4
+    block = pl.BlockSpec((per, frames, BLK), lambda i, *_: (i, 0, 0))
+    flat = pl.BlockSpec((frames, per * BLK), lambda i, *_: (0, i))
+    return pl.pallas_call(
+        join_kernel,
+        grid_spec=pltpu.PrefetchScalarGridSpec(
+            num_scalar_prefetch=1, grid=(4,), in_specs=[flat, block, block, block], out_specs=flat
+        ),
+        out_shape=jax.ShapeDtypeStruct(acoustic.shape, jnp.bfloat16),
+        name="join",
+    )(lengths, acoustic, mine, from_core, from_side)
+
+
+def swap(value, axis, size, step):
+    return lax.ppermute(value, axis, [(i, i ^ step) for i in range(size)])
+
+
+def split_body(acoustic, norm_gain, up_weight, down_weight, up_keep, down_keep, language, lengths, *, dp):
+    frames, features = acoustic.shape
+    nlangs, hidden_blocks, feat_blocks = up_keep.shape
+    runs = feat_blocks // GROUP
+    across = dp // 2
+    members = list(range(across))
+    here = lax.axis_index("dp").astype(jnp.int32)
+    core = lax.axis_index("tensor").astype(jnp.int32)
+    side = (here // across)[None]
+
+    heard = {0: language}
+    for k in [across] + members[1:] + [across + k for k in members[1:]]:
+        heard[k] = swap(language, "dp", dp, k)
+    langs = jnp.concatenate([heard[k ^ far] for k in members for far in (0, across)])
+    chooser = (langs[:, None] == jnp.arange(nlangs, dtype=jnp.int32)).astype(jnp.int32)
+    wanted_up = jnp.einsum("nl,lhg->nhg", chooser, kept_within(up_keep))
+    wanted_down = jnp.einsum("nl,lhg->nhg", chooser, kept_within(down_keep))
+    up_own = wanted_up[:2] + jnp.arange(runs, dtype=jnp.int32) * GROUP
+    slots = (up_own ^ (core * (feat_blocks // 2))).reshape(2, -1)
+    wanted_up = wanted_up.reshape(2 * across, -1)
+    wanted_down = wanted_down.reshape(2 * across, -1)
+    place = jnp.stack([(here ^ k) % across for k in members])
+    turns = jnp.stack([HALF * (1 - side[0]), HALF * side[0]])
+
+    peer = swap(acoustic, "tensor", 2, 1)
+    gains = norm_gain.reshape(2, 1, features)
+    gains = jnp.where(core == 0, gains, gains[::-1])
+    near, far = norm_parts(side, acoustic, peer, gains)
+    far = swap(far, "dp", dp, across)
+
+    def within_side(blocks):
+        return [blocks[0]] + [swap(blocks[k], "dp", dp, k) for k in members[1:]]
+
+    count = hidden_blocks // CHUNKS
+    kept, crossed, last = [], [], None
+    for c in range(CHUNKS):
+        blocks = pick_blocks(up_weight, wanted_up, turns, c * count, count, True)
+        got = within_side(blocks)
+        last = got
+        mine, sent = up_project(place, slots[:, c * count * runs:(c + 1) * count * runs], near, far, got)
+        kept.append(mine)
+        crossed.append(swap(sent, "dp", dp, across))
+    blocks = pick_blocks(down_weight, wanted_down, turns, 0, hidden_blocks, False)
+    blocks, _ = lax.optimization_barrier((blocks, last))
+    got = within_side(blocks)
+    other_core = (1 - core)[None]
+    this_core = core[None]
+    rows_down = wanted_down[:2]
+    for_peer, active = down_project(other_core, place, rows_down, kept + crossed, got, 1, jnp.bfloat16)
+    from_peer = swap(for_peer, "tensor", 2, 1)
+    (partner_mine,) = down_project(this_core, place, rows_down, [active], got, 1, jnp.float32)
+    for_side = (partner_mine + from_peer.astype(jnp.float32)).astype(jnp.bfloat16)
+    from_side = swap(for_side, "dp", dp, across)
+    (own_peer,) = down_project(other_core, place, rows_down, [active], got, 0, jnp.bfloat16)
+    from_core = swap(own_peer, "tensor", 2, 1)
+    (own_mine,) = down_project(this_core, place, rows_down, [active], got, 0, jnp.float32)
+    return join(lengths, acoustic, own_mine, from_core, from_side)
+
+
+def exchange_body(acoustic, norm_gain, up_weight, down_weight, up_keep, down_keep, language, lengths):
     frames = acoustic.shape[0]
     nlangs, hidden_blocks, feat_blocks = up_keep.shape
     block_side = BLK
@@ -72,4 +419,8 @@
         P(("parts", "dp")),
     )
     out_specs = P(("parts", "dp"), "tensor")
+    dp = mesh.shape["dp"]
+    rows = BLK // dp
+    whole_tiles = mesh.shape["tensor"] == 2 and dp & (dp - 1) == 0 and dp > 1 and rows % 16 == 0
+    body = functools.partial(split_body, dp=dp) if whole_tiles else exchange_body
     return jax.shard_map(body, mesh=mesh, in_specs=in_specs, out_specs=out_specs, check_vma=False)

time: 305 us -> 238 us (0.78)
  local copies, waits for them, and re-layouts: 104 us -> 16.9 us
  Pallas kernels: 0 us -> 65.4 us
  matrix products: 21.4 us -> 0.59 us
  starting transfers between devices: 9.41 us -> 25.8 us
  between operations: 14.9 us -> 1.55 us
  blocking collectives: 13.1 us -> 0 us
  waiting for transfers between devices: 133 us -> 122 us
  other arithmetic: 8.02 us -> 4.31 us
    ppermute x0 -> x23, waiting for transfers between devices: none -> 122 us  [swap(): return lax.ppermute(value, axis, [(i, i ^ step) for i in range(size)])]
    all_to_all x2 -> x0, waiting for transfers between devices: 113 us -> none  [the longest x1 57.4 us: body(): lax.all_to_all(send_up, 'dp', split_axis=0, concat_axis=3, tiled=True)]
    gather x5 -> x0, local copies, waits for them, and re-layouts: 69.2 us -> none  [the longest x2 32.6 us: body(): send_down = down_weight[row_index, down_wanted]]
    pallas_call x0 -> x11, Pallas kernels: none -> 65.4 us  [the longest x4 27.3 us: down_project(): pl.pallas_call(functools.partial(down_kernel, utt=utt, parts=parts, runs=...]
    ppermute x0 -> x23, starting transfers between devices: none -> 25.8 us  [swap(): return lax.ppermute(value, axis, [(i, i ^ step) for i in range(size)])]
    another operation x3 -> x0, local copies, waits for them, and re-layouts: 21.3 us -> none  [the longest x2 13.9 us: body(): got_down[0].reshape(hidden_blocks, runs, block_side, block_side)]
    dot_general x13 -> x2, matrix products: 21.4 us -> 0.59 us  [the longest x1 0.3 us: split_body(): wanted_up = jnp.einsum('nl,lhg->nhg', chooser, kept_within(up_keep))]
    unnamed x1 -> x0, blocking collectives: 13.1 us -> none
  transfers between devices with their start and end apart: 4 -> 23, of which waited for: 4 -> 9; matrix products, arithmetic and copies ran while one was open for 19% -> 5% of each run, Pallas kernels for 0% -> 22%
where the time goes in v2:
time: 238 us; the launch traced here: 237 us
  waiting for transfers between devices  122 us (51%)
  Pallas kernels  65.4 us (27%)
  starting transfers between devices  25.8 us (11%)
  local copies, waits for them, and re-layouts  16.9 us (7%)
  other arithmetic  4.31 us (2%)
    ppermute x23, waiting for transfers between devices, swap(): return lax.ppermute(value, axis, [(i, i ^ step) for i in range(size)])  122 us
    pallas_call x4, Pallas kernels, down_project(): pl.pallas_call(functools.partial(down_kernel, utt=utt, parts=parts, runs=...  27.3 us
    ppermute x23, starting transfers between devices, swap(): return lax.ppermute(value, axis, [(i, i ^ step) for i in range(size)])  25.8 us
    pallas_call x3, Pallas kernels, pick_blocks(): pl.pallas_call(functools.partial(pick_kernel, rows=rows, runs=runs, base=...  19.2 us
    pallas_call x2, Pallas kernels, up_project(): pl.pallas_call(functools.partial(up_kernel, runs=runs, rows=rows), grid_s...  10.9 us
    unnamed x40, local copies, waits for them, and re-layouts  10.3 us
  transfers between devices with their start and end apart: 23, of which 9 were waited for; matrix products, arithmetic and copies ran while one was open for 5% of the time, Pallas kernels for 22%

profile of v2, /device:TPU:0, one launch (start us, length us, event | category | flops | bytes accessed | tf_op | source)
XLA Modules:
  0.0 236.8 jit_solution(11932731968518536534)
XLA Ops:
  0.0 4.0 %collective-permute-start.5 = (s32[1]{0:T(128)}, s32[1]{0:T(128)}, u32[]{:S(2)}, u32[]{:S(2)}) collective-permute-start(s32[1]{0:T(128)} %param.14), channel_id=1, source_target_pairs={{0,6},{2,4},{4,2},{6,0},{8,14},{10,12},{12,10},{14,8},{1,7},{3,5},... | collective-permute-start | bytes 20 | tf_op jit(solution)/shard_map/ppermute | solution.py:303
  4.0 2.5 %collective-permute-start.4 = (s32[1]{0:T(128)}, s32[1]{0:T(128)}, u32[]{:S(2)}, u32[]{:S(2)}) collective-permute-start(s32[1]{0:T(128)} %param.14), channel_id=1, source_target_pairs={{0,12},{2,14},{4,8},{6,10},{8,4},{10,6},{12,0},{14,2},{1,13},{3,15... | collective-permute-start | bytes 20 | tf_op jit(solution)/shard_map/ppermute | solution.py:303
  6.4 0.7 collective-permute-start.3
  7.1 1.2 collective-permute-start.2
  9.0 1.2 fusion
  10.2 0.7 pad_add_fusion.1.turns
  10.9 1.5 collective-permute-start.1
  12.4 1.7 collective-permute-start
  14.1 0.9 collective-permute-start.6
  15.0 2.1 collective-permute-done
  17.1 3.3 %collective-permute-done.6 = s32[1]{0:T(128)} collective-permute-done((s32[1]{0:T(128)}, s32[1]{0:T(128)}, u32[]{:S(2)}, u32[]{:S(2)}) %collective-permute-start.6) | collective-permute-done | bytes 36 | tf_op jit(solution)/shard_map/ppermute | solution.py:303
  20.4 4.5 %concatenate.3 = s32[8]{0:T(128)S(1)} concatenate(s32[1]{0:T(128)S(6)} %copy.47, s32[1]{0:T(128)} %collective-permute-done, s32[1]{0:T(128)} %collective-permute-done.1, s32[1]{0:T(128)} %collective-permute-done.2, s32[1]{0:T(128)} %collective-permute-done.3, s32[1]{0:T(128)} %collective-permute-done.4, s32[1]{0:T(128)} %collective-permute-done.5, s32[1]{0:T(128)} %collective-permute-done.6), dimensions={0} | concatenate | bytes 64 | tf_op jit(solution)/shard_map/concatenate | solution.py:319
  24.9 0.3 fusion.2
  25.2 0.1 copy.34
  25.3 0.7 copy.35.wanted
  26.0 5.4 %pick_up.3 = (bf16[2,16,4,16,128]{4,3,2,1,0:T(8,128)(2,1)}, bf16[2,16,4,16,128]{4,3,2,1,0:T(8,128)(2,1)}, bf16[2,16,4,16,128]{4,3,2,1,0:T(8,128)(2,1)}, bf16[2,16,4,16,128]{4,3,2,1,0:T(8,128)(2,1)}) custom-call(s32[2]{0:T(128)} %pad_add_fusion.1.turns, s32[8,128]{1,0:T(8,128)} %copy.35.wanted, bf16[32,32,2048]{2,1,0:T(8,128)(2,1)} %weight_ref.4), custom_call_target="tpu_custom_call" | custom-call | tf_op jit(solution)/shard_map/pick_up/pallas_call | solution.py:118
  31.4 0.5 collective-permute-start.12
  32.0 0.6 broadcast_select_fusion.gain_ref
  32.6 5.3 %pick_up.2 = (bf16[2,16,4,16,128]{4,3,2,1,0:T(8,128)(2,1)}, bf16[2,16,4,16,128]{4,3,2,1,0:T(8,128)(2,1)}, bf16[2,16,4,16,128]{4,3,2,1,0:T(8,128)(2,1)}, bf16[2,16,4,16,128]{4,3,2,1,0:T(8,128)(2,1)}) custom-call(s32[2]{0:T(128)} %pad_add_fusion.1.turns, s32[8,128]{1,0:T(8,128)} %copy.35.wanted, bf16[32,32,2048]{2,1,0:T(8,128)(2,1)} %weight_ref.4), custom_call_target="tpu_custom_call" | custom-call | tf_op jit(solution)/shard_map/pick_up/pallas_call | solution.py:118
  37.9 3.0 %collective-permute-start.14 = (bf16[2,16,4,16,128]{4,3,2,1,0:T(8,128)(2,1)}, bf16[2,16,4,16,128]{4,3,2,1,0:T(8,128)(2,1)S(1)}, u32[]{:S(2)}, u32[]{:S(2)}) collective-permute-start(bf16[2,16,4,16,128]{4,3,2,1,0:T(8,128)(2,1)} %get-tuple-element.39), channel_id=1, source_target_pairs={{0,6},{2,4},{4,2},{6,0},{8,14},{10,12},{12,10},{14,8},{1,7},{3,5},... | collective-permute-start | bytes 1572872 | tf_op jit(solution)/shard_map/ppermute | solution.py:303
  40.8 0.5 collective-permute-start.9
  41.5 1.4 fusion.1
  42.9 4.0 %norm_parts.1 = (bf16[32,192,128]{2,1,0:T(8,128)(2,1)}, bf16[16,192,128]{2,1,0:T(8,128)(2,1)}) custom-call(s32[1]{0:T(128)} %bitcast.9.side, bf16[192,2048]{1,0:T(8,128)(2,1)} %acoustic_ref.1, bf16[192,2048]{1,0:T(8,128)(2,1)} %copy-done.17, f32[2,1,2048]{2,1,0:T(1,128)} %broadcast_select_fusion.gain_ref), custom_call_target="tpu_custom_call" | custom-call | tf_op jit(solution)/shard_map/norm_parts/pallas_call | solution.py:68
  46.9 4.2 %collective-permute-done.12.refs_1_ = bf16[2,16,4,16,128]{4,3,2,1,0:T(8,128)(2,1)S(1)} collective-permute-done((bf16[2,16,4,16,128]{4,3,2,1,0:T(8,128)(2,1)}, bf16[2,16,4,16,128]{4,3,2,1,0:T(8,128)(2,1)S(1)}, u32[]{:S(2)}, u32[]{:S(2)}) %collective-permute-start.12) | collective-permute-done | bytes 524320 | tf_op jit(solution)/shard_map/ppermute | solution.py:303
  51.1 0.8 copy-done.7
  51.9 4.6 %collective-permute-start.8 = (bf16[16,192,128]{2,1,0:T(8,128)(2,1)}, bf16[16,192,128]{2,1,0:T(8,128)(2,1)S(1)}, u32[]{:S(2)}, u32[]{:S(2)}) collective-permute-start(bf16[16,192,128]{2,1,0:T(8,128)(2,1)} %get-tuple-element.30), channel_id=1, source_target_pairs={{0,8},{2,10},{4,12},{6,14},{8,0},{10,2},{12,4},{14,6},{1,9},{3,11}... | collective-permute-start | bytes 2359304 | tf_op jit(solution)/shard_map/ppermute | solution.py:303
  56.4 0.1 pad_add_fusion.place
  56.6 0.3 fusion.4
  56.9 0.1 copy.37
  57.0 0.7 copy.38.wanted
  57.7 8.5 %pick_down.1 = (bf16[2,32,4,16,128]{4,3,2,1,0:T(8,128)(2,1)}, bf16[2,32,4,16,128]{4,3,2,1,0:T(8,128)(2,1)}, bf16[2,32,4,16,128]{4,3,2,1,0:T(8,128)(2,1)}, bf16[2,32,4,16,128]{4,3,2,1,0:T(8,128)(2,1)}) custom-call(s32[2]{0:T(128)} %pad_add_fusion.1.turns, s32[8,128]{1,0:T(8,128)} %copy.38.wanted, bf16[32,32,2048]{2,1,0:T(8,128)(2,1)} %weight_ref.5), custom_call_target="tpu_custom_call" | custom-call | tf_op jit(solution)/shard_map/pick_down/pallas_call | solution.py:118
  66.2 9.9 %collective-permute-done.14.refs_3_ = bf16[2,16,4,16,128]{4,3,2,1,0:T(8,128)(2,1)S(1)} collective-permute-done((bf16[2,16,4,16,128]{4,3,2,1,0:T(8,128)(2,1)}, bf16[2,16,4,16,128]{4,3,2,1,0:T(8,128)(2,1)S(1)}, u32[]{:S(2)}, u32[]{:S(2)}) %collective-permute-start.14) | collective-permute-done | bytes 524320 | tf_op jit(solution)/shard_map/ppermute | solution.py:303
  76.1 0.8 copy-done.11
  76.9 0.5 collective-permute-start.17
  77.4 0.8 copy-done.14
  78.2 8.3 %collective-permute-done.10.refs_2_ = bf16[2,16,4,16,128]{4,3,2,1,0:T(8,128)(2,1)} collective-permute-done((bf16[2,16,4,16,128]{4,3,2,1,0:T(8,128)(2,1)}, bf16[2,16,4,16,128]{4,3,2,1,0:T(8,128)(2,1)}, u32[]{:S(2)}, u32[]{:S(2)}) %collective-permute-start.10) | collective-permute-done | bytes 524320 | tf_op jit(solution)/shard_map/ppermute | solution.py:303
  86.5 0.5 collective-permute-start.19
  87.1 0.1 copy.33
  87.1 0.1 reshape.26
  87.3 0.1 fusion.12
  87.3 11.4 %collective-permute-done.11.refs_3_ = bf16[2,16,4,16,128]{4,3,2,1,0:T(8,128)(2,1)} collective-permute-done((bf16[2,16,4,16,128]{4,3,2,1,0:T(8,128)(2,1)}, bf16[2,16,4,16,128]{4,3,2,1,0:T(8,128)(2,1)}, u32[]{:S(2)}, u32[]{:S(2)}) %collective-permute-start.11) | collective-permute-done | bytes 524320 | tf_op jit(solution)/shard_map/ppermute | solution.py:303
  98.7 1.3 copy-done.13
  100.0 1.0 copy-done.15
  101.1 5.8 %up_project.2 = (f32[16,192,128]{2,1,0:T(8,128)S(1)}, bf16[16,192,128]{2,1,0:T(8,128)(2,1)}) custom-call(s32[4]{0:T(128)S(1)} %pad_add_fusion.place, s32[2,64]{1,0:T(2,128)S(1)} %get-tuple-element.54.slots, bf16[32,192,128]{2,1,0:T(8,128)(2,1)} %get-tuple-element.29.own_ref, bf16[16,192,128]{2,1,0:T(8,128)(2,1)S(1)} %collective-permute-done.8.far_ref, ...), custom_call_target="tpu_custom_call" | custom-call | tf_op jit(solution)/shard_map/up_project/pallas_call | solution.py:170
  106.9 1.2 copy-done.4
  108.1 1.1 copy-done.3
  109.2 5.1 %up_project.3 = (f32[16,192,128]{2,1,0:T(8,128)S(1)}, bf16[16,192,128]{2,1,0:T(8,128)(2,1)}) custom-call(s32[4]{0:T(128)S(1)} %pad_add_fusion.place, s32[2,64]{1,0:T(2,128)S(1)} %get-tuple-element.53.slots, bf16[32,192,128]{2,1,0:T(8,128)(2,1)} %get-tuple-element.29.own_ref, bf16[16,192,128]{2,1,0:T(8,128)(2,1)S(1)} %copy-done.3, ...), custom_call_target="tpu_custom_call" | custom-call | tf_op jit(solution)/shard_map/up_project/pallas_call | solution.py:170
  114.3 1.2 copy-done.5
  115.5 2.9 %collective-permute-start.16 = (bf16[16,192,128]{2,1,0:T(8,128)(2,1)}, bf16[16,192,128]{2,1,0:T(8,128)(2,1)}, u32[]{:S(2)}, u32[]{:S(2)}) collective-permute-start(bf16[16,192,128]{2,1,0:T(8,128)(2,1)} %get-tuple-element.42), channel_id=1, source_target_pairs={{0,8},{2,10},{4,12},{6,14},{8,0},{10,2},{12,4},{14,6},{1,9},{3,11}... | collective-permute-start | bytes 2359304 | tf_op jit(solution)/shard_map/ppermute | solution.py:303
  118.4 0.1 copy.30
  118.5 0.1 slice.16.wanted
  118.6 34.2 %collective-permute-done.18.refs_6_.refs_3_ = bf16[2,32,4,16,128]{4,3,2,1,0:T(8,128)(2,1)S(1)} collective-permute-done((bf16[2,32,4,16,128]{4,3,2,1,0:T(8,128)(2,1)}, bf16[2,32,4,16,128]{4,3,2,1,0:T(8,128)(2,1)S(1)}, u32[]{:S(2)}, u32[]{:S(2)}) %collective-permute-start.18) | collective-permute-done | bytes 1048608 | tf_op jit(solution)/shard_map/ppermute | solution.py:303
  152.8 22.2 %collective-permute-done.19.refs_7_.refs_4_ = bf16[2,32,4,16,128]{4,3,2,1,0:T(8,128)(2,1)} collective-permute-done((bf16[2,32,4,16,128]{4,3,2,1,0:T(8,128)(2,1)}, bf16[2,32,4,16,128]{4,3,2,1,0:T(8,128)(2,1)}, u32[]{:S(2)}, u32[]{:S(2)}) %collective-permute-start.19) | collective-permute-done | bytes 1048608 | tf_op jit(solution)/shard_map/ppermute | solution.py:303
  175.0 8.5 %down_1.2 = (bf16[16,192,128]{2,1,0:T(8,128)(2,1)S(1)}, bf16[32,192,128]{2,1,0:T(8,128)(2,1)}) custom-call(s32[1]{0:T(128)} %bitcast.7.which, s32[4]{0:T(128)S(1)} %pad_add_fusion.place, s32[2,128]{1,0:T(2,128)S(1)} %slice.16.wanted, f32[16,192,128]{2,1,0:T(8,128)} %copy-done.4, f32[16,192,128]{2,1,0:T(8,128)} %copy-done.5, ...), custom_call_target="tpu_custom_call" | custom-call | tf_op jit(solution)/shard_map/down_1/pallas_call | solution.py:256
  183.5 6.2 %down_0.3 = bf16[16,192,128]{2,1,0:T(8,128)(2,1)S(1)} custom-call(s32[1]{0:T(128)} %bitcast.7.which, s32[4]{0:T(128)S(1)} %pad_add_fusion.place, s32[2,128]{1,0:T(2,128)S(1)} %slice.16.wanted, bf16[32,192,128]{2,1,0:T(8,128)(2,1)} %get-tuple-element.51.refs_0_, bf16[2,32,4,16,128]{4,3,2,1,0:T(8,128)(2,1)S(1)} %copy-done, ...), custom_call_target="tpu_custom_call" | custom-call | tf_op jit(solution)/shard_map/down_0/pallas_call | solution.py:256
  189.7 0.6 collective-permute-start.20
  190.3 6.3 %down_1.3 = f32[16,192,128]{2,1,0:T(8,128)S(1)} custom-call(s32[1]{0:T(128)} %bitcast.which, s32[4]{0:T(128)S(1)} %pad_add_fusion.place, s32[2,128]{1,0:T(2,128)S(1)} %slice.16.wanted, bf16[32,192,128]{2,1,0:T(8,128)(2,1)} %get-tuple-element.51.refs_0_, bf16[2,32,4,16,128]{4,3,2,1,0:T(8,128)(2,1)S(1)} %copy-done, ...), custom_call_target="tpu_custom_call" | custom-call | tf_op jit(solution)/shard_map/down_1/pallas_call | solution.py:256
  196.6 0.2 add_convert_fusion
  196.8 0.3 collective-permute-start.22
  197.8 6.3 %down_0.2.mine_ref = f32[16,192,128]{2,1,0:T(8,128)S(1)} custom-call(s32[1]{0:T(128)} %bitcast.which, s32[4]{0:T(128)S(1)} %pad_add_fusion.place, s32[2,128]{1,0:T(2,128)S(1)} %slice.16.wanted, bf16[32,192,128]{2,1,0:T(8,128)(2,1)} %get-tuple-element.51.refs_0_, bf16[2,32,4,16,128]{4,3,2,1,0:T(8,128)(2,1)S(1)} %copy-done, ...), custom_call_target="tpu_custom_call" | custom-call | tf_op jit(solution)/shard_map/down_0/pallas_call | solution.py:256
  204.1 1.2 copy-done.1
  205.2 0.9 copy-done.16
  206.1 26.7 %collective-permute-done.22.side_ref = bf16[16,192,128]{2,1,0:T(8,128)(2,1)} collective-permute-done((bf16[16,192,128]{2,1,0:T(8,128)(2,1)S(1)}, bf16[16,192,128]{2,1,0:T(8,128)(2,1)}, u32[]{:S(2)}, u32[]{:S(2)}) %collective-permute-start.22) | collective-permute-done | bytes 786464 | tf_op jit(solution)/shard_map/ppermute | solution.py:303
  232.8 4.0 %join.1 = bf16[192,2048]{1,0:T(8,128)(2,1)} custom-call(s32[1]{0:T(128)S(6)} %copy.48.length, bf16[192,2048]{1,0:T(8,128)(2,1)} %acoustic_ref.1, f32[16,192,128]{2,1,0:T(8,128)} %copy-done.1, bf16[16,192,128]{2,1,0:T(8,128)(2,1)} %copy-done.16, bf16[16,192,128]{2,1,0:T(8,128)(2,1)} %collective-permute-done.22.side_ref), custom_call_target="tpu_custom_call" | custom-call | tf_op jit(solution)/shard_map/join/pallas_call | solution.py:292
  (56 shorter events, 0.3 us)
Async XLA Ops:
  0.0 10.9 %collective-permute-start.5 = (s32[1]{0:T(128)}, s32[1]{0:T(128)}, u32[]{:S(2)}, u32[]{:S(2)}) collective-permute-start(s32[1]{0:T(128)} %param.14), channel_id=1, source_target_pairs={{0,6},{2,4},{4,2},{6,0},{8,14},{10,12},{12,10},{14,8},{1,7},{3,5},... | collective-permute-start | bytes 20 | tf_op jit(solution)/shard_map/ppermute | solution.py:303
  4.0 8.5 %collective-permute-start.4 = (s32[1]{0:T(128)}, s32[1]{0:T(128)}, u32[]{:S(2)}, u32[]{:S(2)}) collective-permute-start(s32[1]{0:T(128)} %param.14), channel_id=1, source_target_pairs={{0,12},{2,14},{4,8},{6,10},{8,4},{10,6},{12,0},{14,2},{1,13},{3,15... | collective-permute-start | bytes 20 | tf_op jit(solution)/shard_map/ppermute | solution.py:303
  6.4 7.7 %collective-permute-start.3 = (s32[1]{0:T(128)}, s32[1]{0:T(128)}, u32[]{:S(2)}, u32[]{:S(2)}) collective-permute-start(s32[1]{0:T(128)} %param.14), channel_id=1, source_target_pairs={{0,4},{2,6},{4,0},{6,2},{8,12},{10,14},{12,8},{14,10},{1,5},{3,7},... | collective-permute-start | bytes 20 | tf_op jit(solution)/shard_map/ppermute | solution.py:303
  7.1 7.9 %collective-permute-start.2 = (s32[1]{0:T(128)}, s32[1]{0:T(128)}, u32[]{:S(2)}, u32[]{:S(2)}) collective-permute-start(s32[1]{0:T(128)} %param.14), channel_id=1, source_target_pairs={{0,10},{2,8},{4,14},{6,12},{8,2},{10,0},{12,6},{14,4},{1,11},{3,9}... | collective-permute-start | bytes 20 | tf_op jit(solution)/shard_map/ppermute | solution.py:303
  8.3 33.1 %collective-permute-start.7 = (bf16[192,2048]{1,0:T(8,128)(2,1)}, bf16[192,2048]{1,0:T(8,128)(2,1)S(1)}, u32[]{:S(2)}, u32[]{:S(2)}) collective-permute-start(bf16[192,2048]{1,0:T(8,128)(2,1)} %acoustic_ref.1), channel_id=1, source_target_pairs={{0,1},{1,0},{2,3},{3,2},{4,5},{5,4},{6,7},{7,6},{8,9},{9,8},{10,11... | collective-permute-start | bytes 2359304 | tf_op jit(solution)/shard_map/ppermute | solution.py:303
  10.9 4.1 %collective-permute-start.1 = (s32[1]{0:T(128)}, s32[1]{0:T(128)}, u32[]{:S(2)}, u32[]{:S(2)}) collective-permute-start(s32[1]{0:T(128)} %param.14), channel_id=1, source_target_pairs={{0,2},{2,0},{4,6},{6,4},{8,10},{10,8},{12,14},{14,12},{1,3},{3,1},... | collective-permute-start | bytes 20 | tf_op jit(solution)/shard_map/ppermute | solution.py:303
  12.4 4.7 %collective-permute-start = (s32[1]{0:T(128)}, s32[1]{0:T(128)}, u32[]{:S(2)}, u32[]{:S(2)}) collective-permute-start(s32[1]{0:T(128)} %param.14), channel_id=1, source_target_pairs={{0,8},{2,10},{4,12},{6,14},{8,0},{10,2},{12,4},{14,6},{1,9},{3,11}... | collective-permute-start | bytes 20 | tf_op jit(solution)/shard_map/ppermute | solution.py:303
  14.1 6.3 %collective-permute-start.6 = (s32[1]{0:T(128)}, s32[1]{0:T(128)}, u32[]{:S(2)}, u32[]{:S(2)}) collective-permute-start(s32[1]{0:T(128)} %param.14), channel_id=1, source_target_pairs={{0,14},{2,12},{4,10},{6,8},{8,6},{10,4},{12,2},{14,0},{1,15},{3,13... | collective-permute-start | bytes 20 | tf_op jit(solution)/shard_map/ppermute | solution.py:303
  25.2 31.6 %copy-start.18 = (s32[8,32,4]{1,0,2:T(8,128)}, s32[8,32,4]{1,0,2:T(8,128)S(1)}, u32[]{:S(2)}) copy-start(s32[8,32,4]{1,0,2:T(8,128)S(1)} %fusion.2) | copy-start | bytes 12292
  26.0 5.9 %copy-start.19 = (f32[4096]{0:T(1024)S(1)}, f32[4096]{0:T(1024)}, u32[]{:S(2)}) copy-start(f32[4096]{0:T(1024)} %param.9) | copy-start | bytes 49156
  31.4 19.7 %collective-permute-start.12 = (bf16[2,16,4,16,128]{4,3,2,1,0:T(8,128)(2,1)}, bf16[2,16,4,16,128]{4,3,2,1,0:T(8,128)(2,1)S(1)}, u32[]{:S(2)}, u32[]{:S(2)}) collective-permute-start(bf16[2,16,4,16,128]{4,3,2,1,0:T(8,128)(2,1)} %get-tuple-element.37), channel_id=1, source_target_pairs={{0,2},{2,0},{4,6},{6,4},{8,10},{10,8},{12,14},{14,12},{1,3},{3,1},... | collective-permute-start | bytes 1572872 | tf_op jit(solution)/shard_map/ppermute | solution.py:303
  32.0 24.6 %collective-permute-start.13 = (bf16[2,16,4,16,128]{4,3,2,1,0:T(8,128)(2,1)}, bf16[2,16,4,16,128]{4,3,2,1,0:T(8,128)(2,1)S(1)}, u32[]{:S(2)}, u32[]{:S(2)}) collective-permute-start(bf16[2,16,4,16,128]{4,3,2,1,0:T(8,128)(2,1)} %get-tuple-element.38), channel_id=1, source_target_pairs={{0,4},{2,6},{4,0},{6,2},{8,12},{10,14},{12,8},{14,10},{1,5},{3,7},... | collective-permute-start | bytes 1572872 | tf_op jit(solution)/shard_map/ppermute | solution.py:303
  37.9 38.2 %collective-permute-start.14 = (bf16[2,16,4,16,128]{4,3,2,1,0:T(8,128)(2,1)}, bf16[2,16,4,16,128]{4,3,2,1,0:T(8,128)(2,1)S(1)}, u32[]{:S(2)}, u32[]{:S(2)}) collective-permute-start(bf16[2,16,4,16,128]{4,3,2,1,0:T(8,128)(2,1)} %get-tuple-element.39), channel_id=1, source_target_pairs={{0,6},{2,4},{4,2},{6,0},{8,14},{10,12},{12,10},{14,8},{1,7},{3,5},... | collective-permute-start | bytes 1572872 | tf_op jit(solution)/shard_map/ppermute | solution.py:303
  40.8 36.6 %collective-permute-start.9 = (bf16[2,16,4,16,128]{4,3,2,1,0:T(8,128)(2,1)}, bf16[2,16,4,16,128]{4,3,2,1,0:T(8,128)(2,1)S(1)}, u32[]{:S(2)}, u32[]{:S(2)}) collective-permute-start(bf16[2,16,4,16,128]{4,3,2,1,0:T(8,128)(2,1)} %get-tuple-element.32), channel_id=1, source_target_pairs={{0,2},{2,0},{4,6},{6,4},{8,10},{10,8},{12,14},{14,12},{1,3},{3,1},... | collective-permute-start | bytes 1572872 | tf_op jit(solution)/shard_map/ppermute | solution.py:303
  41.4 1.5 copy-start.17
  41.4 45.1 %collective-permute-start.10 = (bf16[2,16,4,16,128]{4,3,2,1,0:T(8,128)(2,1)}, bf16[2,16,4,16,128]{4,3,2,1,0:T(8,128)(2,1)}, u32[]{:S(2)}, u32[]{:S(2)}) collective-permute-start(bf16[2,16,4,16,128]{4,3,2,1,0:T(8,128)(2,1)} %get-tuple-element.33), channel_id=1, source_target_pairs={{0,4},{2,6},{4,0},{6,2},{8,12},{10,14},{12,8},{14,10},{1,5},{3,7},... | collective-permute-start | bytes 1572872 | tf_op jit(solution)/shard_map/ppermute | solution.py:303
  51.1 0.8 copy-start.7
  51.9 46.8 %collective-permute-start.8 = (bf16[16,192,128]{2,1,0:T(8,128)(2,1)}, bf16[16,192,128]{2,1,0:T(8,128)(2,1)S(1)}, u32[]{:S(2)}, u32[]{:S(2)}) collective-permute-start(bf16[16,192,128]{2,1,0:T(8,128)(2,1)} %get-tuple-element.30), channel_id=1, source_target_pairs={{0,8},{2,10},{4,12},{6,14},{8,0},{10,2},{12,4},{14,6},{1,9},{3,11}... | collective-permute-start | bytes 2359304 | tf_op jit(solution)/shard_map/ppermute | solution.py:303
  56.5 9.6 %copy-start.9 = (bf16[2,16,4,16,128]{4,3,2,1,0:T(8,128)(2,1)}, bf16[2,16,4,16,128]{4,3,2,1,0:T(8,128)(2,1)S(1)}, u32[]{:S(2)}) copy-start(bf16[2,16,4,16,128]{4,3,2,1,0:T(8,128)(2,1)S(1)} %collective-permute-done.13.refs_2_) | copy-start | bytes 1572868
  56.5 42.2 %collective-permute-start.11 = (bf16[2,16,4,16,128]{4,3,2,1,0:T(8,128)(2,1)}, bf16[2,16,4,16,128]{4,3,2,1,0:T(8,128)(2,1)}, u32[]{:S(2)}, u32[]{:S(2)}) collective-permute-start(bf16[2,16,4,16,128]{4,3,2,1,0:T(8,128)(2,1)} %get-tuple-element.34), channel_id=1, source_target_pairs={{0,6},{2,4},{4,2},{6,0},{8,14},{10,12},{12,10},{14,8},{1,7},{3,5},... | collective-permute-start | bytes 1572872 | tf_op jit(solution)/shard_map/ppermute | solution.py:303
  57.7 29.3 %slice-start = ((s32[8,32,4]{1,0,2:T(8,128)}), s32[2,32,4]{1,0,2:T(2,128)S(1)}, s32[]{:S(2)}) async-start(s32[8,32,4]{1,0,2:T(8,128)} %copy-done.18), calls=%async_computation | async-start | bytes 8192 | tf_op jit(solution)/shard_map/slice | solution.py:323
  76.1 0.8 copy-start.11
  76.9 41.7 %collective-permute-start.17 = (bf16[2,32,4,16,128]{4,3,2,1,0:T(8,128)(2,1)}, bf16[2,32,4,16,128]{4,3,2,1,0:T(8,128)(2,1)S(1)}, u32[]{:S(2)}, u32[]{:S(2)}) collective-permute-start(bf16[2,32,4,16,128]{4,3,2,1,0:T(8,128)(2,1)} %get-tuple-element.48), channel_id=1, source_target_pairs={{0,2},{2,0},{4,6},{6,4},{8,10},{10,8},{12,14},{14,12},{1,3},{3,1},... | collective-permute-start | bytes 3145736 | tf_op jit(solution)/shard_map/ppermute | solution.py:303
  77.4 0.8 copy-start.14
  78.2 74.6 %collective-permute-start.18 = (bf16[2,32,4,16,128]{4,3,2,1,0:T(8,128)(2,1)}, bf16[2,32,4,16,128]{4,3,2,1,0:T(8,128)(2,1)S(1)}, u32[]{:S(2)}, u32[]{:S(2)}) collective-permute-start(bf16[2,32,4,16,128]{4,3,2,1,0:T(8,128)(2,1)} %get-tuple-element.49), channel_id=1, source_target_pairs={{0,4},{2,6},{4,0},{6,2},{8,12},{10,14},{12,8},{14,10},{1,5},{3,7},... | collective-permute-start | bytes 3145736 | tf_op jit(solution)/shard_map/ppermute | solution.py:303
  86.5 88.5 %collective-permute-start.19 = (bf16[2,32,4,16,128]{4,3,2,1,0:T(8,128)(2,1)}, bf16[2,32,4,16,128]{4,3,2,1,0:T(8,128)(2,1)}, u32[]{:S(2)}, u32[]{:S(2)}) collective-permute-start(bf16[2,32,4,16,128]{4,3,2,1,0:T(8,128)(2,1)} %get-tuple-element.50), channel_id=1, source_target_pairs={{0,6},{2,4},{4,2},{6,0},{8,14},{10,12},{12,10},{14,8},{1,7},{3,5},... | collective-permute-start | bytes 3145736 | tf_op jit(solution)/shard_map/ppermute | solution.py:303
  98.7 8.2 %copy-start.2 = (bf16[16,192,128]{2,1,0:T(8,128)(2,1)}, bf16[16,192,128]{2,1,0:T(8,128)(2,1)S(1)}, u32[]{:S(2)}) copy-start(bf16[16,192,128]{2,1,0:T(8,128)(2,1)S(1)} %collective-permute-done.8.far_ref) | copy-start | bytes 2359300
  98.7 1.3 copy-start.13
  100.0 1.0 copy-start.15
  101.1 7.0 %copy-start.6 = (bf16[2,16,4,16,128]{4,3,2,1,0:T(8,128)(2,1)S(1)}, bf16[2,16,4,16,128]{4,3,2,1,0:T(8,128)(2,1)}, u32[]{:S(2)}) copy-start(bf16[2,16,4,16,128]{4,3,2,1,0:T(8,128)(2,1)} %get-tuple-element.36.refs_0_) | copy-start | bytes 1572868
  101.1 7.0 %copy-start.8 = (bf16[2,16,4,16,128]{4,3,2,1,0:T(8,128)(2,1)S(1)}, bf16[2,16,4,16,128]{4,3,2,1,0:T(8,128)(2,1)}, u32[]{:S(2)}) copy-start(bf16[2,16,4,16,128]{4,3,2,1,0:T(8,128)(2,1)} %copy-done.7) | copy-start | bytes 1572868
  101.1 7.0 %copy-start.10 = (bf16[2,16,4,16,128]{4,3,2,1,0:T(8,128)(2,1)S(1)}, bf16[2,16,4,16,128]{4,3,2,1,0:T(8,128)(2,1)}, u32[]{:S(2)}) copy-start(bf16[2,16,4,16,128]{4,3,2,1,0:T(8,128)(2,1)} %copy-done.9) | copy-start | bytes 1572868
  101.1 7.0 %copy-start.12 = (bf16[2,16,4,16,128]{4,3,2,1,0:T(8,128)(2,1)S(1)}, bf16[2,16,4,16,128]{4,3,2,1,0:T(8,128)(2,1)}, u32[]{:S(2)}) copy-start(bf16[2,16,4,16,128]{4,3,2,1,0:T(8,128)(2,1)} %copy-done.11) | copy-start | bytes 1572868
  106.9 1.2 copy-start.4
  108.0 66.9 %collective-permute-start.15 = (bf16[16,192,128]{2,1,0:T(8,128)(2,1)}, bf16[16,192,128]{2,1,0:T(8,128)(2,1)}, u32[]{:S(2)}, u32[]{:S(2)}) collective-permute-start(bf16[16,192,128]{2,1,0:T(8,128)(2,1)} %get-tuple-element.41), channel_id=1, source_target_pairs={{0,8},{2,10},{4,12},{6,14},{8,0},{10,2},{12,4},{14,6},{1,9},{3,11}... | collective-permute-start | bytes 2359304 | tf_op jit(solution)/shard_map/ppermute | solution.py:303
  108.1 1.1 copy-start.3
  109.2 65.8 %copy-start = (bf16[2,32,4,16,128]{4,3,2,1,0:T(8,128)(2,1)S(1)}, bf16[2,32,4,16,128]{4,3,2,1,0:T(8,128)(2,1)}, u32[]{:S(2)}) copy-start(bf16[2,32,4,16,128]{4,3,2,1,0:T(8,128)(2,1)} %get-tuple-element.47.refs_4_.refs_1_) | copy-start | bytes 3145732
  114.3 1.2 copy-start.5
  115.5 59.5 %collective-permute-start.16 = (bf16[16,192,128]{2,1,0:T(8,128)(2,1)}, bf16[16,192,128]{2,1,0:T(8,128)(2,1)}, u32[]{:S(2)}, u32[]{:S(2)}) collective-permute-start(bf16[16,192,128]{2,1,0:T(8,128)(2,1)} %get-tuple-element.42), channel_id=1, source_target_pairs={{0,8},{2,10},{4,12},{6,14},{8,0},{10,2},{12,4},{14,6},{1,9},{3,11}... | collective-permute-start | bytes 2359304 | tf_op jit(solution)/shard_map/ppermute | solution.py:303
  183.5 13.1 %collective-permute-start.21 = (bf16[16,192,128]{2,1,0:T(8,128)(2,1)S(1)}, bf16[16,192,128]{2,1,0:T(8,128)(2,1)S(1)}, u32[]{:S(2)}, u32[]{:S(2)}) collective-permute-start(bf16[16,192,128]{2,1,0:T(8,128)(2,1)S(1)} %get-tuple-element.52), channel_id=1, source_target_pairs={{0,1},{1,0},{2,3},{3,2},{4,5},{5,4},{6,7},{7,6},{8,9},{9,8},{10,11... | collective-permute-start | bytes 2359304 | tf_op jit(solution)/shard_map/ppermute | solution.py:303
  189.7 15.5 %collective-permute-start.20 = (bf16[16,192,128]{2,1,0:T(8,128)(2,1)S(1)}, bf16[16,192,128]{2,1,0:T(8,128)(2,1)S(1)}, u32[]{:S(2)}, u32[]{:S(2)}) collective-permute-start(bf16[16,192,128]{2,1,0:T(8,128)(2,1)S(1)} %down_0.3), channel_id=1, source_target_pairs={{0,1},{1,0},{2,3},{3,2},{4,5},{5,4},{6,7},{7,6},{8,9},{9,8},{10,11... | collective-permute-start | bytes 2359304 | tf_op jit(solution)/shard_map/ppermute | solution.py:303
  196.8 36.0 %collective-permute-start.22 = (bf16[16,192,128]{2,1,0:T(8,128)(2,1)S(1)}, bf16[16,192,128]{2,1,0:T(8,128)(2,1)}, u32[]{:S(2)}, u32[]{:S(2)}) collective-permute-start(bf16[16,192,128]{2,1,0:T(8,128)(2,1)S(1)} %add_convert_fusion), channel_id=1, source_target_pairs={{0,8},{2,10},{4,12},{6,14},{8,0},{10,2},{12,4},{14,6},{1,9},{3,11}... | collective-permute-start | bytes 2359304 | tf_op jit(solution)/shard_map/ppermute | solution.py:303
  204.1 1.2 copy-start.1
  205.2 0.9 copy-start.16

commit v3 on v2

--- a/solution.py
+++ b/solution.py
@@ -10,7 +10,7 @@
 BLK = 128
 HALF = BLK // 2
 GROUP = 8
-HSTEP = 4
+HSTEP = 8
 CHUNKS = 2
 
 
@@ -88,7 +88,7 @@
     )(side, own, peer, gains)
 
 
-def pick_kernel(turns, wanted, weight_ref, *refs, rows, runs, base, turning):
+def pick_kernel(wanted, weight_ref, *refs, rows, runs, base, turning):
     out_refs, spread = refs[:-1], refs[-1]
     step = pl.program_id(0) + base
     for h in range(HSTEP):
@@ -102,12 +102,12 @@
                 for g in range(runs):
                     at = wanted[2 * k + u, (step * HSTEP + h) * runs + g]
                     block = spread[h * runs + g, pl.ds(at, rows, stride=GROUP), :]
-                    if turning:
-                        block = pltpu.roll(block, turns[u], 1)
+                    if turning and h % 2:
+                        block = half_turn(block)
                     out_ref[u, h, g] = block.astype(jnp.bfloat16)
 
 
-def pick_blocks(weight, wanted, turns, first, count, turning):
+def pick_blocks(weight, wanted, first, count, turning):
     _, feat_blocks, width = weight.shape
     rows = width // BLK
     runs = feat_blocks // GROUP
@@ -118,7 +118,7 @@
     return pl.pallas_call(
         functools.partial(pick_kernel, rows=rows, runs=runs, base=base, turning=turning),
         grid_spec=pltpu.PrefetchScalarGridSpec(
-            num_scalar_prefetch=2,
+            num_scalar_prefetch=1,
             grid=(count // HSTEP,),
             in_specs=[pl.BlockSpec((HSTEP, feat_blocks, width), lambda i, *_: (i + base, 0, 0))],
             out_specs=[out_spec] * targets,
@@ -126,14 +126,16 @@
         ),
         out_shape=[out_shape] * targets,
         name="pick_up" if turning else "pick_down",
-    )(turns, wanted, weight)
-
-
-def up_kernel(place, slots, own_ref, far_ref, *refs, runs, rows):
-    weight_refs, kept_ref, sent_ref, partner, held = refs[:-4], refs[-4], refs[-3], refs[-2], refs[-1]
+    )(wanted, weight)
+
+
+def up_kernel(side, place, slots, own_ref, far_ref, *refs, runs, rows):
+    weight_refs, refs = refs[:-6], refs[-6:]
+    kept_refs, sent_refs, partner, held = refs[:2], refs[2:4], refs[4], refs[5]
     step = pl.program_id(0)
     frames = own_ref.shape[1]
     low = low_lanes((frames, BLK))
+    even = low == (side[0] == 0)
     side_rows = rows * len(weight_refs)
 
     @pl.when(step == 0)
@@ -150,55 +152,53 @@
             for h in range(HSTEP):
                 for g in range(runs):
                     held[u, h, pl.ds(start + g * side_rows, rows), :] = ref[u, h, g]
-    for h in range(HSTEP):
-        parts = []
+    for m in range(HSTEP // 2):
         for u, source in enumerate((own_ref, partner)):
-            at = [slots[u, (step * HSTEP + h) * runs + g] for g in range(runs)]
-            left = jnp.concatenate(
-                [jnp.where(low, source[at[g]], source[at[g + 1]]) for g in range(0, runs, 2)], axis=1
-            )
-            parts.append(jnp.dot(left, held[u, h], preferred_element_type=jnp.float32))
-        own, other = parts
-        kept_ref[h] = jnp.where(low, other, own)
-        sent_ref[h] = jnp.where(low, own, other).astype(jnp.bfloat16)
-
-
-def up_project(place, slots, own, far, weights):
+            pair = []
+            for h in (2 * m, 2 * m + 1):
+                at = [slots[u, (step * HSTEP + h) * runs + g] for g in range(runs)]
+                left = jnp.concatenate(
+                    [jnp.where(low, source[at[g]], source[at[g + 1]]) for g in range(0, runs, 2)], axis=1
+                )
+                pair.append(jnp.dot(left, held[u, h], preferred_element_type=jnp.float32))
+            kept_refs[u][m] = jnp.where(even, pair[0], pair[1])
+            sent_refs[u][m] = jnp.where(even, pair[1], pair[0]).astype(jnp.bfloat16)
+
+
+def up_project(side, place, slots, own, far, weights):
     _, hidden_blocks, runs, rows, _ = weights[0].shape
     slots_all, frames, _ = own.shape
-    out_spec = pl.BlockSpec((HSTEP, frames, BLK), lambda i, *_: (i, 0, 0))
+    out_spec = pl.BlockSpec((HSTEP // 2, frames, BLK), lambda i, *_: (i, 0, 0))
     return pl.pallas_call(
         functools.partial(up_kernel, runs=runs, rows=rows),
         grid_spec=pltpu.PrefetchScalarGridSpec(
-            num_scalar_prefetch=2,
+            num_scalar_prefetch=3,
             grid=(hidden_blocks // HSTEP,),
             in_specs=[
                 pl.BlockSpec((slots_all, frames, BLK), lambda i, *_: (0, 0, 0)),
                 pl.BlockSpec((slots_all // 2, frames, BLK), lambda i, *_: (0, 0, 0)),
             ]
             + [pl.BlockSpec((2, HSTEP, runs, rows, BLK), lambda i, *_: (0, i, 0, 0, 0))] * len(weights),
-            out_specs=[out_spec, out_spec],
+            out_specs=[out_spec] * 4,
             scratch_shapes=[
                 pltpu.VMEM((slots_all, frames, BLK), jnp.bfloat16),
                 pltpu.VMEM((2, HSTEP, runs * rows * len(weights), BLK), jnp.bfloat16),
             ],
         ),
-        out_shape=[
-            jax.ShapeDtypeStruct((hidden_blocks, frames, BLK), jnp.float32),
-            jax.ShapeDtypeStruct((hidden_blocks, frames, BLK), jnp.bfloat16),
-        ],
+        out_shape=[jax.ShapeDtypeStruct((hidden_blocks // 2, frames, BLK), jnp.float32)] * 2
+        + [jax.ShapeDtypeStruct((hidden_blocks // 2, frames, BLK), jnp.bfloat16)] * 2,
         compiler_params=pltpu.CompilerParams(vmem_limit_bytes=48 << 20),
         name="up_project",
-    )(place, slots, own, far, *weights)
-
-
-def down_kernel(which, place, wanted, *refs, utt, parts, runs, rows):
+    )(side, place, slots, own, far, *weights)
+
+
+def down_kernel(side, which, place, wanted, *refs, utt, parts, runs, rows):
     refs = list(refs)
     step = pl.program_id(0)
-    per_part = pl.num_programs(0) // max(parts, 1)
     if parts:
         kept_refs, got_refs, refs = refs[:parts], refs[parts:2 * parts], refs[2 * parts:]
         weight_refs, out_ref, active_ref, held, total = refs[:-4], refs[-4], refs[-3], refs[-2], refs[-1]
+        per_part = pl.num_programs(0) // parts
         for p in range(parts):
             @pl.when(step // per_part == p)
             def _():
@@ -212,25 +212,29 @@
         total[...] = jnp.zeros_like(total)
         held[...] = jnp.zeros_like(held)
 
-    top = HALF if utt == 0 else 0
     for k, ref in enumerate(weight_refs):
-        start = pl.multiple_of(place[k] * rows, rows)
         for h in range(HSTEP):
+            top = HALF * (side[0] ^ (h % 2))
+            start = pl.multiple_of(place[k] * rows + top, rows)
             for g in range(runs):
-                held[h, pl.ds(start + top, rows), g * BLK:(g + 1) * BLK] = ref[0, h, g]
+                at = (h % 2) * runs + g
+                held[h // 2, pl.ds(start, rows), at * BLK:(at + 1) * BLK] = ref[0, h, g]
     all_runs = 2 * runs
-    for h in range(HSTEP):
-        product = jnp.dot(active_ref[h], held[h], preferred_element_type=jnp.float32)
-        for g in range(runs):
-            at = g * GROUP + wanted[utt, (step * HSTEP + h) * all_runs + which[0] * runs + g]
-            total[at] += product[:, g * BLK:(g + 1) * BLK]
+    for m in range(HSTEP // 2):
+        product = jnp.dot(active_ref[m], held[m], preferred_element_type=jnp.float32)
+        for odd in range(2):
+            for g in range(runs):
+                h = step * HSTEP + 2 * m + odd
+                at = g * GROUP + wanted[utt, h * all_runs + which[0] * runs + g]
+                lane = (odd * runs + g) * BLK
+                total[at] += product[:, lane:lane + BLK]
 
     @pl.when(step == pl.num_programs(0) - 1)
     def _():
         out_ref[...] = total[...].astype(out_ref.dtype)
 
 
-def down_project(which, place, wanted, sources, weights, utt, out_dtype):
+def down_project(side, which, place, wanted, sources, weights, utt, out_dtype):
     _, hidden_blocks, all_runs, rows, _ = weights[0].shape
     runs = all_runs // 2
     outs = runs * GROUP
@@ -238,11 +242,12 @@
     parts = len(sources) // 2
     steps = hidden_blocks // HSTEP
     per_part = steps // max(parts, 1)
-    active_spec = pl.BlockSpec((HSTEP, frames, BLK), lambda i, *_: (i, 0, 0))
+    half_step = HSTEP // 2
+    active_spec = pl.BlockSpec((half_step, frames, BLK), lambda i, *_: (i, 0, 0))
     if parts:
         source_specs = [
             pl.BlockSpec(
-                (HSTEP, frames, BLK), lambda i, *_, p=p: (jnp.clip(i - p * per_part, 0, per_part - 1), 0, 0)
+                (half_step, frames, BLK), lambda i, *_, p=p: (jnp.clip(i - p * per_part, 0, per_part - 1), 0, 0)
             )
             for p in range(parts)
         ] * 2
@@ -252,26 +257,26 @@
     out_shape = [jax.ShapeDtypeStruct((outs, frames, BLK), out_dtype)]
     if parts:
         out_specs.append(active_spec)
-        out_shape.append(jax.ShapeDtypeStruct((hidden_blocks, frames, BLK), jnp.bfloat16))
+        out_shape.append(jax.ShapeDtypeStruct((hidden_blocks // 2, frames, BLK), jnp.bfloat16))
     return pl.pallas_call(
         functools.partial(down_kernel, utt=utt, parts=parts, runs=runs, rows=rows),
         grid_spec=pltpu.PrefetchScalarGridSpec(
-            num_scalar_prefetch=3,
+            num_scalar_prefetch=4,
             grid=(steps,),
             in_specs=source_specs
             + [
-                pl.BlockSpec((1, HSTEP, runs, rows, BLK), lambda i, which, *_: (utt, i, which[0], 0, 0))
+                pl.BlockSpec((1, HSTEP, runs, rows, BLK), lambda i, side, which, *_: (utt, i, which[0], 0, 0))
             ] * len(weights),
             out_specs=out_specs,
             scratch_shapes=[
-                pltpu.VMEM((HSTEP, BLK, runs * BLK), jnp.bfloat16),
+                pltpu.VMEM((half_step, BLK, 2 * runs * BLK), jnp.bfloat16),
                 pltpu.VMEM((outs, frames, BLK), jnp.float32),
             ],
         ),
         out_shape=out_shape,
         compiler_params=pltpu.CompilerParams(vmem_limit_bytes=48 << 20),
         name=f"down_{utt}",
-    )(which, place, wanted, *sources, *weights)
+    )(side, which, place, wanted, *sources, *weights)
 
 
 def join_kernel(length, acoustic_ref, mine_ref, core_ref, side_ref, out_ref):
@@ -313,10 +318,12 @@
     core = lax.axis_index("tensor").astype(jnp.int32)
     side = (here // across)[None]
 
-    heard = {0: language}
-    for k in [across] + members[1:] + [across + k for k in members[1:]]:
-        heard[k] = swap(language, "dp", dp, k)
-    langs = jnp.concatenate([heard[k ^ far] for k in members for far in (0, across)])
+    langs = language
+    step = across
+    while step != 0:
+        langs = jnp.concatenate([langs, swap(langs, "dp", dp, step)])
+        step = 1 if step == across else 2 * step
+        step = 0 if step == across else step
     chooser = (langs[:, None] == jnp.arange(nlangs, dtype=jnp.int32)).astype(jnp.int32)
     wanted_up = jnp.einsum("nl,lhg->nhg", chooser, kept_within(up_keep))
     wanted_down = jnp.einsum("nl,lhg->nhg", chooser, kept_within(down_keep))
@@ -325,40 +332,48 @@
     wanted_up = wanted_up.reshape(2 * across, -1)
     wanted_down = wanted_down.reshape(2 * across, -1)
     place = jnp.stack([(here ^ k) % across for k in members])
-    turns = jnp.stack([HALF * (1 - side[0]), HALF * side[0]])
-
     peer = swap(acoustic, "tensor", 2, 1)
     gains = norm_gain.reshape(2, 1, features)
     gains = jnp.where(core == 0, gains, gains[::-1])
-    near, far = norm_parts(side, acoustic, peer, gains)
-    far = swap(far, "dp", dp, across)
+    near, own_far = norm_parts(side, acoustic, peer, gains)
+    far = swap(own_far, "dp", dp, across)
+    wanted_up, _ = lax.optimization_barrier((wanted_up, own_far))
 
     def within_side(blocks):
         return [blocks[0]] + [swap(blocks[k], "dp", dp, k) for k in members[1:]]
 
     count = hidden_blocks // CHUNKS
-    kept, crossed, last = [], [], None
+    kept, crossed, last = ([], []), ([], []), None
     for c in range(CHUNKS):
-        blocks = pick_blocks(up_weight, wanted_up, turns, c * count, count, True)
+        blocks = pick_blocks(up_weight, wanted_up, c * count, count, True)
         got = within_side(blocks)
         last = got
-        mine, sent = up_project(place, slots[:, c * count * runs:(c + 1) * count * runs], near, far, got)
-        kept.append(mine)
-        crossed.append(swap(sent, "dp", dp, across))
-    blocks = pick_blocks(down_weight, wanted_down, turns, 0, hidden_blocks, False)
+        span = slice(c * count * runs, (c + 1) * count * runs)
+        kept_own, kept_far, sent_own, sent_far = up_project(side, place, slots[:, span], near, far, got)
+        got_far = swap(sent_own, "dp", dp, across)
+        sent_far, _ = lax.optimization_barrier((sent_far, got_far))
+        got_own = swap(sent_far, "dp", dp, across)
+        for u, (mine, theirs) in enumerate(((kept_own, got_own), (kept_far, got_far))):
+            kept[u].append(mine)
+            crossed[u].append(theirs)
+    blocks = pick_blocks(down_weight, wanted_down, 0, hidden_blocks, False)
     blocks, _ = lax.optimization_barrier((blocks, last))
     got = within_side(blocks)
+    rows_down = wanted_down[:2]
+
+    def down(which, sources, utt, dtype):
+        return down_project(side, which, place, rows_down, sources, got, utt, dtype)
+
     other_core = (1 - core)[None]
     this_core = core[None]
-    rows_down = wanted_down[:2]
-    for_peer, active = down_project(other_core, place, rows_down, kept + crossed, got, 1, jnp.bfloat16)
+    for_peer, active_far = down(other_core, kept[1] + crossed[1], 1, jnp.bfloat16)
     from_peer = swap(for_peer, "tensor", 2, 1)
-    (partner_mine,) = down_project(this_core, place, rows_down, [active], got, 1, jnp.float32)
-    for_side = (partner_mine + from_peer.astype(jnp.float32)).astype(jnp.bfloat16)
+    (far_mine,) = down(this_core, [active_far], 1, jnp.float32)
+    for_side = (far_mine + from_peer.astype(jnp.float32)).astype(jnp.bfloat16)
     from_side = swap(for_side, "dp", dp, across)
-    (own_peer,) = down_project(other_core, place, rows_down, [active], got, 0, jnp.bfloat16)
+    own_peer, active_own = down(other_core, kept[0] + crossed[0], 0, jnp.bfloat16)
     from_core = swap(own_peer, "tensor", 2, 1)
-    (own_mine,) = down_project(this_core, place, rows_down, [active], got, 0, jnp.float32)
+    (own_mine,) = down(this_core, [active_own], 0, jnp.float32)
     return join(lengths, acoustic, own_mine, from_core, from_side)
 
 

time: 238 us -> 272 us (1.14)
  waiting for transfers between devices: 122 us -> 159 us
  Pallas kernels: 65.4 us -> 52.3 us
  starting transfers between devices: 25.8 us -> 32.5 us
    ppermute x23 -> x21, waiting for transfers between devices: 122 us -> 159 us  [swap(): return lax.ppermute(value, axis, [(i, i ^ step) for i in range(size)])]
    pallas_call x4, Pallas kernels: 27.3 us -> 19.3 us  [down_project(): pl.pallas_call(functools.partial(down_kernel, utt=utt, parts=parts, runs=...]
    ppermute x23 -> x21, starting transfers between devices: 25.8 us -> 32.5 us  [swap(): return lax.ppermute(value, axis, [(i, i ^ step) for i in range(size)])]
    unnamed x40 -> x62, local copies, waits for them, and re-layouts: 10.3 us -> 15.5 us
    concatenate x1 -> x0, local copies, waits for them, and re-layouts: 4.5 us -> none  [split_body(): jnp.concatenate([heard[k ^ far] for k in members for far in (0, across)])]
    pallas_call x3, Pallas kernels: 19.2 us -> 15.8 us  [pick_blocks(): pl.pallas_call(functools.partial(pick_kernel, rows=rows, runs=runs, base=...]
  transfers between devices with their start and end apart: 23 -> 21, of which waited for: 9 -> 11; matrix products, arithmetic and copies ran while one was open for 5% -> 3% of each run, Pallas kernels for 22% -> 13%
where the time goes in v3:
time: 272 us; the launch traced here: 270 us
  waiting for transfers between devices  159 us (58%)
  Pallas kernels  52.3 us (19%)
  starting transfers between devices  32.5 us (12%)
  local copies, waits for them, and re-layouts  18.8 us (7%)
  other arithmetic  5.4 us (2%)
    ppermute x21, waiting for transfers between devices, swap(): return lax.ppermute(value, axis, [(i, i ^ step) for i in range(size)])  159 us
    ppermute x21, starting transfers between devices, swap(): return lax.ppermute(value, axis, [(i, i ^ step) for i in range(size)])  32.5 us
    pallas_call x4, Pallas kernels, down_project(): pl.pallas_call(functools.partial(down_kernel, utt=utt, parts=parts, runs=...  19.3 us
    pallas_call x3, Pallas kernels, pick_blocks(): pl.pallas_call(functools.partial(pick_kernel, rows=rows, runs=runs, base=...  15.8 us
    unnamed x62, local copies, waits for them, and re-layouts  15.5 us
    pallas_call x2, Pallas kernels, up_project(): pl.pallas_call(functools.partial(up_kernel, runs=runs, rows=rows), grid_s...  9.26 us
  transfers between devices with their start and end apart: 21, of which 11 were waited for; matrix products, arithmetic and copies ran while one was open for 3% of the time, Pallas kernels for 13%

profile of v3, /device:TPU:0, one launch (start us, length us, event | category | flops | bytes accessed | tf_op | source)
XLA Modules:
  0.0 270.2 jit_solution(29903713941778547)
XLA Ops:
  0.0 4.0 %collective-permute-start = (s32[1]{0:T(128)}, s32[1]{0:T(128)}, u32[]{:S(2)}, u32[]{:S(2)}) collective-permute-start(s32[1]{0:T(128)} %param.14), channel_id=1, source_target_pairs={{0,8},{2,10},{4,12},{6,14},{8,0},{10,2},{12,4},{14,6},{1,9},{3,11}... | collective-permute-start | bytes 20 | tf_op jit(solution)/shard_map/ppermute | solution.py:308
  4.0 1.4 broadcast_select_fusion.gain_ref
  6.1 1.2 fusion
  7.4 0.7 pad_add_fusion.1
  8.1 1.5 collective-permute-start.1
  9.6 2.0 collective-permute-done.1
  11.6 0.7 pad_add_fusion.2
  12.4 1.6 collective-permute-start.2
  14.0 2.0 collective-permute-done.2
  15.9 0.7 pad_add_fusion.3
  16.7 0.3 fusion.2
  17.1 0.9 copy-done.28
  18.0 4.0 %norm_parts.1 = (bf16[32,192,128]{2,1,0:T(8,128)(2,1)}, bf16[16,192,128]{2,1,0:T(8,128)(2,1)}) custom-call(s32[1]{0:T(128)} %bitcast.side, bf16[192,2048]{1,0:T(8,128)(2,1)} %acoustic_ref.1, bf16[192,2048]{1,0:T(8,128)(2,1)} %copy-done.28, f32[2,1,2048]{2,1,0:T(1,128)} %broadcast_select_fusion.gain_ref), custom_call_target="tpu_custom_call" | custom-call | tf_op jit(solution)/shard_map/norm_parts/pallas_call | solution.py:68
  22.0 0.6 copy.35.wanted
  22.6 4.5 %pick_up.3 = (bf16[2,16,4,16,128]{4,3,2,1,0:T(8,128)(2,1)}, bf16[2,16,4,16,128]{4,3,2,1,0:T(8,128)(2,1)}, bf16[2,16,4,16,128]{4,3,2,1,0:T(8,128)(2,1)}, bf16[2,16,4,16,128]{4,3,2,1,0:T(8,128)(2,1)}) custom-call(s32[8,128]{1,0:T(8,128)} %copy.35.wanted, bf16[32,32,2048]{2,1,0:T(8,128)(2,1)} %weight_ref.4), custom_call_target="tpu_custom_call" | custom-call | tf_op jit(solution)/shard_map/pick_up/pallas_call | solution.py:118
  27.2 1.5 collective-permute-start.8
  28.7 1.6 collective-permute-start.9
  30.2 0.4 collective-permute-start.10
  30.7 4.5 %pick_up.2 = (bf16[2,16,4,16,128]{4,3,2,1,0:T(8,128)(2,1)}, bf16[2,16,4,16,128]{4,3,2,1,0:T(8,128)(2,1)}, bf16[2,16,4,16,128]{4,3,2,1,0:T(8,128)(2,1)}, bf16[2,16,4,16,128]{4,3,2,1,0:T(8,128)(2,1)}) custom-call(s32[8,128]{1,0:T(8,128)} %copy.35.wanted, bf16[32,32,2048]{2,1,0:T(8,128)(2,1)} %weight_ref.4), custom_call_target="tpu_custom_call" | custom-call | tf_op jit(solution)/shard_map/pick_up/pallas_call | solution.py:118
  35.2 1.5 collective-permute-start.5
  36.7 1.6 collective-permute-start.6
  38.4 6.2 %collective-permute-done.8.refs_1_ = bf16[2,16,4,16,128]{4,3,2,1,0:T(8,128)(2,1)S(1)} collective-permute-done((bf16[2,16,4,16,128]{4,3,2,1,0:T(8,128)(2,1)}, bf16[2,16,4,16,128]{4,3,2,1,0:T(8,128)(2,1)S(1)}, u32[]{:S(2)}, u32[]{:S(2)}) %collective-permute-start.8) | collective-permute-done | bytes 524320 | tf_op jit(solution)/shard_map/ppermute | solution.py:308
  44.6 0.8 copy-done.15
  45.4 8.6 %collective-permute-start.4 = (bf16[16,192,128]{2,1,0:T(8,128)(2,1)}, bf16[16,192,128]{2,1,0:T(8,128)(2,1)S(1)}, u32[]{:S(2)}, u32[]{:S(2)}) collective-permute-start(bf16[16,192,128]{2,1,0:T(8,128)(2,1)} %get-tuple-element.39), channel_id=1, source_target_pairs={{0,8},{2,10},{4,12},{6,14},{8,0},{10,2},{12,4},{14,6},{1,9},{3,11}... | collective-permute-start | bytes 2359304 | tf_op jit(solution)/shard_map/ppermute | solution.py:308
  54.0 0.3 fusion.4
  54.4 0.7 copy.38.wanted
  55.0 6.7 %pick_down.1 = (bf16[2,32,4,16,128]{4,3,2,1,0:T(8,128)(2,1)}, bf16[2,32,4,16,128]{4,3,2,1,0:T(8,128)(2,1)}, bf16[2,32,4,16,128]{4,3,2,1,0:T(8,128)(2,1)}, bf16[2,32,4,16,128]{4,3,2,1,0:T(8,128)(2,1)}) custom-call(s32[8,128]{1,0:T(8,128)} %copy.38.wanted, bf16[32,32,2048]{2,1,0:T(8,128)(2,1)} %weight_ref.5), custom_call_target="tpu_custom_call" | custom-call | tf_op jit(solution)/shard_map/pick_down/pallas_call | solution.py:118
  61.8 0.8 copy-done.17
  62.6 7.0 %collective-permute-done.10.refs_3_ = bf16[2,16,4,16,128]{4,3,2,1,0:T(8,128)(2,1)S(1)} collective-permute-done((bf16[2,16,4,16,128]{4,3,2,1,0:T(8,128)(2,1)}, bf16[2,16,4,16,128]{4,3,2,1,0:T(8,128)(2,1)S(1)}, u32[]{:S(2)}, u32[]{:S(2)}) %collective-permute-start.10) | collective-permute-done | bytes 524320 | tf_op jit(solution)/shard_map/ppermute | solution.py:308
  69.5 0.8 copy-done.19
  70.3 2.6 collective-permute-start.15
  73.0 1.5 collective-permute-start.17
  74.4 8.8 %collective-permute-done.6.refs_2_ = bf16[2,16,4,16,128]{4,3,2,1,0:T(8,128)(2,1)} collective-permute-done((bf16[2,16,4,16,128]{4,3,2,1,0:T(8,128)(2,1)}, bf16[2,16,4,16,128]{4,3,2,1,0:T(8,128)(2,1)}, u32[]{:S(2)}, u32[]{:S(2)}) %collective-permute-start.6) | collective-permute-done | bytes 524320 | tf_op jit(solution)/shard_map/ppermute | solution.py:308
  83.6 52.6 %collective-permute-done.7.refs_3_ = bf16[2,16,4,16,128]{4,3,2,1,0:T(8,128)(2,1)} collective-permute-done((bf16[2,16,4,16,128]{4,3,2,1,0:T(8,128)(2,1)}, bf16[2,16,4,16,128]{4,3,2,1,0:T(8,128)(2,1)}, u32[]{:S(2)}, u32[]{:S(2)}) %collective-permute-start.7) | collective-permute-done | bytes 524320 | tf_op jit(solution)/shard_map/ppermute | solution.py:308
  136.3 1.3 copy-done.21
  137.6 4.7 %up_project.2 = (f32[8,192,128]{2,1,0:T(8,128)S(1)}, f32[8,192,128]{2,1,0:T(8,128)S(1)}, bf16[8,192,128]{2,1,0:T(8,128)(2,1)}, bf16[8,192,128]{2,1,0:T(8,128)(2,1)S(1)}) custom-call(s32[1]{0:T(128)} %bitcast.side, s32[4]{0:T(128)S(1)} %pad_add_fusion.place, s32[2,64]{1,0:T(2,128)S(1)} %get-tuple-element.72.slots, ...), custom_call_target="tpu_custom_call" | custom-call | tf_op jit(solution)/shard_map/up_project/pallas_call | solution.py:172
  142.3 0.9 copy-done.6
  143.2 0.9 copy-done.10
  144.1 0.8 copy-done.22
  144.9 0.2 collective-permute-start.11
  145.1 1.1 copy-done.5
  146.3 4.5 %up_project.3 = (f32[8,192,128]{2,1,0:T(8,128)S(1)}, f32[8,192,128]{2,1,0:T(8,128)S(1)}, bf16[8,192,128]{2,1,0:T(8,128)(2,1)}, bf16[8,192,128]{2,1,0:T(8,128)(2,1)S(1)}) custom-call(s32[1]{0:T(128)} %bitcast.side, s32[4]{0:T(128)S(1)} %pad_add_fusion.place, s32[2,64]{1,0:T(2,128)S(1)} %get-tuple-element.71.slots, ...), custom_call_target="tpu_custom_call" | custom-call | tf_op jit(solution)/shard_map/up_project/pallas_call | solution.py:172
  150.8 0.9 copy-done.8
  151.7 0.9 copy-done.12
  152.6 0.8 copy-done.24
  153.3 2.7 %collective-permute-start.13 = (bf16[8,192,128]{2,1,0:T(8,128)(2,1)}, bf16[8,192,128]{2,1,0:T(8,128)(2,1)}, u32[]{:S(2)}, u32[]{:S(2)}) collective-permute-start(bf16[8,192,128]{2,1,0:T(8,128)(2,1)} %get-tuple-element.55), channel_id=1, source_target_pairs={{0,8},{2,10},{4,12},{6,14},{8,0},{10,2},{12,4},{14,6},{1,9},{3,11}... | collective-permute-start | bytes 1179656 | tf_op jit(solution)/shard_map/ppermute | solution.py:308
  156.0 0.7 copy.30
  156.7 0.9 slice.16.wanted
  157.6 14.5 %collective-permute-done.11.refs_2_ = bf16[8,192,128]{2,1,0:T(8,128)(2,1)S(1)} collective-permute-done((bf16[8,192,128]{2,1,0:T(8,128)(2,1)}, bf16[8,192,128]{2,1,0:T(8,128)(2,1)S(1)}, u32[]{:S(2)}, u32[]{:S(2)}) %collective-permute-start.11) | collective-permute-done | bytes 393248 | tf_op jit(solution)/shard_map/ppermute | solution.py:308
  172.1 7.3 %collective-permute-done.13.refs_3_ = bf16[8,192,128]{2,1,0:T(8,128)(2,1)} collective-permute-done((bf16[8,192,128]{2,1,0:T(8,128)(2,1)}, bf16[8,192,128]{2,1,0:T(8,128)(2,1)}, u32[]{:S(2)}, u32[]{:S(2)}) %collective-permute-start.13) | collective-permute-done | bytes 393248 | tf_op jit(solution)/shard_map/ppermute | solution.py:308
  179.4 1.0 copy-done.1
  180.4 1.1 copy-done.11
  181.5 1.1 copy-done.13
  182.7 4.6 %down_1.2 = (bf16[16,192,128]{2,1,0:T(8,128)(2,1)S(1)}, bf16[16,192,128]{2,1,0:T(8,128)(2,1)S(1)}) custom-call(s32[1]{0:T(128)} %bitcast.side, s32[1]{0:T(128)} %bitcast.8.which, s32[4]{0:T(128)S(1)} %pad_add_fusion.place, s32[2,128]{1,0:T(2,128)S(1)} %slice.16.wanted, f32[8,192,128]{2,1,0:T(8,128)S(1)} %copy-done.11, f32[8,192,128]{2,1,0:T(8,128)S(1)} %copy-done.13, ...), custom_call_target="tpu_custom_call" | custom-call | tf_op jit(solution)/shard_map/down_1/pallas_call | solution.py:261
  187.5 2.9 %collective-permute-start.14 = (bf16[8,192,128]{2,1,0:T(8,128)(2,1)S(1)}, bf16[8,192,128]{2,1,0:T(8,128)(2,1)S(1)}, u32[]{:S(2)}, u32[]{:S(2)}) collective-permute-start(bf16[8,192,128]{2,1,0:T(8,128)(2,1)S(1)} %copy-done.25), channel_id=1, source_target_pairs={{0,8},{2,10},{4,12},{6,14},{8,0},{10,2},{12,4},{14,6},{1,9},{3,11}... | collective-permute-start | bytes 1179656 | tf_op jit(solution)/shard_map/ppermute | solution.py:308
  190.4 1.2 copy-done.2
  191.6 5.1 %down_1.3 = f32[16,192,128]{2,1,0:T(8,128)} custom-call(s32[1]{0:T(128)} %bitcast.side, s32[1]{0:T(128)} %bitcast.1.which, s32[4]{0:T(128)S(1)} %pad_add_fusion.place, s32[2,128]{1,0:T(2,128)S(1)} %slice.16.wanted, bf16[16,192,128]{2,1,0:T(8,128)(2,1)S(1)} %get-tuple-element.69.refs_0_, bf16[2,32,4,16,128]{4,3,2,1,0:T(8,128)(2,1)S(1)} %copy-done, ...), custom_call_target="tpu_custom_call" | custom-call | tf_op jit(solution)/shard_map/down_1/pallas_call | solution.py:261
  196.7 18.5 %collective-permute-done.12.refs_2_ = bf16[8,192,128]{2,1,0:T(8,128)(2,1)S(1)} collective-permute-done((bf16[8,192,128]{2,1,0:T(8,128)(2,1)S(1)}, bf16[8,192,128]{2,1,0:T(8,128)(2,1)S(1)}, u32[]{:S(2)}, u32[]{:S(2)}) %collective-permute-start.12) | collective-permute-done | bytes 393248 | tf_op jit(solution)/shard_map/ppermute | solution.py:308
  215.2 8.4 %collective-permute-done.14.refs_3_ = bf16[8,192,128]{2,1,0:T(8,128)(2,1)S(1)} collective-permute-done((bf16[8,192,128]{2,1,0:T(8,128)(2,1)S(1)}, bf16[8,192,128]{2,1,0:T(8,128)(2,1)S(1)}, u32[]{:S(2)}, u32[]{:S(2)}) %collective-permute-start.14) | collective-permute-done | bytes 393248 | tf_op jit(solution)/shard_map/ppermute | solution.py:308
  223.6 4.4 %down_0.2 = (bf16[16,192,128]{2,1,0:T(8,128)(2,1)S(1)}, bf16[16,192,128]{2,1,0:T(8,128)(2,1)S(1)}) custom-call(s32[1]{0:T(128)} %bitcast.side, s32[1]{0:T(128)} %bitcast.8.which, s32[4]{0:T(128)S(1)} %pad_add_fusion.place, s32[2,128]{1,0:T(2,128)S(1)} %slice.16.wanted, f32[8,192,128]{2,1,0:T(8,128)S(1)} %copy-done.7, f32[8,192,128]{2,1,0:T(8,128)S(1)} %copy-done.9, ...), custom_call_target="tpu_custom_call" | custom-call | tf_op jit(solution)/shard_map/down_0/pallas_call | solution.py:261
  228.2 0.2 add_convert_fusion
  229.3 5.1 %down_0.3.mine_ref = f32[16,192,128]{2,1,0:T(8,128)} custom-call(s32[1]{0:T(128)} %bitcast.side, s32[1]{0:T(128)} %bitcast.1.which, s32[4]{0:T(128)S(1)} %pad_add_fusion.place, s32[2,128]{1,0:T(2,128)S(1)} %slice.16.wanted, bf16[16,192,128]{2,1,0:T(8,128)(2,1)S(1)} %get-tuple-element.65.refs_0_, bf16[2,32,4,16,128]{4,3,2,1,0:T(8,128)(2,1)S(1)} %copy-done, ...), custom_call_target="tpu_custom_call" | custom-call | tf_op jit(solution)/shard_map/down_0/pallas_call | solution.py:261
  234.4 31.8 %collective-permute-done.20.side_ref = bf16[16,192,128]{2,1,0:T(8,128)(2,1)} collective-permute-done((bf16[16,192,128]{2,1,0:T(8,128)(2,1)S(1)}, bf16[16,192,128]{2,1,0:T(8,128)(2,1)}, u32[]{:S(2)}, u32[]{:S(2)}) %collective-permute-start.20) | collective-permute-done | bytes 786464 | tf_op jit(solution)/shard_map/ppermute | solution.py:308
  266.2 4.0 %join.1 = bf16[192,2048]{1,0:T(8,128)(2,1)} custom-call(s32[1]{0:T(128)S(6)} %copy.48.length, bf16[192,2048]{1,0:T(8,128)(2,1)} %acoustic_ref.1, f32[16,192,128]{2,1,0:T(8,128)} %down_0.3.mine_ref, bf16[16,192,128]{2,1,0:T(8,128)(2,1)} %copy-done.27, bf16[16,192,128]{2,1,0:T(8,128)(2,1)} %collective-permute-done.20.side_ref), custom_call_target="tpu_custom_call" | custom-call | tf_op jit(solution)/shard_map/join/pallas_call | solution.py:297
  (75 shorter events, 1.4 us)
Async XLA Ops:
  0.0 7.3 %collective-permute-start = (s32[1]{0:T(128)}, s32[1]{0:T(128)}, u32[]{:S(2)}, u32[]{:S(2)}) collective-permute-start(s32[1]{0:T(128)} %param.14), channel_id=1, source_target_pairs={{0,8},{2,10},{4,12},{6,14},{8,0},{10,2},{12,4},{14,6},{1,9},{3,11}... | collective-permute-start | bytes 20 | tf_op jit(solution)/shard_map/ppermute | solution.py:308
  4.0 13.1 %collective-permute-start.3 = (bf16[192,2048]{1,0:T(8,128)(2,1)}, bf16[192,2048]{1,0:T(8,128)(2,1)S(1)}, u32[]{:S(2)}, u32[]{:S(2)}) collective-permute-start(bf16[192,2048]{1,0:T(8,128)(2,1)} %acoustic_ref.1), channel_id=1, source_target_pairs={{0,1},{1,0},{2,3},{3,2},{4,5},{5,4},{6,7},{7,6},{8,9},{9,8},{10,11... | collective-permute-start | bytes 2359304 | tf_op jit(solution)/shard_map/ppermute | solution.py:308
  8.1 3.5 %collective-permute-start.1 = (s32[2]{0:T(128)S(1)}, s32[2]{0:T(128)S(1)}, u32[]{:S(2)}, u32[]{:S(2)}) collective-permute-start(s32[2]{0:T(128)S(1)} %pad_add_fusion.1), channel_id=1, source_target_pairs={{0,2},{2,0},{4,6},{6,4},{8,10},{10,8},{12,14},{14,12},{1,3},{3,1},... | collective-permute-start | bytes 32 | tf_op jit(solution)/shard_map/ppermute | solution.py:308
  12.4 3.5 %collective-permute-start.2 = (s32[4]{0:T(128)S(1)}, s32[4]{0:T(128)S(1)}, u32[]{:S(2)}, u32[]{:S(2)}) collective-permute-start(s32[4]{0:T(128)S(1)} %pad_add_fusion.2), channel_id=1, source_target_pairs={{0,4},{2,6},{4,0},{6,2},{8,12},{10,14},{12,8},{14,10},{1,5},{3,7},... | collective-permute-start | bytes 56 | tf_op jit(solution)/shard_map/ppermute | solution.py:308
  17.1 0.9 copy-start.28
  27.2 17.4 %collective-permute-start.8 = (bf16[2,16,4,16,128]{4,3,2,1,0:T(8,128)(2,1)}, bf16[2,16,4,16,128]{4,3,2,1,0:T(8,128)(2,1)S(1)}, u32[]{:S(2)}, u32[]{:S(2)}) collective-permute-start(bf16[2,16,4,16,128]{4,3,2,1,0:T(8,128)(2,1)} %get-tuple-element.47), channel_id=1, source_target_pairs={{0,2},{2,0},{4,6},{6,4},{8,10},{10,8},{12,14},{14,12},{1,3},{3,1},... | collective-permute-start | bytes 1572872 | tf_op jit(solution)/shard_map/ppermute | solution.py:308
  28.7 33.1 %collective-permute-start.9 = (bf16[2,16,4,16,128]{4,3,2,1,0:T(8,128)(2,1)}, bf16[2,16,4,16,128]{4,3,2,1,0:T(8,128)(2,1)S(1)}, u32[]{:S(2)}, u32[]{:S(2)}) collective-permute-start(bf16[2,16,4,16,128]{4,3,2,1,0:T(8,128)(2,1)} %get-tuple-element.48), channel_id=1, source_target_pairs={{0,4},{2,6},{4,0},{6,2},{8,12},{10,14},{12,8},{14,10},{1,5},{3,7},... | collective-permute-start | bytes 1572872 | tf_op jit(solution)/shard_map/ppermute | solution.py:308
  30.2 8.0 %copy-start.29 = (s32[64,32,32]{0,2,1:T(8,128)S(1)}, s32[64,32,32]{0,2,1:T(8,128)}, u32[]{:S(2)}) copy-start(s32[64,32,32]{0,2,1:T(8,128)} %param.13) | copy-start | bytes 786436
  30.2 39.3 %collective-permute-start.10 = (bf16[2,16,4,16,128]{4,3,2,1,0:T(8,128)(2,1)}, bf16[2,16,4,16,128]{4,3,2,1,0:T(8,128)(2,1)S(1)}, u32[]{:S(2)}, u32[]{:S(2)}) collective-permute-start(bf16[2,16,4,16,128]{4,3,2,1,0:T(8,128)(2,1)} %get-tuple-element.49), channel_id=1, source_target_pairs={{0,6},{2,4},{4,2},{6,0},{8,14},{10,12},{12,10},{14,8},{1,7},{3,5},... | collective-permute-start | bytes 1572872 | tf_op jit(solution)/shard_map/ppermute | solution.py:308
  35.2 37.8 %collective-permute-start.5 = (bf16[2,16,4,16,128]{4,3,2,1,0:T(8,128)(2,1)}, bf16[2,16,4,16,128]{4,3,2,1,0:T(8,128)(2,1)}, u32[]{:S(2)}, u32[]{:S(2)}) collective-permute-start(bf16[2,16,4,16,128]{4,3,2,1,0:T(8,128)(2,1)} %get-tuple-element.42), channel_id=1, source_target_pairs={{0,2},{2,0},{4,6},{6,4},{8,10},{10,8},{12,14},{14,12},{1,3},{3,1},... | collective-permute-start | bytes 1572872 | tf_op jit(solution)/shard_map/ppermute | solution.py:308
  36.7 46.5 %collective-permute-start.6 = (bf16[2,16,4,16,128]{4,3,2,1,0:T(8,128)(2,1)}, bf16[2,16,4,16,128]{4,3,2,1,0:T(8,128)(2,1)}, u32[]{:S(2)}, u32[]{:S(2)}) collective-permute-start(bf16[2,16,4,16,128]{4,3,2,1,0:T(8,128)(2,1)} %get-tuple-element.43), channel_id=1, source_target_pairs={{0,4},{2,6},{4,0},{6,2},{8,12},{10,14},{12,8},{14,10},{1,5},{3,7},... | collective-permute-start | bytes 1572872 | tf_op jit(solution)/shard_map/ppermute | solution.py:308
  44.6 0.8 copy-start.15
  45.4 90.8 %collective-permute-start.4 = (bf16[16,192,128]{2,1,0:T(8,128)(2,1)}, bf16[16,192,128]{2,1,0:T(8,128)(2,1)S(1)}, u32[]{:S(2)}, u32[]{:S(2)}) collective-permute-start(bf16[16,192,128]{2,1,0:T(8,128)(2,1)} %get-tuple-element.39), channel_id=1, source_target_pairs={{0,8},{2,10},{4,12},{6,14},{8,0},{10,2},{12,4},{14,6},{1,9},{3,11}... | collective-permute-start | bytes 2359304 | tf_op jit(solution)/shard_map/ppermute | solution.py:308
  54.3 16.1 %copy-start.30 = (s32[8,32,4]{1,0,2:T(8,128)}, s32[8,32,4]{1,0,2:T(8,128)S(1)}, u32[]{:S(2)}) copy-start(s32[8,32,4]{1,0,2:T(8,128)S(1)} %fusion.4) | copy-start | bytes 12292
  61.8 0.8 copy-start.17
  69.5 0.8 copy-start.19
  70.3 109.1 %collective-permute-start.15 = (bf16[2,32,4,16,128]{4,3,2,1,0:T(8,128)(2,1)}, bf16[2,32,4,16,128]{4,3,2,1,0:T(8,128)(2,1)S(1)}, u32[]{:S(2)}, u32[]{:S(2)}) collective-permute-start(bf16[2,32,4,16,128]{4,3,2,1,0:T(8,128)(2,1)} %get-tuple-element.62), channel_id=1, source_target_pairs={{0,2},{2,0},{4,6},{6,4},{8,10},{10,8},{12,14},{14,12},{1,3},{3,1},... | collective-permute-start | bytes 3145736 | tf_op jit(solution)/shard_map/ppermute | solution.py:308
  72.9 106.5 %collective-permute-start.16 = (bf16[2,32,4,16,128]{4,3,2,1,0:T(8,128)(2,1)}, bf16[2,32,4,16,128]{4,3,2,1,0:T(8,128)(2,1)S(1)}, u32[]{:S(2)}, u32[]{:S(2)}) collective-permute-start(bf16[2,32,4,16,128]{4,3,2,1,0:T(8,128)(2,1)} %get-tuple-element.63), channel_id=1, source_target_pairs={{0,4},{2,6},{4,0},{6,2},{8,12},{10,14},{12,8},{14,10},{1,5},{3,7},... | collective-permute-start | bytes 3145736 | tf_op jit(solution)/shard_map/ppermute | solution.py:308
  73.0 106.5 %collective-permute-start.17 = (bf16[2,32,4,16,128]{4,3,2,1,0:T(8,128)(2,1)}, bf16[2,32,4,16,128]{4,3,2,1,0:T(8,128)(2,1)}, u32[]{:S(2)}, u32[]{:S(2)}) collective-permute-start(bf16[2,32,4,16,128]{4,3,2,1,0:T(8,128)(2,1)} %get-tuple-element.64), channel_id=1, source_target_pairs={{0,6},{2,4},{4,2},{6,0},{8,14},{10,12},{12,10},{14,8},{1,7},{3,5},... | collective-permute-start | bytes 3145736 | tf_op jit(solution)/shard_map/ppermute | solution.py:308
  83.2 53.0 %collective-permute-start.7 = (bf16[2,16,4,16,128]{4,3,2,1,0:T(8,128)(2,1)}, bf16[2,16,4,16,128]{4,3,2,1,0:T(8,128)(2,1)}, u32[]{:S(2)}, u32[]{:S(2)}) collective-permute-start(bf16[2,16,4,16,128]{4,3,2,1,0:T(8,128)(2,1)} %get-tuple-element.44), channel_id=1, source_target_pairs={{0,6},{2,4},{4,2},{6,0},{8,14},{10,12},{12,10},{14,8},{1,7},{3,5},... | collective-permute-start | bytes 1572872 | tf_op jit(solution)/shard_map/ppermute | solution.py:308
  136.3 6.1 %copy-start.4 = (bf16[16,192,128]{2,1,0:T(8,128)(2,1)}, bf16[16,192,128]{2,1,0:T(8,128)(2,1)S(1)}, u32[]{:S(2)}) copy-start(bf16[16,192,128]{2,1,0:T(8,128)(2,1)S(1)} %collective-permute-done.4.far_ref) | copy-start | bytes 2359300
  136.3 1.3 copy-start.21
  137.6 7.5 %copy-start.14 = (bf16[2,16,4,16,128]{4,3,2,1,0:T(8,128)(2,1)S(1)}, bf16[2,16,4,16,128]{4,3,2,1,0:T(8,128)(2,1)}, u32[]{:S(2)}) copy-start(bf16[2,16,4,16,128]{4,3,2,1,0:T(8,128)(2,1)} %get-tuple-element.46.refs_0_) | copy-start | bytes 1572868
  137.6 7.5 %copy-start.16 = (bf16[2,16,4,16,128]{4,3,2,1,0:T(8,128)(2,1)S(1)}, bf16[2,16,4,16,128]{4,3,2,1,0:T(8,128)(2,1)}, u32[]{:S(2)}) copy-start(bf16[2,16,4,16,128]{4,3,2,1,0:T(8,128)(2,1)} %copy-done.15) | copy-start | bytes 1572868
  137.6 7.5 %copy-start.18 = (bf16[2,16,4,16,128]{4,3,2,1,0:T(8,128)(2,1)S(1)}, bf16[2,16,4,16,128]{4,3,2,1,0:T(8,128)(2,1)}, u32[]{:S(2)}) copy-start(bf16[2,16,4,16,128]{4,3,2,1,0:T(8,128)(2,1)} %copy-done.17) | copy-start | bytes 1572868
  137.6 7.5 %copy-start.20 = (bf16[2,16,4,16,128]{4,3,2,1,0:T(8,128)(2,1)S(1)}, bf16[2,16,4,16,128]{4,3,2,1,0:T(8,128)(2,1)}, u32[]{:S(2)}) copy-start(bf16[2,16,4,16,128]{4,3,2,1,0:T(8,128)(2,1)} %copy-done.19) | copy-start | bytes 1572868
  142.3 0.9 copy-start.6
  143.2 0.9 copy-start.10
  144.1 0.8 copy-start.22
  144.9 27.2 %collective-permute-start.11 = (bf16[8,192,128]{2,1,0:T(8,128)(2,1)}, bf16[8,192,128]{2,1,0:T(8,128)(2,1)S(1)}, u32[]{:S(2)}, u32[]{:S(2)}) collective-permute-start(bf16[8,192,128]{2,1,0:T(8,128)(2,1)} %get-tuple-element.52), channel_id=1, source_target_pairs={{0,8},{2,10},{4,12},{6,14},{8,0},{10,2},{12,4},{14,6},{1,9},{3,11}... | collective-permute-start | bytes 1179656 | tf_op jit(solution)/shard_map/ppermute | solution.py:308
  145.1 1.1 copy-start.5
  146.3 9.8 %slice-start = ((s32[8,32,4]{1,0,2:T(8,128)}), s32[2,32,4]{1,0,2:T(2,128)S(1)}, s32[]{:S(2)}) async-start(s32[8,32,4]{1,0,2:T(8,128)} %copy-done.30), calls=%async_computation | async-start | bytes 8192 | tf_op jit(solution)/shard_map/slice | solution.py:362
  146.3 34.1 %copy-start = (bf16[2,32,4,16,128]{4,3,2,1,0:T(8,128)(2,1)S(1)}, bf16[2,32,4,16,128]{4,3,2,1,0:T(8,128)(2,1)}, u32[]{:S(2)}) copy-start(bf16[2,32,4,16,128]{4,3,2,1,0:T(8,128)(2,1)} %get-tuple-element.61.refs_4_.refs_1_) | copy-start | bytes 3145732
  150.8 0.9 copy-start.8
  151.7 0.9 copy-start.12
  152.6 0.8 copy-start.24
  153.3 26.1 %collective-permute-start.13 = (bf16[8,192,128]{2,1,0:T(8,128)(2,1)}, bf16[8,192,128]{2,1,0:T(8,128)(2,1)}, u32[]{:S(2)}, u32[]{:S(2)}) collective-permute-start(bf16[8,192,128]{2,1,0:T(8,128)(2,1)} %get-tuple-element.55), channel_id=1, source_target_pairs={{0,8},{2,10},{4,12},{6,14},{8,0},{10,2},{12,4},{14,6},{1,9},{3,11}... | collective-permute-start | bytes 1179656 | tf_op jit(solution)/shard_map/ppermute | solution.py:308
  179.4 1.0 copy-start.1
  180.4 1.1 copy-start.11
  181.5 1.1 copy-start.13
  182.7 4.7 %copy-start.23 = (bf16[8,192,128]{2,1,0:T(8,128)(2,1)S(1)}, bf16[8,192,128]{2,1,0:T(8,128)(2,1)}, u32[]{:S(2)}) copy-start(bf16[8,192,128]{2,1,0:T(8,128)(2,1)} %copy-done.22) | copy-start | bytes 1179652
  182.7 4.8 %copy-start.25 = (bf16[8,192,128]{2,1,0:T(8,128)(2,1)S(1)}, bf16[8,192,128]{2,1,0:T(8,128)(2,1)}, u32[]{:S(2)}) copy-start(bf16[8,192,128]{2,1,0:T(8,128)(2,1)} %copy-done.24) | copy-start | bytes 1179652
  187.3 40.9 %collective-permute-start.19 = (bf16[16,192,128]{2,1,0:T(8,128)(2,1)S(1)}, bf16[16,192,128]{2,1,0:T(8,128)(2,1)S(1)}, u32[]{:S(2)}, u32[]{:S(2)}) collective-permute-start(bf16[16,192,128]{2,1,0:T(8,128)(2,1)S(1)} %get-tuple-element.70), channel_id=1, source_target_pairs={{0,1},{1,0},{2,3},{3,2},{4,5},{5,4},{6,7},{7,6},{8,9},{9,8},{10,11... | collective-permute-start | bytes 2359304 | tf_op jit(solution)/shard_map/ppermute | solution.py:308
  187.4 27.8 %collective-permute-start.12 = (bf16[8,192,128]{2,1,0:T(8,128)(2,1)S(1)}, bf16[8,192,128]{2,1,0:T(8,128)(2,1)S(1)}, u32[]{:S(2)}, u32[]{:S(2)}) collective-permute-start(bf16[8,192,128]{2,1,0:T(8,128)(2,1)S(1)} %copy-done.23), channel_id=1, source_target_pairs={{0,8},{2,10},{4,12},{6,14},{8,0},{10,2},{12,4},{14,6},{1,9},{3,11}... | collective-permute-start | bytes 1179656 | tf_op jit(solution)/shard_map/ppermute | solution.py:308
  187.5 36.1 %collective-permute-start.14 = (bf16[8,192,128]{2,1,0:T(8,128)(2,1)S(1)}, bf16[8,192,128]{2,1,0:T(8,128)(2,1)S(1)}, u32[]{:S(2)}, u32[]{:S(2)}) collective-permute-start(bf16[8,192,128]{2,1,0:T(8,128)(2,1)S(1)} %copy-done.25), channel_id=1, source_target_pairs={{0,8},{2,10},{4,12},{6,14},{8,0},{10,2},{12,4},{14,6},{1,9},{3,11}... | collective-permute-start | bytes 1179656 | tf_op jit(solution)/shard_map/ppermute | solution.py:308
  190.4 1.2 copy-start.2
  191.6 32.0 %copy-start.7 = (f32[8,192,128]{2,1,0:T(8,128)S(1)}, f32[8,192,128]{2,1,0:T(8,128)}, u32[]{:S(2)}) copy-start(f32[8,192,128]{2,1,0:T(8,128)} %copy-done.6) | copy-start | bytes 2359300
  191.6 32.0 %copy-start.9 = (f32[8,192,128]{2,1,0:T(8,128)S(1)}, f32[8,192,128]{2,1,0:T(8,128)}, u32[]{:S(2)}) copy-start(f32[8,192,128]{2,1,0:T(8,128)} %copy-done.8) | copy-start | bytes 2359300
  223.6 4.6 %copy-start.26 = (f32[16,192,128]{2,1,0:T(8,128)S(1)}, f32[16,192,128]{2,1,0:T(8,128)}, u32[]{:S(2)}) copy-start(f32[16,192,128]{2,1,0:T(8,128)} %down_1.3) | copy-start | bytes 4718596
  228.0 1.2 copy-start.3
  228.0 6.3 %collective-permute-start.18 = (bf16[16,192,128]{2,1,0:T(8,128)(2,1)S(1)}, bf16[16,192,128]{2,1,0:T(8,128)(2,1)S(1)}, u32[]{:S(2)}, u32[]{:S(2)}) collective-permute-start(bf16[16,192,128]{2,1,0:T(8,128)(2,1)S(1)} %get-tuple-element.66), channel_id=1, source_target_pairs={{0,1},{1,0},{2,3},{3,2},{4,5},{5,4},{6,7},{7,6},{8,9},{9,8},{10,11... | collective-permute-start | bytes 2359304 | tf_op jit(solution)/shard_map/ppermute | solution.py:308
  228.4 37.8 %collective-permute-start.20 = (bf16[16,192,128]{2,1,0:T(8,128)(2,1)S(1)}, bf16[16,192,128]{2,1,0:T(8,128)(2,1)}, u32[]{:S(2)}, u32[]{:S(2)}) collective-permute-start(bf16[16,192,128]{2,1,0:T(8,128)(2,1)S(1)} %add_convert_fusion), channel_id=1, source_target_pairs={{0,8},{2,10},{4,12},{6,14},{8,0},{10,2},{12,4},{14,6},{1,9},{3,11}... | collective-permute-start | bytes 2359304 | tf_op jit(solution)/shard_map/ppermute | solution.py:308
  234.4 31.8 %copy-start.27 = (bf16[16,192,128]{2,1,0:T(8,128)(2,1)}, bf16[16,192,128]{2,1,0:T(8,128)(2,1)S(1)}, u32[]{:S(2)}) copy-start(bf16[16,192,128]{2,1,0:T(8,128)(2,1)S(1)} %collective-permute-done.18.core_ref) | copy-start | bytes 2359300

commit v4 on v3

--- a/solution.py
+++ b/solution.py
@@ -59,7 +59,8 @@
                 turned = half_turn(rounded)
                 near_ref[at * slots + e] = jnp.where(near_low, rounded, turned).astype(jnp.bfloat16)
                 far.append(jnp.where(near_low, turned, rounded))
-            far_ref[(at * slots + d) // 2] = jnp.where(low, far[0], far[1]).astype(jnp.bfloat16)
+            if at == 0:
+                far_ref[d // 2] = jnp.where(low, far[0], far[1]).astype(jnp.bfloat16)
 
 
 def norm_parts(side, own, peer, gains):
@@ -77,81 +78,118 @@
             ],
             out_specs=[
                 pl.BlockSpec((slots, frames, BLK), lambda i, *_: (0, 0, 0)),
-                pl.BlockSpec((slots // 2, frames, BLK), lambda i, *_: (0, 0, 0)),
+                pl.BlockSpec((slots // 4, frames, BLK), lambda i, *_: (0, 0, 0)),
             ],
         ),
         out_shape=[
-            jax.ShapeDtypeStruct((slots, frames, BLK), jnp.bfloat16),
-            jax.ShapeDtypeStruct((slots // 2, frames, BLK), jnp.bfloat16),
+            pltpu.HBM((slots, frames, BLK), jnp.bfloat16),
+            pltpu.HBM((slots // 4, frames, BLK), jnp.bfloat16),
         ],
         name="norm_parts",
     )(side, own, peer, gains)
 
 
-def pick_kernel(wanted, weight_ref, *refs, rows, runs, base, turning):
-    out_refs, spread = refs[:-1], refs[-1]
+def pick_kernel(place, wanted, weight_ref, *refs, rows, runs, base, turning, after):
+    out_refs, spread = refs[after:-1], refs[-1]
     step = pl.program_id(0) + base
     for h in range(HSTEP):
         for row in range(rows):
             tile = weight_ref[h, :, row * BLK:(row + 1) * BLK].astype(jnp.float32)
             for g in range(runs):
                 spread[h * runs + g, row * GROUP:(row + 1) * GROUP, :] = tile[g * GROUP:(g + 1) * GROUP]
-    for k, out_ref in enumerate(out_refs):
+    for member in range(wanted.shape[0] // 2):
+        pair = 2 * (place[0] ^ member)
         for u in range(2):
             for h in range(HSTEP):
                 for g in range(runs):
-                    at = wanted[2 * k + u, (step * HSTEP + h) * runs + g]
+                    at = wanted[pair + u, (step * HSTEP + h) * runs + g]
                     block = spread[h * runs + g, pl.ds(at, rows, stride=GROUP), :]
                     if turning and h % 2:
                         block = half_turn(block)
-                    out_ref[u, h, g] = block.astype(jnp.bfloat16)
-
-
-def pick_blocks(weight, wanted, first, count, turning):
+                    block = block.astype(jnp.bfloat16)
+                    if turning:
+                        out_refs[0][member, u, h, g] = block
+                    else:
+                        out_refs[u][member, h, g] = block
+
+
+def pick_blocks(weight, place, wanted, first, count, turning, after=()):
     _, feat_blocks, width = weight.shape
     rows = width // BLK
     runs = feat_blocks // GROUP
-    targets = wanted.shape[0] // 2
     base = first // HSTEP
-    out_shape = jax.ShapeDtypeStruct((2, count, runs, rows, BLK), jnp.bfloat16)
-    out_spec = pl.BlockSpec((2, HSTEP, runs, rows, BLK), lambda i, *_: (0, i, 0, 0, 0))
-    return pl.pallas_call(
-        functools.partial(pick_kernel, rows=rows, runs=runs, base=base, turning=turning),
+    members = wanted.shape[0] // 2
+    if turning:
+        outs = 1
+        shape = (members, 2, count, runs, rows, BLK)
+        out_spec = pl.BlockSpec((members, 2, HSTEP, runs, rows, BLK), lambda i, *_: (0, 0, i, 0, 0, 0))
+    else:
+        outs = 2
+        shape = (members, count, runs, rows, BLK)
+        out_spec = pl.BlockSpec((members, HSTEP, runs, rows, BLK), lambda i, *_: (0, i, 0, 0, 0))
+    return pl.pallas_call(
+        functools.partial(pick_kernel, rows=rows, runs=runs, base=base, turning=turning, after=len(after)),
         grid_spec=pltpu.PrefetchScalarGridSpec(
-            num_scalar_prefetch=1,
+            num_scalar_prefetch=2,
             grid=(count // HSTEP,),
-            in_specs=[pl.BlockSpec((HSTEP, feat_blocks, width), lambda i, *_: (i + base, 0, 0))],
-            out_specs=[out_spec] * targets,
+            in_specs=[pl.BlockSpec((HSTEP, feat_blocks, width), lambda i, *_: (i + base, 0, 0))]
+            + [corner(value) for value in after],
+            out_specs=[out_spec] * outs,
             scratch_shapes=[pltpu.VMEM((HSTEP * runs, rows * GROUP, BLK), jnp.float32)],
         ),
-        out_shape=[out_shape] * targets,
+        out_shape=[pltpu.HBM(shape, jnp.bfloat16)] * outs,
+        compiler_params=pltpu.CompilerParams(vmem_limit_bytes=48 << 20),
         name="pick_up" if turning else "pick_down",
-    )(wanted, weight)
-
-
-def up_kernel(side, place, slots, own_ref, far_ref, *refs, runs, rows):
-    weight_refs, refs = refs[:-6], refs[-6:]
+    )(place, wanted, *in_hbm([weight]), *after)
+
+
+def corner(value):
+    zeros = (0,) * value.ndim
+    return pl.BlockSpec((1,) * (value.ndim - 2) + (16, BLK), lambda i, *_: zeros)
+
+
+def gate_kernel(*refs):
+    del refs
+
+
+def gate(values, after):
+    anywhere = pl.BlockSpec(memory_space=pl.ANY)
+    return pl.pallas_call(
+        gate_kernel,
+        grid=(1,),
+        in_specs=[anywhere] * len(values) + [corner(value) for value in after],
+        out_specs=[anywhere] * len(values),
+        out_shape=[pltpu.HBM(value.shape, value.dtype) for value in values],
+        input_output_aliases={i: i for i in range(len(values))},
+        name="gate",
+    )(*in_hbm(values), *after)
+
+
+def up_kernel(side, slots, own_ref, far_a_ref, far_b_ref, weight_ref, *refs, runs, rows):
     kept_refs, sent_refs, partner, held = refs[:2], refs[2:4], refs[4], refs[5]
     step = pl.program_id(0)
     frames = own_ref.shape[1]
     low = low_lanes((frames, BLK))
     even = low == (side[0] == 0)
-    side_rows = rows * len(weight_refs)
+    members = weight_ref.shape[0]
+    side_rows = rows * members
 
     @pl.when(step == 0)
     def _():
-        for m in range(far_ref.shape[0]):
-            pair = far_ref[m].astype(jnp.float32)
-            turned = half_turn(pair)
-            partner[2 * m] = jnp.where(low, pair, turned).astype(jnp.bfloat16)
-            partner[2 * m + 1] = jnp.where(low, turned, pair).astype(jnp.bfloat16)
-
-    for k, ref in enumerate(weight_refs):
-        start = pl.multiple_of(place[k] * rows, rows)
+        for at, far_ref in enumerate((far_a_ref, far_b_ref)):
+            for m in range(far_ref.shape[0]):
+                pair = far_ref[m].astype(jnp.float32)
+                turned = half_turn(pair)
+                first = 2 * (at * far_ref.shape[0] + m)
+                partner[first] = jnp.where(low, pair, turned).astype(jnp.bfloat16)
+                partner[first + 1] = jnp.where(low, turned, pair).astype(jnp.bfloat16)
+
+    for member in range(members):
         for u in range(2):
             for h in range(HSTEP):
                 for g in range(runs):
-                    held[u, h, pl.ds(start + g * side_rows, rows), :] = ref[u, h, g]
+                    start = g * side_rows + member * rows
+                    held[u, h, start:start + rows, :] = weight_ref[member, u, h, g]
     for m in range(HSTEP // 2):
         for u, source in enumerate((own_ref, partner)):
             pair = []
@@ -165,39 +203,40 @@
             sent_refs[u][m] = jnp.where(even, pair[1], pair[0]).astype(jnp.bfloat16)
 
 
-def up_project(side, place, slots, own, far, weights):
-    _, hidden_blocks, runs, rows, _ = weights[0].shape
+def up_project(side, slots, own, far, weights):
+    members, _, hidden_blocks, runs, rows, _ = weights.shape
     slots_all, frames, _ = own.shape
     out_spec = pl.BlockSpec((HSTEP // 2, frames, BLK), lambda i, *_: (i, 0, 0))
     return pl.pallas_call(
         functools.partial(up_kernel, runs=runs, rows=rows),
         grid_spec=pltpu.PrefetchScalarGridSpec(
-            num_scalar_prefetch=3,
+            num_scalar_prefetch=2,
             grid=(hidden_blocks // HSTEP,),
             in_specs=[
                 pl.BlockSpec((slots_all, frames, BLK), lambda i, *_: (0, 0, 0)),
-                pl.BlockSpec((slots_all // 2, frames, BLK), lambda i, *_: (0, 0, 0)),
-            ]
-            + [pl.BlockSpec((2, HSTEP, runs, rows, BLK), lambda i, *_: (0, i, 0, 0, 0))] * len(weights),
+                pl.BlockSpec((slots_all // 4, frames, BLK), lambda i, *_: (0, 0, 0)),
+                pl.BlockSpec((slots_all // 4, frames, BLK), lambda i, *_: (0, 0, 0)),
+                pl.BlockSpec((members, 2, HSTEP, runs, rows, BLK), lambda i, *_: (0, 0, i, 0, 0, 0)),
+            ],
             out_specs=[out_spec] * 4,
             scratch_shapes=[
                 pltpu.VMEM((slots_all, frames, BLK), jnp.bfloat16),
-                pltpu.VMEM((2, HSTEP, runs * rows * len(weights), BLK), jnp.bfloat16),
+                pltpu.VMEM((2, HSTEP, runs * rows * members, BLK), jnp.bfloat16),
             ],
         ),
-        out_shape=[jax.ShapeDtypeStruct((hidden_blocks // 2, frames, BLK), jnp.float32)] * 2
-        + [jax.ShapeDtypeStruct((hidden_blocks // 2, frames, BLK), jnp.bfloat16)] * 2,
+        out_shape=[pltpu.HBM((hidden_blocks // 2, frames, BLK), jnp.float32)] * 2
+        + [pltpu.HBM((hidden_blocks // 2, frames, BLK), jnp.bfloat16)] * 2,
         compiler_params=pltpu.CompilerParams(vmem_limit_bytes=48 << 20),
         name="up_project",
-    )(side, place, slots, own, far, *weights)
-
-
-def down_kernel(side, which, place, wanted, *refs, utt, parts, runs, rows):
+    )(side, slots, *in_hbm([own]), *far, weights)
+
+
+def down_kernel(side, which, wanted, *refs, utt, parts, runs, rows):
     refs = list(refs)
     step = pl.program_id(0)
     if parts:
         kept_refs, got_refs, refs = refs[:parts], refs[parts:2 * parts], refs[2 * parts:]
-        weight_refs, out_ref, active_ref, held, total = refs[:-4], refs[-4], refs[-3], refs[-2], refs[-1]
+        weight_ref, out_ref, active_ref, held, total = refs
         per_part = pl.num_programs(0) // parts
         for p in range(parts):
             @pl.when(step // per_part == p)
@@ -205,20 +244,20 @@
                 before = kept_refs[p][...] + got_refs[p][...].astype(jnp.float32)
                 active_ref[...] = (before / (1.0 + jnp.exp(-before))).astype(jnp.bfloat16)
     else:
-        active_ref, weight_refs, out_ref, held, total = refs[0], refs[1:-3], refs[-3], refs[-2], refs[-1]
+        active_ref, weight_ref, out_ref, held, total = refs
 
     @pl.when(step == 0)
     def _():
         total[...] = jnp.zeros_like(total)
         held[...] = jnp.zeros_like(held)
 
-    for k, ref in enumerate(weight_refs):
-        for h in range(HSTEP):
-            top = HALF * (side[0] ^ (h % 2))
-            start = pl.multiple_of(place[k] * rows + top, rows)
+    for h in range(HSTEP):
+        top = HALF * (side[0] ^ (h % 2))
+        for member in range(weight_ref.shape[0]):
+            start = pl.multiple_of(member * rows + top, rows)
             for g in range(runs):
                 at = (h % 2) * runs + g
-                held[h // 2, pl.ds(start, rows), at * BLK:(at + 1) * BLK] = ref[0, h, g]
+                held[h // 2, pl.ds(start, rows), at * BLK:(at + 1) * BLK] = weight_ref[member, h, g]
     all_runs = 2 * runs
     for m in range(HSTEP // 2):
         product = jnp.dot(active_ref[m], held[m], preferred_element_type=jnp.float32)
@@ -234,8 +273,8 @@
         out_ref[...] = total[...].astype(out_ref.dtype)
 
 
-def down_project(side, which, place, wanted, sources, weights, utt, out_dtype):
-    _, hidden_blocks, all_runs, rows, _ = weights[0].shape
+def down_project(side, which, wanted, sources, weights, utt, out_dtype):
+    members, hidden_blocks, all_runs, rows, _ = weights.shape
     runs = all_runs // 2
     outs = runs * GROUP
     frames = sources[-1].shape[1]
@@ -254,19 +293,19 @@
     else:
         source_specs = [active_spec]
     out_specs = [pl.BlockSpec((outs, frames, BLK), lambda i, *_: (0, 0, 0))]
-    out_shape = [jax.ShapeDtypeStruct((outs, frames, BLK), out_dtype)]
+    out_shape = [pltpu.HBM((outs, frames, BLK), out_dtype)]
     if parts:
         out_specs.append(active_spec)
-        out_shape.append(jax.ShapeDtypeStruct((hidden_blocks // 2, frames, BLK), jnp.bfloat16))
+        out_shape.append(pltpu.HBM((hidden_blocks // 2, frames, BLK), jnp.bfloat16))
     return pl.pallas_call(
         functools.partial(down_kernel, utt=utt, parts=parts, runs=runs, rows=rows),
         grid_spec=pltpu.PrefetchScalarGridSpec(
-            num_scalar_prefetch=4,
+            num_scalar_prefetch=3,
             grid=(steps,),
             in_specs=source_specs
             + [
-                pl.BlockSpec((1, HSTEP, runs, rows, BLK), lambda i, side, which, *_: (utt, i, which[0], 0, 0))
-            ] * len(weights),
+                pl.BlockSpec((members, HSTEP, runs, rows, BLK), lambda i, side, which, *_: (0, i, which[0], 0, 0))
+            ],
             out_specs=out_specs,
             scratch_shapes=[
                 pltpu.VMEM((half_step, BLK, 2 * runs * BLK), jnp.bfloat16),
@@ -276,7 +315,7 @@
         out_shape=out_shape,
         compiler_params=pltpu.CompilerParams(vmem_limit_bytes=48 << 20),
         name=f"down_{utt}",
-    )(side, which, place, wanted, *sources, *weights)
+    )(side, which, wanted, *in_hbm(sources[:-parts] if parts else sources), *sources[len(sources) - parts:], weights)
 
 
 def join_kernel(length, acoustic_ref, mine_ref, core_ref, side_ref, out_ref):
@@ -299,13 +338,17 @@
         grid_spec=pltpu.PrefetchScalarGridSpec(
             num_scalar_prefetch=1, grid=(4,), in_specs=[flat, block, block, block], out_specs=flat
         ),
-        out_shape=jax.ShapeDtypeStruct(acoustic.shape, jnp.bfloat16),
+        out_shape=pltpu.HBM(acoustic.shape, jnp.bfloat16),
         name="join",
     )(lengths, acoustic, mine, from_core, from_side)
 
 
 def swap(value, axis, size, step):
     return lax.ppermute(value, axis, [(i, i ^ step) for i in range(size)])
+
+
+def in_hbm(values):
+    return [pltpu.with_memory_space_constraint(value, pltpu.HBM) for value in values]
 
 
 def split_body(acoustic, norm_gain, up_weight, down_weight, up_keep, down_keep, language, lengths, *, dp):
@@ -331,49 +374,56 @@
     slots = (up_own ^ (core * (feat_blocks // 2))).reshape(2, -1)
     wanted_up = wanted_up.reshape(2 * across, -1)
     wanted_down = wanted_down.reshape(2 * across, -1)
-    place = jnp.stack([(here ^ k) % across for k in members])
+    place = (here % across)[None]
     peer = swap(acoustic, "tensor", 2, 1)
     gains = norm_gain.reshape(2, 1, features)
     gains = jnp.where(core == 0, gains, gains[::-1])
     near, own_far = norm_parts(side, acoustic, peer, gains)
     far = swap(own_far, "dp", dp, across)
-    wanted_up, _ = lax.optimization_barrier((wanted_up, own_far))
+    far = (far, swap(far, "tensor", 2, 1))
+
+    groups = [[start + k for k in members] for start in (0, across)]
 
     def within_side(blocks):
-        return [blocks[0]] + [swap(blocks[k], "dp", dp, k) for k in members[1:]]
+        return lax.all_to_all(blocks, "dp", split_axis=0, concat_axis=0, axis_index_groups=groups, tiled=True)
 
     count = hidden_blocks // CHUNKS
-    kept, crossed, last = ([], []), ([], []), None
+    kept, crossed, after, got = ([], []), ([], []), in_hbm([own_far]), None
     for c in range(CHUNKS):
-        blocks = pick_blocks(up_weight, wanted_up, c * count, count, True)
+        (blocks,) = pick_blocks(up_weight, place, wanted_up, c * count, count, True, after)
+        after = in_hbm([blocks])
+        if got is not None:
+            (blocks,) = gate([blocks], [got, *far])
+            after = [got]
         got = within_side(blocks)
-        last = got
         span = slice(c * count * runs, (c + 1) * count * runs)
-        kept_own, kept_far, sent_own, sent_far = up_project(side, place, slots[:, span], near, far, got)
+        kept_own, kept_far, sent_own, sent_far = up_project(side, slots[:, span], near, far, got)
         got_far = swap(sent_own, "dp", dp, across)
-        sent_far, _ = lax.optimization_barrier((sent_far, got_far))
+        (sent_far,) = gate([sent_far], [got_far])
         got_own = swap(sent_far, "dp", dp, across)
         for u, (mine, theirs) in enumerate(((kept_own, got_own), (kept_far, got_far))):
             kept[u].append(mine)
             crossed[u].append(theirs)
-    blocks = pick_blocks(down_weight, wanted_down, 0, hidden_blocks, False)
-    blocks, _ = lax.optimization_barrier((blocks, last))
-    got = within_side(blocks)
+    own_blocks, far_blocks = pick_blocks(down_weight, place, wanted_down, 0, hidden_blocks, False, after)
+    (far_blocks,) = gate([far_blocks], [got, *crossed[1][:-1]])
+    far_down = within_side(far_blocks)
+    (own_blocks,) = gate([own_blocks], [far_down, *crossed[1], *crossed[0][:-1]])
+    own_down = within_side(own_blocks)
     rows_down = wanted_down[:2]
 
-    def down(which, sources, utt, dtype):
-        return down_project(side, which, place, rows_down, sources, got, utt, dtype)
+    def down(which, sources, weights, utt, dtype):
+        return down_project(side, which, rows_down, sources, weights, utt, dtype)
 
     other_core = (1 - core)[None]
     this_core = core[None]
-    for_peer, active_far = down(other_core, kept[1] + crossed[1], 1, jnp.bfloat16)
+    for_peer, active_far = down(other_core, kept[1] + crossed[1], far_down, 1, jnp.bfloat16)
     from_peer = swap(for_peer, "tensor", 2, 1)
-    (far_mine,) = down(this_core, [active_far], 1, jnp.float32)
+    (far_mine,) = down(this_core, [active_far], far_down, 1, jnp.float32)
     for_side = (far_mine + from_peer.astype(jnp.float32)).astype(jnp.bfloat16)
     from_side = swap(for_side, "dp", dp, across)
-    own_peer, active_own = down(other_core, kept[0] + crossed[0], 0, jnp.bfloat16)
+    own_peer, active_own = down(other_core, kept[0] + crossed[0], own_down, 0, jnp.bfloat16)
     from_core = swap(own_peer, "tensor", 2, 1)
-    (own_mine,) = down(this_core, [active_own], 0, jnp.float32)
+    (own_mine,) = down(this_core, [active_own], own_down, 0, jnp.float32)
     return join(lengths, acoustic, own_mine, from_core, from_side)
 
 

time: 272 us -> 230 us (0.85)
  waiting for transfers between devices: 159 us -> 117 us
  local copies, waits for them, and re-layouts: 18.8 us -> 6.99 us
  Pallas kernels: 52.3 us -> 58.5 us
  starting transfers between devices: 32.5 us -> 36.7 us
    ppermute x21 -> x13, waiting for transfers between devices: 159 us -> 107 us  [swap(): return lax.ppermute(value, axis, [(i, i ^ step) for i in range(size)])]
    all_to_all x0 -> x4, starting transfers between devices: none -> 19.1 us  [within_side(): lax.all_to_all(blocks, 'dp', split_axis=0, concat_axis=0, axis_index_grou...]
    ppermute x21 -> x13, starting transfers between devices: 32.5 us -> 17.7 us  [swap(): return lax.ppermute(value, axis, [(i, i ^ step) for i in range(size)])]
    all_to_all x0 -> x4, waiting for transfers between devices: none -> 10.2 us  [within_side(): lax.all_to_all(blocks, 'dp', split_axis=0, concat_axis=0, axis_index_grou...]
    unnamed x62 -> x38, local copies, waits for them, and re-layouts: 15.5 us -> 6.2 us
    pallas_call x0 -> x5, Pallas kernels: none -> 3.47 us  [gate(): pl.pallas_call(gate_kernel, grid=(1,), in_specs=[anywhere] * len(values)...]
    pallas_call x4, Pallas kernels: 19.3 us -> 22.3 us  [down_project(): pl.pallas_call(functools.partial(down_kernel, utt=utt, parts=parts, runs=...]
  transfers between devices with their start and end apart: 21 -> 17, of which waited for: 11 -> 11; matrix products, arithmetic and copies ran while one was open for 3% -> 4% of each run, Pallas kernels for 13% -> 19%
where the time goes in v4:
time: 230 us; the launch traced here: 228 us
  waiting for transfers between devices  117 us (51%)
  Pallas kernels  58.5 us (25%)
  starting transfers between devices  36.7 us (16%)
  local copies, waits for them, and re-layouts  6.99 us (3%)
  other arithmetic  6.67 us (3%)
    ppermute x13, waiting for transfers between devices, swap(): return lax.ppermute(value, axis, [(i, i ^ step) for i in range(size)])  107 us
    pallas_call x4, Pallas kernels, down_project(): pl.pallas_call(functools.partial(down_kernel, utt=utt, parts=parts, runs=...  22.3 us
    all_to_all x4, starting transfers between devices, within_side(): lax.all_to_all(blocks, 'dp', split_axis=0, concat_axis=0, axis_index_grou...  19.1 us
    ppermute x13, starting transfers between devices, swap(): return lax.ppermute(value, axis, [(i, i ^ step) for i in range(size)])  17.7 us
    pallas_call x3, Pallas kernels, pick_blocks(): pl.pallas_call(functools.partial(pick_kernel, rows=rows, runs=runs, base=...  15.3 us
    all_to_all x4, waiting for transfers between devices, within_side(): lax.all_to_all(blocks, 'dp', split_axis=0, concat_axis=0, axis_index_grou...  10.2 us
    pallas_call x2, Pallas kernels, up_project(): pl.pallas_call(functools.partial(up_kernel, runs=runs, rows=rows), grid_s...  9.84 us
    unnamed x38, local copies, waits for them, and re-layouts  6.2 us
  transfers between devices with their start and end apart: 17, of which 11 were waited for; matrix products, arithmetic and copies ran while one was open for 4% of the time, Pallas kernels for 19%

profile of v4, /device:TPU:0, one launch (start us, length us, event | category | flops | bytes accessed | tf_op | source)
XLA Modules:
  0.0 228.2 jit_solution(12393319734926306317)
XLA Ops:
  0.0 4.0 %collective-permute-start = (s32[1]{0:T(128)}, s32[1]{0:T(128)}, u32[]{:S(2)}, u32[]{:S(2)}) collective-permute-start(s32[1]{0:T(128)} %param.14), channel_id=1, source_target_pairs={{0,8},{2,10},{4,12},{6,14},{8,0},{10,2},{12,4},{14,6},{1,9},{3,11}... | collective-permute-start | bytes 20 | tf_op jit(solution)/shard_map/ppermute | solution.py:347
  4.0 1.4 broadcast_select_fusion.gain_ref
  6.1 1.2 fusion
  7.3 0.6 pad_add_fusion
  8.0 1.5 collective-permute-start.1
  9.5 2.0 collective-permute-done.1
  11.5 0.6 pad_add_fusion.1
  12.2 1.6 collective-permute-start.2
  13.8 2.0 collective-permute-done.2
  15.7 0.6 pad_add_fusion.2
  16.4 0.3 fusion.2
  16.7 0.1 copy.39
  16.8 0.0 collective-permute-done.3.peer_ref
  16.8 0.9 copy-done.16
  17.8 3.6 %norm_parts.1 = (bf16[32,192,128]{2,1,0:T(8,128)(2,1)}, bf16[8,192,128]{2,1,0:T(8,128)(2,1)}) custom-call(s32[1]{0:T(128)} %bitcast.side, bf16[192,2048]{1,0:T(8,128)(2,1)} %acoustic_ref.1, bf16[192,2048]{1,0:T(8,128)(2,1)} %copy-done.16, f32[2,1,2048]{2,1,0:T(1,128)} %broadcast_select_fusion.gain_ref), custom_call_target="tpu_custom_call" | custom-call | tf_op jit(solution)/shard_map/norm_parts/pallas_call | solution.py:69
  21.4 4.3 %pick_up.2.refs_0_ = bf16[4,2,16,4,16,128]{5,4,3,2,1,0:T(8,128)(2,1)} custom-call(s32[1]{0:T(128)} %bitcast.7.place, s32[8,128]{1,0:T(8,128)S(1)} %copy.40.wanted, bf16[32,32,2048]{2,1,0:T(8,128)(2,1)} %weight_ref.4, bf16[8,192,128]{2,1,0:T(8,128)(2,1)} %get-tuple-element.22.refs_0_), custom_call_target="tpu_custom_call" | custom-call | tf_op jit(solution)/shard_map/pick_up/pallas_call | solution.py:130
  25.7 3.9 %all-to-all-start = ((bf16[4,2,16,4,16,128]{5,4,3,2,1,0:T(8,128)(2,1)}), bf16[4,2,16,4,16,128]{5,4,3,2,1,0:T(8,128)(2,1)S(1)}, u32[]{:S(2)}, u32[]{:S(2)}) async-start(bf16[4,2,16,4,16,128]{5,4,3,2,1,0:T(8,128)(2,1)} %pick_up.2.refs_0_), calls=%async_computation | async-start | bytes 4194304 | tf_op jit(solution)/shard_map/all_to_all | solution.py:388
  29.6 1.4 collective-permute-start.4
  31.0 28.2 %collective-permute-done.4.far_a_ref.refs_2_ = bf16[8,192,128]{2,1,0:T(8,128)(2,1)S(1)} collective-permute-done((bf16[8,192,128]{2,1,0:T(8,128)(2,1)S(1)}, bf16[8,192,128]{2,1,0:T(8,128)(2,1)S(1)}, u32[]{:S(2)}, u32[]{:S(2)}) %collective-permute-start.4) | collective-permute-done | bytes 393248 | tf_op jit(solution)/shard_map/ppermute | solution.py:347
  59.2 4.4 %pick_up.3.refs_0_ = bf16[4,2,16,4,16,128]{5,4,3,2,1,0:T(8,128)(2,1)} custom-call(s32[1]{0:T(128)} %bitcast.7.place, s32[8,128]{1,0:T(8,128)S(1)} %copy.40.wanted, bf16[32,32,2048]{2,1,0:T(8,128)(2,1)} %weight_ref.4, bf16[4,2,16,4,16,128]{5,4,3,2,1,0:T(8,128)(2,1)} %pick_up.2.refs_0_), custom_call_target="tpu_custom_call" | custom-call | tf_op jit(solution)/shard_map/pick_up/pallas_call | solution.py:130
  63.6 0.7 copy-done.10
  64.3 1.3 copy-done.2
  65.7 0.7 gate.5
  66.4 4.9 %all-to-all-start.1 = ((bf16[4,2,16,4,16,128]{5,4,3,2,1,0:T(8,128)(2,1)}), bf16[4,2,16,4,16,128]{5,4,3,2,1,0:T(8,128)(2,1)}, u32[]{:S(2)}, u32[]{:S(2)}) async-start(bf16[4,2,16,4,16,128]{5,4,3,2,1,0:T(8,128)(2,1)} %gate.5), calls=%async_computation.1 | async-start | bytes 4194304 | tf_op jit(solution)/shard_map/all_to_all | solution.py:388
  71.3 0.1 fusion.6
  71.3 0.1 copy.38
  71.4 0.1 reshape.26
  71.5 0.1 fusion.12
  71.6 0.0 copy-start.17
  71.6 4.8 %up_project.2 = (f32[8,192,128]{2,1,0:T(8,128)}, f32[8,192,128]{2,1,0:T(8,128)}, bf16[8,192,128]{2,1,0:T(8,128)(2,1)}, bf16[8,192,128]{2,1,0:T(8,128)(2,1)}) custom-call(s32[1]{0:T(128)} %bitcast.side, s32[2,64]{1,0:T(2,128)S(1)} %get-tuple-element.38.slots, bf16[32,192,128]{2,1,0:T(8,128)(2,1)} %get-tuple-element.21.own_ref, ...), custom_call_target="tpu_custom_call" | custom-call | tf_op jit(solution)/shard_map/up_project/pallas_call | solution.py:210
  76.4 3.2 %collective-permute-start.6 = (bf16[8,192,128]{2,1,0:T(8,128)(2,1)}, bf16[8,192,128]{2,1,0:T(8,128)(2,1)S(1)}, u32[]{:S(2)}, u32[]{:S(2)}) collective-permute-start(bf16[8,192,128]{2,1,0:T(8,128)(2,1)} %get-tuple-element.26), channel_id=1, source_target_pairs={{0,8},{2,10},{4,12},{6,14},{8,0},{10,2},{12,4},{14,6},{1,9},{3,11}... | collective-permute-start | bytes 1179656 | tf_op jit(solution)/shard_map/ppermute | solution.py:347
  79.7 0.2 fusion.1
  79.8 0.3 fusion.4
  80.1 0.1 copy.42
  80.3 6.6 %pick_down.1 = (bf16[4,32,4,16,128]{4,3,2,1,0:T(8,128)(2,1)}, bf16[4,32,4,16,128]{4,3,2,1,0:T(8,128)(2,1)}) custom-call(s32[1]{0:T(128)} %bitcast.7.place, s32[8,128]{1,0:T(8,128)S(1)} %copy.43.wanted, bf16[32,32,2048]{2,1,0:T(8,128)(2,1)} %weight_ref.5, bf16[4,2,16,4,16,128]{5,4,3,2,1,0:T(8,128)(2,1)S(1)} %copy-done.3), custom_call_target="tpu_custom_call" | custom-call | tf_op jit(solution)/shard_map/pick_down/pallas_call | solution.py:130
  86.9 16.4 %collective-permute-done.6.refs_1_.refs_2_ = bf16[8,192,128]{2,1,0:T(8,128)(2,1)S(1)} collective-permute-done((bf16[8,192,128]{2,1,0:T(8,128)(2,1)}, bf16[8,192,128]{2,1,0:T(8,128)(2,1)S(1)}, u32[]{:S(2)}, u32[]{:S(2)}) %collective-permute-start.6) | collective-permute-done | bytes 393248 | tf_op jit(solution)/shard_map/ppermute | solution.py:347
  103.2 2.9 %all-to-all-done.1.weight_ref.refs_1_ = bf16[4,2,16,4,16,128]{5,4,3,2,1,0:T(8,128)(2,1)} async-done(((bf16[4,2,16,4,16,128]{5,4,3,2,1,0:T(8,128)(2,1)}), bf16[4,2,16,4,16,128]{5,4,3,2,1,0:T(8,128)(2,1)}, u32[]{:S(2)}, u32[]{:S(2)}) %all-to-all-start.1) | async-done | bytes 2097184 | tf_op jit(solution)/shard_map/all_to_all | solution.py:388
  106.2 0.7 gate.8
  106.9 5.4 %all-to-all-start.2 = ((bf16[4,32,4,16,128]{4,3,2,1,0:T(8,128)(2,1)}), bf16[4,32,4,16,128]{4,3,2,1,0:T(8,128)(2,1)S(1)}, u32[]{:S(2)}, u32[]{:S(2)}) async-start(bf16[4,32,4,16,128]{4,3,2,1,0:T(8,128)(2,1)} %gate.8), calls=%async_computation.2 | async-start | bytes 4194304 | tf_op jit(solution)/shard_map/all_to_all | solution.py:388
  112.3 0.7 gate.6
  113.0 5.1 %up_project.3 = (f32[8,192,128]{2,1,0:T(8,128)}, f32[8,192,128]{2,1,0:T(8,128)}, bf16[8,192,128]{2,1,0:T(8,128)(2,1)}, bf16[8,192,128]{2,1,0:T(8,128)(2,1)}) custom-call(s32[1]{0:T(128)} %bitcast.side, s32[2,64]{1,0:T(2,128)S(1)} %get-tuple-element.37.slots, bf16[32,192,128]{2,1,0:T(8,128)(2,1)} %get-tuple-element.21.own_ref, ...), custom_call_target="tpu_custom_call" | custom-call | tf_op jit(solution)/shard_map/up_project/pallas_call | solution.py:210
  118.1 2.9 %collective-permute-start.8 = (bf16[8,192,128]{2,1,0:T(8,128)(2,1)}, bf16[8,192,128]{2,1,0:T(8,128)(2,1)S(1)}, u32[]{:S(2)}, u32[]{:S(2)}) collective-permute-start(bf16[8,192,128]{2,1,0:T(8,128)(2,1)} %get-tuple-element.28), channel_id=1, source_target_pairs={{0,8},{2,10},{4,12},{6,14},{8,0},{10,2},{12,4},{14,6},{1,9},{3,11}... | collective-permute-start | bytes 1179656 | tf_op jit(solution)/shard_map/ppermute | solution.py:347
  121.0 23.7 %collective-permute-done.7.refs_4_.refs_2_ = bf16[8,192,128]{2,1,0:T(8,128)(2,1)S(1)} collective-permute-done((bf16[8,192,128]{2,1,0:T(8,128)(2,1)}, bf16[8,192,128]{2,1,0:T(8,128)(2,1)S(1)}, u32[]{:S(2)}, u32[]{:S(2)}) %collective-permute-start.7) | collective-permute-done | bytes 393248 | tf_op jit(solution)/shard_map/ppermute | solution.py:347
  144.7 7.2 %collective-permute-done.8.refs_1_.refs_3_ = bf16[8,192,128]{2,1,0:T(8,128)(2,1)S(1)} collective-permute-done((bf16[8,192,128]{2,1,0:T(8,128)(2,1)}, bf16[8,192,128]{2,1,0:T(8,128)(2,1)S(1)}, u32[]{:S(2)}, u32[]{:S(2)}) %collective-permute-start.8) | collective-permute-done | bytes 393248 | tf_op jit(solution)/shard_map/ppermute | solution.py:347
  151.8 2.1 all-to-all-done.2.refs_1_.refs_4_
  153.9 1.4 copy-done
  155.3 0.7 gate.9
  156.0 4.9 %all-to-all-start.3 = ((bf16[4,32,4,16,128]{4,3,2,1,0:T(8,128)(2,1)}), bf16[4,32,4,16,128]{4,3,2,1,0:T(8,128)(2,1)}, u32[]{:S(2)}, u32[]{:S(2)}) async-start(bf16[4,32,4,16,128]{4,3,2,1,0:T(8,128)(2,1)} %gate.9), calls=%async_computation.3 | async-start | bytes 4194304 | tf_op jit(solution)/shard_map/all_to_all | solution.py:388
  160.9 0.1 copy.35
  161.0 0.1 slice.16.wanted
  161.1 5.8 %down_1.2 = (bf16[16,192,128]{2,1,0:T(8,128)(2,1)}, bf16[16,192,128]{2,1,0:T(8,128)(2,1)}) custom-call(s32[1]{0:T(128)} %bitcast.side, s32[1]{0:T(128)} %bitcast.4.which, s32[2,128]{1,0:T(2,128)S(1)} %slice.16.wanted, f32[8,192,128]{2,1,0:T(8,128)} %get-tuple-element.33.refs_0_, f32[8,192,128]{2,1,0:T(8,128)} %get-tuple-element.34.refs_1_, ...), custom_call_target="tpu_custom_call" | custom-call | tf_op jit(solution)/shard_map/down_1/pallas_call | solution.py:300
  166.9 0.7 gate.7
  167.6 1.3 collective-permute-start.9
  168.9 5.2 %down_1.3 = f32[16,192,128]{2,1,0:T(8,128)} custom-call(s32[1]{0:T(128)} %bitcast.side, s32[1]{0:T(128)} %bitcast.1.which, s32[2,128]{1,0:T(2,128)S(1)} %slice.16.wanted, bf16[16,192,128]{2,1,0:T(8,128)(2,1)} %get-tuple-element.35.refs_0_, bf16[4,32,4,16,128]{4,3,2,1,0:T(8,128)(2,1)S(1)} %copy-done.1), custom_call_target="tpu_custom_call" | custom-call | tf_op jit(solution)/shard_map/down_1/pallas_call | solution.py:300
  174.1 1.8 add_convert_fusion
  175.9 1.7 collective-permute-start.12
  177.6 15.6 %collective-permute-done.9.refs_3_ = bf16[8,192,128]{2,1,0:T(8,128)(2,1)S(1)} collective-permute-done((bf16[8,192,128]{2,1,0:T(8,128)(2,1)}, bf16[8,192,128]{2,1,0:T(8,128)(2,1)S(1)}, u32[]{:S(2)}, u32[]{:S(2)}) %collective-permute-start.9) | collective-permute-done | bytes 393248 | tf_op jit(solution)/shard_map/ppermute | solution.py:347
  193.3 5.2 %all-to-all-done.3.refs_4_.refs_1_ = bf16[4,32,4,16,128]{4,3,2,1,0:T(8,128)(2,1)} async-done(((bf16[4,32,4,16,128]{4,3,2,1,0:T(8,128)(2,1)}), bf16[4,32,4,16,128]{4,3,2,1,0:T(8,128)(2,1)}, u32[]{:S(2)}, u32[]{:S(2)}) %all-to-all-start.3) | async-done | bytes 2097184 | tf_op jit(solution)/shard_map/all_to_all | solution.py:388
  198.5 5.9 %down_0.2 = (bf16[16,192,128]{2,1,0:T(8,128)(2,1)}, bf16[16,192,128]{2,1,0:T(8,128)(2,1)}) custom-call(s32[1]{0:T(128)} %bitcast.side, s32[1]{0:T(128)} %bitcast.4.which, s32[2,128]{1,0:T(2,128)S(1)} %slice.16.wanted, f32[8,192,128]{2,1,0:T(8,128)} %get-tuple-element.23.refs_0_, f32[8,192,128]{2,1,0:T(8,128)} %get-tuple-element.24.refs_1_, ...), custom_call_target="tpu_custom_call" | custom-call | tf_op jit(solution)/shard_map/down_0/pallas_call | solution.py:300
  205.0 5.5 %down_0.3.mine_ref = f32[16,192,128]{2,1,0:T(8,128)} custom-call(s32[1]{0:T(128)} %bitcast.side, s32[1]{0:T(128)} %bitcast.1.which, s32[2,128]{1,0:T(2,128)S(1)} %slice.16.wanted, bf16[16,192,128]{2,1,0:T(8,128)(2,1)} %get-tuple-element.31.refs_0_, bf16[4,32,4,16,128]{4,3,2,1,0:T(8,128)(2,1)} %all-to-all-done.3.refs_4_.refs_1_), custom_call_target="tpu_custom_call" | custom-call | tf_op jit(solution)/shard_map/down_0/pallas_call | solution.py:300
  210.5 11.9 %collective-permute-done.12.side_ref = bf16[16,192,128]{2,1,0:T(8,128)(2,1)S(1)} collective-permute-done((bf16[16,192,128]{2,1,0:T(8,128)(2,1)S(1)}, bf16[16,192,128]{2,1,0:T(8,128)(2,1)S(1)}, u32[]{:S(2)}, u32[]{:S(2)}) %collective-permute-start.12) | collective-permute-done | bytes 786464 | tf_op jit(solution)/shard_map/ppermute | solution.py:347
  222.4 0.9 copy-done.14
  223.3 0.9 copy-done.15
  224.2 4.0 %join.1 = bf16[192,2048]{1,0:T(8,128)(2,1)} custom-call(s32[1]{0:T(128)S(6)} %copy.58.length, bf16[192,2048]{1,0:T(8,128)(2,1)} %acoustic_ref.1, f32[16,192,128]{2,1,0:T(8,128)} %down_0.3.mine_ref, bf16[16,192,128]{2,1,0:T(8,128)(2,1)} %copy-done.15, bf16[16,192,128]{2,1,0:T(8,128)(2,1)} %copy-done.14), custom_call_target="tpu_custom_call" | custom-call | tf_op jit(solution)/shard_map/join/pallas_call | solution.py:336
  (46 shorter events, 0.2 us)
Async XLA Ops:
  0.0 7.3 %collective-permute-start = (s32[1]{0:T(128)}, s32[1]{0:T(128)}, u32[]{:S(2)}, u32[]{:S(2)}) collective-permute-start(s32[1]{0:T(128)} %param.14), channel_id=1, source_target_pairs={{0,8},{2,10},{4,12},{6,14},{8,0},{10,2},{12,4},{14,6},{1,9},{3,11}... | collective-permute-start | bytes 20 | tf_op jit(solution)/shard_map/ppermute | solution.py:347
  4.0 12.8 %collective-permute-start.3 = (bf16[192,2048]{1,0:T(8,128)(2,1)}, bf16[192,2048]{1,0:T(8,128)(2,1)S(1)}, u32[]{:S(2)}, u32[]{:S(2)}) collective-permute-start(bf16[192,2048]{1,0:T(8,128)(2,1)} %acoustic_ref.1), channel_id=1, source_target_pairs={{0,1},{1,0},{2,3},{3,2},{4,5},{5,4},{6,7},{7,6},{8,9},{9,8},{10,11... | collective-permute-start | bytes 2359304 | tf_op jit(solution)/shard_map/ppermute | solution.py:347
  8.0 3.5 %collective-permute-start.1 = (s32[2]{0:T(128)S(1)}, s32[2]{0:T(128)S(1)}, u32[]{:S(2)}, u32[]{:S(2)}) collective-permute-start(s32[2]{0:T(128)S(1)} %pad_add_fusion), channel_id=1, source_target_pairs={{0,2},{2,0},{4,6},{6,4},{8,10},{10,8},{12,14},{14,12},{1,3},{3,1},... | collective-permute-start | bytes 32 | tf_op jit(solution)/shard_map/ppermute | solution.py:347
  12.2 3.5 %collective-permute-start.2 = (s32[4]{0:T(128)S(1)}, s32[4]{0:T(128)S(1)}, u32[]{:S(2)}, u32[]{:S(2)}) collective-permute-start(s32[4]{0:T(128)S(1)} %pad_add_fusion.1), channel_id=1, source_target_pairs={{0,4},{2,6},{4,0},{6,2},{8,12},{10,14},{12,8},{14,10},{1,5},{3,7},... | collective-permute-start | bytes 56 | tf_op jit(solution)/shard_map/ppermute | solution.py:347
  16.8 0.9 copy-start.16
  25.7 3.9 %copy-start.18 = (bf16[8,192,128]{2,1,0:T(8,128)(2,1)S(1)}, bf16[8,192,128]{2,1,0:T(8,128)(2,1)}, u32[]{:S(2)}) copy-start(bf16[8,192,128]{2,1,0:T(8,128)(2,1)} %get-tuple-element.22.refs_0_) | copy-start | bytes 1179652
  25.7 37.9 %all-to-all-start = ((bf16[4,2,16,4,16,128]{5,4,3,2,1,0:T(8,128)(2,1)}), bf16[4,2,16,4,16,128]{5,4,3,2,1,0:T(8,128)(2,1)S(1)}, u32[]{:S(2)}, u32[]{:S(2)}) async-start(bf16[4,2,16,4,16,128]{5,4,3,2,1,0:T(8,128)(2,1)} %pick_up.2.refs_0_), calls=%async_computation | async-start | bytes 4194304 | tf_op jit(solution)/shard_map/all_to_all | solution.py:388
  29.6 29.6 %collective-permute-start.4 = (bf16[8,192,128]{2,1,0:T(8,128)(2,1)S(1)}, bf16[8,192,128]{2,1,0:T(8,128)(2,1)S(1)}, u32[]{:S(2)}, u32[]{:S(2)}) collective-permute-start(bf16[8,192,128]{2,1,0:T(8,128)(2,1)S(1)} %copy-done.18), channel_id=1, source_target_pairs={{0,8},{2,10},{4,12},{6,14},{8,0},{10,2},{12,4},{14,6},{1,9},{3,11}... | collective-permute-start | bytes 1179656 | tf_op jit(solution)/shard_map/ppermute | solution.py:347
  59.2 4.4 %copy-start.8 = (bf16[8,192,128]{2,1,0:T(8,128)(2,1)}, bf16[8,192,128]{2,1,0:T(8,128)(2,1)S(1)}, u32[]{:S(2)}) copy-start(bf16[8,192,128]{2,1,0:T(8,128)(2,1)S(1)} %collective-permute-done.4.far_a_ref.refs_2_) | copy-start | bytes 1179652
  59.2 4.4 %collective-permute-start.5 = (bf16[8,192,128]{2,1,0:T(8,128)(2,1)S(1)}, bf16[8,192,128]{2,1,0:T(8,128)(2,1)S(1)}, u32[]{:S(2)}, u32[]{:S(2)}) collective-permute-start(bf16[8,192,128]{2,1,0:T(8,128)(2,1)S(1)} %collective-permute-done.4.far_a_ref.refs_2_), channel_id=1, source_target_pairs={{0,1},{1,0},{2,3},{3,2},{4,5},{5,4},{6,7},{7,6},{8,9},{9,8},{10,11... | collective-permute-start | bytes 1179656 | tf_op jit(solution)/shard_map/ppermute | solution.py:347
  63.6 0.8 copy-start.10
  64.3 1.3 copy-start.2
  66.4 5.2 %copy-start.3 = (bf16[4,2,16,4,16,128]{5,4,3,2,1,0:T(8,128)(2,1)S(1)}, bf16[4,2,16,4,16,128]{5,4,3,2,1,0:T(8,128)(2,1)}, u32[]{:S(2)}) copy-start(bf16[4,2,16,4,16,128]{5,4,3,2,1,0:T(8,128)(2,1)} %copy-done.2) | copy-start | bytes 6291460
  66.4 5.2 %copy-start.9 = (bf16[8,192,128]{2,1,0:T(8,128)(2,1)S(1)}, bf16[8,192,128]{2,1,0:T(8,128)(2,1)}, u32[]{:S(2)}) copy-start(bf16[8,192,128]{2,1,0:T(8,128)(2,1)} %copy-done.8) | copy-start | bytes 1179652
  66.4 5.2 %copy-start.11 = (bf16[8,192,128]{2,1,0:T(8,128)(2,1)S(1)}, bf16[8,192,128]{2,1,0:T(8,128)(2,1)}, u32[]{:S(2)}) copy-start(bf16[8,192,128]{2,1,0:T(8,128)(2,1)} %copy-done.10) | copy-start | bytes 1179652
  66.4 39.8 %all-to-all-start.1 = ((bf16[4,2,16,4,16,128]{5,4,3,2,1,0:T(8,128)(2,1)}), bf16[4,2,16,4,16,128]{5,4,3,2,1,0:T(8,128)(2,1)}, u32[]{:S(2)}, u32[]{:S(2)}) async-start(bf16[4,2,16,4,16,128]{5,4,3,2,1,0:T(8,128)(2,1)} %gate.5), calls=%async_computation.1 | async-start | bytes 4194304 | tf_op jit(solution)/shard_map/all_to_all | solution.py:388
  71.6 8.0 %copy-start.17 = (s32[64,32,32]{0,2,1:T(8,128)S(1)}, s32[64,32,32]{0,2,1:T(8,128)}, u32[]{:S(2)}) copy-start(s32[64,32,32]{0,2,1:T(8,128)} %param.13) | copy-start | bytes 786436
  76.4 26.8 %collective-permute-start.6 = (bf16[8,192,128]{2,1,0:T(8,128)(2,1)}, bf16[8,192,128]{2,1,0:T(8,128)(2,1)S(1)}, u32[]{:S(2)}, u32[]{:S(2)}) collective-permute-start(bf16[8,192,128]{2,1,0:T(8,128)(2,1)} %get-tuple-element.26), channel_id=1, source_target_pairs={{0,8},{2,10},{4,12},{6,14},{8,0},{10,2},{12,4},{14,6},{1,9},{3,11}... | collective-permute-start | bytes 1179656 | tf_op jit(solution)/shard_map/ppermute | solution.py:347
  103.2 2.9 %copy-start.4 = (bf16[8,192,128]{2,1,0:T(8,128)(2,1)}, bf16[8,192,128]{2,1,0:T(8,128)(2,1)S(1)}, u32[]{:S(2)}) copy-start(bf16[8,192,128]{2,1,0:T(8,128)(2,1)S(1)} %collective-permute-done.6.refs_1_.refs_2_) | copy-start | bytes 1179652
  106.9 47.0 %all-to-all-start.2 = ((bf16[4,32,4,16,128]{4,3,2,1,0:T(8,128)(2,1)}), bf16[4,32,4,16,128]{4,3,2,1,0:T(8,128)(2,1)S(1)}, u32[]{:S(2)}, u32[]{:S(2)}) async-start(bf16[4,32,4,16,128]{4,3,2,1,0:T(8,128)(2,1)} %gate.8), calls=%async_computation.2 | async-start | bytes 4194304 | tf_op jit(solution)/shard_map/all_to_all | solution.py:388
  113.0 31.7 %collective-permute-start.7 = (bf16[8,192,128]{2,1,0:T(8,128)(2,1)}, bf16[8,192,128]{2,1,0:T(8,128)(2,1)S(1)}, u32[]{:S(2)}, u32[]{:S(2)}) collective-permute-start(bf16[8,192,128]{2,1,0:T(8,128)(2,1)} %gate.6), channel_id=1, source_target_pairs={{0,8},{2,10},{4,12},{6,14},{8,0},{10,2},{12,4},{14,6},{1,9},{3,11}... | collective-permute-start | bytes 1179656 | tf_op jit(solution)/shard_map/ppermute | solution.py:347
  118.1 33.8 %collective-permute-start.8 = (bf16[8,192,128]{2,1,0:T(8,128)(2,1)}, bf16[8,192,128]{2,1,0:T(8,128)(2,1)S(1)}, u32[]{:S(2)}, u32[]{:S(2)}) collective-permute-start(bf16[8,192,128]{2,1,0:T(8,128)(2,1)} %get-tuple-element.28), channel_id=1, source_target_pairs={{0,8},{2,10},{4,12},{6,14},{8,0},{10,2},{12,4},{14,6},{1,9},{3,11}... | collective-permute-start | bytes 1179656 | tf_op jit(solution)/shard_map/ppermute | solution.py:347
  144.7 9.3 %copy-start.12 = (bf16[8,192,128]{2,1,0:T(8,128)(2,1)}, bf16[8,192,128]{2,1,0:T(8,128)(2,1)S(1)}, u32[]{:S(2)}) copy-start(bf16[8,192,128]{2,1,0:T(8,128)(2,1)S(1)} %collective-permute-done.7.refs_4_.refs_2_) | copy-start | bytes 1179652
  151.8 2.1 copy-start.6
  153.9 1.4 copy-start
  156.0 5.1 %copy-start.1 = (bf16[4,32,4,16,128]{4,3,2,1,0:T(8,128)(2,1)S(1)}, bf16[4,32,4,16,128]{4,3,2,1,0:T(8,128)(2,1)}, u32[]{:S(2)}) copy-start(bf16[4,32,4,16,128]{4,3,2,1,0:T(8,128)(2,1)} %copy-done) | copy-start | bytes 6291460
  156.0 5.1 %copy-start.5 = (bf16[8,192,128]{2,1,0:T(8,128)(2,1)S(1)}, bf16[8,192,128]{2,1,0:T(8,128)(2,1)}, u32[]{:S(2)}) copy-start(bf16[8,192,128]{2,1,0:T(8,128)(2,1)} %copy-done.4) | copy-start | bytes 1179652
  156.0 5.1 %copy-start.7 = (bf16[8,192,128]{2,1,0:T(8,128)(2,1)S(1)}, bf16[8,192,128]{2,1,0:T(8,128)(2,1)}, u32[]{:S(2)}) copy-start(bf16[8,192,128]{2,1,0:T(8,128)(2,1)} %copy-done.6) | copy-start | bytes 1179652
  156.0 42.5 %all-to-all-start.3 = ((bf16[4,32,4,16,128]{4,3,2,1,0:T(8,128)(2,1)}), bf16[4,32,4,16,128]{4,3,2,1,0:T(8,128)(2,1)}, u32[]{:S(2)}, u32[]{:S(2)}) async-start(bf16[4,32,4,16,128]{4,3,2,1,0:T(8,128)(2,1)} %gate.9), calls=%async_computation.3 | async-start | bytes 4194304 | tf_op jit(solution)/shard_map/all_to_all | solution.py:388
  166.9 7.2 %collective-permute-start.11 = (bf16[16,192,128]{2,1,0:T(8,128)(2,1)}, bf16[16,192,128]{2,1,0:T(8,128)(2,1)}, u32[]{:S(2)}, u32[]{:S(2)}) collective-permute-start(bf16[16,192,128]{2,1,0:T(8,128)(2,1)} %get-tuple-element.36), channel_id=1, source_target_pairs={{0,1},{1,0},{2,3},{3,2},{4,5},{5,4},{6,7},{7,6},{8,9},{9,8},{10,11... | collective-permute-start | bytes 2359304 | tf_op jit(solution)/shard_map/ppermute | solution.py:347
  167.6 25.7 %collective-permute-start.9 = (bf16[8,192,128]{2,1,0:T(8,128)(2,1)}, bf16[8,192,128]{2,1,0:T(8,128)(2,1)S(1)}, u32[]{:S(2)}, u32[]{:S(2)}) collective-permute-start(bf16[8,192,128]{2,1,0:T(8,128)(2,1)} %gate.7), channel_id=1, source_target_pairs={{0,8},{2,10},{4,12},{6,14},{8,0},{10,2},{12,4},{14,6},{1,9},{3,11}... | collective-permute-start | bytes 1179656 | tf_op jit(solution)/shard_map/ppermute | solution.py:347
  174.1 24.4 %copy-start.13 = (bf16[8,192,128]{2,1,0:T(8,128)(2,1)S(1)}, bf16[8,192,128]{2,1,0:T(8,128)(2,1)}, u32[]{:S(2)}) copy-start(bf16[8,192,128]{2,1,0:T(8,128)(2,1)} %copy-done.12) | copy-start | bytes 1179652
  175.9 46.5 %collective-permute-start.12 = (bf16[16,192,128]{2,1,0:T(8,128)(2,1)S(1)}, bf16[16,192,128]{2,1,0:T(8,128)(2,1)S(1)}, u32[]{:S(2)}, u32[]{:S(2)}) collective-permute-start(bf16[16,192,128]{2,1,0:T(8,128)(2,1)S(1)} %add_convert_fusion), channel_id=1, source_target_pairs={{0,8},{2,10},{4,12},{6,14},{8,0},{10,2},{12,4},{14,6},{1,9},{3,11}... | collective-permute-start | bytes 2359304 | tf_op jit(solution)/shard_map/ppermute | solution.py:347
  204.4 18.0 %collective-permute-start.10 = (bf16[16,192,128]{2,1,0:T(8,128)(2,1)}, bf16[16,192,128]{2,1,0:T(8,128)(2,1)S(1)}, u32[]{:S(2)}, u32[]{:S(2)}) collective-permute-start(bf16[16,192,128]{2,1,0:T(8,128)(2,1)} %get-tuple-element.32), channel_id=1, source_target_pairs={{0,1},{1,0},{2,3},{3,2},{4,5},{5,4},{6,7},{7,6},{8,9},{9,8},{10,11... | collective-permute-start | bytes 2359304 | tf_op jit(solution)/shard_map/ppermute | solution.py:347
  222.4 0.9 copy-start.14
  223.3 0.9 copy-start.15

commit v5 on v4

--- a/solution.py
+++ b/solution.py
@@ -12,6 +12,7 @@
 GROUP = 8
 HSTEP = 8
 CHUNKS = 2
+PSTEP = 4
 
 
 def kept_within(keep_mask):
@@ -89,9 +90,9 @@
     )(side, own, peer, gains)
 
 
-def pick_kernel(place, wanted, weight_ref, *refs, rows, runs, base, turning, after):
+def pick_kernel(place, wanted, weight_ref, *refs, rows, runs, after):
     out_refs, spread = refs[after:-1], refs[-1]
-    step = pl.program_id(0) + base
+    step = pl.program_id(0)
     for h in range(HSTEP):
         for row in range(rows):
             tile = weight_ref[h, :, row * BLK:(row + 1) * BLK].astype(jnp.float32)
@@ -104,43 +105,83 @@
                 for g in range(runs):
                     at = wanted[pair + u, (step * HSTEP + h) * runs + g]
                     block = spread[h * runs + g, pl.ds(at, rows, stride=GROUP), :]
-                    if turning and h % 2:
-                        block = half_turn(block)
-                    block = block.astype(jnp.bfloat16)
-                    if turning:
-                        out_refs[0][member, u, h, g] = block
-                    else:
-                        out_refs[u][member, h, g] = block
-
-
-def pick_blocks(weight, place, wanted, first, count, turning, after=()):
-    _, feat_blocks, width = weight.shape
+                    out_refs[u][member, h, g] = block.astype(jnp.bfloat16)
+
+
+def pick_blocks(weight, place, wanted, after=()):
+    hidden_blocks, feat_blocks, width = weight.shape
     rows = width // BLK
     runs = feat_blocks // GROUP
-    base = first // HSTEP
     members = wanted.shape[0] // 2
-    if turning:
-        outs = 1
-        shape = (members, 2, count, runs, rows, BLK)
-        out_spec = pl.BlockSpec((members, 2, HSTEP, runs, rows, BLK), lambda i, *_: (0, 0, i, 0, 0, 0))
-    else:
-        outs = 2
-        shape = (members, count, runs, rows, BLK)
-        out_spec = pl.BlockSpec((members, HSTEP, runs, rows, BLK), lambda i, *_: (0, i, 0, 0, 0))
+    shape = (members, hidden_blocks, runs, rows, BLK)
+    out_spec = pl.BlockSpec((members, HSTEP, runs, rows, BLK), lambda i, *_: (0, i, 0, 0, 0))
     return pl.pallas_call(
-        functools.partial(pick_kernel, rows=rows, runs=runs, base=base, turning=turning, after=len(after)),
+        functools.partial(pick_kernel, rows=rows, runs=runs, after=len(after)),
         grid_spec=pltpu.PrefetchScalarGridSpec(
             num_scalar_prefetch=2,
-            grid=(count // HSTEP,),
-            in_specs=[pl.BlockSpec((HSTEP, feat_blocks, width), lambda i, *_: (i + base, 0, 0))]
+            grid=(hidden_blocks // HSTEP,),
+            in_specs=[pl.BlockSpec((HSTEP, feat_blocks, width), lambda i, *_: (i, 0, 0))]
             + [corner(value) for value in after],
-            out_specs=[out_spec] * outs,
+            out_specs=[out_spec] * 2,
             scratch_shapes=[pltpu.VMEM((HSTEP * runs, rows * GROUP, BLK), jnp.float32)],
         ),
-        out_shape=[pltpu.HBM(shape, jnp.bfloat16)] * outs,
+        out_shape=[pltpu.HBM(shape, jnp.bfloat16)] * 2,
         compiler_params=pltpu.CompilerParams(vmem_limit_bytes=48 << 20),
-        name="pick_up" if turning else "pick_down",
+        name="pick_down",
     )(place, wanted, *in_hbm([weight]), *after)
+
+
+def pick_both_kernel(at_home, wanted, own_ref, other_ref, *refs, rows, runs, base, half, after):
+    out_ref, spread = refs[after], refs[after + 1]
+    step = pl.program_id(0)
+    for s, ref in enumerate((own_ref, other_ref)):
+        for h in range(PSTEP):
+            for row in range(rows):
+                tile = ref[h, :, row * BLK:(row + 1) * BLK].astype(jnp.float32)
+                for g in range(runs):
+                    spread[s, h * runs + g, row * GROUP:(row + 1) * GROUP, :] = tile[g * GROUP:(g + 1) * GROUP]
+    first = base + at_home[2] * half + step * PSTEP
+    places = [pl.multiple_of(group * rows, rows) for group in (at_home[1], 1 - at_home[1])]
+    for member in range(wanted.shape[0] // 2):
+        pair = 2 * (at_home[0] ^ member)
+        for u in range(2):
+            for h in range(PSTEP):
+                for g in range(runs):
+                    at = wanted[pair + u, (first + h) * runs + g]
+                    for s in range(2):
+                        block = spread[s, h * runs + g, pl.ds(at, rows, stride=GROUP), :]
+                        if h % 2:
+                            block = half_turn(block)
+                        out_ref[member, u, h, g, pl.ds(places[s], rows), :] = block.astype(jnp.bfloat16)
+
+
+def pick_both(weight, other, at_home, wanted, base, after=()):
+    _, feat_blocks, width = weight.shape
+    half = other.shape[0]
+    rows = width // BLK
+    runs = feat_blocks // GROUP
+    members = wanted.shape[0] // 2
+    per_half = half // PSTEP
+    first = base // PSTEP
+    return pl.pallas_call(
+        functools.partial(pick_both_kernel, rows=rows, runs=runs, base=base, half=half, after=len(after)),
+        grid_spec=pltpu.PrefetchScalarGridSpec(
+            num_scalar_prefetch=2,
+            grid=(per_half,),
+            in_specs=[
+                pl.BlockSpec(
+                    (PSTEP, feat_blocks, width), lambda i, at_home, wanted: (first + at_home[2] * per_half + i, 0, 0)
+                ),
+                pl.BlockSpec((PSTEP, feat_blocks, width), lambda i, *_: (i, 0, 0)),
+            ]
+            + [corner(value) for value in after],
+            out_specs=pl.BlockSpec((members, 2, PSTEP, runs, 2 * rows, BLK), lambda i, *_: (0, 0, i, 0, 0, 0)),
+            scratch_shapes=[pltpu.VMEM((2, PSTEP * runs, rows * GROUP, BLK), jnp.float32)],
+        ),
+        out_shape=pltpu.HBM((members, 2, half, runs, 2 * rows, BLK), jnp.bfloat16),
+        compiler_params=pltpu.CompilerParams(vmem_limit_bytes=48 << 20),
+        name="pick_both",
+    )(at_home, wanted, *in_hbm([weight]), other, *after)
 
 
 def corner(value):
@@ -165,14 +206,14 @@
     )(*in_hbm(values), *after)
 
 
-def up_kernel(side, slots, own_ref, far_a_ref, far_b_ref, weight_ref, *refs, runs, rows):
+def up_kernel(side, slots, own_ref, far_a_ref, far_b_ref, weight_ref, *refs, runs, rows, half):
     kept_refs, sent_refs, partner, held = refs[:2], refs[2:4], refs[4], refs[5]
     step = pl.program_id(0)
     frames = own_ref.shape[1]
     low = low_lanes((frames, BLK))
     even = low == (side[0] == 0)
-    members = weight_ref.shape[0]
-    side_rows = rows * members
+    members, half_step = weight_ref.shape[0], weight_ref.shape[2]
+    side_rows = 4 * rows
 
     @pl.when(step == 0)
     def _():
@@ -185,50 +226,59 @@
                 partner[first + 1] = jnp.where(low, turned, pair).astype(jnp.bfloat16)
 
     for member in range(members):
+        part, place = divmod(member, 2)
         for u in range(2):
-            for h in range(HSTEP):
+            for h in range(half_step):
                 for g in range(runs):
-                    start = g * side_rows + member * rows
-                    held[u, h, start:start + rows, :] = weight_ref[member, u, h, g]
-    for m in range(HSTEP // 2):
+                    for group in range(2):
+                        start = g * side_rows + (2 * group + place) * rows
+                        held[u, part * half_step + h, start:start + rows, :] = weight_ref[
+                            member, u, h, g, group * rows:(group + 1) * rows
+                        ]
+    for m in range(half_step):
+        part, within = divmod(m, half_step // 2)
         for u, source in enumerate((own_ref, partner)):
             pair = []
             for h in (2 * m, 2 * m + 1):
-                at = [slots[u, (step * HSTEP + h) * runs + g] for g in range(runs)]
+                hidden = part * half + step * half_step + h % half_step
+                at = [slots[u, hidden * runs + g] for g in range(runs)]
                 left = jnp.concatenate(
                     [jnp.where(low, source[at[g]], source[at[g + 1]]) for g in range(0, runs, 2)], axis=1
                 )
                 pair.append(jnp.dot(left, held[u, h], preferred_element_type=jnp.float32))
-            kept_refs[u][m] = jnp.where(even, pair[0], pair[1])
-            sent_refs[u][m] = jnp.where(even, pair[1], pair[0]).astype(jnp.bfloat16)
+            kept_refs[u][part, within] = jnp.where(even, pair[0], pair[1])
+            sent_refs[u][part, within] = jnp.where(even, pair[1], pair[0]).astype(jnp.bfloat16)
 
 
 def up_project(side, slots, own, far, weights):
-    members, _, hidden_blocks, runs, rows, _ = weights.shape
+    members, _, half, runs, both, _ = weights.shape
+    rows = both // 2
+    half_step = HSTEP // 2
     slots_all, frames, _ = own.shape
-    out_spec = pl.BlockSpec((HSTEP // 2, frames, BLK), lambda i, *_: (i, 0, 0))
-    return pl.pallas_call(
-        functools.partial(up_kernel, runs=runs, rows=rows),
+    out_spec = pl.BlockSpec((2, half_step // 2, frames, BLK), lambda i, *_: (0, i, 0, 0))
+    out_dims = (2, half // 2, frames, BLK)
+    out = pl.pallas_call(
+        functools.partial(up_kernel, runs=runs, rows=rows, half=half),
         grid_spec=pltpu.PrefetchScalarGridSpec(
             num_scalar_prefetch=2,
-            grid=(hidden_blocks // HSTEP,),
+            grid=(half // half_step,),
             in_specs=[
                 pl.BlockSpec((slots_all, frames, BLK), lambda i, *_: (0, 0, 0)),
                 pl.BlockSpec((slots_all // 4, frames, BLK), lambda i, *_: (0, 0, 0)),
                 pl.BlockSpec((slots_all // 4, frames, BLK), lambda i, *_: (0, 0, 0)),
-                pl.BlockSpec((members, 2, HSTEP, runs, rows, BLK), lambda i, *_: (0, 0, i, 0, 0, 0)),
+                pl.BlockSpec((members, 2, half_step, runs, both, BLK), lambda i, *_: (0, 0, i, 0, 0, 0)),
             ],
             out_specs=[out_spec] * 4,
             scratch_shapes=[
                 pltpu.VMEM((slots_all, frames, BLK), jnp.bfloat16),
-                pltpu.VMEM((2, HSTEP, runs * rows * members, BLK), jnp.bfloat16),
+                pltpu.VMEM((2, HSTEP, runs * rows * 4, BLK), jnp.bfloat16),
             ],
         ),
-        out_shape=[pltpu.HBM((hidden_blocks // 2, frames, BLK), jnp.float32)] * 2
-        + [pltpu.HBM((hidden_blocks // 2, frames, BLK), jnp.bfloat16)] * 2,
+        out_shape=[pltpu.HBM(out_dims, jnp.float32)] * 2 + [pltpu.HBM(out_dims, jnp.bfloat16)] * 2,
         compiler_params=pltpu.CompilerParams(vmem_limit_bytes=48 << 20),
         name="up_project",
     )(side, slots, *in_hbm([own]), *far, weights)
+    return [value.reshape(half, frames, BLK) for value in out]
 
 
 def down_kernel(side, which, wanted, *refs, utt, parts, runs, rows):
@@ -361,24 +411,38 @@
     core = lax.axis_index("tensor").astype(jnp.int32)
     side = (here // across)[None]
 
+    part = lax.axis_index("parts").astype(jnp.int32)
+    count = hidden_blocks // CHUNKS
+    half = count // 2
+    other_rows, raw = [], None
+    for c in range(CHUNKS):
+        mine = lax.dynamic_slice_in_dim(up_weight, c * count + part * half, half, 0)
+        if raw is not None:
+            (mine,) = gate([mine], [raw])
+        raw = swap(mine, "dp", dp, 2)
+        other_rows.append(raw)
+
     langs = language
-    step = across
-    while step != 0:
+    for step in (across, 1):
         langs = jnp.concatenate([langs, swap(langs, "dp", dp, step)])
-        step = 1 if step == across else 2 * step
-        step = 0 if step == across else step
-    chooser = (langs[:, None] == jnp.arange(nlangs, dtype=jnp.int32)).astype(jnp.int32)
-    wanted_up = jnp.einsum("nl,lhg->nhg", chooser, kept_within(up_keep))
-    wanted_down = jnp.einsum("nl,lhg->nhg", chooser, kept_within(down_keep))
+
+    def wanted_of(langs, table):
+        chooser = (langs[:, None] == jnp.arange(nlangs, dtype=jnp.int32)).astype(jnp.int32)
+        return jnp.einsum("nl,lhg->nhg", chooser, table)
+
+    wanted_up = wanted_of(jnp.concatenate([langs, swap(langs, "parts", 2, 1)]), kept_within(up_keep))
+    wanted_down = wanted_of(jnp.concatenate([langs, swap(langs, "dp", dp, 2)]), kept_within(down_keep))
     up_own = wanted_up[:2] + jnp.arange(runs, dtype=jnp.int32) * GROUP
     slots = (up_own ^ (core * (feat_blocks // 2))).reshape(2, -1)
     wanted_up = wanted_up.reshape(2 * across, -1)
     wanted_down = wanted_down.reshape(2 * across, -1)
     place = (here % across)[None]
+    at_home = jnp.stack([2 * part + here % 2, here % across // 2, part])
     peer = swap(acoustic, "tensor", 2, 1)
     gains = norm_gain.reshape(2, 1, features)
     gains = jnp.where(core == 0, gains, gains[::-1])
     near, own_far = norm_parts(side, acoustic, peer, gains)
+    (own_far,) = gate([own_far], [other_rows[0]])
     far = swap(own_far, "dp", dp, across)
     far = (far, swap(far, "tensor", 2, 1))
 
@@ -387,15 +451,20 @@
     def within_side(blocks):
         return lax.all_to_all(blocks, "dp", split_axis=0, concat_axis=0, axis_index_groups=groups, tiled=True)
 
-    count = hidden_blocks // CHUNKS
-    kept, crossed, after, got = ([], []), ([], []), in_hbm([own_far]), None
+    trades = [[p * dp + 2 * z + x for p in range(2) for x in range(2)] for z in range(dp // 2)]
+
+    def traded(blocks):
+        return lax.all_to_all(
+            blocks, ("parts", "dp"), split_axis=0, concat_axis=0, axis_index_groups=trades, tiled=True
+        )
+
+    kept, crossed, got, after = ([], []), ([], []), None, ()
     for c in range(CHUNKS):
-        (blocks,) = pick_blocks(up_weight, place, wanted_up, c * count, count, True, after)
+        blocks = pick_both(up_weight, other_rows[c], at_home, wanted_up, c * count, after)
         after = in_hbm([blocks])
         if got is not None:
-            (blocks,) = gate([blocks], [got, *far])
-            after = [got]
-        got = within_side(blocks)
+            (blocks,) = gate([blocks], [got])
+        got = traded(blocks)
         span = slice(c * count * runs, (c + 1) * count * runs)
         kept_own, kept_far, sent_own, sent_far = up_project(side, slots[:, span], near, far, got)
         got_far = swap(sent_own, "dp", dp, across)
@@ -404,10 +473,10 @@
         for u, (mine, theirs) in enumerate(((kept_own, got_own), (kept_far, got_far))):
             kept[u].append(mine)
             crossed[u].append(theirs)
-    own_blocks, far_blocks = pick_blocks(down_weight, place, wanted_down, 0, hidden_blocks, False, after)
-    (far_blocks,) = gate([far_blocks], [got, *crossed[1][:-1]])
+    own_blocks, far_blocks = pick_blocks(down_weight, place, wanted_down, [other_rows[-1]])
+    (far_blocks,) = gate([far_blocks], [got, *crossed[1][:-1], *crossed[0][:-1]])
     far_down = within_side(far_blocks)
-    (own_blocks,) = gate([own_blocks], [far_down, *crossed[1], *crossed[0][:-1]])
+    (own_blocks,) = gate([own_blocks], [far_down, *crossed[1]])
     own_down = within_side(own_blocks)
     rows_down = wanted_down[:2]
 
@@ -485,7 +554,6 @@
     )
     out_specs = P(("parts", "dp"), "tensor")
     dp = mesh.shape["dp"]
-    rows = BLK // dp
-    whole_tiles = mesh.shape["tensor"] == 2 and dp & (dp - 1) == 0 and dp > 1 and rows % 16 == 0
-    body = functools.partial(split_body, dp=dp) if whole_tiles else exchange_body
+    in_pairs = mesh.shape["tensor"] == 2 and mesh.shape["parts"] == 2 and dp == 8
+    body = functools.partial(split_body, dp=dp) if in_pairs else exchange_body
     return jax.shard_map(body, mesh=mesh, in_specs=in_specs, out_specs=out_specs, check_vma=False)

time: 230 us -> 253 us (1.10)
  waiting for transfers between devices: 117 us -> 137 us
  local copies, waits for them, and re-layouts: 6.99 us -> 10.9 us
    ppermute x13 -> x16, waiting for transfers between devices: 107 us -> 128 us  [swap(): return lax.ppermute(value, axis, [(i, i ^ step) for i in range(size)])]
    all_to_all x4 -> x2, starting transfers between devices: 19.1 us -> 8.65 us  [within_side(): lax.all_to_all(blocks, 'dp', split_axis=0, concat_axis=0, axis_index_grou...]
    all_to_all x0 -> x2, starting transfers between devices: none -> 8.31 us  [traded(): lax.all_to_all(blocks, ('parts', 'dp'), split_axis=0, concat_axis=0, axis...]
    dynamic_slice x0 -> x1, local copies, waits for them, and re-layouts: none -> 2.75 us  [split_body(): mine = lax.dynamic_slice_in_dim(up_weight, c * count + part * half, half, 0)]
    all_to_all x4 -> x2, waiting for transfers between devices: 10.2 us -> 8.5 us  [within_side(): lax.all_to_all(blocks, 'dp', split_axis=0, concat_axis=0, axis_index_grou...]
    ppermute x13 -> x16, starting transfers between devices: 17.7 us -> 18.6 us  [swap(): return lax.ppermute(value, axis, [(i, i ^ step) for i in range(size)])]
    unnamed x38 -> x40, local copies, waits for them, and re-layouts: 6.2 us -> 6.02 us
  transfers between devices with their start and end apart: 17 -> 20, of which waited for: 11 -> 13; matrix products, arithmetic and copies ran while one was open for 4% -> 3% of each run, Pallas kernels for 19% -> 20%
where the time goes in v5:
time: 253 us; the launch traced here: 251 us
  waiting for transfers between devices  137 us (54%)
  Pallas kernels  60 us (24%)
  starting transfers between devices  35.5 us (14%)
  local copies, waits for them, and re-layouts  10.9 us (4%)
  other arithmetic  5.76 us (2%)
    ppermute x16, waiting for transfers between devices, swap(): return lax.ppermute(value, axis, [(i, i ^ step) for i in range(size)])  128 us
    pallas_call x4, Pallas kernels, down_project(): pl.pallas_call(functools.partial(down_kernel, utt=utt, parts=parts, runs=...  22.4 us
    ppermute x16, starting transfers between devices, swap(): return lax.ppermute(value, axis, [(i, i ^ step) for i in range(size)])  18.6 us
    pallas_call x2, Pallas kernels, up_project(): pl.pallas_call(functools.partial(up_kernel, runs=runs, rows=rows, half=ha...  10 us
    all_to_all x2, starting transfers between devices, within_side(): lax.all_to_all(blocks, 'dp', split_axis=0, concat_axis=0, axis_index_grou...  8.65 us
    all_to_all x2, waiting for transfers between devices, within_side(): lax.all_to_all(blocks, 'dp', split_axis=0, concat_axis=0, axis_index_grou...  8.5 us
    pallas_call x2, Pallas kernels, pick_both(): pl.pallas_call(functools.partial(pick_both_kernel, rows=rows, runs=runs,...  8.48 us
    all_to_all x2, starting transfers between devices, traded(): lax.all_to_all(blocks, ('parts', 'dp'), split_axis=0, concat_axis=0, axis...  8.31 us
  transfers between devices with their start and end apart: 20, of which 13 were waited for; matrix products, arithmetic and copies ran while one was open for 3% of the time, Pallas kernels for 20%

profile of v5, /device:TPU:0, one launch (start us, length us, event | category | flops | bytes accessed | tf_op | source)
XLA Modules:
  0.0 251.3 jit_solution(7363861705031532089)
XLA Ops:
  0.0 2.8 %constant_dynamic-slice_fusion = (bf16[8,32,2048]{2,1,0:T(8,128)(2,1)}, bf16[8,32,2048]{2,1,0:T(8,128)(2,1)S(1)}) fusion(bf16[32,32,2048]{2,1,0:T(8,128)(2,1)} %own_ref.5, s32[]{:T(128)S(6)} %select_n.41, s32[]{:T(128)S(6)} %select_n.37), kind=kLoop, calls=%fused_computation.25 | loop fusion | bytes 4194312 | tf_op jit(solution)/shard_map/dynamic_slice | solution.py:419
  2.8 3.0 %collective-permute-start.5 = (bf16[8,32,2048]{2,1,0:T(8,128)(2,1)S(1)}, bf16[8,32,2048]{2,1,0:T(8,128)(2,1)S(1)}, u32[]{:S(2)}, u32[]{:S(2)}) collective-permute-start(bf16[8,32,2048]{2,1,0:T(8,128)(2,1)S(1)} %get-tuple-element.40), channel_id=1, source_target_pairs={{0,4},{2,6},{4,0},{6,2},{8,12},{10,14},{12,8},{14,10},{1,5},{3,7},... | collective-permute-start | bytes 3145736 | tf_op jit(solution)/shard_map/ppermute | solution.py:397
  5.8 2.6 %collective-permute-start = (s32[1]{0:T(128)}, s32[1]{0:T(128)}, u32[]{:S(2)}, u32[]{:S(2)}) collective-permute-start(s32[1]{0:T(128)} %param.14), channel_id=1, source_target_pairs={{0,8},{2,10},{4,12},{6,14},{8,0},{10,2},{12,4},{14,6},{1,9},{3,11}... | collective-permute-start | bytes 20 | tf_op jit(solution)/shard_map/ppermute | solution.py:397
  9.1 0.2 fusion
  9.3 18.9 %collective-permute-done = s32[1]{0:T(128)} collective-permute-done((s32[1]{0:T(128)}, s32[1]{0:T(128)}, u32[]{:S(2)}, u32[]{:S(2)}) %collective-permute-start) | collective-permute-done | bytes 36 | tf_op jit(solution)/shard_map/ppermute | solution.py:397
  28.2 0.7 pad_add_fusion
  28.9 1.5 collective-permute-start.1
  30.4 2.0 collective-permute-done.1
  32.5 0.7 pad_add_fusion.1
  33.2 1.5 collective-permute-start.3
  34.7 2.0 collective-permute-done.3
  36.7 1.3 pad_add_fusion.4
  38.0 0.3 fusion.2
  38.5 4.2 %pick_both.2.refs_0_ = bf16[4,2,8,4,32,128]{5,4,3,2,1,0:T(8,128)(2,1)} custom-call(s32[3]{0:T(128)S(1)} %pad_add_fusion.5.at_home, s32[8,128]{1,0:T(8,128)S(1)} %copy.42.wanted, bf16[32,32,2048]{2,1,0:T(8,128)(2,1)} %own_ref.5, bf16[8,32,2048]{2,1,0:T(8,128)(2,1)S(1)} %collective-permute-done.5.refs_1_.other_ref), custom_call_target="tpu_custom_call" | custom-call | tf_op jit(solution)/shard_map/pick_both/pallas_call | solution.py:166
  42.7 3.7 %all-to-all-start = ((bf16[4,2,8,4,32,128]{5,4,3,2,1,0:T(8,128)(2,1)}), bf16[4,2,8,4,32,128]{5,4,3,2,1,0:T(8,128)(2,1)S(1)}, u32[]{:S(2)}, u32[]{:S(2)}) async-start(bf16[4,2,8,4,32,128]{5,4,3,2,1,0:T(8,128)(2,1)} %pick_both.2.refs_0_), calls=%async_computation | async-start | bytes 4194304 | tf_op jit(solution)/shard_map/all_to_all | solution.py:457
  46.5 0.7 gate.8
  47.2 3.5 %collective-permute-start.8 = (bf16[8,32,2048]{2,1,0:T(8,128)(2,1)}, bf16[8,32,2048]{2,1,0:T(8,128)(2,1)S(1)}, u32[]{:S(2)}, u32[]{:S(2)}) collective-permute-start(bf16[8,32,2048]{2,1,0:T(8,128)(2,1)} %gate.8), channel_id=1, source_target_pairs={{0,4},{2,6},{4,0},{6,2},{8,12},{10,14},{12,8},{14,10},{1,5},{3,7},... | collective-permute-start | bytes 3145736 | tf_op jit(solution)/shard_map/ppermute | solution.py:397
  50.7 0.6 broadcast_select_fusion.gain_ref
  51.3 2.0 collective-permute-done.4.peer_ref
  53.3 3.6 %norm_parts.1 = (bf16[32,192,128]{2,1,0:T(8,128)(2,1)}, bf16[8,192,128]{2,1,0:T(8,128)(2,1)}) custom-call(s32[1]{0:T(128)} %bitcast.side, bf16[192,2048]{1,0:T(8,128)(2,1)} %acoustic_ref.1, bf16[192,2048]{1,0:T(8,128)(2,1)} %collective-permute-done.4.peer_ref, f32[2,1,2048]{2,1,0:T(1,128)} %broadcast_select_fusion.gain_ref), custom_call_target="tpu_custom_call" | custom-call | tf_op jit(solution)/shard_map/norm_parts/pallas_call | solution.py:70
  56.9 0.7 gate.7
  57.6 21.2 %collective-permute-done.8.other_ref.refs_0_ = bf16[8,32,2048]{2,1,0:T(8,128)(2,1)S(1)} collective-permute-done((bf16[8,32,2048]{2,1,0:T(8,128)(2,1)}, bf16[8,32,2048]{2,1,0:T(8,128)(2,1)S(1)}, u32[]{:S(2)}, u32[]{:S(2)}) %collective-permute-start.8) | collective-permute-done | bytes 1048608 | tf_op jit(solution)/shard_map/ppermute | solution.py:397
  78.8 4.2 %pick_both.3.refs_0_ = bf16[4,2,8,4,32,128]{5,4,3,2,1,0:T(8,128)(2,1)} custom-call(s32[3]{0:T(128)S(1)} %pad_add_fusion.5.at_home, s32[8,128]{1,0:T(8,128)S(1)} %copy.42.wanted, bf16[32,32,2048]{2,1,0:T(8,128)(2,1)} %own_ref.5, bf16[8,32,2048]{2,1,0:T(8,128)(2,1)S(1)} %collective-permute-done.8.other_ref.refs_0_, ...), custom_call_target="tpu_custom_call" | custom-call | tf_op jit(solution)/shard_map/pick_both/pallas_call | solution.py:166
  83.0 1.3 copy-done.2
  84.3 0.7 gate.9
  85.0 4.6 %all-to-all-start.1 = ((bf16[4,2,8,4,32,128]{5,4,3,2,1,0:T(8,128)(2,1)}), bf16[4,2,8,4,32,128]{5,4,3,2,1,0:T(8,128)(2,1)}, u32[]{:S(2)}, u32[]{:S(2)}) async-start(bf16[4,2,8,4,32,128]{5,4,3,2,1,0:T(8,128)(2,1)} %gate.9), calls=%async_computation.1 | async-start | bytes 4194304 | tf_op jit(solution)/shard_map/all_to_all | solution.py:457
  89.8 0.7 copy.40
  90.5 0.9 reshape.51
  91.5 0.1 collective-permute-done.7.far_b_ref
  91.6 4.9 %up_project.2 = (f32[2,4,192,128]{3,2,1,0:T(8,128)}, f32[2,4,192,128]{3,2,1,0:T(8,128)}, bf16[2,4,192,128]{3,2,1,0:T(8,128)(2,1)}, bf16[2,4,192,128]{3,2,1,0:T(8,128)(2,1)}) custom-call(s32[1]{0:T(128)} %bitcast.side, s32[2,64]{1,0:T(2,128)S(1)} %get-tuple-element.42.slots, bf16[32,192,128]{2,1,0:T(8,128)(2,1)} %get-tuple-element.21.own_ref, ...), custom_call_target="tpu_custom_call" | custom-call | tf_op jit(solution)/shard_map/up_project/pallas_call | solution.py:260
  96.5 0.2 fusion.1
  96.7 2.0 collective-permute-start.2
  98.6 17.9 %collective-permute-done.9.refs_1_.refs_2_ = bf16[8,192,128]{2,1,0:T(8,128)(2,1)S(1)} collective-permute-done((bf16[8,192,128]{2,1,0:T(8,128)(2,1)}, bf16[8,192,128]{2,1,0:T(8,128)(2,1)S(1)}, u32[]{:S(2)}, u32[]{:S(2)}) %collective-permute-start.9) | collective-permute-done | bytes 393248 | tf_op jit(solution)/shard_map/ppermute | solution.py:397
  116.5 0.7 copy-done.5
  117.2 0.7 gate.10
  118.0 0.3 fusion.4
  118.3 0.1 copy.44
  118.5 6.6 %pick_down.1 = (bf16[4,32,4,16,128]{4,3,2,1,0:T(8,128)(2,1)}, bf16[4,32,4,16,128]{4,3,2,1,0:T(8,128)(2,1)}) custom-call(s32[1]{0:T(128)} %bitcast.18.place, s32[8,128]{1,0:T(8,128)S(1)} %copy.45.wanted, bf16[32,32,2048]{2,1,0:T(8,128)(2,1)} %weight_ref.1, bf16[8,32,2048]{2,1,0:T(8,128)(2,1)S(1)} %collective-permute-done.8.other_ref.refs_0_), custom_call_target="tpu_custom_call" | custom-call | tf_op jit(solution)/shard_map/pick_down/pallas_call | solution.py:118
  125.1 12.9 %collective-permute-done.10.refs_3_.refs_2_ = bf16[8,192,128]{2,1,0:T(8,128)(2,1)S(1)} collective-permute-done((bf16[8,192,128]{2,1,0:T(8,128)(2,1)}, bf16[8,192,128]{2,1,0:T(8,128)(2,1)S(1)}, u32[]{:S(2)}, u32[]{:S(2)}) %collective-permute-start.10) | collective-permute-done | bytes 393248 | tf_op jit(solution)/shard_map/ppermute | solution.py:397
  138.0 0.7 copy-done.9
  138.8 0.7 gate.12
  139.4 3.7 %all-to-all-start.2 = ((bf16[4,32,4,16,128]{4,3,2,1,0:T(8,128)(2,1)}), bf16[4,32,4,16,128]{4,3,2,1,0:T(8,128)(2,1)S(1)}, u32[]{:S(2)}, u32[]{:S(2)}) async-start(bf16[4,32,4,16,128]{4,3,2,1,0:T(8,128)(2,1)} %gate.12), calls=%async_computation.2 | async-start | bytes 4194304 | tf_op jit(solution)/shard_map/all_to_all | solution.py:452
  143.2 5.2 %up_project.3 = (f32[2,4,192,128]{3,2,1,0:T(8,128)}, f32[2,4,192,128]{3,2,1,0:T(8,128)}, bf16[2,4,192,128]{3,2,1,0:T(8,128)(2,1)}, bf16[2,4,192,128]{3,2,1,0:T(8,128)(2,1)}) custom-call(s32[1]{0:T(128)} %bitcast.side, s32[2,64]{1,0:T(2,128)S(1)} %get-tuple-element.41.slots, bf16[32,192,128]{2,1,0:T(8,128)(2,1)} %get-tuple-element.21.own_ref, ...), custom_call_target="tpu_custom_call" | custom-call | tf_op jit(solution)/shard_map/up_project/pallas_call | solution.py:260
  148.4 1.4 collective-permute-start.11
  149.7 25.1 %collective-permute-done.11.refs_1_.refs_3_ = bf16[8,192,128]{2,1,0:T(8,128)(2,1)S(1)} collective-permute-done((bf16[8,192,128]{2,1,0:T(8,128)(2,1)}, bf16[8,192,128]{2,1,0:T(8,128)(2,1)S(1)}, u32[]{:S(2)}, u32[]{:S(2)}) %collective-permute-start.11) | collective-permute-done | bytes 393248 | tf_op jit(solution)/shard_map/ppermute | solution.py:397
  174.9 2.1 all-to-all-done.2.refs_1_.refs_4_
  177.0 1.4 copy-done
  178.3 0.7 gate.13
  179.0 4.9 %all-to-all-start.3 = ((bf16[4,32,4,16,128]{4,3,2,1,0:T(8,128)(2,1)}), bf16[4,32,4,16,128]{4,3,2,1,0:T(8,128)(2,1)}, u32[]{:S(2)}, u32[]{:S(2)}) async-start(bf16[4,32,4,16,128]{4,3,2,1,0:T(8,128)(2,1)} %gate.13), calls=%async_computation.3 | async-start | bytes 4194304 | tf_op jit(solution)/shard_map/all_to_all | solution.py:452
  184.0 0.1 slice.16.wanted
  184.2 5.8 %down_1.2 = (bf16[16,192,128]{2,1,0:T(8,128)(2,1)}, bf16[16,192,128]{2,1,0:T(8,128)(2,1)}) custom-call(s32[1]{0:T(128)} %bitcast.side, s32[1]{0:T(128)} %bitcast.4.which, s32[2,128]{1,0:T(2,128)S(1)} %slice.16.wanted, f32[8,192,128]{2,1,0:T(8,128)} %bitcast.33, f32[8,192,128]{2,1,0:T(8,128)} %bitcast.35, bf16[8,192,128]{2,1,0:T(8,128)(2,1)S(1)} %copy-done.6, ...), custom_call_target="tpu_custom_call" | custom-call | tf_op jit(solution)/shard_map/down_1/pallas_call | solution.py:350
  190.0 0.7 gate.11
  190.7 1.3 collective-permute-start.12
  191.9 5.2 %down_1.3 = f32[16,192,128]{2,1,0:T(8,128)} custom-call(s32[1]{0:T(128)} %bitcast.side, s32[1]{0:T(128)} %bitcast.1.which, s32[2,128]{1,0:T(2,128)S(1)} %slice.16.wanted, bf16[16,192,128]{2,1,0:T(8,128)(2,1)} %get-tuple-element.35.refs_0_, bf16[4,32,4,16,128]{4,3,2,1,0:T(8,128)(2,1)S(1)} %copy-done.1), custom_call_target="tpu_custom_call" | custom-call | tf_op jit(solution)/shard_map/down_1/pallas_call | solution.py:350
  197.2 1.8 add_convert_fusion
  199.0 1.7 collective-permute-start.15
  200.7 15.6 %collective-permute-done.12.refs_3_ = bf16[8,192,128]{2,1,0:T(8,128)(2,1)S(1)} collective-permute-done((bf16[8,192,128]{2,1,0:T(8,128)(2,1)}, bf16[8,192,128]{2,1,0:T(8,128)(2,1)S(1)}, u32[]{:S(2)}, u32[]{:S(2)}) %collective-permute-start.12) | collective-permute-done | bytes 393248 | tf_op jit(solution)/shard_map/ppermute | solution.py:397
  216.4 6.4 %all-to-all-done.3.refs_4_.refs_1_ = bf16[4,32,4,16,128]{4,3,2,1,0:T(8,128)(2,1)} async-done(((bf16[4,32,4,16,128]{4,3,2,1,0:T(8,128)(2,1)}), bf16[4,32,4,16,128]{4,3,2,1,0:T(8,128)(2,1)}, u32[]{:S(2)}, u32[]{:S(2)}) %all-to-all-start.3) | async-done | bytes 2097184 | tf_op jit(solution)/shard_map/all_to_all | solution.py:452
  222.8 5.9 %down_0.2 = (bf16[16,192,128]{2,1,0:T(8,128)(2,1)}, bf16[16,192,128]{2,1,0:T(8,128)(2,1)}) custom-call(s32[1]{0:T(128)} %bitcast.side, s32[1]{0:T(128)} %bitcast.4.which, s32[2,128]{1,0:T(2,128)S(1)} %slice.16.wanted, f32[8,192,128]{2,1,0:T(8,128)} %bitcast.32, f32[8,192,128]{2,1,0:T(8,128)} %bitcast.34, bf16[8,192,128]{2,1,0:T(8,128)(2,1)S(1)} %copy-done.10, ...), custom_call_target="tpu_custom_call" | custom-call | tf_op jit(solution)/shard_map/down_0/pallas_call | solution.py:350
  229.3 5.5 %down_0.3.mine_ref = f32[16,192,128]{2,1,0:T(8,128)} custom-call(s32[1]{0:T(128)} %bitcast.side, s32[1]{0:T(128)} %bitcast.1.which, s32[2,128]{1,0:T(2,128)S(1)} %slice.16.wanted, bf16[16,192,128]{2,1,0:T(8,128)(2,1)} %get-tuple-element.31.refs_0_, bf16[4,32,4,16,128]{4,3,2,1,0:T(8,128)(2,1)} %all-to-all-done.3.refs_4_.refs_1_), custom_call_target="tpu_custom_call" | custom-call | tf_op jit(solution)/shard_map/down_0/pallas_call | solution.py:350
  234.8 10.7 %collective-permute-done.15.side_ref = bf16[16,192,128]{2,1,0:T(8,128)(2,1)S(1)} collective-permute-done((bf16[16,192,128]{2,1,0:T(8,128)(2,1)S(1)}, bf16[16,192,128]{2,1,0:T(8,128)(2,1)S(1)}, u32[]{:S(2)}, u32[]{:S(2)}) %collective-permute-start.15) | collective-permute-done | bytes 786464 | tf_op jit(solution)/shard_map/ppermute | solution.py:397
  245.5 0.9 copy-done.13
  246.4 0.9 copy-done.14
  247.3 4.0 %join.1 = bf16[192,2048]{1,0:T(8,128)(2,1)} custom-call(s32[1]{0:T(128)S(6)} %copy.62.length, bf16[192,2048]{1,0:T(8,128)(2,1)} %acoustic_ref.1, f32[16,192,128]{2,1,0:T(8,128)} %down_0.3.mine_ref, bf16[16,192,128]{2,1,0:T(8,128)(2,1)} %copy-done.14, bf16[16,192,128]{2,1,0:T(8,128)(2,1)} %copy-done.13), custom_call_target="tpu_custom_call" | custom-call | tf_op jit(solution)/shard_map/join/pallas_call | solution.py:386
  (60 shorter events, 0.8 us)
Async XLA Ops:
  0.0 9.1 %copy-start.15 = (s32[64,32,32]{0,2,1:T(8,128)S(1)}, s32[64,32,32]{0,2,1:T(8,128)}, u32[]{:S(2)}) copy-start(s32[64,32,32]{0,2,1:T(8,128)} %param.12) | copy-start | bytes 786436
  2.8 35.7 %collective-permute-start.5 = (bf16[8,32,2048]{2,1,0:T(8,128)(2,1)S(1)}, bf16[8,32,2048]{2,1,0:T(8,128)(2,1)S(1)}, u32[]{:S(2)}, u32[]{:S(2)}) collective-permute-start(bf16[8,32,2048]{2,1,0:T(8,128)(2,1)S(1)} %get-tuple-element.40), channel_id=1, source_target_pairs={{0,4},{2,6},{4,0},{6,2},{8,12},{10,14},{12,8},{14,10},{1,5},{3,7},... | collective-permute-start | bytes 3145736 | tf_op jit(solution)/shard_map/ppermute | solution.py:397
  5.8 22.5 %collective-permute-start = (s32[1]{0:T(128)}, s32[1]{0:T(128)}, u32[]{:S(2)}, u32[]{:S(2)}) collective-permute-start(s32[1]{0:T(128)} %param.14), channel_id=1, source_target_pairs={{0,8},{2,10},{4,12},{6,14},{8,0},{10,2},{12,4},{14,6},{1,9},{3,11}... | collective-permute-start | bytes 20 | tf_op jit(solution)/shard_map/ppermute | solution.py:397
  28.9 3.5 %collective-permute-start.1 = (s32[2]{0:T(128)S(1)}, s32[2]{0:T(128)S(1)}, u32[]{:S(2)}, u32[]{:S(2)}) collective-permute-start(s32[2]{0:T(128)S(1)} %pad_add_fusion), channel_id=1, source_target_pairs={{0,2},{2,0},{4,6},{6,4},{8,10},{10,8},{12,14},{14,12},{1,3},{3,1},... | collective-permute-start | bytes 32 | tf_op jit(solution)/shard_map/ppermute | solution.py:397
  33.2 3.5 %collective-permute-start.3 = (s32[4]{0:T(128)S(1)}, s32[4]{0:T(128)S(1)}, u32[]{:S(2)}, u32[]{:S(2)}) collective-permute-start(s32[4]{0:T(128)S(1)} %pad_add_fusion.1), channel_id=1, source_target_pairs={{0,16},{16,0},{1,17},{17,1},{2,18},{18,2},{3,19},{19,3},{4,20},{20... | collective-permute-start | bytes 56 | tf_op jit(solution)/shard_map/ppermute | solution.py:397
  38.3 4.4 %copy-start.17 = (s32[8,32,4]{1,0,2:T(8,128)}, s32[8,32,4]{1,0,2:T(8,128)S(1)}, u32[]{:S(2)}) copy-start(s32[8,32,4]{1,0,2:T(8,128)S(1)} %fusion.2) | copy-start | bytes 12292
  38.5 4.2 %copy-start.4 = (bf16[8,32,2048]{2,1,0:T(8,128)(2,1)}, bf16[8,32,2048]{2,1,0:T(8,128)(2,1)S(1)}, u32[]{:S(2)}) copy-start(bf16[8,32,2048]{2,1,0:T(8,128)(2,1)S(1)} %collective-permute-done.5.refs_1_.other_ref) | copy-start | bytes 3145732
  42.7 40.3 %all-to-all-start = ((bf16[4,2,8,4,32,128]{5,4,3,2,1,0:T(8,128)(2,1)}), bf16[4,2,8,4,32,128]{5,4,3,2,1,0:T(8,128)(2,1)S(1)}, u32[]{:S(2)}, u32[]{:S(2)}) async-start(bf16[4,2,8,4,32,128]{5,4,3,2,1,0:T(8,128)(2,1)} %pick_both.2.refs_0_), calls=%async_computation | async-start | bytes 4194304 | tf_op jit(solution)/shard_map/all_to_all | solution.py:457
  46.5 4.2 %copy-start.18 = (f32[4096]{0:T(1024)S(1)}, f32[4096]{0:T(1024)}, u32[]{:S(2)}) copy-start(f32[4096]{0:T(1024)} %param.9) | copy-start | bytes 49156
  47.2 31.6 %collective-permute-start.8 = (bf16[8,32,2048]{2,1,0:T(8,128)(2,1)}, bf16[8,32,2048]{2,1,0:T(8,128)(2,1)S(1)}, u32[]{:S(2)}, u32[]{:S(2)}) collective-permute-start(bf16[8,32,2048]{2,1,0:T(8,128)(2,1)} %gate.8), channel_id=1, source_target_pairs={{0,4},{2,6},{4,0},{6,2},{8,12},{10,14},{12,8},{14,10},{1,5},{3,7},... | collective-permute-start | bytes 3145736 | tf_op jit(solution)/shard_map/ppermute | solution.py:397
  50.7 2.6 %collective-permute-start.4 = (bf16[192,2048]{1,0:T(8,128)(2,1)}, bf16[192,2048]{1,0:T(8,128)(2,1)}, u32[]{:S(2)}, u32[]{:S(2)}) collective-permute-start(bf16[192,2048]{1,0:T(8,128)(2,1)} %acoustic_ref.1), channel_id=1, source_target_pairs={{0,1},{1,0},{2,3},{3,2},{4,5},{5,4},{6,7},{7,6},{8,9},{9,8},{10,11... | collective-permute-start | bytes 2359304 | tf_op jit(solution)/shard_map/ppermute | solution.py:397
  57.6 32.0 %collective-permute-start.6 = (bf16[8,192,128]{2,1,0:T(8,128)(2,1)}, bf16[8,192,128]{2,1,0:T(8,128)(2,1)S(1)}, u32[]{:S(2)}, u32[]{:S(2)}) collective-permute-start(bf16[8,192,128]{2,1,0:T(8,128)(2,1)} %gate.7), channel_id=1, source_target_pairs={{0,8},{2,10},{4,12},{6,14},{8,0},{10,2},{12,4},{14,6},{1,9},{3,11}... | collective-permute-start | bytes 1179656 | tf_op jit(solution)/shard_map/ppermute | solution.py:397
  83.0 1.3 copy-start.2
  85.0 4.7 %slice-start = ((s32[8,32,4]{1,0,2:T(8,128)}), s32[2,32,4]{1,0,2:T(2,128)S(1)}, s32[]{:S(2)}) async-start(s32[8,32,4]{1,0,2:T(8,128)} %copy-done.17), calls=%async_computation.4 | async-start | bytes 8192 | tf_op jit(solution)/shard_map/slice | solution.py:435
  85.0 6.6 %copy-start.3 = (bf16[4,2,8,4,32,128]{5,4,3,2,1,0:T(8,128)(2,1)S(1)}, bf16[4,2,8,4,32,128]{5,4,3,2,1,0:T(8,128)(2,1)}, u32[]{:S(2)}) copy-start(bf16[4,2,8,4,32,128]{5,4,3,2,1,0:T(8,128)(2,1)} %copy-done.2) | copy-start | bytes 6291460
  85.0 53.0 %all-to-all-start.1 = ((bf16[4,2,8,4,32,128]{5,4,3,2,1,0:T(8,128)(2,1)}), bf16[4,2,8,4,32,128]{5,4,3,2,1,0:T(8,128)(2,1)}, u32[]{:S(2)}, u32[]{:S(2)}) async-start(bf16[4,2,8,4,32,128]{5,4,3,2,1,0:T(8,128)(2,1)} %gate.9), calls=%async_computation.1 | async-start | bytes 4194304 | tf_op jit(solution)/shard_map/all_to_all | solution.py:457
  89.6 6.8 %copy-start.11 = (bf16[8,192,128]{2,1,0:T(8,128)(2,1)}, bf16[8,192,128]{2,1,0:T(8,128)(2,1)S(1)}, u32[]{:S(2)}) copy-start(bf16[8,192,128]{2,1,0:T(8,128)(2,1)S(1)} %collective-permute-done.6.far_a_ref) | copy-start | bytes 1179652
  89.7 1.9 collective-permute-start.7
  91.6 4.9 %copy-start.16 = (s32[64,32,32]{0,2,1:T(8,128)S(1)}, s32[64,32,32]{0,2,1:T(8,128)}, u32[]{:S(2)}) copy-start(s32[64,32,32]{0,2,1:T(8,128)} %param.13) | copy-start | bytes 786436
  91.6 26.4 %copy-start.19 = (s32[8]{0:T(128)S(1)}, s32[8]{0:T(128)}, u32[]{:S(2)}) copy-start(s32[8]{0:T(128)} %get-tuple-element.38) | copy-start | bytes 100
  96.5 20.0 %collective-permute-start.9 = (bf16[8,192,128]{2,1,0:T(8,128)(2,1)}, bf16[8,192,128]{2,1,0:T(8,128)(2,1)S(1)}, u32[]{:S(2)}, u32[]{:S(2)}) collective-permute-start(bf16[8,192,128]{2,1,0:T(8,128)(2,1)} %bitcast.41), channel_id=1, source_target_pairs={{0,8},{2,10},{4,12},{6,14},{8,0},{10,2},{12,4},{14,6},{1,9},{3,11}... | collective-permute-start | bytes 1179656 | tf_op jit(solution)/shard_map/ppermute | solution.py:397
  96.7 21.3 %collective-permute-start.2 = (s32[4]{0:T(128)S(1)}, s32[4]{0:T(128)S(1)}, u32[]{:S(2)}, u32[]{:S(2)}) collective-permute-start(s32[4]{0:T(128)S(1)} %pad_add_fusion.1), channel_id=1, source_target_pairs={{0,4},{2,6},{4,0},{6,2},{8,12},{10,14},{12,8},{14,10},{1,5},{3,7},... | collective-permute-start | bytes 56 | tf_op jit(solution)/shard_map/ppermute | solution.py:397
  116.5 0.7 copy-start.5
  117.9 20.1 %collective-permute-start.10 = (bf16[8,192,128]{2,1,0:T(8,128)(2,1)}, bf16[8,192,128]{2,1,0:T(8,128)(2,1)S(1)}, u32[]{:S(2)}, u32[]{:S(2)}) collective-permute-start(bf16[8,192,128]{2,1,0:T(8,128)(2,1)} %gate.10), channel_id=1, source_target_pairs={{0,8},{2,10},{4,12},{6,14},{8,0},{10,2},{12,4},{14,6},{1,9},{3,11}... | collective-permute-start | bytes 1179656 | tf_op jit(solution)/shard_map/ppermute | solution.py:397
  138.0 0.7 copy-start.9
  139.4 3.8 %copy-start.12 = (bf16[8,192,128]{2,1,0:T(8,128)(2,1)S(1)}, bf16[8,192,128]{2,1,0:T(8,128)(2,1)}, u32[]{:S(2)}) copy-start(bf16[8,192,128]{2,1,0:T(8,128)(2,1)} %copy-done.11) | copy-start | bytes 1179652
  139.4 37.5 %all-to-all-start.2 = ((bf16[4,32,4,16,128]{4,3,2,1,0:T(8,128)(2,1)}), bf16[4,32,4,16,128]{4,3,2,1,0:T(8,128)(2,1)S(1)}, u32[]{:S(2)}, u32[]{:S(2)}) async-start(bf16[4,32,4,16,128]{4,3,2,1,0:T(8,128)(2,1)} %gate.12), calls=%async_computation.2 | async-start | bytes 4194304 | tf_op jit(solution)/shard_map/all_to_all | solution.py:452
  148.4 26.5 %collective-permute-start.11 = (bf16[8,192,128]{2,1,0:T(8,128)(2,1)}, bf16[8,192,128]{2,1,0:T(8,128)(2,1)S(1)}, u32[]{:S(2)}, u32[]{:S(2)}) collective-permute-start(bf16[8,192,128]{2,1,0:T(8,128)(2,1)} %bitcast.42), channel_id=1, source_target_pairs={{0,8},{2,10},{4,12},{6,14},{8,0},{10,2},{12,4},{14,6},{1,9},{3,11}... | collective-permute-start | bytes 1179656 | tf_op jit(solution)/shard_map/ppermute | solution.py:397
  174.8 2.1 copy-start.7
  177.0 1.4 copy-start
  179.0 5.1 %copy-start.1 = (bf16[4,32,4,16,128]{4,3,2,1,0:T(8,128)(2,1)S(1)}, bf16[4,32,4,16,128]{4,3,2,1,0:T(8,128)(2,1)}, u32[]{:S(2)}) copy-start(bf16[4,32,4,16,128]{4,3,2,1,0:T(8,128)(2,1)} %copy-done) | copy-start | bytes 6291460
  179.0 5.1 %copy-start.6 = (bf16[8,192,128]{2,1,0:T(8,128)(2,1)S(1)}, bf16[8,192,128]{2,1,0:T(8,128)(2,1)}, u32[]{:S(2)}) copy-start(bf16[8,192,128]{2,1,0:T(8,128)(2,1)} %copy-done.5) | copy-start | bytes 1179652
  179.0 5.2 %copy-start.8 = (bf16[8,192,128]{2,1,0:T(8,128)(2,1)S(1)}, bf16[8,192,128]{2,1,0:T(8,128)(2,1)}, u32[]{:S(2)}) copy-start(bf16[8,192,128]{2,1,0:T(8,128)(2,1)} %copy-done.7) | copy-start | bytes 1179652
  179.0 43.7 %all-to-all-start.3 = ((bf16[4,32,4,16,128]{4,3,2,1,0:T(8,128)(2,1)}), bf16[4,32,4,16,128]{4,3,2,1,0:T(8,128)(2,1)}, u32[]{:S(2)}, u32[]{:S(2)}) async-start(bf16[4,32,4,16,128]{4,3,2,1,0:T(8,128)(2,1)} %gate.13), calls=%async_computation.3 | async-start | bytes 4194304 | tf_op jit(solution)/shard_map/all_to_all | solution.py:452
  190.0 7.2 %collective-permute-start.14 = (bf16[16,192,128]{2,1,0:T(8,128)(2,1)}, bf16[16,192,128]{2,1,0:T(8,128)(2,1)}, u32[]{:S(2)}, u32[]{:S(2)}) collective-permute-start(bf16[16,192,128]{2,1,0:T(8,128)(2,1)} %get-tuple-element.36), channel_id=1, source_target_pairs={{0,1},{1,0},{2,3},{3,2},{4,5},{5,4},{6,7},{7,6},{8,9},{9,8},{10,11... | collective-permute-start | bytes 2359304 | tf_op jit(solution)/shard_map/ppermute | solution.py:397
  190.7 25.7 %collective-permute-start.12 = (bf16[8,192,128]{2,1,0:T(8,128)(2,1)}, bf16[8,192,128]{2,1,0:T(8,128)(2,1)S(1)}, u32[]{:S(2)}, u32[]{:S(2)}) collective-permute-start(bf16[8,192,128]{2,1,0:T(8,128)(2,1)} %gate.11), channel_id=1, source_target_pairs={{0,8},{2,10},{4,12},{6,14},{8,0},{10,2},{12,4},{14,6},{1,9},{3,11}... | collective-permute-start | bytes 1179656 | tf_op jit(solution)/shard_map/ppermute | solution.py:397
  197.2 25.6 %copy-start.10 = (bf16[8,192,128]{2,1,0:T(8,128)(2,1)S(1)}, bf16[8,192,128]{2,1,0:T(8,128)(2,1)}, u32[]{:S(2)}) copy-start(bf16[8,192,128]{2,1,0:T(8,128)(2,1)} %copy-done.9) | copy-start | bytes 1179652
  199.0 46.4 %collective-permute-start.15 = (bf16[16,192,128]{2,1,0:T(8,128)(2,1)S(1)}, bf16[16,192,128]{2,1,0:T(8,128)(2,1)S(1)}, u32[]{:S(2)}, u32[]{:S(2)}) collective-permute-start(bf16[16,192,128]{2,1,0:T(8,128)(2,1)S(1)} %add_convert_fusion), channel_id=1, source_target_pairs={{0,8},{2,10},{4,12},{6,14},{8,0},{10,2},{12,4},{14,6},{1,9},{3,11}... | collective-permute-start | bytes 2359304 | tf_op jit(solution)/shard_map/ppermute | solution.py:397
  228.7 16.8 %collective-permute-start.13 = (bf16[16,192,128]{2,1,0:T(8,128)(2,1)}, bf16[16,192,128]{2,1,0:T(8,128)(2,1)S(1)}, u32[]{:S(2)}, u32[]{:S(2)}) collective-permute-start(bf16[16,192,128]{2,1,0:T(8,128)(2,1)} %get-tuple-element.32), channel_id=1, source_target_pairs={{0,1},{1,0},{2,3},{3,2},{4,5},{5,4},{6,7},{7,6},{8,9},{9,8},{10,11... | collective-permute-start | bytes 2359304 | tf_op jit(solution)/shard_map/ppermute | solution.py:397
  245.5 0.9 copy-start.13
  246.4 0.9 copy-start.14

commit v6 on v4

--- a/solution.py
+++ b/solution.py
@@ -89,7 +89,7 @@
     )(side, own, peer, gains)
 
 
-def pick_kernel(place, wanted, weight_ref, *refs, rows, runs, base, turning, after):
+def pick_kernel(place, wanted, weight_ref, *refs, rows, runs, base, up, after):
     out_refs, spread = refs[after:-1], refs[-1]
     step = pl.program_id(0) + base
     for h in range(HSTEP):
@@ -98,48 +98,41 @@
             for g in range(runs):
                 spread[h * runs + g, row * GROUP:(row + 1) * GROUP, :] = tile[g * GROUP:(g + 1) * GROUP]
     for member in range(wanted.shape[0] // 2):
-        pair = 2 * (place[0] ^ member)
+        pair = 2 * member if up else 2 * (place[0] ^ member)
         for u in range(2):
             for h in range(HSTEP):
                 for g in range(runs):
                     at = wanted[pair + u, (step * HSTEP + h) * runs + g]
                     block = spread[h * runs + g, pl.ds(at, rows, stride=GROUP), :]
-                    if turning and h % 2:
+                    if up and h % 2:
                         block = half_turn(block)
                     block = block.astype(jnp.bfloat16)
-                    if turning:
-                        out_refs[0][member, u, h, g] = block
+                    if up:
+                        out_refs[member][u, h, g] = block
                     else:
                         out_refs[u][member, h, g] = block
 
 
-def pick_blocks(weight, place, wanted, first, count, turning, after=()):
+def pick_blocks(weight, place, wanted, first, count, up, after=()):
     _, feat_blocks, width = weight.shape
     rows = width // BLK
     runs = feat_blocks // GROUP
     base = first // HSTEP
     members = wanted.shape[0] // 2
-    if turning:
-        outs = 1
-        shape = (members, 2, count, runs, rows, BLK)
-        out_spec = pl.BlockSpec((members, 2, HSTEP, runs, rows, BLK), lambda i, *_: (0, 0, i, 0, 0, 0))
-    else:
-        outs = 2
-        shape = (members, count, runs, rows, BLK)
-        out_spec = pl.BlockSpec((members, HSTEP, runs, rows, BLK), lambda i, *_: (0, i, 0, 0, 0))
-    return pl.pallas_call(
-        functools.partial(pick_kernel, rows=rows, runs=runs, base=base, turning=turning, after=len(after)),
+    outs, lead = (members, 2) if up else (2, members)
+    return pl.pallas_call(
+        functools.partial(pick_kernel, rows=rows, runs=runs, base=base, up=up, after=len(after)),
         grid_spec=pltpu.PrefetchScalarGridSpec(
             num_scalar_prefetch=2,
             grid=(count // HSTEP,),
             in_specs=[pl.BlockSpec((HSTEP, feat_blocks, width), lambda i, *_: (i + base, 0, 0))]
             + [corner(value) for value in after],
-            out_specs=[out_spec] * outs,
+            out_specs=[pl.BlockSpec((lead, HSTEP, runs, rows, BLK), lambda i, *_: (0, i, 0, 0, 0))] * outs,
             scratch_shapes=[pltpu.VMEM((HSTEP * runs, rows * GROUP, BLK), jnp.float32)],
         ),
-        out_shape=[pltpu.HBM(shape, jnp.bfloat16)] * outs,
+        out_shape=[pltpu.HBM((lead, count, runs, rows, BLK), jnp.bfloat16)] * outs,
         compiler_params=pltpu.CompilerParams(vmem_limit_bytes=48 << 20),
-        name="pick_up" if turning else "pick_down",
+        name="pick_up" if up else "pick_down",
     )(place, wanted, *in_hbm([weight]), *after)
 
 
@@ -165,14 +158,14 @@
     )(*in_hbm(values), *after)
 
 
-def up_kernel(side, slots, own_ref, far_a_ref, far_b_ref, weight_ref, *refs, runs, rows):
+def up_kernel(side, place, slots, own_ref, far_a_ref, far_b_ref, *refs, runs, rows):
+    weight_refs, refs = refs[:-6], refs[-6:]
     kept_refs, sent_refs, partner, held = refs[:2], refs[2:4], refs[4], refs[5]
     step = pl.program_id(0)
     frames = own_ref.shape[1]
     low = low_lanes((frames, BLK))
     even = low == (side[0] == 0)
-    members = weight_ref.shape[0]
-    side_rows = rows * members
+    side_rows = rows * len(weight_refs)
 
     @pl.when(step == 0)
     def _():
@@ -184,12 +177,12 @@
                 partner[first] = jnp.where(low, pair, turned).astype(jnp.bfloat16)
                 partner[first + 1] = jnp.where(low, turned, pair).astype(jnp.bfloat16)
 
-    for member in range(members):
+    for k, ref in enumerate(weight_refs):
+        start = pl.multiple_of(place[k] * rows, rows)
         for u in range(2):
             for h in range(HSTEP):
                 for g in range(runs):
-                    start = g * side_rows + member * rows
-                    held[u, h, start:start + rows, :] = weight_ref[member, u, h, g]
+                    held[u, h, pl.ds(start + g * side_rows, rows), :] = ref[u, h, g]
     for m in range(HSTEP // 2):
         for u, source in enumerate((own_ref, partner)):
             pair = []
@@ -203,32 +196,32 @@
             sent_refs[u][m] = jnp.where(even, pair[1], pair[0]).astype(jnp.bfloat16)
 
 
-def up_project(side, slots, own, far, weights):
-    members, _, hidden_blocks, runs, rows, _ = weights.shape
+def up_project(side, place, slots, own, far, weights):
+    _, hidden_blocks, runs, rows, _ = weights[0].shape
     slots_all, frames, _ = own.shape
     out_spec = pl.BlockSpec((HSTEP // 2, frames, BLK), lambda i, *_: (i, 0, 0))
     return pl.pallas_call(
         functools.partial(up_kernel, runs=runs, rows=rows),
         grid_spec=pltpu.PrefetchScalarGridSpec(
-            num_scalar_prefetch=2,
+            num_scalar_prefetch=3,
             grid=(hidden_blocks // HSTEP,),
             in_specs=[
                 pl.BlockSpec((slots_all, frames, BLK), lambda i, *_: (0, 0, 0)),
                 pl.BlockSpec((slots_all // 4, frames, BLK), lambda i, *_: (0, 0, 0)),
                 pl.BlockSpec((slots_all // 4, frames, BLK), lambda i, *_: (0, 0, 0)),
-                pl.BlockSpec((members, 2, HSTEP, runs, rows, BLK), lambda i, *_: (0, 0, i, 0, 0, 0)),
-            ],
+            ]
+            + [pl.BlockSpec((2, HSTEP, runs, rows, BLK), lambda i, *_: (0, i, 0, 0, 0))] * len(weights),
             out_specs=[out_spec] * 4,
             scratch_shapes=[
                 pltpu.VMEM((slots_all, frames, BLK), jnp.bfloat16),
-                pltpu.VMEM((2, HSTEP, runs * rows * members, BLK), jnp.bfloat16),
+                pltpu.VMEM((2, HSTEP, runs * rows * len(weights), BLK), jnp.bfloat16),
             ],
         ),
         out_shape=[pltpu.HBM((hidden_blocks // 2, frames, BLK), jnp.float32)] * 2
         + [pltpu.HBM((hidden_blocks // 2, frames, BLK), jnp.bfloat16)] * 2,
         compiler_params=pltpu.CompilerParams(vmem_limit_bytes=48 << 20),
         name="up_project",
-    )(side, slots, *in_hbm([own]), *far, weights)
+    )(side, place, slots, own, *far, *weights)
 
 
 def down_kernel(side, which, wanted, *refs, utt, parts, runs, rows):
@@ -374,7 +367,7 @@
     slots = (up_own ^ (core * (feat_blocks // 2))).reshape(2, -1)
     wanted_up = wanted_up.reshape(2 * across, -1)
     wanted_down = wanted_down.reshape(2 * across, -1)
-    place = (here % across)[None]
+    place = jnp.stack([(here ^ k) % across for k in members])
     peer = swap(acoustic, "tensor", 2, 1)
     gains = norm_gain.reshape(2, 1, features)
     gains = jnp.where(core == 0, gains, gains[::-1])
@@ -384,31 +377,32 @@
 
     groups = [[start + k for k in members] for start in (0, across)]
 
-    def within_side(blocks):
+    def by_distance(blocks):
+        return [blocks[0]] + [swap(blocks[k], "dp", dp, k) for k in members[1:]]
+
+    def in_order(blocks):
         return lax.all_to_all(blocks, "dp", split_axis=0, concat_axis=0, axis_index_groups=groups, tiled=True)
 
     count = hidden_blocks // CHUNKS
-    kept, crossed, after, got = ([], []), ([], []), in_hbm([own_far]), None
+    kept, crossed, after = ([], []), ([], []), in_hbm([own_far])
     for c in range(CHUNKS):
-        (blocks,) = pick_blocks(up_weight, place, wanted_up, c * count, count, True, after)
-        after = in_hbm([blocks])
-        if got is not None:
-            (blocks,) = gate([blocks], [got, *far])
-            after = [got]
-        got = within_side(blocks)
+        blocks = pick_blocks(up_weight, place, wanted_up, c * count, count, True, after)
+        after = [*in_hbm(blocks[:1]), far[0]]
+        got = by_distance(blocks)
         span = slice(c * count * runs, (c + 1) * count * runs)
-        kept_own, kept_far, sent_own, sent_far = up_project(side, slots[:, span], near, far, got)
+        kept_own, kept_far, sent_own, sent_far = up_project(side, place, slots[:, span], near, far, got)
         got_far = swap(sent_own, "dp", dp, across)
-        (sent_far,) = gate([sent_far], [got_far])
         got_own = swap(sent_far, "dp", dp, across)
         for u, (mine, theirs) in enumerate(((kept_own, got_own), (kept_far, got_far))):
             kept[u].append(mine)
             crossed[u].append(theirs)
-    own_blocks, far_blocks = pick_blocks(down_weight, place, wanted_down, 0, hidden_blocks, False, after)
-    (far_blocks,) = gate([far_blocks], [got, *crossed[1][:-1]])
-    far_down = within_side(far_blocks)
-    (own_blocks,) = gate([own_blocks], [far_down, *crossed[1], *crossed[0][:-1]])
-    own_down = within_side(own_blocks)
+    own_blocks, far_blocks = pick_blocks(
+        down_weight, place, wanted_down, 0, hidden_blocks, False, in_hbm(kept[0][:1])
+    )
+    (far_blocks,) = gate([far_blocks], [*crossed[1][:1], *got[1:]])
+    far_down = in_order(far_blocks)
+    (own_blocks,) = gate([own_blocks], [far_down, crossed[1][-1], crossed[0][0]])
+    own_down = in_order(own_blocks)
     rows_down = wanted_down[:2]
 
     def down(which, sources, weights, utt, dtype):

time: 230 us -> 211 us (0.917)
  waiting for transfers between devices: 117 us -> 102 us
  local copies, waits for them, and re-layouts: 6.99 us -> 11.6 us
  starting transfers between devices: 36.7 us -> 32.6 us
  Pallas kernels: 58.5 us -> 55 us
    ppermute x13 -> x19, waiting for transfers between devices: 107 us -> 94.5 us  [swap(): return lax.ppermute(value, axis, [(i, i ^ step) for i in range(size)])]
    all_to_all x4 -> x2, starting transfers between devices: 19.1 us -> 12.2 us  [in_order(): lax.all_to_all(blocks, 'dp', split_axis=0, concat_axis=0, axis_index_grou...]
    unnamed x38 -> x52, local copies, waits for them, and re-layouts: 6.2 us -> 10.8 us
    ppermute x13 -> x19, starting transfers between devices: 17.7 us -> 20.4 us  [swap(): return lax.ppermute(value, axis, [(i, i ^ step) for i in range(size)])]
    all_to_all x4 -> x2, waiting for transfers between devices: 10.2 us -> 7.65 us  [in_order(): lax.all_to_all(blocks, 'dp', split_axis=0, concat_axis=0, axis_index_grou...]
  transfers between devices with their start and end apart: 17 -> 21, of which waited for: 11 -> 13; matrix products, arithmetic and copies ran while one was open for 4% -> 4% of each run, Pallas kernels for 19% -> 22%
where the time goes in v6:
time: 211 us; the launch traced here: 210 us
  waiting for transfers between devices  102 us (48%)
  Pallas kernels  55 us (26%)
  starting transfers between devices  32.6 us (15%)
  local copies, waits for them, and re-layouts  11.6 us (5%)
  other arithmetic  6.65 us (3%)
    ppermute x19, waiting for transfers between devices, swap(): return lax.ppermute(value, axis, [(i, i ^ step) for i in range(size)])  94.5 us
    pallas_call x4, Pallas kernels, down_project(): pl.pallas_call(functools.partial(down_kernel, utt=utt, parts=parts, runs=...  22.3 us
    ppermute x19, starting transfers between devices, swap(): return lax.ppermute(value, axis, [(i, i ^ step) for i in range(size)])  20.4 us
    pallas_call x3, Pallas kernels, pick_blocks(): pl.pallas_call(functools.partial(pick_kernel, rows=rows, runs=runs, base=...  15.6 us
    all_to_all x2, starting transfers between devices, in_order(): lax.all_to_all(blocks, 'dp', split_axis=0, concat_axis=0, axis_index_grou...  12.2 us
    unnamed x52, local copies, waits for them, and re-layouts  10.8 us
    pallas_call x2, Pallas kernels, up_project(): pl.pallas_call(functools.partial(up_kernel, runs=runs, rows=rows), grid_s...  7.95 us
    all_to_all x2, waiting for transfers between devices, in_order(): lax.all_to_all(blocks, 'dp', split_axis=0, concat_axis=0, axis_index_grou...  7.65 us
  transfers between devices with their start and end apart: 21, of which 13 were waited for; matrix products, arithmetic and copies ran while one was open for 4% of the time, Pallas kernels for 22%

profile of v6, /device:TPU:0, one launch (start us, length us, event | category | flops | bytes accessed | tf_op | source)
XLA Modules:
  0.0 210.1 jit_solution(18212735387982864400)
XLA Ops:
  0.0 4.0 %collective-permute-start = (s32[1]{0:T(128)}, s32[1]{0:T(128)}, u32[]{:S(2)}, u32[]{:S(2)}) collective-permute-start(s32[1]{0:T(128)} %param.14), channel_id=1, source_target_pairs={{0,8},{2,10},{4,12},{6,14},{8,0},{10,2},{12,4},{14,6},{1,9},{3,11}... | collective-permute-start | bytes 20 | tf_op jit(solution)/shard_map/ppermute | solution.py:340
  4.0 1.2 fusion
  6.0 1.4 broadcast_select_fusion.gain_ref
  7.5 0.7 pad_add_fusion
  8.1 1.5 collective-permute-start.1
  9.6 2.0 collective-permute-done.1
  11.7 0.7 pad_add_fusion.1
  12.4 1.6 collective-permute-start.2
  14.0 2.0 collective-permute-done.2
  15.9 0.7 pad_add_fusion.2
  16.6 0.9 copy-done.22
  17.5 3.6 %norm_parts.1 = (bf16[32,192,128]{2,1,0:T(8,128)(2,1)}, bf16[8,192,128]{2,1,0:T(8,128)(2,1)}) custom-call(s32[1]{0:T(128)} %bitcast.side, bf16[192,2048]{1,0:T(8,128)(2,1)} %acoustic_ref.1, bf16[192,2048]{1,0:T(8,128)(2,1)} %copy-done.22, f32[2,1,2048]{2,1,0:T(1,128)} %broadcast_select_fusion.gain_ref), custom_call_target="tpu_custom_call" | custom-call | tf_op jit(solution)/shard_map/norm_parts/pallas_call | solution.py:69
  21.1 1.1 collective-permute-start.4
  22.2 0.3 fusion.2
  22.5 0.1 copy.36
  22.7 4.4 %pick_up.2 = (bf16[2,16,4,16,128]{4,3,2,1,0:T(8,128)(2,1)}, bf16[2,16,4,16,128]{4,3,2,1,0:T(8,128)(2,1)}, bf16[2,16,4,16,128]{4,3,2,1,0:T(8,128)(2,1)}, bf16[2,16,4,16,128]{4,3,2,1,0:T(8,128)(2,1)}) custom-call(s32[4]{0:T(128)S(1)} %pad_add_fusion.3.place, s32[8,128]{1,0:T(8,128)S(1)} %copy.37.wanted, bf16[32,32,2048]{2,1,0:T(8,128)(2,1)} %weight_ref.4, ...), custom_call_target="tpu_custom_call" | custom-call | tf_op jit(solution)/shard_map/pick_up/pallas_call | solution.py:123
  27.1 1.5 collective-permute-start.6
  28.6 1.6 collective-permute-start.7
  30.2 0.4 collective-permute-start.8
  30.6 9.4 %collective-permute-done.4.far_a_ref.refs_1_ = bf16[8,192,128]{2,1,0:T(8,128)(2,1)S(1)} collective-permute-done((bf16[8,192,128]{2,1,0:T(8,128)(2,1)}, bf16[8,192,128]{2,1,0:T(8,128)(2,1)S(1)}, u32[]{:S(2)}, u32[]{:S(2)}) %collective-permute-start.4) | collective-permute-done | bytes 393248 | tf_op jit(solution)/shard_map/ppermute | solution.py:340
  40.2 0.1 reshape.26
  40.3 4.6 %pick_up.3 = (bf16[2,16,4,16,128]{4,3,2,1,0:T(8,128)(2,1)}, bf16[2,16,4,16,128]{4,3,2,1,0:T(8,128)(2,1)}, bf16[2,16,4,16,128]{4,3,2,1,0:T(8,128)(2,1)}, bf16[2,16,4,16,128]{4,3,2,1,0:T(8,128)(2,1)}) custom-call(s32[4]{0:T(128)S(1)} %pad_add_fusion.3.place, s32[8,128]{1,0:T(8,128)S(1)} %copy.37.wanted, bf16[32,32,2048]{2,1,0:T(8,128)(2,1)} %weight_ref.4, ...), custom_call_target="tpu_custom_call" | custom-call | tf_op jit(solution)/shard_map/pick_up/pallas_call | solution.py:123
  44.9 1.5 collective-permute-start.9
  46.4 3.7 %collective-permute-done.7.refs_2_ = bf16[2,16,4,16,128]{4,3,2,1,0:T(8,128)(2,1)S(1)} collective-permute-done((bf16[2,16,4,16,128]{4,3,2,1,0:T(8,128)(2,1)}, bf16[2,16,4,16,128]{4,3,2,1,0:T(8,128)(2,1)S(1)}, u32[]{:S(2)}, u32[]{:S(2)}) %collective-permute-start.7) | collective-permute-done | bytes 524320 | tf_op jit(solution)/shard_map/ppermute | solution.py:340
  50.1 11.4 %collective-permute-done.8.refs_3_ = bf16[2,16,4,16,128]{4,3,2,1,0:T(8,128)(2,1)} collective-permute-done((bf16[2,16,4,16,128]{4,3,2,1,0:T(8,128)(2,1)}, bf16[2,16,4,16,128]{4,3,2,1,0:T(8,128)(2,1)}, u32[]{:S(2)}, u32[]{:S(2)}) %collective-permute-start.8) | collective-permute-done | bytes 524320 | tf_op jit(solution)/shard_map/ppermute | solution.py:340
  61.6 4.4 %up_project.2 = (f32[8,192,128]{2,1,0:T(8,128)}, f32[8,192,128]{2,1,0:T(8,128)}, bf16[8,192,128]{2,1,0:T(8,128)(2,1)}, bf16[8,192,128]{2,1,0:T(8,128)(2,1)}) custom-call(s32[1]{0:T(128)} %bitcast.side, s32[4]{0:T(128)S(1)} %pad_add_fusion.3.place, s32[2,64]{1,0:T(2,128)S(1)} %get-tuple-element.54.slots, bf16[32,192,128]{2,1,0:T(8,128)(2,1)S(1)} %copy-done.2, ...), custom_call_target="tpu_custom_call" | custom-call | tf_op jit(solution)/shard_map/up_project/pallas_call | solution.py:203
  66.0 0.4 collective-permute-start.14
  66.3 0.2 fusion.1
  66.5 0.3 fusion.4
  66.9 0.5 copy-done.24
  67.5 6.6 %pick_down.1 = (bf16[4,32,4,16,128]{4,3,2,1,0:T(8,128)(2,1)}, bf16[4,32,4,16,128]{4,3,2,1,0:T(8,128)(2,1)}) custom-call(s32[4]{0:T(128)S(1)} %pad_add_fusion.3.place, s32[8,128]{1,0:T(8,128)S(1)} %copy.40.wanted, bf16[32,32,2048]{2,1,0:T(8,128)(2,1)} %weight_ref.5, f32[8,192,128]{2,1,0:T(8,128)} %get-tuple-element.35.refs_0_), custom_call_target="tpu_custom_call" | custom-call | tf_op jit(solution)/shard_map/pick_down/pallas_call | solution.py:123
  74.1 6.9 %collective-permute-done.10.refs_2_.refs_3_ = bf16[2,16,4,16,128]{4,3,2,1,0:T(8,128)(2,1)S(1)} collective-permute-done((bf16[2,16,4,16,128]{4,3,2,1,0:T(8,128)(2,1)}, bf16[2,16,4,16,128]{4,3,2,1,0:T(8,128)(2,1)S(1)}, u32[]{:S(2)}, u32[]{:S(2)}) %collective-permute-start.10) | collective-permute-done | bytes 524320 | tf_op jit(solution)/shard_map/ppermute | solution.py:340
  81.0 7.9 %collective-permute-done.11.refs_3_.refs_4_ = bf16[2,16,4,16,128]{4,3,2,1,0:T(8,128)(2,1)S(1)} collective-permute-done((bf16[2,16,4,16,128]{4,3,2,1,0:T(8,128)(2,1)}, bf16[2,16,4,16,128]{4,3,2,1,0:T(8,128)(2,1)S(1)}, u32[]{:S(2)}, u32[]{:S(2)}) %collective-permute-start.11) | collective-permute-done | bytes 524320 | tf_op jit(solution)/shard_map/ppermute | solution.py:340
  89.0 0.8 copy-done.8
  89.8 0.1 copy-done.13
  89.9 0.7 gate.2
  90.6 3.7 %all-to-all-start = ((bf16[4,32,4,16,128]{4,3,2,1,0:T(8,128)(2,1)}), bf16[4,32,4,16,128]{4,3,2,1,0:T(8,128)(2,1)S(1)}, u32[]{:S(2)}, u32[]{:S(2)}) async-start(bf16[4,32,4,16,128]{4,3,2,1,0:T(8,128)(2,1)} %gate.2), calls=%async_computation | async-start | bytes 4194304 | tf_op jit(solution)/shard_map/all_to_all | solution.py:384
  94.4 3.8 %collective-permute-start.12 = (bf16[8,192,128]{2,1,0:T(8,128)(2,1)}, bf16[8,192,128]{2,1,0:T(8,128)(2,1)S(1)}, u32[]{:S(2)}, u32[]{:S(2)}) collective-permute-start(bf16[8,192,128]{2,1,0:T(8,128)(2,1)} %get-tuple-element.41), channel_id=1, source_target_pairs={{0,8},{2,10},{4,12},{6,14},{8,0},{10,2},{12,4},{14,6},{1,9},{3,11}... | collective-permute-start | bytes 1179656 | tf_op jit(solution)/shard_map/ppermute | solution.py:340
  98.2 1.4 copy-done.3
  99.6 1.0 copy-done.9
  100.6 1.0 copy-done.18
  101.6 1.0 copy-done.19
  102.6 3.6 %up_project.3 = (f32[8,192,128]{2,1,0:T(8,128)}, f32[8,192,128]{2,1,0:T(8,128)}, bf16[8,192,128]{2,1,0:T(8,128)(2,1)}, bf16[8,192,128]{2,1,0:T(8,128)(2,1)}) custom-call(s32[1]{0:T(128)} %bitcast.side, s32[4]{0:T(128)S(1)} %pad_add_fusion.3.place, s32[2,64]{1,0:T(2,128)S(1)} %get-tuple-element.53.slots, bf16[32,192,128]{2,1,0:T(8,128)(2,1)S(1)} %copy-done.3, ...), custom_call_target="tpu_custom_call" | custom-call | tf_op jit(solution)/shard_map/up_project/pallas_call | solution.py:203
  106.3 20.5 %collective-permute-done.12.refs_3_.refs_2_ = bf16[8,192,128]{2,1,0:T(8,128)(2,1)S(1)} collective-permute-done((bf16[8,192,128]{2,1,0:T(8,128)(2,1)}, bf16[8,192,128]{2,1,0:T(8,128)(2,1)S(1)}, u32[]{:S(2)}, u32[]{:S(2)}) %collective-permute-start.12) | collective-permute-done | bytes 393248 | tf_op jit(solution)/shard_map/ppermute | solution.py:340
  126.7 0.8 copy-done.11
  127.5 3.6 %collective-permute-done.15.refs_2_.refs_3_ = bf16[8,192,128]{2,1,0:T(8,128)(2,1)S(1)} collective-permute-done((bf16[8,192,128]{2,1,0:T(8,128)(2,1)}, bf16[8,192,128]{2,1,0:T(8,128)(2,1)S(1)}, u32[]{:S(2)}, u32[]{:S(2)}) %collective-permute-start.15) | collective-permute-done | bytes 393248 | tf_op jit(solution)/shard_map/ppermute | solution.py:340
  131.2 2.1 all-to-all-done.refs_1_.refs_4_
  133.2 1.3 copy-done
  134.6 0.7 gate.3
  135.3 8.4 %all-to-all-start.1 = ((bf16[4,32,4,16,128]{4,3,2,1,0:T(8,128)(2,1)}), bf16[4,32,4,16,128]{4,3,2,1,0:T(8,128)(2,1)}, u32[]{:S(2)}, u32[]{:S(2)}) async-start(bf16[4,32,4,16,128]{4,3,2,1,0:T(8,128)(2,1)} %gate.3), calls=%async_computation.1 | async-start | bytes 4194304 | tf_op jit(solution)/shard_map/all_to_all | solution.py:384
  143.8 0.1 slice.16.wanted
  144.0 5.7 %down_1.2 = (bf16[16,192,128]{2,1,0:T(8,128)(2,1)}, bf16[16,192,128]{2,1,0:T(8,128)(2,1)}) custom-call(s32[1]{0:T(128)} %bitcast.side, s32[1]{0:T(128)} %bitcast.4.which, s32[2,128]{1,0:T(2,128)S(1)} %slice.16.wanted, f32[8,192,128]{2,1,0:T(8,128)} %get-tuple-element.49.refs_0_, f32[8,192,128]{2,1,0:T(8,128)} %get-tuple-element.50.refs_1_, ...), custom_call_target="tpu_custom_call" | custom-call | tf_op jit(solution)/shard_map/down_1/pallas_call | solution.py:293
  149.7 0.5 collective-permute-start.13
  150.2 5.2 %down_1.3 = f32[16,192,128]{2,1,0:T(8,128)} custom-call(s32[1]{0:T(128)} %bitcast.side, s32[1]{0:T(128)} %bitcast.1.which, s32[2,128]{1,0:T(2,128)S(1)} %slice.16.wanted, bf16[16,192,128]{2,1,0:T(8,128)(2,1)} %get-tuple-element.51.refs_0_, bf16[4,32,4,16,128]{4,3,2,1,0:T(8,128)(2,1)S(1)} %copy-done.1), custom_call_target="tpu_custom_call" | custom-call | tf_op jit(solution)/shard_map/down_1/pallas_call | solution.py:293
  155.4 1.6 add_convert_fusion
  157.1 2.5 %collective-permute-start.18 = (bf16[16,192,128]{2,1,0:T(8,128)(2,1)S(1)}, bf16[16,192,128]{2,1,0:T(8,128)(2,1)S(1)}, u32[]{:S(2)}, u32[]{:S(2)}) collective-permute-start(bf16[16,192,128]{2,1,0:T(8,128)(2,1)S(1)} %add_convert_fusion), channel_id=1, source_target_pairs={{0,8},{2,10},{4,12},{6,14},{8,0},{10,2},{12,4},{14,6},{1,9},{3,11}... | collective-permute-start | bytes 2359304 | tf_op jit(solution)/shard_map/ppermute | solution.py:340
  159.6 16.4 %collective-permute-done.13.refs_3_ = bf16[8,192,128]{2,1,0:T(8,128)(2,1)S(1)} collective-permute-done((bf16[8,192,128]{2,1,0:T(8,128)(2,1)S(1)}, bf16[8,192,128]{2,1,0:T(8,128)(2,1)S(1)}, u32[]{:S(2)}, u32[]{:S(2)}) %collective-permute-start.13) | collective-permute-done | bytes 393248 | tf_op jit(solution)/shard_map/ppermute | solution.py:340
  176.0 5.6 %all-to-all-done.1.refs_4_.refs_1_ = bf16[4,32,4,16,128]{4,3,2,1,0:T(8,128)(2,1)} async-done(((bf16[4,32,4,16,128]{4,3,2,1,0:T(8,128)(2,1)}), bf16[4,32,4,16,128]{4,3,2,1,0:T(8,128)(2,1)}, u32[]{:S(2)}, u32[]{:S(2)}) %all-to-all-start.1) | async-done | bytes 2097184 | tf_op jit(solution)/shard_map/all_to_all | solution.py:384
  181.6 5.9 %down_0.2 = (bf16[16,192,128]{2,1,0:T(8,128)(2,1)}, bf16[16,192,128]{2,1,0:T(8,128)(2,1)}) custom-call(s32[1]{0:T(128)} %bitcast.side, s32[1]{0:T(128)} %bitcast.4.which, s32[2,128]{1,0:T(2,128)S(1)} %slice.16.wanted, f32[8,192,128]{2,1,0:T(8,128)} %get-tuple-element.35.refs_0_, f32[8,192,128]{2,1,0:T(8,128)} %get-tuple-element.40.refs_1_, ...), custom_call_target="tpu_custom_call" | custom-call | tf_op jit(solution)/shard_map/down_0/pallas_call | solution.py:293
  188.2 5.5 %down_0.3.mine_ref = f32[16,192,128]{2,1,0:T(8,128)} custom-call(s32[1]{0:T(128)} %bitcast.side, s32[1]{0:T(128)} %bitcast.1.which, s32[2,128]{1,0:T(2,128)S(1)} %slice.16.wanted, bf16[16,192,128]{2,1,0:T(8,128)(2,1)} %get-tuple-element.47.refs_0_, bf16[4,32,4,16,128]{4,3,2,1,0:T(8,128)(2,1)} %all-to-all-done.1.refs_4_.refs_1_), custom_call_target="tpu_custom_call" | custom-call | tf_op jit(solution)/shard_map/down_0/pallas_call | solution.py:293
  193.7 10.6 %collective-permute-done.18.side_ref = bf16[16,192,128]{2,1,0:T(8,128)(2,1)S(1)} collective-permute-done((bf16[16,192,128]{2,1,0:T(8,128)(2,1)S(1)}, bf16[16,192,128]{2,1,0:T(8,128)(2,1)S(1)}, u32[]{:S(2)}, u32[]{:S(2)}) %collective-permute-start.18) | collective-permute-done | bytes 786464 | tf_op jit(solution)/shard_map/ppermute | solution.py:340
  204.3 0.9 copy-done.20
  205.2 0.9 copy-done.21
  206.1 4.0 %join.1 = bf16[192,2048]{1,0:T(8,128)(2,1)} custom-call(s32[1]{0:T(128)S(6)} %copy.52.length, bf16[192,2048]{1,0:T(8,128)(2,1)} %acoustic_ref.1, f32[16,192,128]{2,1,0:T(8,128)} %down_0.3.mine_ref, bf16[16,192,128]{2,1,0:T(8,128)(2,1)} %copy-done.21, bf16[16,192,128]{2,1,0:T(8,128)(2,1)} %copy-done.20), custom_call_target="tpu_custom_call" | custom-call | tf_op jit(solution)/shard_map/join/pallas_call | solution.py:329
  (67 shorter events, 0.7 us)
Async XLA Ops:
  0.0 7.5 %collective-permute-start = (s32[1]{0:T(128)}, s32[1]{0:T(128)}, u32[]{:S(2)}, u32[]{:S(2)}) collective-permute-start(s32[1]{0:T(128)} %param.14), channel_id=1, source_target_pairs={{0,8},{2,10},{4,12},{6,14},{8,0},{10,2},{12,4},{14,6},{1,9},{3,11}... | collective-permute-start | bytes 20 | tf_op jit(solution)/shard_map/ppermute | solution.py:340
  4.0 12.6 %collective-permute-start.3 = (bf16[192,2048]{1,0:T(8,128)(2,1)}, bf16[192,2048]{1,0:T(8,128)(2,1)S(1)}, u32[]{:S(2)}, u32[]{:S(2)}) collective-permute-start(bf16[192,2048]{1,0:T(8,128)(2,1)} %acoustic_ref.1), channel_id=1, source_target_pairs={{0,1},{1,0},{2,3},{3,2},{4,5},{5,4},{6,7},{7,6},{8,9},{9,8},{10,11... | collective-permute-start | bytes 2359304 | tf_op jit(solution)/shard_map/ppermute | solution.py:340
  8.1 3.5 %collective-permute-start.1 = (s32[2]{0:T(128)S(1)}, s32[2]{0:T(128)S(1)}, u32[]{:S(2)}, u32[]{:S(2)}) collective-permute-start(s32[2]{0:T(128)S(1)} %pad_add_fusion), channel_id=1, source_target_pairs={{0,2},{2,0},{4,6},{6,4},{8,10},{10,8},{12,14},{14,12},{1,3},{3,1},... | collective-permute-start | bytes 32 | tf_op jit(solution)/shard_map/ppermute | solution.py:340
  12.4 3.5 %collective-permute-start.2 = (s32[4]{0:T(128)S(1)}, s32[4]{0:T(128)S(1)}, u32[]{:S(2)}, u32[]{:S(2)}) collective-permute-start(s32[4]{0:T(128)S(1)} %pad_add_fusion.1), channel_id=1, source_target_pairs={{0,4},{2,6},{4,0},{6,2},{8,12},{10,14},{12,8},{14,10},{1,5},{3,7},... | collective-permute-start | bytes 56 | tf_op jit(solution)/shard_map/ppermute | solution.py:340
  16.6 0.9 copy-start.22
  21.1 18.9 %collective-permute-start.4 = (bf16[8,192,128]{2,1,0:T(8,128)(2,1)}, bf16[8,192,128]{2,1,0:T(8,128)(2,1)S(1)}, u32[]{:S(2)}, u32[]{:S(2)}) collective-permute-start(bf16[8,192,128]{2,1,0:T(8,128)(2,1)} %get-tuple-element.30.refs_0_), channel_id=1, source_target_pairs={{0,8},{2,10},{4,12},{6,14},{8,0},{10,2},{12,4},{14,6},{1,9},{3,11}... | collective-permute-start | bytes 1179656 | tf_op jit(solution)/shard_map/ppermute | solution.py:340
  27.1 19.3 %collective-permute-start.6 = (bf16[2,16,4,16,128]{4,3,2,1,0:T(8,128)(2,1)}, bf16[2,16,4,16,128]{4,3,2,1,0:T(8,128)(2,1)S(1)}, u32[]{:S(2)}, u32[]{:S(2)}) collective-permute-start(bf16[2,16,4,16,128]{4,3,2,1,0:T(8,128)(2,1)} %get-tuple-element.32), channel_id=1, source_target_pairs={{0,2},{2,0},{4,6},{6,4},{8,10},{10,8},{12,14},{14,12},{1,3},{3,1},... | collective-permute-start | bytes 1572872 | tf_op jit(solution)/shard_map/ppermute | solution.py:340
  28.6 21.4 %collective-permute-start.7 = (bf16[2,16,4,16,128]{4,3,2,1,0:T(8,128)(2,1)}, bf16[2,16,4,16,128]{4,3,2,1,0:T(8,128)(2,1)S(1)}, u32[]{:S(2)}, u32[]{:S(2)}) collective-permute-start(bf16[2,16,4,16,128]{4,3,2,1,0:T(8,128)(2,1)} %get-tuple-element.33), channel_id=1, source_target_pairs={{0,4},{2,6},{4,0},{6,2},{8,12},{10,14},{12,8},{14,10},{1,5},{3,7},... | collective-permute-start | bytes 1572872 | tf_op jit(solution)/shard_map/ppermute | solution.py:340
  30.2 31.4 %collective-permute-start.8 = (bf16[2,16,4,16,128]{4,3,2,1,0:T(8,128)(2,1)}, bf16[2,16,4,16,128]{4,3,2,1,0:T(8,128)(2,1)}, u32[]{:S(2)}, u32[]{:S(2)}) collective-permute-start(bf16[2,16,4,16,128]{4,3,2,1,0:T(8,128)(2,1)} %get-tuple-element.34), channel_id=1, source_target_pairs={{0,6},{2,4},{4,2},{6,0},{8,14},{10,12},{12,10},{14,8},{1,7},{3,5},... | collective-permute-start | bytes 1572872 | tf_op jit(solution)/shard_map/ppermute | solution.py:340
  40.0 21.6 %collective-permute-start.5 = (bf16[8,192,128]{2,1,0:T(8,128)(2,1)S(1)}, bf16[8,192,128]{2,1,0:T(8,128)(2,1)S(1)}, u32[]{:S(2)}, u32[]{:S(2)}) collective-permute-start(bf16[8,192,128]{2,1,0:T(8,128)(2,1)S(1)} %collective-permute-done.4.far_a_ref.refs_1_), channel_id=1, source_target_pairs={{0,1},{1,0},{2,3},{3,2},{4,5},{5,4},{6,7},{7,6},{8,9},{9,8},{10,11... | collective-permute-start | bytes 1179656 | tf_op jit(solution)/shard_map/ppermute | solution.py:340
  40.3 21.3 %copy-start.2 = (bf16[32,192,128]{2,1,0:T(8,128)(2,1)S(1)}, bf16[32,192,128]{2,1,0:T(8,128)(2,1)}, u32[]{:S(2)}) copy-start(bf16[32,192,128]{2,1,0:T(8,128)(2,1)} %get-tuple-element.29.own_ref) | copy-start | bytes 4718596
  40.3 21.3 %copy-start.10 = (bf16[2,16,4,16,128]{4,3,2,1,0:T(8,128)(2,1)S(1)}, bf16[2,16,4,16,128]{4,3,2,1,0:T(8,128)(2,1)}, u32[]{:S(2)}) copy-start(bf16[2,16,4,16,128]{4,3,2,1,0:T(8,128)(2,1)} %get-tuple-element.31.refs_0_) | copy-start | bytes 1572868
  44.9 29.2 %collective-permute-start.9 = (bf16[2,16,4,16,128]{4,3,2,1,0:T(8,128)(2,1)}, bf16[2,16,4,16,128]{4,3,2,1,0:T(8,128)(2,1)S(1)}, u32[]{:S(2)}, u32[]{:S(2)}) collective-permute-start(bf16[2,16,4,16,128]{4,3,2,1,0:T(8,128)(2,1)} %get-tuple-element.37), channel_id=1, source_target_pairs={{0,2},{2,0},{4,6},{6,4},{8,10},{10,8},{12,14},{14,12},{1,3},{3,1},... | collective-permute-start | bytes 1572872 | tf_op jit(solution)/shard_map/ppermute | solution.py:340
  46.4 34.6 %collective-permute-start.10 = (bf16[2,16,4,16,128]{4,3,2,1,0:T(8,128)(2,1)}, bf16[2,16,4,16,128]{4,3,2,1,0:T(8,128)(2,1)S(1)}, u32[]{:S(2)}, u32[]{:S(2)}) collective-permute-start(bf16[2,16,4,16,128]{4,3,2,1,0:T(8,128)(2,1)} %get-tuple-element.38), channel_id=1, source_target_pairs={{0,4},{2,6},{4,0},{6,2},{8,12},{10,14},{12,8},{14,10},{1,5},{3,7},... | collective-permute-start | bytes 1572872 | tf_op jit(solution)/shard_map/ppermute | solution.py:340
  50.1 38.9 %collective-permute-start.11 = (bf16[2,16,4,16,128]{4,3,2,1,0:T(8,128)(2,1)}, bf16[2,16,4,16,128]{4,3,2,1,0:T(8,128)(2,1)S(1)}, u32[]{:S(2)}, u32[]{:S(2)}) collective-permute-start(bf16[2,16,4,16,128]{4,3,2,1,0:T(8,128)(2,1)} %get-tuple-element.39), channel_id=1, source_target_pairs={{0,6},{2,4},{4,2},{6,0},{8,14},{10,12},{12,10},{14,8},{1,7},{3,5},... | collective-permute-start | bytes 1572872 | tf_op jit(solution)/shard_map/ppermute | solution.py:340
  61.6 4.4 %copy-start.17 = (bf16[8,192,128]{2,1,0:T(8,128)(2,1)}, bf16[8,192,128]{2,1,0:T(8,128)(2,1)S(1)}, u32[]{:S(2)}) copy-start(bf16[8,192,128]{2,1,0:T(8,128)(2,1)S(1)} %collective-permute-done.5.far_b_ref) | copy-start | bytes 1179652
  61.6 4.7 %copy-start.23 = (s32[64,32,32]{0,2,1:T(8,128)S(1)}, s32[64,32,32]{0,2,1:T(8,128)}, u32[]{:S(2)}) copy-start(s32[64,32,32]{0,2,1:T(8,128)} %param.13) | copy-start | bytes 786436
  66.0 23.0 %collective-permute-start.14 = (bf16[8,192,128]{2,1,0:T(8,128)(2,1)}, bf16[8,192,128]{2,1,0:T(8,128)(2,1)S(1)}, u32[]{:S(2)}, u32[]{:S(2)}) collective-permute-start(bf16[8,192,128]{2,1,0:T(8,128)(2,1)} %get-tuple-element.45), channel_id=1, source_target_pairs={{0,8},{2,10},{4,12},{6,14},{8,0},{10,2},{12,4},{14,6},{1,9},{3,11}... | collective-permute-start | bytes 1179656 | tf_op jit(solution)/shard_map/ppermute | solution.py:340
  66.8 0.6 copy-start.24
  74.1 14.9 %copy-start.4 = (bf16[2,16,4,16,128]{4,3,2,1,0:T(8,128)(2,1)}, bf16[2,16,4,16,128]{4,3,2,1,0:T(8,128)(2,1)S(1)}, u32[]{:S(2)}) copy-start(bf16[2,16,4,16,128]{4,3,2,1,0:T(8,128)(2,1)S(1)} %collective-permute-done.9.refs_1_.refs_2_) | copy-start | bytes 1572868
  81.0 8.0 %copy-start.6 = (bf16[2,16,4,16,128]{4,3,2,1,0:T(8,128)(2,1)}, bf16[2,16,4,16,128]{4,3,2,1,0:T(8,128)(2,1)S(1)}, u32[]{:S(2)}) copy-start(bf16[2,16,4,16,128]{4,3,2,1,0:T(8,128)(2,1)S(1)} %collective-permute-done.10.refs_2_.refs_3_) | copy-start | bytes 1572868
  88.9 0.8 copy-start.8
  88.9 1.0 copy-start.13
  90.6 7.5 %copy-start.5 = (bf16[2,16,4,16,128]{4,3,2,1,0:T(8,128)(2,1)S(1)}, bf16[2,16,4,16,128]{4,3,2,1,0:T(8,128)(2,1)}, u32[]{:S(2)}) copy-start(bf16[2,16,4,16,128]{4,3,2,1,0:T(8,128)(2,1)} %copy-done.4) | copy-start | bytes 1572868
  90.6 7.5 %copy-start.7 = (bf16[2,16,4,16,128]{4,3,2,1,0:T(8,128)(2,1)S(1)}, bf16[2,16,4,16,128]{4,3,2,1,0:T(8,128)(2,1)}, u32[]{:S(2)}) copy-start(bf16[2,16,4,16,128]{4,3,2,1,0:T(8,128)(2,1)} %copy-done.6) | copy-start | bytes 1572868
  90.6 42.6 %all-to-all-start = ((bf16[4,32,4,16,128]{4,3,2,1,0:T(8,128)(2,1)}), bf16[4,32,4,16,128]{4,3,2,1,0:T(8,128)(2,1)S(1)}, u32[]{:S(2)}, u32[]{:S(2)}) async-start(bf16[4,32,4,16,128]{4,3,2,1,0:T(8,128)(2,1)} %gate.2), calls=%async_computation | async-start | bytes 4194304 | tf_op jit(solution)/shard_map/all_to_all | solution.py:384
  94.4 32.4 %collective-permute-start.12 = (bf16[8,192,128]{2,1,0:T(8,128)(2,1)}, bf16[8,192,128]{2,1,0:T(8,128)(2,1)S(1)}, u32[]{:S(2)}, u32[]{:S(2)}) collective-permute-start(bf16[8,192,128]{2,1,0:T(8,128)(2,1)} %get-tuple-element.41), channel_id=1, source_target_pairs={{0,8},{2,10},{4,12},{6,14},{8,0},{10,2},{12,4},{14,6},{1,9},{3,11}... | collective-permute-start | bytes 1179656 | tf_op jit(solution)/shard_map/ppermute | solution.py:340
  98.2 1.4 copy-start.3
  99.6 1.0 copy-start.9
  100.6 1.0 copy-start.18
  101.6 1.0 copy-start.19
  106.2 24.9 %collective-permute-start.15 = (bf16[8,192,128]{2,1,0:T(8,128)(2,1)}, bf16[8,192,128]{2,1,0:T(8,128)(2,1)S(1)}, u32[]{:S(2)}, u32[]{:S(2)}) collective-permute-start(bf16[8,192,128]{2,1,0:T(8,128)(2,1)} %get-tuple-element.46), channel_id=1, source_target_pairs={{0,8},{2,10},{4,12},{6,14},{8,0},{10,2},{12,4},{14,6},{1,9},{3,11}... | collective-permute-start | bytes 1179656 | tf_op jit(solution)/shard_map/ppermute | solution.py:340
  126.7 0.8 copy-start.11
  131.2 2.1 copy-start.15
  133.2 1.4 copy-start
  135.3 8.4 %slice-start = ((s32[8,32,4]{1,0,2:T(8,128)}), s32[2,32,4]{1,0,2:T(2,128)S(1)}, s32[]{:S(2)}) async-start(s32[8,32,4]{1,0,2:T(8,128)} %copy-done.24), calls=%async_computation.2 | async-start | bytes 8192 | tf_op jit(solution)/shard_map/slice | solution.py:406
  135.3 8.7 %copy-start.1 = (bf16[4,32,4,16,128]{4,3,2,1,0:T(8,128)(2,1)S(1)}, bf16[4,32,4,16,128]{4,3,2,1,0:T(8,128)(2,1)}, u32[]{:S(2)}) copy-start(bf16[4,32,4,16,128]{4,3,2,1,0:T(8,128)(2,1)} %copy-done) | copy-start | bytes 6291460
  135.3 8.7 %copy-start.14 = (bf16[8,192,128]{2,1,0:T(8,128)(2,1)S(1)}, bf16[8,192,128]{2,1,0:T(8,128)(2,1)}, u32[]{:S(2)}) copy-start(bf16[8,192,128]{2,1,0:T(8,128)(2,1)} %copy-done.13) | copy-start | bytes 1179652
  135.3 8.7 %copy-start.16 = (bf16[8,192,128]{2,1,0:T(8,128)(2,1)S(1)}, bf16[8,192,128]{2,1,0:T(8,128)(2,1)}, u32[]{:S(2)}) copy-start(bf16[8,192,128]{2,1,0:T(8,128)(2,1)} %copy-done.15) | copy-start | bytes 1179652
  135.3 46.3 %all-to-all-start.1 = ((bf16[4,32,4,16,128]{4,3,2,1,0:T(8,128)(2,1)}), bf16[4,32,4,16,128]{4,3,2,1,0:T(8,128)(2,1)}, u32[]{:S(2)}, u32[]{:S(2)}) async-start(bf16[4,32,4,16,128]{4,3,2,1,0:T(8,128)(2,1)} %gate.3), calls=%async_computation.1 | async-start | bytes 4194304 | tf_op jit(solution)/shard_map/all_to_all | solution.py:384
  144.0 5.7 %copy-start.25 = (bf16[8,192,128]{2,1,0:T(8,128)(2,1)S(1)}, bf16[8,192,128]{2,1,0:T(8,128)(2,1)}, u32[]{:S(2)}) copy-start(bf16[8,192,128]{2,1,0:T(8,128)(2,1)} %get-tuple-element.42) | copy-start | bytes 1179652
  149.7 5.8 %collective-permute-start.17 = (bf16[16,192,128]{2,1,0:T(8,128)(2,1)}, bf16[16,192,128]{2,1,0:T(8,128)(2,1)S(1)}, u32[]{:S(2)}, u32[]{:S(2)}) collective-permute-start(bf16[16,192,128]{2,1,0:T(8,128)(2,1)} %get-tuple-element.52), channel_id=1, source_target_pairs={{0,1},{1,0},{2,3},{3,2},{4,5},{5,4},{6,7},{7,6},{8,9},{9,8},{10,11... | collective-permute-start | bytes 2359304 | tf_op jit(solution)/shard_map/ppermute | solution.py:340
  149.7 26.3 %collective-permute-start.13 = (bf16[8,192,128]{2,1,0:T(8,128)(2,1)S(1)}, bf16[8,192,128]{2,1,0:T(8,128)(2,1)S(1)}, u32[]{:S(2)}, u32[]{:S(2)}) collective-permute-start(bf16[8,192,128]{2,1,0:T(8,128)(2,1)S(1)} %copy-done.25), channel_id=1, source_target_pairs={{0,8},{2,10},{4,12},{6,14},{8,0},{10,2},{12,4},{14,6},{1,9},{3,11}... | collective-permute-start | bytes 1179656 | tf_op jit(solution)/shard_map/ppermute | solution.py:340
  155.4 26.2 %copy-start.12 = (bf16[8,192,128]{2,1,0:T(8,128)(2,1)S(1)}, bf16[8,192,128]{2,1,0:T(8,128)(2,1)}, u32[]{:S(2)}) copy-start(bf16[8,192,128]{2,1,0:T(8,128)(2,1)} %copy-done.11) | copy-start | bytes 1179652
  157.1 47.2 %collective-permute-start.18 = (bf16[16,192,128]{2,1,0:T(8,128)(2,1)S(1)}, bf16[16,192,128]{2,1,0:T(8,128)(2,1)S(1)}, u32[]{:S(2)}, u32[]{:S(2)}) collective-permute-start(bf16[16,192,128]{2,1,0:T(8,128)(2,1)S(1)} %add_convert_fusion), channel_id=1, source_target_pairs={{0,8},{2,10},{4,12},{6,14},{8,0},{10,2},{12,4},{14,6},{1,9},{3,11}... | collective-permute-start | bytes 2359304 | tf_op jit(solution)/shard_map/ppermute | solution.py:340
  187.5 16.8 %collective-permute-start.16 = (bf16[16,192,128]{2,1,0:T(8,128)(2,1)}, bf16[16,192,128]{2,1,0:T(8,128)(2,1)S(1)}, u32[]{:S(2)}, u32[]{:S(2)}) collective-permute-start(bf16[16,192,128]{2,1,0:T(8,128)(2,1)} %get-tuple-element.48), channel_id=1, source_target_pairs={{0,1},{1,0},{2,3},{3,2},{4,5},{5,4},{6,7},{7,6},{8,9},{9,8},{10,11... | collective-permute-start | bytes 2359304 | tf_op jit(solution)/shard_map/ppermute | solution.py:340
  204.3 0.9 copy-start.20
  205.2 0.9 copy-start.21

commit v7 on v6

--- a/solution.py
+++ b/solution.py
@@ -311,31 +311,6 @@
     )(side, which, wanted, *in_hbm(sources[:-parts] if parts else sources), *sources[len(sources) - parts:], weights)
 
 
-def join_kernel(length, acoustic_ref, mine_ref, core_ref, side_ref, out_ref):
-    frames = out_ref.shape[0]
-    valid = lax.broadcasted_iota(jnp.int32, (frames, BLK), 0) < length[0]
-    for d in range(mine_ref.shape[0]):
-        lanes = slice(d * BLK, (d + 1) * BLK)
-        feedfwd = mine_ref[d] + core_ref[d].astype(jnp.float32) + side_ref[d].astype(jnp.float32)
-        summed = acoustic_ref[:, lanes].astype(jnp.float32) + feedfwd
-        out_ref[:, lanes] = jnp.where(valid, summed, 0.0).astype(jnp.bfloat16)
-
-
-def join(lengths, acoustic, mine, from_core, from_side):
-    outs, frames, _ = mine.shape
-    per = outs // 4
-    block = pl.BlockSpec((per, frames, BLK), lambda i, *_: (i, 0, 0))
-    flat = pl.BlockSpec((frames, per * BLK), lambda i, *_: (0, i))
-    return pl.pallas_call(
-        join_kernel,
-        grid_spec=pltpu.PrefetchScalarGridSpec(
-            num_scalar_prefetch=1, grid=(4,), in_specs=[flat, block, block, block], out_specs=flat
-        ),
-        out_shape=pltpu.HBM(acoustic.shape, jnp.bfloat16),
-        name="join",
-    )(lengths, acoustic, mine, from_core, from_side)
-
-
 def swap(value, axis, size, step):
     return lax.ppermute(value, axis, [(i, i ^ step) for i in range(size)])
 
@@ -354,12 +329,18 @@
     core = lax.axis_index("tensor").astype(jnp.int32)
     side = (here // across)[None]
 
-    langs = language
-    step = across
-    while step != 0:
+    peer = swap(acoustic, "tensor", 2, 1)
+    gains = norm_gain.reshape(2, 1, features)
+    gains = jnp.where(core == 0, gains, gains[::-1])
+    near, own_far = norm_parts(side, acoustic, peer, gains)
+    far = swap(own_far, "dp", dp, across)
+    far = (far, swap(far, "tensor", 2, 1))
+    langs = jnp.concatenate([language, swap(language, "dp", dp, across)])
+    (langs,) = gate([langs], in_hbm([own_far]))
+    step = 1
+    while step != across:
         langs = jnp.concatenate([langs, swap(langs, "dp", dp, step)])
-        step = 1 if step == across else 2 * step
-        step = 0 if step == across else step
+        step = 2 * step
     chooser = (langs[:, None] == jnp.arange(nlangs, dtype=jnp.int32)).astype(jnp.int32)
     wanted_up = jnp.einsum("nl,lhg->nhg", chooser, kept_within(up_keep))
     wanted_down = jnp.einsum("nl,lhg->nhg", chooser, kept_within(down_keep))
@@ -368,12 +349,6 @@
     wanted_up = wanted_up.reshape(2 * across, -1)
     wanted_down = wanted_down.reshape(2 * across, -1)
     place = jnp.stack([(here ^ k) % across for k in members])
-    peer = swap(acoustic, "tensor", 2, 1)
-    gains = norm_gain.reshape(2, 1, features)
-    gains = jnp.where(core == 0, gains, gains[::-1])
-    near, own_far = norm_parts(side, acoustic, peer, gains)
-    far = swap(own_far, "dp", dp, across)
-    far = (far, swap(far, "tensor", 2, 1))
 
     groups = [[start + k for k in members] for start in (0, across)]
 
@@ -418,7 +393,10 @@
     own_peer, active_own = down(other_core, kept[0] + crossed[0], own_down, 0, jnp.bfloat16)
     from_core = swap(own_peer, "tensor", 2, 1)
     (own_mine,) = down(this_core, [active_own], own_down, 0, jnp.float32)
-    return join(lengths, acoustic, own_mine, from_core, from_side)
+    feedfwd = own_mine + from_core.astype(jnp.float32) + from_side.astype(jnp.float32)
+    feedfwd = feedfwd.transpose(1, 0, 2).reshape(frames, features)
+    valid = jnp.arange(frames, dtype=jnp.int32)[:, None] < lengths[0]
+    return jnp.where(valid, acoustic.astype(jnp.float32) + feedfwd, 0.0).astype(jnp.bfloat16)
 
 
 def exchange_body(acoustic, norm_gain, up_weight, down_weight, up_keep, down_keep, language, lengths):

time: 211 us -> 208 us (0.986)
  waiting for transfers between devices: 102 us -> 95.1 us
  starting transfers between devices: 32.6 us -> 38.3 us
  Pallas kernels: 55 us -> 51.5 us
  other arithmetic: 6.65 us -> 10.1 us
  local copies, waits for them, and re-layouts: 11.6 us -> 9.28 us
    ppermute x19, starting transfers between devices: 20.4 us -> 29.7 us  [swap(): return lax.ppermute(value, axis, [(i, i ^ step) for i in range(size)])]
    ppermute x19, waiting for transfers between devices: 94.5 us -> 85.6 us  [swap(): return lax.ppermute(value, axis, [(i, i ^ step) for i in range(size)])]
    pallas_call x1 -> x0, Pallas kernels: 4.03 us -> none  [join(): pl.pallas_call(join_kernel, grid_spec=pltpu.PrefetchScalarGridSpec(num_sc...]
    all_to_all x2, starting transfers between devices: 12.2 us -> 8.64 us  [in_order(): lax.all_to_all(blocks, 'dp', split_axis=0, concat_axis=0, axis_index_grou...]
    convert_element_type x0 -> x1, other arithmetic: none -> 2.74 us  [split_body(): jnp.where(valid, acoustic.astype(jnp.float32) + feedfwd, 0.0)]
    unnamed x52 -> x50, local copies, waits for them, and re-layouts: 10.8 us -> 8.49 us
  transfers between devices with their start and end apart: 21 -> 21, of which waited for: 13 -> 13; matrix products, arithmetic and copies ran while one was open for 4% -> 4% of each run, Pallas kernels for 22% -> 23%
where the time goes in v7:
time: 208 us; the launch traced here: 207 us
  waiting for transfers between devices  95.1 us (46%)
  Pallas kernels  51.5 us (25%)
  starting transfers between devices  38.3 us (18%)
  other arithmetic  10.1 us (5%)
  local copies, waits for them, and re-layouts  9.28 us (4%)
    ppermute x19, waiting for transfers between devices, swap(): return lax.ppermute(value, axis, [(i, i ^ step) for i in range(size)])  85.6 us
    ppermute x19, starting transfers between devices, swap(): return lax.ppermute(value, axis, [(i, i ^ step) for i in range(size)])  29.7 us
    pallas_call x4, Pallas kernels, down_project(): pl.pallas_call(functools.partial(down_kernel, utt=utt, parts=parts, runs=...  22.3 us
    pallas_call x3, Pallas kernels, pick_blocks(): pl.pallas_call(functools.partial(pick_kernel, rows=rows, runs=runs, base=...  15.5 us
    all_to_all x2, waiting for transfers between devices, in_order(): lax.all_to_all(blocks, 'dp', split_axis=0, concat_axis=0, axis_index_grou...  9.52 us
    all_to_all x2, starting transfers between devices, in_order(): lax.all_to_all(blocks, 'dp', split_axis=0, concat_axis=0, axis_index_grou...  8.64 us
    unnamed x50, local copies, waits for them, and re-layouts  8.49 us
    pallas_call x2, Pallas kernels, up_project(): pl.pallas_call(functools.partial(up_kernel, runs=runs, rows=rows), grid_s...  7.91 us
  transfers between devices with their start and end apart: 21, of which 13 were waited for; matrix products, arithmetic and copies ran while one was open for 4% of the time, Pallas kernels for 23%

profile of v7, /device:TPU:0, one launch (start us, length us, event | category | flops | bytes accessed | tf_op | source)
XLA Modules:
  0.0 206.5 jit_solution(9087105623798974298)
XLA Ops:
  0.0 4.0 %collective-permute-start = (s32[1]{0:T(128)}, s32[1]{0:T(128)}, u32[]{:S(2)}, u32[]{:S(2)}) collective-permute-start(s32[1]{0:T(128)} %param.14), channel_id=1, source_target_pairs={{0,8},{2,10},{4,12},{6,14},{8,0},{10,2},{12,4},{14,6},{1,9},{3,11}... | collective-permute-start | bytes 20 | tf_op jit(solution)/shard_map/ppermute | solution.py:315
  4.8 1.2 fusion.2
  6.1 1.4 broadcast_select_fusion.gain_ref
  7.5 1.3 pad_add_fusion.refs_0_
  8.8 0.9 copy-done.21
  9.6 3.7 %norm_parts.1 = (bf16[32,192,128]{2,1,0:T(8,128)(2,1)}, bf16[8,192,128]{2,1,0:T(8,128)(2,1)}) custom-call(s32[1]{0:T(128)} %bitcast.1.side, bf16[192,2048]{1,0:T(8,128)(2,1)} %own_ref.1, bf16[192,2048]{1,0:T(8,128)(2,1)} %copy-done.21, f32[2,1,2048]{2,1,0:T(1,128)} %broadcast_select_fusion.gain_ref), custom_call_target="tpu_custom_call" | custom-call | tf_op jit(solution)/shard_map/norm_parts/pallas_call | solution.py:69
  13.3 1.1 collective-permute-start.4
  14.4 0.7 gate.3
  15.1 1.5 collective-permute-start.2
  16.6 2.1 %collective-permute-done.2 = s32[2]{0:T(128)S(1)} collective-permute-done((s32[2]{0:T(128)}, s32[2]{0:T(128)S(1)}, u32[]{:S(2)}, u32[]{:S(2)}) %collective-permute-start.2) | collective-permute-done | bytes 40 | tf_op jit(solution)/shard_map/ppermute | solution.py:315
  18.7 0.7 pad_add_fusion.1
  19.4 1.6 collective-permute-start.3
  21.0 2.0 collective-permute-done.3
  23.0 0.7 pad_add_fusion.2
  23.7 0.3 fusion.4
  24.0 0.1 copy.39
  24.1 4.4 %pick_up.2 = (bf16[2,16,4,16,128]{4,3,2,1,0:T(8,128)(2,1)}, bf16[2,16,4,16,128]{4,3,2,1,0:T(8,128)(2,1)}, bf16[2,16,4,16,128]{4,3,2,1,0:T(8,128)(2,1)}, bf16[2,16,4,16,128]{4,3,2,1,0:T(8,128)(2,1)}) custom-call(s32[4]{0:T(128)S(1)} %pad_add_fusion.3.place, s32[8,128]{1,0:T(8,128)S(1)} %copy.40.wanted, bf16[32,32,2048]{2,1,0:T(8,128)(2,1)} %weight_ref.4, ...), custom_call_target="tpu_custom_call" | custom-call | tf_op jit(solution)/shard_map/pick_up/pallas_call | solution.py:123
  28.5 1.5 collective-permute-start.6
  30.1 2.4 %collective-permute-start.7 = (bf16[2,16,4,16,128]{4,3,2,1,0:T(8,128)(2,1)}, bf16[2,16,4,16,128]{4,3,2,1,0:T(8,128)(2,1)S(1)}, u32[]{:S(2)}, u32[]{:S(2)}) collective-permute-start(bf16[2,16,4,16,128]{4,3,2,1,0:T(8,128)(2,1)} %get-tuple-element.33), channel_id=1, source_target_pairs={{0,4},{2,6},{4,0},{6,2},{8,12},{10,14},{12,8},{14,10},{1,5},{3,7},... | collective-permute-start | bytes 1572872 | tf_op jit(solution)/shard_map/ppermute | solution.py:315
  32.4 2.0 collective-permute-done.4.far_a_ref.refs_1_
  34.6 0.1 reshape.35
  34.7 4.5 %pick_up.3 = (bf16[2,16,4,16,128]{4,3,2,1,0:T(8,128)(2,1)}, bf16[2,16,4,16,128]{4,3,2,1,0:T(8,128)(2,1)}, bf16[2,16,4,16,128]{4,3,2,1,0:T(8,128)(2,1)}, bf16[2,16,4,16,128]{4,3,2,1,0:T(8,128)(2,1)}) custom-call(s32[4]{0:T(128)S(1)} %pad_add_fusion.3.place, s32[8,128]{1,0:T(8,128)S(1)} %copy.40.wanted, bf16[32,32,2048]{2,1,0:T(8,128)(2,1)} %weight_ref.4, ...), custom_call_target="tpu_custom_call" | custom-call | tf_op jit(solution)/shard_map/pick_up/pallas_call | solution.py:123
  39.2 1.5 collective-permute-start.9
  40.7 0.6 collective-permute-done.6.refs_1_
  41.3 6.0 %collective-permute-start.10 = (bf16[2,16,4,16,128]{4,3,2,1,0:T(8,128)(2,1)}, bf16[2,16,4,16,128]{4,3,2,1,0:T(8,128)(2,1)S(1)}, u32[]{:S(2)}, u32[]{:S(2)}) collective-permute-start(bf16[2,16,4,16,128]{4,3,2,1,0:T(8,128)(2,1)} %get-tuple-element.38), channel_id=1, source_target_pairs={{0,4},{2,6},{4,0},{6,2},{8,12},{10,14},{12,8},{14,10},{1,5},{3,7},... | collective-permute-start | bytes 1572872 | tf_op jit(solution)/shard_map/ppermute | solution.py:315
  47.4 1.0 collective-permute-start.11
  48.5 9.5 %collective-permute-done.8.refs_3_ = bf16[2,16,4,16,128]{4,3,2,1,0:T(8,128)(2,1)} collective-permute-done((bf16[2,16,4,16,128]{4,3,2,1,0:T(8,128)(2,1)}, bf16[2,16,4,16,128]{4,3,2,1,0:T(8,128)(2,1)}, u32[]{:S(2)}, u32[]{:S(2)}) %collective-permute-start.8) | collective-permute-done | bytes 524320 | tf_op jit(solution)/shard_map/ppermute | solution.py:315
  58.0 4.4 %up_project.2 = (f32[8,192,128]{2,1,0:T(8,128)}, f32[8,192,128]{2,1,0:T(8,128)}, bf16[8,192,128]{2,1,0:T(8,128)(2,1)}, bf16[8,192,128]{2,1,0:T(8,128)(2,1)}) custom-call(s32[1]{0:T(128)} %bitcast.1.side, s32[4]{0:T(128)S(1)} %pad_add_fusion.3.place, s32[2,64]{1,0:T(2,128)S(1)} %get-tuple-element.54.slots, bf16[32,192,128]{2,1,0:T(8,128)(2,1)S(1)} %copy-done.2, ...), custom_call_target="tpu_custom_call" | custom-call | tf_op jit(solution)/shard_map/up_project/pallas_call | solution.py:203
  62.4 3.0 %collective-permute-start.14 = (bf16[8,192,128]{2,1,0:T(8,128)(2,1)}, bf16[8,192,128]{2,1,0:T(8,128)(2,1)S(1)}, u32[]{:S(2)}, u32[]{:S(2)}) collective-permute-start(bf16[8,192,128]{2,1,0:T(8,128)(2,1)} %get-tuple-element.45), channel_id=1, source_target_pairs={{0,8},{2,10},{4,12},{6,14},{8,0},{10,2},{12,4},{14,6},{1,9},{3,11}... | collective-permute-start | bytes 1179656 | tf_op jit(solution)/shard_map/ppermute | solution.py:315
  65.4 0.2 fusion.3
  65.6 0.3 fusion.6
  65.9 0.1 copy.42
  66.0 6.6 %pick_down.1 = (bf16[4,32,4,16,128]{4,3,2,1,0:T(8,128)(2,1)}, bf16[4,32,4,16,128]{4,3,2,1,0:T(8,128)(2,1)}) custom-call(s32[4]{0:T(128)S(1)} %pad_add_fusion.3.place, s32[8,128]{1,0:T(8,128)S(1)} %copy.43.wanted, bf16[32,32,2048]{2,1,0:T(8,128)(2,1)} %weight_ref.5, f32[8,192,128]{2,1,0:T(8,128)} %get-tuple-element.35.refs_0_), custom_call_target="tpu_custom_call" | custom-call | tf_op jit(solution)/shard_map/pick_down/pallas_call | solution.py:123
  72.7 3.9 %collective-permute-done.10.refs_2_.refs_3_ = bf16[2,16,4,16,128]{4,3,2,1,0:T(8,128)(2,1)S(1)} collective-permute-done((bf16[2,16,4,16,128]{4,3,2,1,0:T(8,128)(2,1)}, bf16[2,16,4,16,128]{4,3,2,1,0:T(8,128)(2,1)S(1)}, u32[]{:S(2)}, u32[]{:S(2)}) %collective-permute-start.10) | collective-permute-done | bytes 524320 | tf_op jit(solution)/shard_map/ppermute | solution.py:315
  76.6 12.1 %collective-permute-done.11.refs_3_.refs_4_ = bf16[2,16,4,16,128]{4,3,2,1,0:T(8,128)(2,1)S(1)} collective-permute-done((bf16[2,16,4,16,128]{4,3,2,1,0:T(8,128)(2,1)}, bf16[2,16,4,16,128]{4,3,2,1,0:T(8,128)(2,1)S(1)}, u32[]{:S(2)}, u32[]{:S(2)}) %collective-permute-start.11) | collective-permute-done | bytes 524320 | tf_op jit(solution)/shard_map/ppermute | solution.py:315
  88.7 0.8 copy-done.8
  89.5 0.1 copy-done.13
  89.6 0.7 gate.4
  90.3 3.7 %all-to-all-start = ((bf16[4,32,4,16,128]{4,3,2,1,0:T(8,128)(2,1)}), bf16[4,32,4,16,128]{4,3,2,1,0:T(8,128)(2,1)S(1)}, u32[]{:S(2)}, u32[]{:S(2)}) async-start(bf16[4,32,4,16,128]{4,3,2,1,0:T(8,128)(2,1)} %gate.4), calls=%async_computation | async-start | bytes 4194304 | tf_op jit(solution)/shard_map/all_to_all | solution.py:359
  94.2 1.4 copy-done.3
  95.6 1.0 copy-done.9
  96.6 1.0 copy-done.18
  97.6 1.0 copy-done.19
  98.7 3.6 %up_project.3 = (f32[8,192,128]{2,1,0:T(8,128)}, f32[8,192,128]{2,1,0:T(8,128)}, bf16[8,192,128]{2,1,0:T(8,128)(2,1)}, bf16[8,192,128]{2,1,0:T(8,128)(2,1)}) custom-call(s32[1]{0:T(128)} %bitcast.1.side, s32[4]{0:T(128)S(1)} %pad_add_fusion.3.place, s32[2,64]{1,0:T(2,128)S(1)} %get-tuple-element.53.slots, bf16[32,192,128]{2,1,0:T(8,128)(2,1)S(1)} %copy-done.3, ...), custom_call_target="tpu_custom_call" | custom-call | tf_op jit(solution)/shard_map/up_project/pallas_call | solution.py:203
  102.2 2.9 %collective-permute-start.15 = (bf16[8,192,128]{2,1,0:T(8,128)(2,1)}, bf16[8,192,128]{2,1,0:T(8,128)(2,1)S(1)}, u32[]{:S(2)}, u32[]{:S(2)}) collective-permute-start(bf16[8,192,128]{2,1,0:T(8,128)(2,1)} %get-tuple-element.46), channel_id=1, source_target_pairs={{0,8},{2,10},{4,12},{6,14},{8,0},{10,2},{12,4},{14,6},{1,9},{3,11}... | collective-permute-start | bytes 1179656 | tf_op jit(solution)/shard_map/ppermute | solution.py:315
  105.1 21.2 %collective-permute-done.12.refs_3_.refs_2_ = bf16[8,192,128]{2,1,0:T(8,128)(2,1)S(1)} collective-permute-done((bf16[8,192,128]{2,1,0:T(8,128)(2,1)}, bf16[8,192,128]{2,1,0:T(8,128)(2,1)S(1)}, u32[]{:S(2)}, u32[]{:S(2)}) %collective-permute-start.12) | collective-permute-done | bytes 393248 | tf_op jit(solution)/shard_map/ppermute | solution.py:315
  126.4 0.8 copy-done.11
  127.1 7.0 %collective-permute-done.15.refs_2_.refs_3_ = bf16[8,192,128]{2,1,0:T(8,128)(2,1)S(1)} collective-permute-done((bf16[8,192,128]{2,1,0:T(8,128)(2,1)}, bf16[8,192,128]{2,1,0:T(8,128)(2,1)S(1)}, u32[]{:S(2)}, u32[]{:S(2)}) %collective-permute-start.15) | collective-permute-done | bytes 393248 | tf_op jit(solution)/shard_map/ppermute | solution.py:315
  134.2 2.1 all-to-all-done.refs_1_.refs_4_
  136.2 1.4 copy-done
  137.6 0.7 gate.5
  138.3 4.9 %all-to-all-start.1 = ((bf16[4,32,4,16,128]{4,3,2,1,0:T(8,128)(2,1)}), bf16[4,32,4,16,128]{4,3,2,1,0:T(8,128)(2,1)}, u32[]{:S(2)}, u32[]{:S(2)}) async-start(bf16[4,32,4,16,128]{4,3,2,1,0:T(8,128)(2,1)} %gate.5), calls=%async_computation.1 | async-start | bytes 4194304 | tf_op jit(solution)/shard_map/all_to_all | solution.py:359
  143.3 0.1 slice.16.wanted
  143.4 5.7 %down_1.2 = (bf16[16,192,128]{2,1,0:T(8,128)(2,1)}, bf16[16,192,128]{2,1,0:T(8,128)(2,1)}) custom-call(s32[1]{0:T(128)} %bitcast.1.side, s32[1]{0:T(128)} %bitcast.6.which, s32[2,128]{1,0:T(2,128)S(1)} %slice.16.wanted, f32[8,192,128]{2,1,0:T(8,128)} %get-tuple-element.49.refs_0_, f32[8,192,128]{2,1,0:T(8,128)} %get-tuple-element.50.refs_1_, ...), custom_call_target="tpu_custom_call" | custom-call | tf_op jit(solution)/shard_map/down_1/pallas_call | solution.py:293
  149.2 1.4 collective-permute-start.13
  150.6 5.2 %down_1.3 = f32[16,192,128]{2,1,0:T(8,128)} custom-call(s32[1]{0:T(128)} %bitcast.1.side, s32[1]{0:T(128)} %bitcast.2.which, s32[2,128]{1,0:T(2,128)S(1)} %slice.16.wanted, bf16[16,192,128]{2,1,0:T(8,128)(2,1)} %get-tuple-element.51.refs_0_, bf16[4,32,4,16,128]{4,3,2,1,0:T(8,128)(2,1)S(1)} %copy-done.1), custom_call_target="tpu_custom_call" | custom-call | tf_op jit(solution)/shard_map/down_1/pallas_call | solution.py:293
  155.8 1.7 add_convert_fusion
  157.5 1.7 collective-permute-start.18
  159.1 16.4 %collective-permute-done.13.refs_3_ = bf16[8,192,128]{2,1,0:T(8,128)(2,1)S(1)} collective-permute-done((bf16[8,192,128]{2,1,0:T(8,128)(2,1)S(1)}, bf16[8,192,128]{2,1,0:T(8,128)(2,1)S(1)}, u32[]{:S(2)}, u32[]{:S(2)}) %collective-permute-start.13) | collective-permute-done | bytes 393248 | tf_op jit(solution)/shard_map/ppermute | solution.py:315
  175.5 7.5 %all-to-all-done.1.refs_4_.refs_1_ = bf16[4,32,4,16,128]{4,3,2,1,0:T(8,128)(2,1)} async-done(((bf16[4,32,4,16,128]{4,3,2,1,0:T(8,128)(2,1)}), bf16[4,32,4,16,128]{4,3,2,1,0:T(8,128)(2,1)}, u32[]{:S(2)}, u32[]{:S(2)}) %all-to-all-start.1) | async-done | bytes 2097184 | tf_op jit(solution)/shard_map/all_to_all | solution.py:359
  183.0 5.9 %down_0.2 = (bf16[16,192,128]{2,1,0:T(8,128)(2,1)}, bf16[16,192,128]{2,1,0:T(8,128)(2,1)}) custom-call(s32[1]{0:T(128)} %bitcast.1.side, s32[1]{0:T(128)} %bitcast.6.which, s32[2,128]{1,0:T(2,128)S(1)} %slice.16.wanted, f32[8,192,128]{2,1,0:T(8,128)} %get-tuple-element.35.refs_0_, f32[8,192,128]{2,1,0:T(8,128)} %get-tuple-element.40.refs_1_, ...), custom_call_target="tpu_custom_call" | custom-call | tf_op jit(solution)/shard_map/down_0/pallas_call | solution.py:293
  189.6 5.5 %down_0.3 = f32[16,192,128]{2,1,0:T(8,128)} custom-call(s32[1]{0:T(128)} %bitcast.1.side, s32[1]{0:T(128)} %bitcast.2.which, s32[2,128]{1,0:T(2,128)S(1)} %slice.16.wanted, bf16[16,192,128]{2,1,0:T(8,128)(2,1)} %get-tuple-element.47.refs_0_, bf16[4,32,4,16,128]{4,3,2,1,0:T(8,128)(2,1)} %all-to-all-done.1.refs_4_.refs_1_), custom_call_target="tpu_custom_call" | custom-call | tf_op jit(solution)/shard_map/down_0/pallas_call | solution.py:293
  195.0 8.7 %collective-permute-done.18 = bf16[16,192,128]{2,1,0:T(8,128)(2,1)S(1)} collective-permute-done((bf16[16,192,128]{2,1,0:T(8,128)(2,1)S(1)}, bf16[16,192,128]{2,1,0:T(8,128)(2,1)S(1)}, u32[]{:S(2)}, u32[]{:S(2)}) %collective-permute-start.18) | collective-permute-done | bytes 786464 | tf_op jit(solution)/shard_map/ppermute | solution.py:315
  203.8 2.7 %fusion.1 = bf16[192,2048]{1,0:T(8,128)(2,1)} fusion(bf16[192,2048]{1,0:T(8,128)(2,1)S(1)} %copy-done.20, pred[192]{0:T(512)(128)(4,1)S(1)} %iota_compare_fusion.1, bf16[16,192,128]{2,1,0:T(8,128)(2,1)S(1)} %collective-permute-done.18, f32[16,192,128]{2,1,0:T(8,128)} %down_0.3, bf16[16,192,128]{2,1,0:T(8,128)(2,1)S(1)} %collective-permute-done.16), kind=kLoop, calls=%fused_computation.2 | loop fusion | flops 3145728 | bytes 4718784 | tf_op jit(solution)/shard_map/convert_element_type | solution.py:399
  (67 shorter events, 0.7 us)
Async XLA Ops:
  0.0 7.5 %collective-permute-start = (s32[1]{0:T(128)}, s32[1]{0:T(128)}, u32[]{:S(2)}, u32[]{:S(2)}) collective-permute-start(s32[1]{0:T(128)} %param.14), channel_id=1, source_target_pairs={{0,8},{2,10},{4,12},{6,14},{8,0},{10,2},{12,4},{14,6},{1,9},{3,11}... | collective-permute-start | bytes 20 | tf_op jit(solution)/shard_map/ppermute | solution.py:315
  4.0 4.7 %collective-permute-start.1 = (bf16[192,2048]{1,0:T(8,128)(2,1)}, bf16[192,2048]{1,0:T(8,128)(2,1)S(1)}, u32[]{:S(2)}, u32[]{:S(2)}) collective-permute-start(bf16[192,2048]{1,0:T(8,128)(2,1)} %own_ref.1), channel_id=1, source_target_pairs={{0,1},{1,0},{2,3},{3,2},{4,5},{5,4},{6,7},{7,6},{8,9},{9,8},{10,11... | collective-permute-start | bytes 2359304 | tf_op jit(solution)/shard_map/ppermute | solution.py:315
  8.8 0.9 copy-start.21
  13.3 21.1 %collective-permute-start.4 = (bf16[8,192,128]{2,1,0:T(8,128)(2,1)}, bf16[8,192,128]{2,1,0:T(8,128)(2,1)S(1)}, u32[]{:S(2)}, u32[]{:S(2)}) collective-permute-start(bf16[8,192,128]{2,1,0:T(8,128)(2,1)} %get-tuple-element.29.refs_1_.refs_0_), channel_id=1, source_target_pairs={{0,8},{2,10},{4,12},{6,14},{8,0},{10,2},{12,4},{14,6},{1,9},{3,11}... | collective-permute-start | bytes 1179656 | tf_op jit(solution)/shard_map/ppermute | solution.py:315
  15.1 3.6 %collective-permute-start.2 = (s32[2]{0:T(128)}, s32[2]{0:T(128)S(1)}, u32[]{:S(2)}, u32[]{:S(2)}) collective-permute-start(s32[2]{0:T(128)} %gate.3), channel_id=1, source_target_pairs={{0,2},{2,0},{4,6},{6,4},{8,10},{10,8},{12,14},{14,12},{1,3},{3,1},... | collective-permute-start | bytes 32 | tf_op jit(solution)/shard_map/ppermute | solution.py:315
  19.4 3.5 %collective-permute-start.3 = (s32[4]{0:T(128)S(1)}, s32[4]{0:T(128)S(1)}, u32[]{:S(2)}, u32[]{:S(2)}) collective-permute-start(s32[4]{0:T(128)S(1)} %pad_add_fusion.1), channel_id=1, source_target_pairs={{0,4},{2,6},{4,0},{6,2},{8,12},{10,14},{12,8},{14,10},{1,5},{3,7},... | collective-permute-start | bytes 56 | tf_op jit(solution)/shard_map/ppermute | solution.py:315
  28.5 12.8 %collective-permute-start.6 = (bf16[2,16,4,16,128]{4,3,2,1,0:T(8,128)(2,1)}, bf16[2,16,4,16,128]{4,3,2,1,0:T(8,128)(2,1)S(1)}, u32[]{:S(2)}, u32[]{:S(2)}) collective-permute-start(bf16[2,16,4,16,128]{4,3,2,1,0:T(8,128)(2,1)} %get-tuple-element.32), channel_id=1, source_target_pairs={{0,2},{2,0},{4,6},{6,4},{8,10},{10,8},{12,14},{14,12},{1,3},{3,1},... | collective-permute-start | bytes 1572872 | tf_op jit(solution)/shard_map/ppermute | solution.py:315
  30.1 17.3 %collective-permute-start.7 = (bf16[2,16,4,16,128]{4,3,2,1,0:T(8,128)(2,1)}, bf16[2,16,4,16,128]{4,3,2,1,0:T(8,128)(2,1)S(1)}, u32[]{:S(2)}, u32[]{:S(2)}) collective-permute-start(bf16[2,16,4,16,128]{4,3,2,1,0:T(8,128)(2,1)} %get-tuple-element.33), channel_id=1, source_target_pairs={{0,4},{2,6},{4,0},{6,2},{8,12},{10,14},{12,8},{14,10},{1,5},{3,7},... | collective-permute-start | bytes 1572872 | tf_op jit(solution)/shard_map/ppermute | solution.py:315
  32.4 25.5 %collective-permute-start.8 = (bf16[2,16,4,16,128]{4,3,2,1,0:T(8,128)(2,1)}, bf16[2,16,4,16,128]{4,3,2,1,0:T(8,128)(2,1)}, u32[]{:S(2)}, u32[]{:S(2)}) collective-permute-start(bf16[2,16,4,16,128]{4,3,2,1,0:T(8,128)(2,1)} %get-tuple-element.34), channel_id=1, source_target_pairs={{0,6},{2,4},{4,2},{6,0},{8,14},{10,12},{12,10},{14,8},{1,7},{3,5},... | collective-permute-start | bytes 1572872 | tf_op jit(solution)/shard_map/ppermute | solution.py:315
  34.4 23.5 %collective-permute-start.5 = (bf16[8,192,128]{2,1,0:T(8,128)(2,1)S(1)}, bf16[8,192,128]{2,1,0:T(8,128)(2,1)S(1)}, u32[]{:S(2)}, u32[]{:S(2)}) collective-permute-start(bf16[8,192,128]{2,1,0:T(8,128)(2,1)S(1)} %collective-permute-done.4.far_a_ref.refs_1_), channel_id=1, source_target_pairs={{0,1},{1,0},{2,3},{3,2},{4,5},{5,4},{6,7},{7,6},{8,9},{9,8},{10,11... | collective-permute-start | bytes 1179656 | tf_op jit(solution)/shard_map/ppermute | solution.py:315
  34.7 23.3 %copy-start.2 = (bf16[32,192,128]{2,1,0:T(8,128)(2,1)S(1)}, bf16[32,192,128]{2,1,0:T(8,128)(2,1)}, u32[]{:S(2)}) copy-start(bf16[32,192,128]{2,1,0:T(8,128)(2,1)} %get-tuple-element.30.own_ref) | copy-start | bytes 4718596
  34.7 23.3 %copy-start.10 = (bf16[2,16,4,16,128]{4,3,2,1,0:T(8,128)(2,1)S(1)}, bf16[2,16,4,16,128]{4,3,2,1,0:T(8,128)(2,1)}, u32[]{:S(2)}) copy-start(bf16[2,16,4,16,128]{4,3,2,1,0:T(8,128)(2,1)} %get-tuple-element.31.refs_0_) | copy-start | bytes 1572868
  39.2 33.4 %collective-permute-start.9 = (bf16[2,16,4,16,128]{4,3,2,1,0:T(8,128)(2,1)}, bf16[2,16,4,16,128]{4,3,2,1,0:T(8,128)(2,1)S(1)}, u32[]{:S(2)}, u32[]{:S(2)}) collective-permute-start(bf16[2,16,4,16,128]{4,3,2,1,0:T(8,128)(2,1)} %get-tuple-element.37), channel_id=1, source_target_pairs={{0,2},{2,0},{4,6},{6,4},{8,10},{10,8},{12,14},{14,12},{1,3},{3,1},... | collective-permute-start | bytes 1572872 | tf_op jit(solution)/shard_map/ppermute | solution.py:315
  41.3 35.3 %collective-permute-start.10 = (bf16[2,16,4,16,128]{4,3,2,1,0:T(8,128)(2,1)}, bf16[2,16,4,16,128]{4,3,2,1,0:T(8,128)(2,1)S(1)}, u32[]{:S(2)}, u32[]{:S(2)}) collective-permute-start(bf16[2,16,4,16,128]{4,3,2,1,0:T(8,128)(2,1)} %get-tuple-element.38), channel_id=1, source_target_pairs={{0,4},{2,6},{4,0},{6,2},{8,12},{10,14},{12,8},{14,10},{1,5},{3,7},... | collective-permute-start | bytes 1572872 | tf_op jit(solution)/shard_map/ppermute | solution.py:315
  47.4 41.3 %collective-permute-start.11 = (bf16[2,16,4,16,128]{4,3,2,1,0:T(8,128)(2,1)}, bf16[2,16,4,16,128]{4,3,2,1,0:T(8,128)(2,1)S(1)}, u32[]{:S(2)}, u32[]{:S(2)}) collective-permute-start(bf16[2,16,4,16,128]{4,3,2,1,0:T(8,128)(2,1)} %get-tuple-element.39), channel_id=1, source_target_pairs={{0,6},{2,4},{4,2},{6,0},{8,14},{10,12},{12,10},{14,8},{1,7},{3,5},... | collective-permute-start | bytes 1572872 | tf_op jit(solution)/shard_map/ppermute | solution.py:315
  58.0 4.4 %copy-start.17 = (bf16[8,192,128]{2,1,0:T(8,128)(2,1)}, bf16[8,192,128]{2,1,0:T(8,128)(2,1)S(1)}, u32[]{:S(2)}) copy-start(bf16[8,192,128]{2,1,0:T(8,128)(2,1)S(1)} %collective-permute-done.5.far_b_ref) | copy-start | bytes 1179652
  58.0 7.4 %copy-start.22 = (s32[64,32,32]{0,2,1:T(8,128)S(1)}, s32[64,32,32]{0,2,1:T(8,128)}, u32[]{:S(2)}) copy-start(s32[64,32,32]{0,2,1:T(8,128)} %param.13) | copy-start | bytes 786436
  62.4 26.3 %collective-permute-start.14 = (bf16[8,192,128]{2,1,0:T(8,128)(2,1)}, bf16[8,192,128]{2,1,0:T(8,128)(2,1)S(1)}, u32[]{:S(2)}, u32[]{:S(2)}) collective-permute-start(bf16[8,192,128]{2,1,0:T(8,128)(2,1)} %get-tuple-element.45), channel_id=1, source_target_pairs={{0,8},{2,10},{4,12},{6,14},{8,0},{10,2},{12,4},{14,6},{1,9},{3,11}... | collective-permute-start | bytes 1179656 | tf_op jit(solution)/shard_map/ppermute | solution.py:315
  65.9 22.8 %copy-start.23 = (s32[8,32,4]{1,0,2:T(8,128)}, s32[8,32,4]{1,0,2:T(8,128)S(1)}, u32[]{:S(2)}) copy-start(s32[8,32,4]{1,0,2:T(8,128)S(1)} %fusion.6) | copy-start | bytes 12292
  72.6 16.0 %copy-start.4 = (bf16[2,16,4,16,128]{4,3,2,1,0:T(8,128)(2,1)}, bf16[2,16,4,16,128]{4,3,2,1,0:T(8,128)(2,1)S(1)}, u32[]{:S(2)}) copy-start(bf16[2,16,4,16,128]{4,3,2,1,0:T(8,128)(2,1)S(1)} %collective-permute-done.9.refs_1_.refs_2_) | copy-start | bytes 1572868
  76.6 12.1 %copy-start.6 = (bf16[2,16,4,16,128]{4,3,2,1,0:T(8,128)(2,1)}, bf16[2,16,4,16,128]{4,3,2,1,0:T(8,128)(2,1)S(1)}, u32[]{:S(2)}) copy-start(bf16[2,16,4,16,128]{4,3,2,1,0:T(8,128)(2,1)S(1)} %collective-permute-done.10.refs_2_.refs_3_) | copy-start | bytes 1572868
  88.7 0.8 copy-start.8
  88.7 1.0 copy-start.13
  90.3 3.8 %copy-start.5 = (bf16[2,16,4,16,128]{4,3,2,1,0:T(8,128)(2,1)S(1)}, bf16[2,16,4,16,128]{4,3,2,1,0:T(8,128)(2,1)}, u32[]{:S(2)}) copy-start(bf16[2,16,4,16,128]{4,3,2,1,0:T(8,128)(2,1)} %copy-done.4) | copy-start | bytes 1572868
  90.3 3.8 %copy-start.7 = (bf16[2,16,4,16,128]{4,3,2,1,0:T(8,128)(2,1)S(1)}, bf16[2,16,4,16,128]{4,3,2,1,0:T(8,128)(2,1)}, u32[]{:S(2)}) copy-start(bf16[2,16,4,16,128]{4,3,2,1,0:T(8,128)(2,1)} %copy-done.6) | copy-start | bytes 1572868
  90.3 45.9 %all-to-all-start = ((bf16[4,32,4,16,128]{4,3,2,1,0:T(8,128)(2,1)}), bf16[4,32,4,16,128]{4,3,2,1,0:T(8,128)(2,1)S(1)}, u32[]{:S(2)}, u32[]{:S(2)}) async-start(bf16[4,32,4,16,128]{4,3,2,1,0:T(8,128)(2,1)} %gate.4), calls=%async_computation | async-start | bytes 4194304 | tf_op jit(solution)/shard_map/all_to_all | solution.py:359
  94.1 32.3 %collective-permute-start.12 = (bf16[8,192,128]{2,1,0:T(8,128)(2,1)}, bf16[8,192,128]{2,1,0:T(8,128)(2,1)S(1)}, u32[]{:S(2)}, u32[]{:S(2)}) collective-permute-start(bf16[8,192,128]{2,1,0:T(8,128)(2,1)} %get-tuple-element.41), channel_id=1, source_target_pairs={{0,8},{2,10},{4,12},{6,14},{8,0},{10,2},{12,4},{14,6},{1,9},{3,11}... | collective-permute-start | bytes 1179656 | tf_op jit(solution)/shard_map/ppermute | solution.py:315
  94.2 1.4 copy-start.3
  95.6 1.0 copy-start.9
  96.6 1.0 copy-start.18
  97.6 1.0 copy-start.19
  102.2 31.9 %collective-permute-start.15 = (bf16[8,192,128]{2,1,0:T(8,128)(2,1)}, bf16[8,192,128]{2,1,0:T(8,128)(2,1)S(1)}, u32[]{:S(2)}, u32[]{:S(2)}) collective-permute-start(bf16[8,192,128]{2,1,0:T(8,128)(2,1)} %get-tuple-element.46), channel_id=1, source_target_pairs={{0,8},{2,10},{4,12},{6,14},{8,0},{10,2},{12,4},{14,6},{1,9},{3,11}... | collective-permute-start | bytes 1179656 | tf_op jit(solution)/shard_map/ppermute | solution.py:315
  126.4 0.8 copy-start.11
  134.2 2.1 %copy-start.15 = (bf16[8,192,128]{2,1,0:T(8,128)(2,1)}, bf16[8,192,128]{2,1,0:T(8,128)(2,1)S(1)}, u32[]{:S(2)}) copy-start(bf16[8,192,128]{2,1,0:T(8,128)(2,1)S(1)} %collective-permute-done.15.refs_2_.refs_3_) | copy-start | bytes 1179652
  136.2 1.4 copy-start
  138.3 4.9 %slice-start = ((s32[8,32,4]{1,0,2:T(8,128)}), s32[2,32,4]{1,0,2:T(2,128)S(1)}, s32[]{:S(2)}) async-start(s32[8,32,4]{1,0,2:T(8,128)} %copy-done.23), calls=%async_computation.2 | async-start | bytes 8192 | tf_op jit(solution)/shard_map/slice | solution.py:381
  138.3 5.1 %copy-start.1 = (bf16[4,32,4,16,128]{4,3,2,1,0:T(8,128)(2,1)S(1)}, bf16[4,32,4,16,128]{4,3,2,1,0:T(8,128)(2,1)}, u32[]{:S(2)}) copy-start(bf16[4,32,4,16,128]{4,3,2,1,0:T(8,128)(2,1)} %copy-done) | copy-start | bytes 6291460
  138.3 5.1 %copy-start.14 = (bf16[8,192,128]{2,1,0:T(8,128)(2,1)S(1)}, bf16[8,192,128]{2,1,0:T(8,128)(2,1)}, u32[]{:S(2)}) copy-start(bf16[8,192,128]{2,1,0:T(8,128)(2,1)} %copy-done.13) | copy-start | bytes 1179652
  138.3 5.1 %copy-start.16 = (bf16[8,192,128]{2,1,0:T(8,128)(2,1)S(1)}, bf16[8,192,128]{2,1,0:T(8,128)(2,1)}, u32[]{:S(2)}) copy-start(bf16[8,192,128]{2,1,0:T(8,128)(2,1)} %copy-done.15) | copy-start | bytes 1179652
  138.3 44.7 %all-to-all-start.1 = ((bf16[4,32,4,16,128]{4,3,2,1,0:T(8,128)(2,1)}), bf16[4,32,4,16,128]{4,3,2,1,0:T(8,128)(2,1)}, u32[]{:S(2)}, u32[]{:S(2)}) async-start(bf16[4,32,4,16,128]{4,3,2,1,0:T(8,128)(2,1)} %gate.5), calls=%async_computation.1 | async-start | bytes 4194304 | tf_op jit(solution)/shard_map/all_to_all | solution.py:359
  143.4 5.7 %copy-start.24 = (bf16[8,192,128]{2,1,0:T(8,128)(2,1)S(1)}, bf16[8,192,128]{2,1,0:T(8,128)(2,1)}, u32[]{:S(2)}) copy-start(bf16[8,192,128]{2,1,0:T(8,128)(2,1)} %get-tuple-element.42) | copy-start | bytes 1179652
  149.2 6.6 %collective-permute-start.17 = (bf16[16,192,128]{2,1,0:T(8,128)(2,1)}, bf16[16,192,128]{2,1,0:T(8,128)(2,1)S(1)}, u32[]{:S(2)}, u32[]{:S(2)}) collective-permute-start(bf16[16,192,128]{2,1,0:T(8,128)(2,1)} %get-tuple-element.52), channel_id=1, source_target_pairs={{0,1},{1,0},{2,3},{3,2},{4,5},{5,4},{6,7},{7,6},{8,9},{9,8},{10,11... | collective-permute-start | bytes 2359304 | tf_op jit(solution)/shard_map/ppermute | solution.py:315
  149.2 26.3 %collective-permute-start.13 = (bf16[8,192,128]{2,1,0:T(8,128)(2,1)S(1)}, bf16[8,192,128]{2,1,0:T(8,128)(2,1)S(1)}, u32[]{:S(2)}, u32[]{:S(2)}) collective-permute-start(bf16[8,192,128]{2,1,0:T(8,128)(2,1)S(1)} %copy-done.24), channel_id=1, source_target_pairs={{0,8},{2,10},{4,12},{6,14},{8,0},{10,2},{12,4},{14,6},{1,9},{3,11}... | collective-permute-start | bytes 1179656 | tf_op jit(solution)/shard_map/ppermute | solution.py:315
  155.8 27.2 %copy-start.12 = (bf16[8,192,128]{2,1,0:T(8,128)(2,1)S(1)}, bf16[8,192,128]{2,1,0:T(8,128)(2,1)}, u32[]{:S(2)}) copy-start(bf16[8,192,128]{2,1,0:T(8,128)(2,1)} %copy-done.11) | copy-start | bytes 1179652
  157.5 46.3 %collective-permute-start.18 = (bf16[16,192,128]{2,1,0:T(8,128)(2,1)S(1)}, bf16[16,192,128]{2,1,0:T(8,128)(2,1)S(1)}, u32[]{:S(2)}, u32[]{:S(2)}) collective-permute-start(bf16[16,192,128]{2,1,0:T(8,128)(2,1)S(1)} %add_convert_fusion), channel_id=1, source_target_pairs={{0,8},{2,10},{4,12},{6,14},{8,0},{10,2},{12,4},{14,6},{1,9},{3,11}... | collective-permute-start | bytes 2359304 | tf_op jit(solution)/shard_map/ppermute | solution.py:315
  188.9 14.9 %collective-permute-start.16 = (bf16[16,192,128]{2,1,0:T(8,128)(2,1)}, bf16[16,192,128]{2,1,0:T(8,128)(2,1)S(1)}, u32[]{:S(2)}, u32[]{:S(2)}) collective-permute-start(bf16[16,192,128]{2,1,0:T(8,128)(2,1)} %get-tuple-element.48), channel_id=1, source_target_pairs={{0,1},{1,0},{2,3},{3,2},{4,5},{5,4},{6,7},{7,6},{8,9},{9,8},{10,11... | collective-permute-start | bytes 2359304 | tf_op jit(solution)/shard_map/ppermute | solution.py:315
  189.6 14.2 %copy-start.20 = (bf16[192,2048]{1,0:T(8,128)(2,1)S(1)}, bf16[192,2048]{1,0:T(8,128)(2,1)}, u32[]{:S(2)}) copy-start(bf16[192,2048]{1,0:T(8,128)(2,1)} %own_ref.1) | copy-start | bytes 2359300

commit v8 on v7

--- a/solution.py
+++ b/solution.py
@@ -10,7 +10,7 @@
 BLK = 128
 HALF = BLK // 2
 GROUP = 8
-HSTEP = 8
+HSTEP = 16
 CHUNKS = 2
 
 

time: 208 us -> 207 us (level)
  Pallas kernels: 51.5 us -> 48.4 us
  waiting for transfers between devices: 95.1 us -> 97.6 us
    pallas_call x4, Pallas kernels: 22.3 us -> 19.5 us  [down_project(): pl.pallas_call(functools.partial(down_kernel, utt=utt, parts=parts, runs=...]
  transfers between devices with their start and end apart: 21 -> 21, of which waited for: 13 -> 13; matrix products, arithmetic and copies ran while one was open for 4% -> 4% of each run, Pallas kernels for 23% -> 21%
where the time goes in v8:
time: 207 us; the launch traced here: 206 us
  waiting for transfers between devices  97.6 us (47%)
  Pallas kernels  48.4 us (23%)
  starting transfers between devices  38.4 us (19%)
  other arithmetic  10.1 us (5%)
  local copies, waits for them, and re-layouts  9.29 us (4%)
    ppermute x19, waiting for transfers between devices, swap(): return lax.ppermute(value, axis, [(i, i ^ step) for i in range(size)])  87.5 us
    ppermute x19, starting transfers between devices, swap(): return lax.ppermute(value, axis, [(i, i ^ step) for i in range(size)])  29.8 us
    pallas_call x4, Pallas kernels, down_project(): pl.pallas_call(functools.partial(down_kernel, utt=utt, parts=parts, runs=...  19.5 us
    pallas_call x3, Pallas kernels, pick_blocks(): pl.pallas_call(functools.partial(pick_kernel, rows=rows, runs=runs, base=...  15.4 us
    all_to_all x2, waiting for transfers between devices, in_order(): lax.all_to_all(blocks, 'dp', split_axis=0, concat_axis=0, axis_index_grou...  10.1 us
    all_to_all x2, starting transfers between devices, in_order(): lax.all_to_all(blocks, 'dp', split_axis=0, concat_axis=0, axis_index_grou...  8.64 us
    unnamed x50, local copies, waits for them, and re-layouts  8.5 us
    pallas_call x2, Pallas kernels, up_project(): pl.pallas_call(functools.partial(up_kernel, runs=runs, rows=rows), grid_s...  7.74 us
  transfers between devices with their start and end apart: 21, of which 13 were waited for; matrix products, arithmetic and copies ran while one was open for 4% of the time, Pallas kernels for 21%

profile of v8, /device:TPU:0, one launch (start us, length us, event | category | flops | bytes accessed | tf_op | source)
XLA Modules:
  0.0 205.9 jit_solution(4333617422662039449)
XLA Ops:
  0.0 4.0 %collective-permute-start = (s32[1]{0:T(128)}, s32[1]{0:T(128)}, u32[]{:S(2)}, u32[]{:S(2)}) collective-permute-start(s32[1]{0:T(128)} %param.14), channel_id=1, source_target_pairs={{0,8},{2,10},{4,12},{6,14},{8,0},{10,2},{12,4},{14,6},{1,9},{3,11}... | collective-permute-start | bytes 20 | tf_op jit(solution)/shard_map/ppermute | solution.py:315
  4.8 1.2 fusion.2
  6.1 1.4 broadcast_select_fusion.gain_ref
  7.5 1.3 pad_add_fusion.refs_0_
  8.8 0.9 copy-done.21
  9.6 3.7 %norm_parts.1 = (bf16[32,192,128]{2,1,0:T(8,128)(2,1)}, bf16[8,192,128]{2,1,0:T(8,128)(2,1)}) custom-call(s32[1]{0:T(128)} %bitcast.1.side, bf16[192,2048]{1,0:T(8,128)(2,1)} %own_ref.1, bf16[192,2048]{1,0:T(8,128)(2,1)} %copy-done.21, f32[2,1,2048]{2,1,0:T(1,128)} %broadcast_select_fusion.gain_ref), custom_call_target="tpu_custom_call" | custom-call | tf_op jit(solution)/shard_map/norm_parts/pallas_call | solution.py:69
  13.3 1.1 collective-permute-start.4
  14.4 0.7 gate.3
  15.1 1.5 collective-permute-start.2
  16.6 2.1 %collective-permute-done.2 = s32[2]{0:T(128)S(1)} collective-permute-done((s32[2]{0:T(128)}, s32[2]{0:T(128)S(1)}, u32[]{:S(2)}, u32[]{:S(2)}) %collective-permute-start.2) | collective-permute-done | bytes 40 | tf_op jit(solution)/shard_map/ppermute | solution.py:315
  18.7 0.7 pad_add_fusion.1
  19.4 1.6 collective-permute-start.3
  21.0 2.0 collective-permute-done.3
  23.0 0.7 pad_add_fusion.2
  23.7 0.3 fusion.4
  24.0 0.1 copy.39
  24.1 4.5 %pick_up.2 = (bf16[2,16,4,16,128]{4,3,2,1,0:T(8,128)(2,1)}, bf16[2,16,4,16,128]{4,3,2,1,0:T(8,128)(2,1)}, bf16[2,16,4,16,128]{4,3,2,1,0:T(8,128)(2,1)}, bf16[2,16,4,16,128]{4,3,2,1,0:T(8,128)(2,1)}) custom-call(s32[4]{0:T(128)S(1)} %pad_add_fusion.3.place, s32[8,128]{1,0:T(8,128)S(1)} %copy.40.wanted, bf16[32,32,2048]{2,1,0:T(8,128)(2,1)} %weight_ref.4, ...), custom_call_target="tpu_custom_call" | custom-call | tf_op jit(solution)/shard_map/pick_up/pallas_call | solution.py:123
  28.6 1.5 collective-permute-start.6
  30.2 2.4 %collective-permute-start.7 = (bf16[2,16,4,16,128]{4,3,2,1,0:T(8,128)(2,1)}, bf16[2,16,4,16,128]{4,3,2,1,0:T(8,128)(2,1)S(1)}, u32[]{:S(2)}, u32[]{:S(2)}) collective-permute-start(bf16[2,16,4,16,128]{4,3,2,1,0:T(8,128)(2,1)} %get-tuple-element.33), channel_id=1, source_target_pairs={{0,4},{2,6},{4,0},{6,2},{8,12},{10,14},{12,8},{14,10},{1,5},{3,7},... | collective-permute-start | bytes 1572872 | tf_op jit(solution)/shard_map/ppermute | solution.py:315
  32.5 1.9 collective-permute-done.4.far_a_ref.refs_1_
  34.6 0.1 reshape.35
  34.7 4.6 %pick_up.3 = (bf16[2,16,4,16,128]{4,3,2,1,0:T(8,128)(2,1)}, bf16[2,16,4,16,128]{4,3,2,1,0:T(8,128)(2,1)}, bf16[2,16,4,16,128]{4,3,2,1,0:T(8,128)(2,1)}, bf16[2,16,4,16,128]{4,3,2,1,0:T(8,128)(2,1)}) custom-call(s32[4]{0:T(128)S(1)} %pad_add_fusion.3.place, s32[8,128]{1,0:T(8,128)S(1)} %copy.40.wanted, bf16[32,32,2048]{2,1,0:T(8,128)(2,1)} %weight_ref.4, ...), custom_call_target="tpu_custom_call" | custom-call | tf_op jit(solution)/shard_map/pick_up/pallas_call | solution.py:123
  39.3 1.5 collective-permute-start.9
  40.8 0.6 collective-permute-done.6.refs_1_
  41.4 6.0 %collective-permute-start.10 = (bf16[2,16,4,16,128]{4,3,2,1,0:T(8,128)(2,1)}, bf16[2,16,4,16,128]{4,3,2,1,0:T(8,128)(2,1)S(1)}, u32[]{:S(2)}, u32[]{:S(2)}) collective-permute-start(bf16[2,16,4,16,128]{4,3,2,1,0:T(8,128)(2,1)} %get-tuple-element.38), channel_id=1, source_target_pairs={{0,4},{2,6},{4,0},{6,2},{8,12},{10,14},{12,8},{14,10},{1,5},{3,7},... | collective-permute-start | bytes 1572872 | tf_op jit(solution)/shard_map/ppermute | solution.py:315
  47.4 1.0 collective-permute-start.11
  48.5 9.5 %collective-permute-done.8.refs_3_ = bf16[2,16,4,16,128]{4,3,2,1,0:T(8,128)(2,1)} collective-permute-done((bf16[2,16,4,16,128]{4,3,2,1,0:T(8,128)(2,1)}, bf16[2,16,4,16,128]{4,3,2,1,0:T(8,128)(2,1)}, u32[]{:S(2)}, u32[]{:S(2)}) %collective-permute-start.8) | collective-permute-done | bytes 524320 | tf_op jit(solution)/shard_map/ppermute | solution.py:315
  58.0 4.4 %up_project.2 = (f32[8,192,128]{2,1,0:T(8,128)}, f32[8,192,128]{2,1,0:T(8,128)}, bf16[8,192,128]{2,1,0:T(8,128)(2,1)}, bf16[8,192,128]{2,1,0:T(8,128)(2,1)}) custom-call(s32[1]{0:T(128)} %bitcast.1.side, s32[4]{0:T(128)S(1)} %pad_add_fusion.3.place, s32[2,64]{1,0:T(2,128)S(1)} %get-tuple-element.54.slots, bf16[32,192,128]{2,1,0:T(8,128)(2,1)S(1)} %copy-done.2, ...), custom_call_target="tpu_custom_call" | custom-call | tf_op jit(solution)/shard_map/up_project/pallas_call | solution.py:203
  62.4 3.1 %collective-permute-start.14 = (bf16[8,192,128]{2,1,0:T(8,128)(2,1)}, bf16[8,192,128]{2,1,0:T(8,128)(2,1)S(1)}, u32[]{:S(2)}, u32[]{:S(2)}) collective-permute-start(bf16[8,192,128]{2,1,0:T(8,128)(2,1)} %get-tuple-element.45), channel_id=1, source_target_pairs={{0,8},{2,10},{4,12},{6,14},{8,0},{10,2},{12,4},{14,6},{1,9},{3,11}... | collective-permute-start | bytes 1179656 | tf_op jit(solution)/shard_map/ppermute | solution.py:315
  65.5 0.2 fusion.3
  65.7 0.3 fusion.6
  66.2 6.3 %pick_down.1 = (bf16[4,32,4,16,128]{4,3,2,1,0:T(8,128)(2,1)}, bf16[4,32,4,16,128]{4,3,2,1,0:T(8,128)(2,1)}) custom-call(s32[4]{0:T(128)S(1)} %pad_add_fusion.3.place, s32[8,128]{1,0:T(8,128)S(1)} %copy.43.wanted, bf16[32,32,2048]{2,1,0:T(8,128)(2,1)} %weight_ref.5, f32[8,192,128]{2,1,0:T(8,128)} %get-tuple-element.35.refs_0_), custom_call_target="tpu_custom_call" | custom-call | tf_op jit(solution)/shard_map/pick_down/pallas_call | solution.py:123
  72.5 4.1 %collective-permute-done.10.refs_2_.refs_3_ = bf16[2,16,4,16,128]{4,3,2,1,0:T(8,128)(2,1)S(1)} collective-permute-done((bf16[2,16,4,16,128]{4,3,2,1,0:T(8,128)(2,1)}, bf16[2,16,4,16,128]{4,3,2,1,0:T(8,128)(2,1)S(1)}, u32[]{:S(2)}, u32[]{:S(2)}) %collective-permute-start.10) | collective-permute-done | bytes 524320 | tf_op jit(solution)/shard_map/ppermute | solution.py:315
  76.6 12.1 %collective-permute-done.11.refs_3_.refs_4_ = bf16[2,16,4,16,128]{4,3,2,1,0:T(8,128)(2,1)S(1)} collective-permute-done((bf16[2,16,4,16,128]{4,3,2,1,0:T(8,128)(2,1)}, bf16[2,16,4,16,128]{4,3,2,1,0:T(8,128)(2,1)S(1)}, u32[]{:S(2)}, u32[]{:S(2)}) %collective-permute-start.11) | collective-permute-done | bytes 524320 | tf_op jit(solution)/shard_map/ppermute | solution.py:315
  88.7 0.8 copy-done.8
  89.5 0.1 copy-done.13
  89.6 0.7 gate.4
  90.3 3.7 %all-to-all-start = ((bf16[4,32,4,16,128]{4,3,2,1,0:T(8,128)(2,1)}), bf16[4,32,4,16,128]{4,3,2,1,0:T(8,128)(2,1)S(1)}, u32[]{:S(2)}, u32[]{:S(2)}) async-start(bf16[4,32,4,16,128]{4,3,2,1,0:T(8,128)(2,1)} %gate.4), calls=%async_computation | async-start | bytes 4194304 | tf_op jit(solution)/shard_map/all_to_all | solution.py:359
  94.1 0.2 collective-permute-start.12
  94.3 1.4 copy-done.3
  95.7 1.0 copy-done.9
  96.7 1.0 copy-done.18
  97.7 1.0 copy-done.19
  98.7 3.4 %up_project.3 = (f32[8,192,128]{2,1,0:T(8,128)}, f32[8,192,128]{2,1,0:T(8,128)}, bf16[8,192,128]{2,1,0:T(8,128)(2,1)}, bf16[8,192,128]{2,1,0:T(8,128)(2,1)}) custom-call(s32[1]{0:T(128)} %bitcast.1.side, s32[4]{0:T(128)S(1)} %pad_add_fusion.3.place, s32[2,64]{1,0:T(2,128)S(1)} %get-tuple-element.53.slots, bf16[32,192,128]{2,1,0:T(8,128)(2,1)S(1)} %copy-done.3, ...), custom_call_target="tpu_custom_call" | custom-call | tf_op jit(solution)/shard_map/up_project/pallas_call | solution.py:203
  102.1 2.8 %collective-permute-start.15 = (bf16[8,192,128]{2,1,0:T(8,128)(2,1)}, bf16[8,192,128]{2,1,0:T(8,128)(2,1)S(1)}, u32[]{:S(2)}, u32[]{:S(2)}) collective-permute-start(bf16[8,192,128]{2,1,0:T(8,128)(2,1)} %get-tuple-element.46), channel_id=1, source_target_pairs={{0,8},{2,10},{4,12},{6,14},{8,0},{10,2},{12,4},{14,6},{1,9},{3,11}... | collective-permute-start | bytes 1179656 | tf_op jit(solution)/shard_map/ppermute | solution.py:315
  104.9 21.4 %collective-permute-done.12.refs_3_.refs_2_ = bf16[8,192,128]{2,1,0:T(8,128)(2,1)S(1)} collective-permute-done((bf16[8,192,128]{2,1,0:T(8,128)(2,1)}, bf16[8,192,128]{2,1,0:T(8,128)(2,1)S(1)}, u32[]{:S(2)}, u32[]{:S(2)}) %collective-permute-start.12) | collective-permute-done | bytes 393248 | tf_op jit(solution)/shard_map/ppermute | solution.py:315
  126.4 0.8 copy-done.11
  127.1 7.0 %collective-permute-done.15.refs_2_.refs_3_ = bf16[8,192,128]{2,1,0:T(8,128)(2,1)S(1)} collective-permute-done((bf16[8,192,128]{2,1,0:T(8,128)(2,1)}, bf16[8,192,128]{2,1,0:T(8,128)(2,1)S(1)}, u32[]{:S(2)}, u32[]{:S(2)}) %collective-permute-start.15) | collective-permute-done | bytes 393248 | tf_op jit(solution)/shard_map/ppermute | solution.py:315
  134.2 2.1 %all-to-all-done.refs_1_.refs_4_ = bf16[4,32,4,16,128]{4,3,2,1,0:T(8,128)(2,1)S(1)} async-done(((bf16[4,32,4,16,128]{4,3,2,1,0:T(8,128)(2,1)}), bf16[4,32,4,16,128]{4,3,2,1,0:T(8,128)(2,1)S(1)}, u32[]{:S(2)}, u32[]{:S(2)}) %all-to-all-start) | async-done | bytes 2097184 | tf_op jit(solution)/shard_map/all_to_all | solution.py:359
  136.2 1.4 copy-done
  137.6 0.7 gate.5
  138.3 4.9 %all-to-all-start.1 = ((bf16[4,32,4,16,128]{4,3,2,1,0:T(8,128)(2,1)}), bf16[4,32,4,16,128]{4,3,2,1,0:T(8,128)(2,1)}, u32[]{:S(2)}, u32[]{:S(2)}) async-start(bf16[4,32,4,16,128]{4,3,2,1,0:T(8,128)(2,1)} %gate.5), calls=%async_computation.1 | async-start | bytes 4194304 | tf_op jit(solution)/shard_map/all_to_all | solution.py:359
  143.3 0.1 slice.16.wanted
  143.4 5.1 %down_1.2 = (bf16[16,192,128]{2,1,0:T(8,128)(2,1)}, bf16[16,192,128]{2,1,0:T(8,128)(2,1)}) custom-call(s32[1]{0:T(128)} %bitcast.1.side, s32[1]{0:T(128)} %bitcast.6.which, s32[2,128]{1,0:T(2,128)S(1)} %slice.16.wanted, f32[8,192,128]{2,1,0:T(8,128)} %get-tuple-element.49.refs_0_, f32[8,192,128]{2,1,0:T(8,128)} %get-tuple-element.50.refs_1_, ...), custom_call_target="tpu_custom_call" | custom-call | tf_op jit(solution)/shard_map/down_1/pallas_call | solution.py:293
  148.6 1.4 collective-permute-start.13
  150.0 4.5 %down_1.3 = f32[16,192,128]{2,1,0:T(8,128)} custom-call(s32[1]{0:T(128)} %bitcast.1.side, s32[1]{0:T(128)} %bitcast.2.which, s32[2,128]{1,0:T(2,128)S(1)} %slice.16.wanted, bf16[16,192,128]{2,1,0:T(8,128)(2,1)} %get-tuple-element.51.refs_0_, bf16[4,32,4,16,128]{4,3,2,1,0:T(8,128)(2,1)S(1)} %copy-done.1), custom_call_target="tpu_custom_call" | custom-call | tf_op jit(solution)/shard_map/down_1/pallas_call | solution.py:293
  154.4 1.7 add_convert_fusion
  156.1 1.7 collective-permute-start.18
  157.8 17.7 %collective-permute-done.13.refs_3_ = bf16[8,192,128]{2,1,0:T(8,128)(2,1)S(1)} collective-permute-done((bf16[8,192,128]{2,1,0:T(8,128)(2,1)S(1)}, bf16[8,192,128]{2,1,0:T(8,128)(2,1)S(1)}, u32[]{:S(2)}, u32[]{:S(2)}) %collective-permute-start.13) | collective-permute-done | bytes 393248 | tf_op jit(solution)/shard_map/ppermute | solution.py:315
  175.5 8.0 %all-to-all-done.1.refs_4_.refs_1_ = bf16[4,32,4,16,128]{4,3,2,1,0:T(8,128)(2,1)} async-done(((bf16[4,32,4,16,128]{4,3,2,1,0:T(8,128)(2,1)}), bf16[4,32,4,16,128]{4,3,2,1,0:T(8,128)(2,1)}, u32[]{:S(2)}, u32[]{:S(2)}) %all-to-all-start.1) | async-done | bytes 2097184 | tf_op jit(solution)/shard_map/all_to_all | solution.py:359
  183.6 5.3 %down_0.2 = (bf16[16,192,128]{2,1,0:T(8,128)(2,1)}, bf16[16,192,128]{2,1,0:T(8,128)(2,1)}) custom-call(s32[1]{0:T(128)} %bitcast.1.side, s32[1]{0:T(128)} %bitcast.6.which, s32[2,128]{1,0:T(2,128)S(1)} %slice.16.wanted, f32[8,192,128]{2,1,0:T(8,128)} %get-tuple-element.35.refs_0_, f32[8,192,128]{2,1,0:T(8,128)} %get-tuple-element.40.refs_1_, ...), custom_call_target="tpu_custom_call" | custom-call | tf_op jit(solution)/shard_map/down_0/pallas_call | solution.py:293
  189.5 4.6 %down_0.3 = f32[16,192,128]{2,1,0:T(8,128)} custom-call(s32[1]{0:T(128)} %bitcast.1.side, s32[1]{0:T(128)} %bitcast.2.which, s32[2,128]{1,0:T(2,128)S(1)} %slice.16.wanted, bf16[16,192,128]{2,1,0:T(8,128)(2,1)} %get-tuple-element.47.refs_0_, bf16[4,32,4,16,128]{4,3,2,1,0:T(8,128)(2,1)} %all-to-all-done.1.refs_4_.refs_1_), custom_call_target="tpu_custom_call" | custom-call | tf_op jit(solution)/shard_map/down_0/pallas_call | solution.py:293
  194.2 9.0 %collective-permute-done.18 = bf16[16,192,128]{2,1,0:T(8,128)(2,1)S(1)} collective-permute-done((bf16[16,192,128]{2,1,0:T(8,128)(2,1)S(1)}, bf16[16,192,128]{2,1,0:T(8,128)(2,1)S(1)}, u32[]{:S(2)}, u32[]{:S(2)}) %collective-permute-start.18) | collective-permute-done | bytes 786464 | tf_op jit(solution)/shard_map/ppermute | solution.py:315
  203.2 2.7 %fusion.1 = bf16[192,2048]{1,0:T(8,128)(2,1)} fusion(bf16[192,2048]{1,0:T(8,128)(2,1)S(1)} %copy-done.20, pred[192]{0:T(512)(128)(4,1)S(1)} %iota_compare_fusion.1, bf16[16,192,128]{2,1,0:T(8,128)(2,1)S(1)} %collective-permute-done.18, f32[16,192,128]{2,1,0:T(8,128)} %down_0.3, bf16[16,192,128]{2,1,0:T(8,128)(2,1)S(1)} %collective-permute-done.16), kind=kLoop, calls=%fused_computation.2 | loop fusion | flops 3145728 | bytes 4718784 | tf_op jit(solution)/shard_map/convert_element_type | solution.py:399
  (67 shorter events, 0.7 us)
Async XLA Ops:
  0.0 7.5 %collective-permute-start = (s32[1]{0:T(128)}, s32[1]{0:T(128)}, u32[]{:S(2)}, u32[]{:S(2)}) collective-permute-start(s32[1]{0:T(128)} %param.14), channel_id=1, source_target_pairs={{0,8},{2,10},{4,12},{6,14},{8,0},{10,2},{12,4},{14,6},{1,9},{3,11}... | collective-permute-start | bytes 20 | tf_op jit(solution)/shard_map/ppermute | solution.py:315
  4.0 4.7 %collective-permute-start.1 = (bf16[192,2048]{1,0:T(8,128)(2,1)}, bf16[192,2048]{1,0:T(8,128)(2,1)S(1)}, u32[]{:S(2)}, u32[]{:S(2)}) collective-permute-start(bf16[192,2048]{1,0:T(8,128)(2,1)} %own_ref.1), channel_id=1, source_target_pairs={{0,1},{1,0},{2,3},{3,2},{4,5},{5,4},{6,7},{7,6},{8,9},{9,8},{10,11... | collective-permute-start | bytes 2359304 | tf_op jit(solution)/shard_map/ppermute | solution.py:315
  8.8 0.9 copy-start.21
  13.3 21.1 %collective-permute-start.4 = (bf16[8,192,128]{2,1,0:T(8,128)(2,1)}, bf16[8,192,128]{2,1,0:T(8,128)(2,1)S(1)}, u32[]{:S(2)}, u32[]{:S(2)}) collective-permute-start(bf16[8,192,128]{2,1,0:T(8,128)(2,1)} %get-tuple-element.29.refs_1_.refs_0_), channel_id=1, source_target_pairs={{0,8},{2,10},{4,12},{6,14},{8,0},{10,2},{12,4},{14,6},{1,9},{3,11}... | collective-permute-start | bytes 1179656 | tf_op jit(solution)/shard_map/ppermute | solution.py:315
  15.1 3.6 %collective-permute-start.2 = (s32[2]{0:T(128)}, s32[2]{0:T(128)S(1)}, u32[]{:S(2)}, u32[]{:S(2)}) collective-permute-start(s32[2]{0:T(128)} %gate.3), channel_id=1, source_target_pairs={{0,2},{2,0},{4,6},{6,4},{8,10},{10,8},{12,14},{14,12},{1,3},{3,1},... | collective-permute-start | bytes 32 | tf_op jit(solution)/shard_map/ppermute | solution.py:315
  19.4 3.5 %collective-permute-start.3 = (s32[4]{0:T(128)S(1)}, s32[4]{0:T(128)S(1)}, u32[]{:S(2)}, u32[]{:S(2)}) collective-permute-start(s32[4]{0:T(128)S(1)} %pad_add_fusion.1), channel_id=1, source_target_pairs={{0,4},{2,6},{4,0},{6,2},{8,12},{10,14},{12,8},{14,10},{1,5},{3,7},... | collective-permute-start | bytes 56 | tf_op jit(solution)/shard_map/ppermute | solution.py:315
  28.6 12.8 %collective-permute-start.6 = (bf16[2,16,4,16,128]{4,3,2,1,0:T(8,128)(2,1)}, bf16[2,16,4,16,128]{4,3,2,1,0:T(8,128)(2,1)S(1)}, u32[]{:S(2)}, u32[]{:S(2)}) collective-permute-start(bf16[2,16,4,16,128]{4,3,2,1,0:T(8,128)(2,1)} %get-tuple-element.32), channel_id=1, source_target_pairs={{0,2},{2,0},{4,6},{6,4},{8,10},{10,8},{12,14},{14,12},{1,3},{3,1},... | collective-permute-start | bytes 1572872 | tf_op jit(solution)/shard_map/ppermute | solution.py:315
  30.2 17.3 %collective-permute-start.7 = (bf16[2,16,4,16,128]{4,3,2,1,0:T(8,128)(2,1)}, bf16[2,16,4,16,128]{4,3,2,1,0:T(8,128)(2,1)S(1)}, u32[]{:S(2)}, u32[]{:S(2)}) collective-permute-start(bf16[2,16,4,16,128]{4,3,2,1,0:T(8,128)(2,1)} %get-tuple-element.33), channel_id=1, source_target_pairs={{0,4},{2,6},{4,0},{6,2},{8,12},{10,14},{12,8},{14,10},{1,5},{3,7},... | collective-permute-start | bytes 1572872 | tf_op jit(solution)/shard_map/ppermute | solution.py:315
  32.5 25.4 %collective-permute-start.8 = (bf16[2,16,4,16,128]{4,3,2,1,0:T(8,128)(2,1)}, bf16[2,16,4,16,128]{4,3,2,1,0:T(8,128)(2,1)}, u32[]{:S(2)}, u32[]{:S(2)}) collective-permute-start(bf16[2,16,4,16,128]{4,3,2,1,0:T(8,128)(2,1)} %get-tuple-element.34), channel_id=1, source_target_pairs={{0,6},{2,4},{4,2},{6,0},{8,14},{10,12},{12,10},{14,8},{1,7},{3,5},... | collective-permute-start | bytes 1572872 | tf_op jit(solution)/shard_map/ppermute | solution.py:315
  34.4 23.5 %collective-permute-start.5 = (bf16[8,192,128]{2,1,0:T(8,128)(2,1)S(1)}, bf16[8,192,128]{2,1,0:T(8,128)(2,1)S(1)}, u32[]{:S(2)}, u32[]{:S(2)}) collective-permute-start(bf16[8,192,128]{2,1,0:T(8,128)(2,1)S(1)} %collective-permute-done.4.far_a_ref.refs_1_), channel_id=1, source_target_pairs={{0,1},{1,0},{2,3},{3,2},{4,5},{5,4},{6,7},{7,6},{8,9},{9,8},{10,11... | collective-permute-start | bytes 1179656 | tf_op jit(solution)/shard_map/ppermute | solution.py:315
  34.7 23.3 %copy-start.2 = (bf16[32,192,128]{2,1,0:T(8,128)(2,1)S(1)}, bf16[32,192,128]{2,1,0:T(8,128)(2,1)}, u32[]{:S(2)}) copy-start(bf16[32,192,128]{2,1,0:T(8,128)(2,1)} %get-tuple-element.30.own_ref) | copy-start | bytes 4718596
  34.7 23.3 %copy-start.10 = (bf16[2,16,4,16,128]{4,3,2,1,0:T(8,128)(2,1)S(1)}, bf16[2,16,4,16,128]{4,3,2,1,0:T(8,128)(2,1)}, u32[]{:S(2)}) copy-start(bf16[2,16,4,16,128]{4,3,2,1,0:T(8,128)(2,1)} %get-tuple-element.31.refs_0_) | copy-start | bytes 1572868
  39.3 33.2 %collective-permute-start.9 = (bf16[2,16,4,16,128]{4,3,2,1,0:T(8,128)(2,1)}, bf16[2,16,4,16,128]{4,3,2,1,0:T(8,128)(2,1)S(1)}, u32[]{:S(2)}, u32[]{:S(2)}) collective-permute-start(bf16[2,16,4,16,128]{4,3,2,1,0:T(8,128)(2,1)} %get-tuple-element.37), channel_id=1, source_target_pairs={{0,2},{2,0},{4,6},{6,4},{8,10},{10,8},{12,14},{14,12},{1,3},{3,1},... | collective-permute-start | bytes 1572872 | tf_op jit(solution)/shard_map/ppermute | solution.py:315
  41.4 35.2 %collective-permute-start.10 = (bf16[2,16,4,16,128]{4,3,2,1,0:T(8,128)(2,1)}, bf16[2,16,4,16,128]{4,3,2,1,0:T(8,128)(2,1)S(1)}, u32[]{:S(2)}, u32[]{:S(2)}) collective-permute-start(bf16[2,16,4,16,128]{4,3,2,1,0:T(8,128)(2,1)} %get-tuple-element.38), channel_id=1, source_target_pairs={{0,4},{2,6},{4,0},{6,2},{8,12},{10,14},{12,8},{14,10},{1,5},{3,7},... | collective-permute-start | bytes 1572872 | tf_op jit(solution)/shard_map/ppermute | solution.py:315
  47.4 41.2 %collective-permute-start.11 = (bf16[2,16,4,16,128]{4,3,2,1,0:T(8,128)(2,1)}, bf16[2,16,4,16,128]{4,3,2,1,0:T(8,128)(2,1)S(1)}, u32[]{:S(2)}, u32[]{:S(2)}) collective-permute-start(bf16[2,16,4,16,128]{4,3,2,1,0:T(8,128)(2,1)} %get-tuple-element.39), channel_id=1, source_target_pairs={{0,6},{2,4},{4,2},{6,0},{8,14},{10,12},{12,10},{14,8},{1,7},{3,5},... | collective-permute-start | bytes 1572872 | tf_op jit(solution)/shard_map/ppermute | solution.py:315
  58.0 4.4 %copy-start.17 = (bf16[8,192,128]{2,1,0:T(8,128)(2,1)}, bf16[8,192,128]{2,1,0:T(8,128)(2,1)S(1)}, u32[]{:S(2)}) copy-start(bf16[8,192,128]{2,1,0:T(8,128)(2,1)S(1)} %collective-permute-done.5.far_b_ref) | copy-start | bytes 1179652
  58.0 7.5 %copy-start.22 = (s32[64,32,32]{0,2,1:T(8,128)S(1)}, s32[64,32,32]{0,2,1:T(8,128)}, u32[]{:S(2)}) copy-start(s32[64,32,32]{0,2,1:T(8,128)} %param.13) | copy-start | bytes 786436
  62.4 26.3 %collective-permute-start.14 = (bf16[8,192,128]{2,1,0:T(8,128)(2,1)}, bf16[8,192,128]{2,1,0:T(8,128)(2,1)S(1)}, u32[]{:S(2)}, u32[]{:S(2)}) collective-permute-start(bf16[8,192,128]{2,1,0:T(8,128)(2,1)} %get-tuple-element.45), channel_id=1, source_target_pairs={{0,8},{2,10},{4,12},{6,14},{8,0},{10,2},{12,4},{14,6},{1,9},{3,11}... | collective-permute-start | bytes 1179656 | tf_op jit(solution)/shard_map/ppermute | solution.py:315
  66.0 22.7 %copy-start.23 = (s32[8,32,4]{1,0,2:T(8,128)}, s32[8,32,4]{1,0,2:T(8,128)S(1)}, u32[]{:S(2)}) copy-start(s32[8,32,4]{1,0,2:T(8,128)S(1)} %fusion.6) | copy-start | bytes 12292
  72.5 16.2 %copy-start.4 = (bf16[2,16,4,16,128]{4,3,2,1,0:T(8,128)(2,1)}, bf16[2,16,4,16,128]{4,3,2,1,0:T(8,128)(2,1)S(1)}, u32[]{:S(2)}) copy-start(bf16[2,16,4,16,128]{4,3,2,1,0:T(8,128)(2,1)S(1)} %collective-permute-done.9.refs_1_.refs_2_) | copy-start | bytes 1572868
  76.6 12.1 %copy-start.6 = (bf16[2,16,4,16,128]{4,3,2,1,0:T(8,128)(2,1)}, bf16[2,16,4,16,128]{4,3,2,1,0:T(8,128)(2,1)S(1)}, u32[]{:S(2)}) copy-start(bf16[2,16,4,16,128]{4,3,2,1,0:T(8,128)(2,1)S(1)} %collective-permute-done.10.refs_2_.refs_3_) | copy-start | bytes 1572868
  88.7 0.8 copy-start.8
  88.7 1.0 copy-start.13
  90.3 3.9 %copy-start.5 = (bf16[2,16,4,16,128]{4,3,2,1,0:T(8,128)(2,1)S(1)}, bf16[2,16,4,16,128]{4,3,2,1,0:T(8,128)(2,1)}, u32[]{:S(2)}) copy-start(bf16[2,16,4,16,128]{4,3,2,1,0:T(8,128)(2,1)} %copy-done.4) | copy-start | bytes 1572868
  90.3 3.9 %copy-start.7 = (bf16[2,16,4,16,128]{4,3,2,1,0:T(8,128)(2,1)S(1)}, bf16[2,16,4,16,128]{4,3,2,1,0:T(8,128)(2,1)}, u32[]{:S(2)}) copy-start(bf16[2,16,4,16,128]{4,3,2,1,0:T(8,128)(2,1)} %copy-done.6) | copy-start | bytes 1572868
  90.3 45.9 %all-to-all-start = ((bf16[4,32,4,16,128]{4,3,2,1,0:T(8,128)(2,1)}), bf16[4,32,4,16,128]{4,3,2,1,0:T(8,128)(2,1)S(1)}, u32[]{:S(2)}, u32[]{:S(2)}) async-start(bf16[4,32,4,16,128]{4,3,2,1,0:T(8,128)(2,1)} %gate.4), calls=%async_computation | async-start | bytes 4194304 | tf_op jit(solution)/shard_map/all_to_all | solution.py:359
  94.1 32.3 %collective-permute-start.12 = (bf16[8,192,128]{2,1,0:T(8,128)(2,1)}, bf16[8,192,128]{2,1,0:T(8,128)(2,1)S(1)}, u32[]{:S(2)}, u32[]{:S(2)}) collective-permute-start(bf16[8,192,128]{2,1,0:T(8,128)(2,1)} %get-tuple-element.41), channel_id=1, source_target_pairs={{0,8},{2,10},{4,12},{6,14},{8,0},{10,2},{12,4},{14,6},{1,9},{3,11}... | collective-permute-start | bytes 1179656 | tf_op jit(solution)/shard_map/ppermute | solution.py:315
  94.3 1.4 copy-start.3
  95.7 1.0 copy-start.9
  96.7 1.0 copy-start.18
  97.7 1.0 copy-start.19
  102.1 32.1 %collective-permute-start.15 = (bf16[8,192,128]{2,1,0:T(8,128)(2,1)}, bf16[8,192,128]{2,1,0:T(8,128)(2,1)S(1)}, u32[]{:S(2)}, u32[]{:S(2)}) collective-permute-start(bf16[8,192,128]{2,1,0:T(8,128)(2,1)} %get-tuple-element.46), channel_id=1, source_target_pairs={{0,8},{2,10},{4,12},{6,14},{8,0},{10,2},{12,4},{14,6},{1,9},{3,11}... | collective-permute-start | bytes 1179656 | tf_op jit(solution)/shard_map/ppermute | solution.py:315
  126.4 0.8 copy-start.11
  134.2 2.1 %copy-start.15 = (bf16[8,192,128]{2,1,0:T(8,128)(2,1)}, bf16[8,192,128]{2,1,0:T(8,128)(2,1)S(1)}, u32[]{:S(2)}) copy-start(bf16[8,192,128]{2,1,0:T(8,128)(2,1)S(1)} %collective-permute-done.15.refs_2_.refs_3_) | copy-start | bytes 1179652
  136.2 1.4 copy-start
  138.3 4.9 %slice-start = ((s32[8,32,4]{1,0,2:T(8,128)}), s32[2,32,4]{1,0,2:T(2,128)S(1)}, s32[]{:S(2)}) async-start(s32[8,32,4]{1,0,2:T(8,128)} %copy-done.23), calls=%async_computation.2 | async-start | bytes 8192 | tf_op jit(solution)/shard_map/slice | solution.py:381
  138.3 5.1 %copy-start.1 = (bf16[4,32,4,16,128]{4,3,2,1,0:T(8,128)(2,1)S(1)}, bf16[4,32,4,16,128]{4,3,2,1,0:T(8,128)(2,1)}, u32[]{:S(2)}) copy-start(bf16[4,32,4,16,128]{4,3,2,1,0:T(8,128)(2,1)} %copy-done) | copy-start | bytes 6291460
  138.3 5.1 %copy-start.14 = (bf16[8,192,128]{2,1,0:T(8,128)(2,1)S(1)}, bf16[8,192,128]{2,1,0:T(8,128)(2,1)}, u32[]{:S(2)}) copy-start(bf16[8,192,128]{2,1,0:T(8,128)(2,1)} %copy-done.13) | copy-start | bytes 1179652
  138.3 5.1 %copy-start.16 = (bf16[8,192,128]{2,1,0:T(8,128)(2,1)S(1)}, bf16[8,192,128]{2,1,0:T(8,128)(2,1)}, u32[]{:S(2)}) copy-start(bf16[8,192,128]{2,1,0:T(8,128)(2,1)} %copy-done.15) | copy-start | bytes 1179652
  138.3 45.3 %all-to-all-start.1 = ((bf16[4,32,4,16,128]{4,3,2,1,0:T(8,128)(2,1)}), bf16[4,32,4,16,128]{4,3,2,1,0:T(8,128)(2,1)}, u32[]{:S(2)}, u32[]{:S(2)}) async-start(bf16[4,32,4,16,128]{4,3,2,1,0:T(8,128)(2,1)} %gate.5), calls=%async_computation.1 | async-start | bytes 4194304 | tf_op jit(solution)/shard_map/all_to_all | solution.py:359
  143.4 5.2 %copy-start.24 = (bf16[8,192,128]{2,1,0:T(8,128)(2,1)S(1)}, bf16[8,192,128]{2,1,0:T(8,128)(2,1)}, u32[]{:S(2)}) copy-start(bf16[8,192,128]{2,1,0:T(8,128)(2,1)} %get-tuple-element.42) | copy-start | bytes 1179652
  148.6 5.9 %collective-permute-start.17 = (bf16[16,192,128]{2,1,0:T(8,128)(2,1)}, bf16[16,192,128]{2,1,0:T(8,128)(2,1)S(1)}, u32[]{:S(2)}, u32[]{:S(2)}) collective-permute-start(bf16[16,192,128]{2,1,0:T(8,128)(2,1)} %get-tuple-element.52), channel_id=1, source_target_pairs={{0,1},{1,0},{2,3},{3,2},{4,5},{5,4},{6,7},{7,6},{8,9},{9,8},{10,11... | collective-permute-start | bytes 2359304 | tf_op jit(solution)/shard_map/ppermute | solution.py:315
  148.6 26.9 %collective-permute-start.13 = (bf16[8,192,128]{2,1,0:T(8,128)(2,1)S(1)}, bf16[8,192,128]{2,1,0:T(8,128)(2,1)S(1)}, u32[]{:S(2)}, u32[]{:S(2)}) collective-permute-start(bf16[8,192,128]{2,1,0:T(8,128)(2,1)S(1)} %copy-done.24), channel_id=1, source_target_pairs={{0,8},{2,10},{4,12},{6,14},{8,0},{10,2},{12,4},{14,6},{1,9},{3,11}... | collective-permute-start | bytes 1179656 | tf_op jit(solution)/shard_map/ppermute | solution.py:315
  154.4 29.1 %copy-start.12 = (bf16[8,192,128]{2,1,0:T(8,128)(2,1)S(1)}, bf16[8,192,128]{2,1,0:T(8,128)(2,1)}, u32[]{:S(2)}) copy-start(bf16[8,192,128]{2,1,0:T(8,128)(2,1)} %copy-done.11) | copy-start | bytes 1179652
  156.1 47.1 %collective-permute-start.18 = (bf16[16,192,128]{2,1,0:T(8,128)(2,1)S(1)}, bf16[16,192,128]{2,1,0:T(8,128)(2,1)S(1)}, u32[]{:S(2)}, u32[]{:S(2)}) collective-permute-start(bf16[16,192,128]{2,1,0:T(8,128)(2,1)S(1)} %add_convert_fusion), channel_id=1, source_target_pairs={{0,8},{2,10},{4,12},{6,14},{8,0},{10,2},{12,4},{14,6},{1,9},{3,11}... | collective-permute-start | bytes 2359304 | tf_op jit(solution)/shard_map/ppermute | solution.py:315
  188.9 14.3 %collective-permute-start.16 = (bf16[16,192,128]{2,1,0:T(8,128)(2,1)}, bf16[16,192,128]{2,1,0:T(8,128)(2,1)S(1)}, u32[]{:S(2)}, u32[]{:S(2)}) collective-permute-start(bf16[16,192,128]{2,1,0:T(8,128)(2,1)} %get-tuple-element.48), channel_id=1, source_target_pairs={{0,1},{1,0},{2,3},{3,2},{4,5},{5,4},{6,7},{7,6},{8,9},{9,8},{10,11... | collective-permute-start | bytes 2359304 | tf_op jit(solution)/shard_map/ppermute | solution.py:315
  189.5 13.7 %copy-start.20 = (bf16[192,2048]{1,0:T(8,128)(2,1)S(1)}, bf16[192,2048]{1,0:T(8,128)(2,1)}, u32[]{:S(2)}) copy-start(bf16[192,2048]{1,0:T(8,128)(2,1)} %own_ref.1) | copy-start | bytes 2359300
